TPU v7x, 256 devices: a whole 4x4x8 slice. The times are simulated.
256 devices in a mesh: snp: 16 (over z, y_hi), samp: 16 (over y_lo, x, core).
Axes of the slice: x: 4, y: 4 (y_hi: 2, y_lo: 2; y = y_hi * 2 + y_lo), z: 8, core: 2. Of those that a mesh axis runs over, the one named last changes fastest.
Arguments:
- dosage: bfloat16 [20480, 16384], P('samp', 'snp'), may hold values from 0 to 2, as said below
- observed: int32 [20480, 16384], P('samp', 'snp'), may hold values 0 or 1
- band: int32 [16], replicated, may hold values from 1 to 2
Outputs:
- linkage: float32 [16384, 5120], P(('snp', 'samp'))
Inputs may be any that keep to these rules, and one draw needn't show every extreme that they name: `dosage`: real-valued dosages.
All inputs are finite; a program needn't handle non-finite values. No bound on the sum of `observed` on one device may be relied on, other than what follows from the above.
Results may differ from a plain program's by a relative error of at most 0.00055.
Values may be sent and summed in bfloat16 or wider, within the bound.
No kernel may reach another device: no remote copies, remote signals or barrier semaphores. Data moves between devices by JAX's collectives and lax.ppermute only.
A program may use at most 128 MiB of HBM per device.

v0:
```python
import jax
import jax.numpy as jnp
from jax import lax
from jax.sharding import PartitionSpec as P

eps = 1e-05


def from_behind(x, axis, by):
    count = lax.axis_size(axis)
    pairs = [(i, i + by) for i in range(count) if 0 <= i + by < count]
    return lax.ppermute(x, axis, pairs)


def pair_kept(band, mine, offset):
    total = band.shape[0]
    other = mine + offset
    inside = (other >= 0) & (other < total)
    other_band = band[jnp.clip(other, 0, total - 1)]
    keep = inside & (abs(offset) <= jnp.minimum(band[mine], other_band))
    return jnp.where(keep, 1.0, 0.0).astype(jnp.float32)


def products(left, right):
    return lax.dot_general(
        left, right, (((0,), (0,)), ((), ())), preferred_element_type=jnp.float32
    )


def on_device(dosage, observed, band):
    width = dosage.shape[1]
    mine = lax.axis_index("snp")
    weight = observed.astype(jnp.float32)
    values = dosage.astype(jnp.float32)
    cnt, first, second = lax.psum(
        (
            jnp.sum(weight, axis=0),
            jnp.sum(weight * values, axis=0),
            jnp.sum(weight * values * values, axis=0),
        ),
        "samp",
    )
    mean = first / cnt
    spread = second - first * mean
    zed = (weight * (values - mean) * lax.rsqrt(spread + eps * cnt)).astype(jnp.bfloat16)
    keeps = [pair_kept(band, mine, offset) for offset in (-2, -1, 0, 1, 2)]
    ahead = [zed]
    for step in (1, 2):
        ahead.append(from_behind(zed, "snp", -step))
    forward = products(zed, jnp.concatenate(ahead, axis=1))
    full = jnp.concatenate(
        [forward[:, 2 * width :].T, forward[:, width : 2 * width].T, forward], axis=1
    )
    rows = lax.psum_scatter(full, "samp", scatter_dimension=0, tiled=True)
    outgoing = [rows[:, width : 2 * width] * keeps[3], rows[:, :width] * keeps[4]]
    arrived = []
    for step in (1, 2):
        arrived.append(from_behind(outgoing[step - 1], "snp", step))
    linkage = jnp.concatenate(
        [
            arrived[1],
            arrived[0],
            rows[:, 2 * width : 3 * width] * keeps[2],
            rows[:, 3 * width : 4 * width] * keeps[3],
            rows[:, 4 * width :] * keeps[4],
        ],
        axis=1,
    )
    return linkage


def solution(mesh):
    return jax.shard_map(
        on_device,
        mesh=mesh,
        in_specs=(P("samp", "snp"), P("samp", "snp"), P()),
        out_specs=P(("snp", "samp"), None),
        check_vma=False,
    )
```

profile of v0, /device:TPU:64, one launch (start us, length us, event | category | flops | bytes accessed | tf_op | source)
XLA Modules:
  0.0 381.7 jit_solution(6292134392581566059)
XLA Ops:
  6.5 0.0 copy-start.1
  6.5 0.0 reduce-scatter.2.cloned.1.call-start
  6.5 4.8 %fusion.10 = (f32[1024]{0:T(1024)S(1)}, f32[1024]{0:T(1024)S(1)}, f32[1024]{0:T(1024)S(1)}) fusion(bf16[1280,1024]{1,0:T(8,128)(2,1)} %param.3, s32[1280,1024]{1,0:T(8,128)} %param.4), kind=kLoop, calls=%fused_computation.15 | loop fusion | flops 9171968 | bytes 7876608 | tf_op jit(solution)/shard_map/reduce_sum | solution.py:38
  11.3 56.0 %all-reduce = (f32[1024]{0:T(1024)S(1)}, f32[1024]{0:T(1024)S(1)}, f32[1024]{0:T(1024)S(1)}) all-reduce(f32[1024]{0:T(1024)S(1)} %get-tuple-element.7, f32[1024]{0:T(1024)S(1)} %get-tuple-element.6, f32[1024]{0:T(1024)S(1)} %get-tuple-element.5), channel_id=1, replica_groups=mesh['snp'=16,'samp'=16] {'samp'}, use_global_device_ids=true, to_apply=%region_3.0 | all-reduce | flops 3072 | bytes 24576 | tf_op jit(solution)/shard_map/psum | solution.py:35
  67.3 0.0 copy-done.1
  67.3 3.6 fusion.8
  70.9 0.0 copy-start.2
  70.9 4.4 %collective-permute-start = (bf16[1280,1024]{1,0:T(8,128)(2,1)S(1)}, bf16[1280,1024]{1,0:T(8,128)(2,1)S(1)}, u32[]{:S(2)}, u32[]{:S(2)}) collective-permute-start(bf16[1280,1024]{1,0:T(8,128)(2,1)S(1)} %fusion.8), channel_id=1, source_target_pairs={{16,0},{32,16},{48,32},{64,48},{80,64},{96,80},{112,96},{128,112},... | collective-permute-start | bytes 7864328 | tf_op jit(solution)/shard_map/ppermute | solution.py:12
  75.3 2.0 collective-permute-start.1
  77.3 55.3 %collective-permute-done = bf16[1280,1024]{1,0:T(8,128)(2,1)S(1)} collective-permute-done((bf16[1280,1024]{1,0:T(8,128)(2,1)S(1)}, bf16[1280,1024]{1,0:T(8,128)(2,1)S(1)}, u32[]{:S(2)}, u32[]{:S(2)}) %collective-permute-start) | collective-permute-done | bytes 2621472 | tf_op jit(solution)/shard_map/ppermute | solution.py:12
  132.6 0.0 copy-done.2
  132.6 53.7 %collective-permute-done.1 = bf16[1280,1024]{1,0:T(8,128)(2,1)} collective-permute-done((bf16[1280,1024]{1,0:T(8,128)(2,1)S(1)}, bf16[1280,1024]{1,0:T(8,128)(2,1)}, u32[]{:S(2)}, u32[]{:S(2)}) %collective-permute-start.1) | collective-permute-done | bytes 2621472 | tf_op jit(solution)/shard_map/ppermute | solution.py:12
  186.2 12.7 %fusion = f32[1024,3072]{1,0:T(8,128)S(1)} fusion(bf16[1280,1024]{1,0:T(8,128)(2,1)} %copy-done.2, bf16[1280,1024]{1,0:T(8,128)(2,1)} %collective-permute-done.1, bf16[1280,1024]{1,0:T(8,128)(2,1)S(1)} %collective-permute-done), kind=kOutput, calls=%fused_computation.1 | convolution fusion | flops 8076656640 | bytes 20447232 | tf_op jit(solution)/shard_map/dot_general | solution.py:25
  198.9 0.0 copy-start
  198.9 4.7 %fusion.15 = (f32[1024,1024]{1,0:T(8,128)}, f32[1024,1024]{1,0:T(8,128)}) fusion(f32[1024,3072]{1,0:T(8,128)S(1)} %fusion), kind=kLoop, calls=%fused_computation.28 | loop fusion | bytes 16777216 | tf_op jit(solution)/shard_map/slice | solution.py:52
  203.6 2.3 copy-done
  205.9 5.4 %copy.6 = f32[1024,1024]{0,1:T(8,128)} copy(f32[1024,1024]{1,0:T(8,128)} %get-tuple-element.13) | data formatting | bytes 8388608
  211.3 5.4 %copy.7 = f32[1024,1024]{0,1:T(8,128)} copy(f32[1024,1024]{1,0:T(8,128)} %get-tuple-element.14) | data formatting | bytes 8388608
  216.6 15.7 %pad_maximum_fusion = f32[1024,5120]{1,0:T(8,128)} fusion(f32[1024,3072]{1,0:T(8,128)} %copy-done, f32[1024,1024]{1,0:T(8,128)} %bitcast.7, f32[1024,1024]{1,0:T(8,128)} %bitcast.6), kind=kLoop, calls=%fused_computation | loop fusion | flops 10485760 | bytes 41943040 | tf_op jit(solution)/shard_map/concatenate | solution.py:51
  232.3 0.0 copy-start.4
  232.3 0.0 reduce-scatter.2.cloned.1.call-update
  232.4 0.6 copy-done.4
  233.0 0.7 fusion.16
  236.1 116.4 %reduce-scatter.2.cloned.1.call-done = f32[64,5120]{1,0:T(8,128)} async-done(((f32[1024,5120]{1,0:T(8,128)}), f32[64,5120]{1,0:T(8,128)}) %reduce-scatter.2.cloned.1.call-update) | async-done | bytes 1310736 | tf_op jit(solution)/shard_map/reduce_scatter | solution.py:54
  352.6 1.1 slice_multiply_fusion.3
  353.6 3.4 collective-permute-start.2
  357.1 4.6 %collective-permute-start.3 = (f32[64,1024]{1,0:T(8,128)S(1)}, f32[64,1024]{1,0:T(8,128)S(1)}, u32[]{:S(2)}, u32[]{:S(2)}) collective-permute-start(f32[64,1024]{1,0:T(8,128)S(1)} %get-tuple-element.15), channel_id=1, source_target_pairs={{0,16},{16,32},{32,48},{48,64},{64,80},{80,96},{96,112},{112,128},... | collective-permute-start | bytes 786440 | tf_op jit(solution)/shard_map/ppermute | solution.py:12
  362.9 0.0 collective-permute-done.2
  363.0 7.2 %collective-permute-done.3 = f32[64,1024]{1,0:T(8,128)S(1)} collective-permute-done((f32[64,1024]{1,0:T(8,128)S(1)}, f32[64,1024]{1,0:T(8,128)S(1)}, u32[]{:S(2)}, u32[]{:S(2)}) %collective-permute-start.3) | collective-permute-done | bytes 262176 | tf_op jit(solution)/shard_map/ppermute | solution.py:12
  370.2 1.0 fusion.13
  371.2 1.0 fusion.12
  372.2 0.0 copy-start.3
  372.2 1.0 copy-done.3
  373.2 1.7 fusion.11
  (3 shorter events, 0.0 us)
Async XLA Ops:
  6.5 60.8 %copy-start.1 = (bf16[1280,1024]{1,0:T(8,128)(2,1)S(1)}, bf16[1280,1024]{1,0:T(8,128)(2,1)}, u32[]{:S(2)}) copy-start(bf16[1280,1024]{1,0:T(8,128)(2,1)} %param.3) | copy-start | bytes 7864324
  6.5 346.0 %reduce-scatter.2.cloned.1.call-start = ((), (), s32[]{:S(2)}) async-start(), calls=%async_computation.1 | async-start | bytes 22282240 | tf_op jit(solution)/shard_map/reduce_scatter | solution.py:54
  70.9 61.7 %copy-start.2 = (bf16[1280,1024]{1,0:T(8,128)(2,1)}, bf16[1280,1024]{1,0:T(8,128)(2,1)S(1)}, u32[]{:S(2)}) copy-start(bf16[1280,1024]{1,0:T(8,128)(2,1)S(1)} %fusion.8) | copy-start | bytes 7864324
  70.9 61.7 %collective-permute-start = (bf16[1280,1024]{1,0:T(8,128)(2,1)S(1)}, bf16[1280,1024]{1,0:T(8,128)(2,1)S(1)}, u32[]{:S(2)}, u32[]{:S(2)}) collective-permute-start(bf16[1280,1024]{1,0:T(8,128)(2,1)S(1)} %fusion.8), channel_id=1, source_target_pairs={{16,0},{32,16},{48,32},{64,48},{80,64},{96,80},{112,96},{128,112},... | collective-permute-start | bytes 7864328 | tf_op jit(solution)/shard_map/ppermute | solution.py:12
  75.3 111.0 %collective-permute-start.1 = (bf16[1280,1024]{1,0:T(8,128)(2,1)S(1)}, bf16[1280,1024]{1,0:T(8,128)(2,1)}, u32[]{:S(2)}, u32[]{:S(2)}) collective-permute-start(bf16[1280,1024]{1,0:T(8,128)(2,1)S(1)} %fusion.8), channel_id=1, source_target_pairs={{32,0},{48,16},{64,32},{80,48},{96,64},{112,80},{128,96},{144,112}... | collective-permute-start | bytes 7864328 | tf_op jit(solution)/shard_map/ppermute | solution.py:12
  198.9 7.0 %copy-start = (f32[1024,3072]{1,0:T(8,128)}, f32[1024,3072]{1,0:T(8,128)S(1)}, u32[]{:S(2)}) copy-start(f32[1024,3072]{1,0:T(8,128)S(1)} %fusion) | copy-start | bytes 37748740
  232.3 0.7 copy-start.4
  353.6 9.3 %collective-permute-start.2 = (f32[64,1024]{1,0:T(8,128)S(1)}, f32[64,1024]{1,0:T(8,128)S(1)}, u32[]{:S(2)}, u32[]{:S(2)}) collective-permute-start(f32[64,1024]{1,0:T(8,128)S(1)} %get-tuple-element.16), channel_id=1, source_target_pairs={{0,32},{16,48},{32,64},{48,80},{64,96},{80,112},{96,128},{112,144}... | collective-permute-start | bytes 786440 | tf_op jit(solution)/shard_map/ppermute | solution.py:12
  357.1 13.1 %collective-permute-start.3 = (f32[64,1024]{1,0:T(8,128)S(1)}, f32[64,1024]{1,0:T(8,128)S(1)}, u32[]{:S(2)}, u32[]{:S(2)}) collective-permute-start(f32[64,1024]{1,0:T(8,128)S(1)} %get-tuple-element.15), channel_id=1, source_target_pairs={{0,16},{16,32},{32,48},{48,64},{64,80},{80,96},{96,112},{112,128},... | collective-permute-start | bytes 786440 | tf_op jit(solution)/shard_map/ppermute | solution.py:12
  372.2 1.1 copy-start.3
Sparse Core Ops, SparseCore 0:
  232.5 120.0 reduce-scatter.1
where the time goes:
time: 383 us; the launch traced here: 382 us
  waiting for transfers between devices  233 us (61%)
  blocking collectives  56 us (15%)
  other arithmetic  28.8 us (8%)
  local copies, waits for them, and re-layouts  20.1 us (5%)
  between operations  17.2 us (4%)
  starting transfers between devices  14.5 us (4%)
  matrix products  12.7 us (3%)
    reduce_scatter x1, waiting for transfers between devices, on_device(): rows = lax.psum_scatter(full, 'samp', scatter_dimension=0, tiled=True)  116 us
    ppermute x4, waiting for transfers between devices, from_behind(): return lax.ppermute(x, axis, pairs)  116 us
    psum x1, blocking collectives, on_device(): lax.psum((jnp.sum(weight, axis=0), jnp.sum(weight * values, axis=0), jnp....  56 us
    concatenate x1, other arithmetic, on_device(): jnp.concatenate([forward[:, 2 * width:].T, forward[:, width:2 * width].T,...  15.7 us
    unnamed x14, local copies, waits for them, and re-layouts  14.7 us
    ppermute x4, starting transfers between devices, from_behind(): return lax.ppermute(x, axis, pairs)  14.4 us
    dot_general x1, matrix products, products(): lax.dot_general(left, right, (((0,), (0,)), ((), ())), preferred_element_...  12.7 us
  transfers between devices with their start and end apart: 5, of which 4 were waited for; matrix products, arithmetic and copies ran while one was open for 0% of the time, Pallas kernels for 0%

commit v1 on v0

v1 whole, which is shorter than its diff:
```python
import jax
import jax.numpy as jnp
from jax import lax
from jax.experimental import pallas as pl
from jax.experimental.pallas import tpu as pltpu
from jax.sharding import Mesh
from jax.sharding import PartitionSpec as P

eps = 1e-05

AXES = ("z", "yh", "yl", "x", "core")
SIZES = (8, 2, 2, 4, 2)
SNP = ("z", "yh")
SAMP = ("yl", "x", "core")
CHIP = ("yl", "x")
NSNP = 16
B = 1024
DEPTH = 1280
HALF = B // 2
STEP = 256
PIECES = 8
ROWS = 64
TURN = 32
SWAP = [(0, 1), (1, 0)]
TO_OTHER = [(i, i ^ 1) for i in range(NSNP)]
EVEN_DOWN = [(i + 2, i) for i in range(0, NSNP - 2, 2)]
ODD_UP = [(i, i + 2) for i in range(1, NSNP - 2, 2)]
EVEN_UP = [(i, i + 2) for i in range(0, NSNP - 2, 2)]
ODD_DOWN = [(i + 2, i) for i in range(1, NSNP - 2, 2)]


def sum_over_samples(x):
    parts = [
        lax.ppermute(x, ("yl", "core"), [(i, i ^ k) for i in range(4)]) for k in (1, 2, 3)
    ]
    x = x + parts[0] + parts[1] + parts[2]
    parts = [
        lax.ppermute(x, "x", [(i, (i + k) % 4) for i in range(4)]) for k in (1, 2, 3)
    ]
    return x + parts[0] + parts[1] + parts[2]


def params():
    return pltpu.CompilerParams(vmem_limit_bytes=56 << 20)


def cost(flops, moved):
    return pl.CostEstimate(flops=1024, bytes_accessed=1024, transcendentals=0)


def whole(shape):
    return pl.BlockSpec(shape, lambda j, m: (0,) * len(shape))


def f32(*shape):
    return jax.ShapeDtypeStruct(shape, jnp.float32)


def bf16(*shape):
    return jax.ShapeDtypeStruct(shape, jnp.bfloat16)


def matmul(left, right):
    return jnp.dot(left, right, preferred_element_type=jnp.float32)


def standard_kernel(meta, dosage, observed, stats, zed, zed0, zed1, kept0, kept1, sent0, sent1):
    weight = observed[...].astype(jnp.float32)
    values = dosage[...].astype(jnp.float32)
    z = (weight * (values - stats[0:1, :]) * stats[1:2, :]).astype(jnp.bfloat16)
    zed[...] = z
    zed0[...] = z[:, :HALF]
    zed1[...] = z[:, HALF:]
    turned = z.T

    def store(*outs):
        for c in range(PIECES):
            for k, out in enumerate(outs):
                at = 2 * ROWS * c + TURN * k
                out[c] = turned[at : at + TURN]

    pl.when(meta[0] == 0)(lambda: store(kept0, kept1, sent0, sent1))
    pl.when(meta[0] != 0)(lambda: store(sent0, sent1, kept0, kept1))


def standardize(meta, dosage, observed, stats):
    rows = 256
    block = lambda width: pl.BlockSpec((rows, width), lambda i, m: (i, 0))
    turned = pl.BlockSpec((PIECES, TURN, rows), lambda i, m: (0, 0, i))
    return pl.pallas_call(
        standard_kernel,
        name="standardize",
        out_shape=(bf16(DEPTH, B), bf16(DEPTH, HALF), bf16(DEPTH, HALF))
        + (bf16(PIECES, TURN, DEPTH),) * 4,
        grid_spec=pltpu.PrefetchScalarGridSpec(
            num_scalar_prefetch=1,
            grid=(DEPTH // rows,),
            in_specs=[block(B), block(B), whole((2, B))],
            out_specs=(block(B), block(HALF), block(HALF)) + (turned,) * 4,
        ),
        compiler_params=params(),
        cost_estimate=cost(4 * DEPTH * B, 12 * DEPTH * B),
    )(meta, dosage, observed, stats)


LEFT = (PIECES * TURN, DEPTH)


def flat(*turned):
    return [t.reshape(LEFT) for t in turned]


def own_kernel(meta, kept0, kept1, sent0, sent1, right, out):
    core = meta[0]
    r = right[...]
    for left, half, at in (
        (kept0, core, 0),
        (kept1, core, TURN),
        (sent0, 1 - core, 0),
        (sent1, 1 - core, TURN),
    ):
        acc = matmul(left[...], r)
        for c in range(PIECES):
            out[c, half, at : at + TURN] = acc[TURN * c : TURN * (c + 1)]


def own_product(meta, turned, zed):
    out = pl.pallas_call(
        own_kernel,
        name="own",
        out_shape=f32(PIECES, 2, ROWS, B),
        grid_spec=pltpu.PrefetchScalarGridSpec(
            num_scalar_prefetch=1,
            grid=(B // STEP,),
            in_specs=[whole(LEFT)] * 4 + [pl.BlockSpec((DEPTH, STEP), lambda j, m: (0, j))],
            out_specs=pl.BlockSpec((PIECES, 2, ROWS, STEP), lambda j, m: (0, 0, 0, j)),
        ),
        compiler_params=params(),
        cost_estimate=cost(2 * DEPTH * B * B, 4 * DEPTH * B + 4 * B * B),
    )(meta, *flat(*turned), zed)
    return out.reshape(B, B)


def turn_kernel(meta, zed, out0, out1):
    turned = zed[...].T

    def store(at):
        out0[0] = turned[at : at + TURN]
        out1[0] = turned[at + TURN : at + ROWS]

    pl.when(meta[0] == 0)(lambda: store(0))
    pl.when(meta[0] != 0)(lambda: store(ROWS))


def turn(meta, zed):
    out = pl.BlockSpec((1, TURN, DEPTH), lambda c, m: (c, 0, 0))
    return pl.pallas_call(
        turn_kernel,
        name="turn",
        out_shape=(bf16(PIECES, TURN, DEPTH),) * 2,
        grid_spec=pltpu.PrefetchScalarGridSpec(
            num_scalar_prefetch=1,
            grid=(PIECES,),
            in_specs=[pl.BlockSpec((DEPTH, 2 * ROWS), lambda c, m: (0, c))],
            out_specs=(out, out),
        ),
        compiler_params=params(),
        cost_estimate=cost(DEPTH * B, 3 * DEPTH * B),
    )(meta, zed)


def store_pieces(out, at, left_a, left_b, right_a, right_b):
    acc = matmul(left_a[...], right_a[...]) + matmul(left_b[...], right_b[...])
    out[:, at : at + TURN] = acc.reshape(PIECES, TURN, STEP)


def early_kernel(
    meta, own0_a, own1_a, own0_b, own1_b, other_a, other_b, near_a, near_b, zed_a, zed_b, out
):
    store_pieces(out, 0, own0_a, own0_b, near_a, near_b)
    store_pieces(out, TURN, own1_a, own1_b, near_a, near_b)
    even = meta[1] == 0
    pl.when(even)(lambda: store_pieces(out, ROWS, other_a, other_b, near_a, near_b))
    pl.when(~even)(lambda: store_pieces(out, ROWS, other_a, other_b, zed_a, zed_b))


def early_product(meta, own_a, own_b, other, near, zed):
    right = pl.BlockSpec((DEPTH, STEP), lambda j, m: (0, j))
    rows = ROWS + TURN
    return pl.pallas_call(
        early_kernel,
        name="early",
        out_shape=f32(PIECES, rows, HALF),
        grid_spec=pltpu.PrefetchScalarGridSpec(
            num_scalar_prefetch=1,
            grid=(HALF // STEP,),
            in_specs=[whole(LEFT)] * 6 + [right] * 4,
            out_specs=pl.BlockSpec((PIECES, rows, STEP), lambda j, m: (0, 0, j)),
        ),
        compiler_params=params(),
        cost_estimate=cost(32 * DEPTH * rows * HALF, 10 * DEPTH * B + 32 * rows * HALF),
    )(meta, *flat(*own_a, *own_b, *other), *near, *zed)


def late_kernel(
    meta,
    own0_a,
    own1_a,
    own0_b,
    own1_b,
    other0_a,
    other0_b,
    other1_a,
    other1_b,
    near0_a,
    near0_b,
    near1_a,
    near1_b,
    zed0_a,
    zed0_b,
    zed1_a,
    zed1_b,
    out,
):
    def across(first_a, first_b, second_a, second_b):
        store_pieces(out, ROWS, other0_a, other0_b, second_a, second_b)
        store_pieces(out, ROWS + TURN, other1_a, other1_b, second_a, second_b)
        store_pieces(out, 2 * ROWS, other1_a, other1_b, first_a, first_b)

    store_pieces(out, 0, own0_a, own0_b, near1_a, near1_b)
    store_pieces(out, TURN, own1_a, own1_b, near1_a, near1_b)
    even = meta[1] == 0
    pl.when(even)(lambda: across(near0_a, near0_b, near1_a, near1_b))
    pl.when(~even)(lambda: across(zed0_a, zed0_b, zed1_a, zed1_b))


def late_product(meta, own_a, own_b, other0, other1, near0, near1, zed):
    right = pl.BlockSpec((DEPTH, STEP), lambda j, m: (0, j))
    second = pl.BlockSpec((DEPTH, STEP), lambda j, m: (0, j + HALF // STEP))
    rows = 2 * ROWS + TURN
    return pl.pallas_call(
        late_kernel,
        name="late",
        out_shape=f32(PIECES, rows, HALF),
        grid_spec=pltpu.PrefetchScalarGridSpec(
            num_scalar_prefetch=1,
            grid=(HALF // STEP,),
            in_specs=[whole(LEFT)] * 8 + [right] * 6 + [second] * 2,
            out_specs=pl.BlockSpec((PIECES, rows, STEP), lambda j, m: (0, 0, j)),
        ),
        compiler_params=params(),
        cost_estimate=cost(32 * DEPTH * rows * HALF, 16 * DEPTH * B + 32 * rows * HALF),
    )(meta, *flat(*own_a, *own_b, *other0, *other1), *near0, *near1, *zed, *zed)


def gather_kernel(meta, early, late, rows2, rows1, both):
    a = early[0]
    b = late[0]
    for r in range(1, PIECES):
        a = a + early[r]
        b = b + late[r]
    rows2[:, :HALF] = a[:ROWS]
    rows2[:, HALF:] = b[:ROWS]
    rows1[:TURN, :HALF] = a[ROWS:]
    rows1[:TURN, HALF:] = b[ROWS : ROWS + TURN]
    rows1[TURN:, HALF:] = b[ROWS + TURN : 2 * ROWS]
    rows1[TURN:, :HALF] = b[2 * ROWS :]
    for s in range(2 * PIECES):
        both[s, :, :ROWS] = rows2[:, ROWS * s : ROWS * (s + 1)]
        both[s, :, ROWS:] = rows1[:, ROWS * s : ROWS * (s + 1)]


def gather_pieces(meta, early, late):
    return pl.pallas_call(
        gather_kernel,
        name="gather",
        out_shape=(f32(ROWS, B), f32(ROWS, B), f32(2 * PIECES, ROWS, 2 * ROWS)),
        grid_spec=pltpu.PrefetchScalarGridSpec(
            num_scalar_prefetch=1,
            grid=(1,),
            in_specs=[whole(early.shape), whole(late.shape)],
            out_specs=(
                whole((ROWS, B)),
                whole((ROWS, B)),
                whole((2 * PIECES, ROWS, 2 * ROWS)),
            ),
        ),
        compiler_params=params(),
        cost_estimate=cost(PIECES * ROWS * 2 * B, 4 * PIECES * ROWS * 2 * B),
    )(meta, early, late)


def assemble_kernel(flags, far, here, rows2, beside, rows0, out):
    even = flags[5] == 0
    far_turned = far[...].T
    near = jnp.where(even, far_turned[ROWS:], here[...].T[ROWS:])
    far2 = far_turned[:ROWS]
    mine2 = rows2[...]
    blocks = (
        jnp.where(even, far2, mine2),
        near,
        rows0[...],
        beside[...],
        jnp.where(even, mine2, far2),
    )
    for d, block in enumerate(blocks):
        out[:, B * d : B * (d + 1)] = jnp.where(flags[d] > 0, block, 0.0)


def assemble(flags, far, here, rows2, beside, rows0):
    return pl.pallas_call(
        assemble_kernel,
        name="assemble",
        out_shape=f32(ROWS, 5 * B),
        grid_spec=pltpu.PrefetchScalarGridSpec(
            num_scalar_prefetch=1,
            grid=(1,),
            in_specs=[whole((B, 2 * ROWS))] * 2 + [whole((ROWS, B))] * 3,
            out_specs=whole((ROWS, 5 * B)),
        ),
        compiler_params=params(),
        cost_estimate=cost(ROWS * 5 * B, 40 * ROWS * B),
    )(flags, far, here, rows2, beside, rows0)


def kept_flags(band, mine):
    total = band.shape[0]
    offsets = jnp.arange(5, dtype=jnp.int32) - 2
    other = mine + offsets
    inside = (other >= 0) & (other < total)
    reach = jnp.minimum(band[mine], band[jnp.clip(other, 0, total - 1)])
    return (inside & (jnp.abs(offsets) <= reach)).astype(jnp.int32)


def on_device(dosage, observed, band):
    mine = lax.axis_index(SNP)
    odd = lax.axis_index("yh").reshape(1)
    core = lax.axis_index("core").reshape(1)
    meta = jnp.concatenate([core, odd]).astype(jnp.int32)

    weight = observed.astype(jnp.float32)
    values = dosage.astype(jnp.float32)
    sums = jnp.stack(
        [
            jnp.sum(weight, axis=0),
            jnp.sum(weight * values, axis=0),
            jnp.sum(weight * values * values, axis=0),
        ]
    )
    cnt, first, second = sum_over_samples(sums)
    mean = first / cnt
    spread = second - first * mean
    stats = jnp.stack([mean, lax.rsqrt(spread + eps * cnt)])

    zed, zed0, zed1, kept0, kept1, sent0, sent1 = standardize(meta, dosage, observed, stats)
    along = lambda t: lax.ppermute(t, SNP, EVEN_DOWN + ODD_UP)
    across = lambda t: lax.ppermute(t, SNP, TO_OTHER)
    athwart = lambda t: lax.ppermute(t, ("yh", "core"), [(i, 3 - i) for i in range(4)])
    swap = lambda t: lax.ppermute(t, "core", SWAP)
    zed_b = swap(zed)
    near0 = along(zed0)
    other0 = (across(kept0), athwart(sent0))
    near1 = along(zed1)
    other1 = (across(kept1), athwart(sent1))

    own = own_product(meta, (kept0, kept1, sent0, sent1), zed)
    rows0 = lax.psum_scatter(own, SAMP, scatter_dimension=0, tiled=True)
    near0, zed_b, other0 = lax.optimization_barrier((near0, zed_b, other0))
    own_a = (kept0, kept1)
    own_b = turn(meta, zed_b)
    near0 = (near0, swap(near0))
    early = early_product(meta, own_a, own_b, other0, near0, (zed, zed_b))
    early = lax.all_to_all(early, CHIP, 0, 0)
    near1, other1 = lax.optimization_barrier((near1, other1))
    near1 = (near1, swap(near1))
    late = late_product(meta, own_a, own_b, other0, other1, near0, near1, (zed, zed_b))
    late = lax.all_to_all(late, CHIP, 0, 0)
    rows2, rows1, both = gather_pieces(meta, early, late)
    beside = lax.ppermute(rows1, SNP, TO_OTHER)
    here = lax.all_to_all(both, SAMP, 0, 0).reshape(B, 2 * ROWS)
    far = lax.ppermute(here, SNP, EVEN_UP + ODD_DOWN)
    flags = jnp.concatenate([kept_flags(band, mine), odd]).astype(jnp.int32)
    return assemble(flags, far, here, rows2, beside, rows0)


def solution(mesh):
    whole_mesh = Mesh(mesh.devices.reshape(SIZES), AXES)
    return jax.shard_map(
        on_device,
        mesh=whole_mesh,
        in_specs=(P(SAMP, SNP), P(SAMP, SNP), P()),
        out_specs=P(AXES, None),
        check_vma=False,
    )
```

time: 383 us -> 246 us (0.64)
  waiting for transfers between devices: 233 us -> 94.9 us
  Pallas kernels: 0 us -> 49.3 us
  starting transfers between devices: 14.5 us -> 37.9 us
  other arithmetic: 28.8 us -> 7.2 us
  blocking collectives: 56 us -> 37.6 us
  local copies, waits for them, and re-layouts: 20.1 us -> 4.19 us
  matrix products: 12.7 us -> 0 us
    reduce_scatter x1, waiting for transfers between devices: 116 us -> 0.01 us  [on_device(): rows0 = lax.psum_scatter(own, SAMP, scatter_dimension=0, tiled=True)]
    psum x1 -> x0, blocking collectives: 56 us -> none  [on_device(): lax.psum((jnp.sum(weight, axis=0), jnp.sum(weight * values, axis=0), jnp....]
    pallas_call x0 -> x7, Pallas kernels: none -> 49.3 us  [the longest x1 10.5 us: late_product(): pl.pallas_call(late_kernel, name='late', out_shape=f32(PIECES, rows, HALF...]
    all_to_all x0 -> x1, blocking collectives: none -> 37.6 us  [on_device(): late = lax.all_to_all(late, CHIP, 0, 0)]
    ppermute x4 -> x17, waiting for transfers between devices: 116 us -> 84.7 us  [the longest x2 48.5 us: on_device(): lax.ppermute(t, ('yh', 'core'), [(i, 3 - i) for i in range(4)])]
    concatenate x2, other arithmetic: 17.4 us -> 1.21 us  [the longest x1 0.62 us: on_device(): flags = jnp.concatenate([kept_flags(band, mine), odd]).astype(jnp.int32)]
    ppermute x4 -> x17, starting transfers between devices: 14.4 us -> 30.3 us  [the longest x2 12.9 us: on_device(): across = lambda t: lax.ppermute(t, SNP, TO_OTHER)]
    dot_general x1 -> x0, matrix products: 12.7 us -> none  [products(): lax.dot_general(left, right, (((0,), (0,)), ((), ())), preferred_element_...]
  transfers between devices with their start and end apart: 5 -> 20, of which waited for: 4 -> 12; matrix products, arithmetic and copies ran while one was open for 0% -> 1% of each run, Pallas kernels for 0% -> 15%
where the time goes in v1:
time: 246 us; the launch traced here: 245 us
  waiting for transfers between devices  94.9 us (39%)
  Pallas kernels  49.3 us (20%)
  starting transfers between devices  37.9 us (15%)
  blocking collectives  37.6 us (15%)
  between operations  13.6 us (6%)
  other arithmetic  7.2 us (3%)
  local copies, waits for them, and re-layouts  4.19 us (2%)
    ppermute x2, waiting for transfers between devices, on_device(): lax.ppermute(t, ('yh', 'core'), [(i, 3 - i) for i in range(4)])  48.5 us
    all_to_all x1, blocking collectives, on_device(): late = lax.all_to_all(late, CHIP, 0, 0)  37.6 us
    ppermute x2, waiting for transfers between devices, on_device(): across = lambda t: lax.ppermute(t, SNP, TO_OTHER)  20.3 us
    ppermute x2, starting transfers between devices, on_device(): across = lambda t: lax.ppermute(t, SNP, TO_OTHER)  12.9 us
    pallas_call x1, Pallas kernels, late_product(): pl.pallas_call(late_kernel, name='late', out_shape=f32(PIECES, rows, HALF...  10.5 us
    all_to_all x1, waiting for transfers between devices, on_device(): here = lax.all_to_all(both, SAMP, 0, 0).reshape(B, 2 * ROWS)  10.2 us
    pallas_call x1, Pallas kernels, standardize(): pl.pallas_call(standard_kernel, name='standardize', out_shape=(bf16(DEPTH...  9.23 us
    pallas_call x1, Pallas kernels, own_product(): pl.pallas_call(own_kernel, name='own', out_shape=f32(PIECES, 2, ROWS, B),...  7.66 us
  transfers between devices with their start and end apart: 20, of which 12 were waited for; matrix products, arithmetic and copies ran while one was open for 1% of the time, Pallas kernels for 15%

profile of v1, /device:TPU:64, one launch (start us, length us, event | category | flops | bytes accessed | tf_op | source)
XLA Modules:
  0.0 244.6 jit_solution(8569339404200166342)
XLA Ops:
  6.5 0.0 reduce-scatter.2.cloned.1.call-start
  6.5 4.7 %fusion.1 = (f32[1024]{0:T(1024)S(1)}, f32[1024]{0:T(1024)S(1)}, f32[1024]{0:T(1024)S(1)}) fusion(bf16[1280,1024]{1,0:T(8,128)(2,1)} %dosage.1, s32[1280,1024]{1,0:T(8,128)} %observed.1), kind=kLoop, calls=%fused_computation.5 | loop fusion | flops 9171968 | bytes 7876608 | tf_op jit(solution)/shard_map/reduce_sum | solution.py:346
  11.2 0.1 collective-permute-start
  11.3 1.7 collective-permute-start.1
  13.0 0.2 collective-permute-start.2
  13.2 0.0 collective-permute-done
  13.2 2.0 collective-permute-done.1
  15.1 1.0 collective-permute-done.2
  16.2 1.6 collective-permute-start.3
  17.7 2.7 %collective-permute-start.4 = (f32[3,1024]{1,0:T(4,128)S(1)}, f32[3,1024]{1,0:T(4,128)S(1)}, u32[]{:S(2)}, u32[]{:S(2)}) collective-permute-start(f32[3,1024]{1,0:T(4,128)S(1)} %add_add_fusion.1), channel_id=1, source_target_pairs={{0,4},{2,6},{4,0},{6,2},{1,5},{3,7},{5,1},{7,3},{8,12},{10,14},{12... | collective-permute-start | bytes 36872 | tf_op jit(solution)/shard_map/ppermute | solution.py:38
  20.5 1.4 collective-permute-start.5
  21.9 0.6 pad_add_fusion.1.meta
  22.5 0.0 collective-permute-done.3
  22.5 0.5 collective-permute-done.4
  23.0 1.2 collective-permute-done.5
  24.3 0.6 pad_maximum_fusion.1.stats
  24.9 9.2 %standardize.1 = (bf16[1280,1024]{1,0:T(8,128)(2,1)}, bf16[1280,512]{1,0:T(8,128)(2,1)}, bf16[1280,512]{1,0:T(8,128)(2,1)}, bf16[8,32,1280]{2,1,0:T(8,128)(2,1)}...) custom-call(s32[2]{0:T(128)} %pad_add_fusion.1.meta, ...), custom_call_target="tpu_custom_call" | custom-call | flops 1024 | bytes 1024 | tf_op jit(solution)/shard_map/standardize/pallas_call | solution.py:90
  34.1 0.1 collective-permute-start.7
  34.2 7.7 %own.1 = f32[8,2,64,1024]{3,2,1,0:T(8,128)} custom-call(s32[2]{0:T(128)} %pad_add_fusion.1.meta, bf16[256,1280]{1,0:T(8,128)(2,1)} %bitcast.21, bf16[256,1280]{1,0:T(8,128)(2,1)} %bitcast.24, bf16[256,1280]{1,0:T(8,128)(2,1)} %bitcast.39, bf16[256,1280]{1,0:T(8,128)(2,1)} %bitcast.37, bf16[1280,1024]{1,0:T(8,128)(2,1)} %get-tuple-element.27.zed_a.zed0_a.zed1_a.right), custom_call_target="tpu_custom_call" | custom-call | flops 1024 | bytes 1024 | tf_op jit(solution)/shard_map/own/pallas_call | solution.py:128
  41.8 0.0 reduce-scatter.2.cloned.1.call-update
  41.9 2.1 collective-permute-start.6
  44.0 0.0 copy-done.3
  44.0 4.8 %collective-permute-start.8 = (bf16[8,32,1280]{2,1,0:T(8,128)(2,1)S(1)}, bf16[8,32,1280]{2,1,0:T(8,128)(2,1)S(1)}, u32[]{:S(2)}, u32[]{:S(2)}) collective-permute-start(bf16[8,32,1280]{2,1,0:T(8,128)(2,1)S(1)} %copy-done.3), channel_id=1, source_target_pairs={{0,16},{16,0},{32,48},{48,32},{64,80},{80,64},{96,112},{112,96},{1... | collective-permute-start | bytes 1966088 | tf_op jit(solution)/shard_map/ppermute | solution.py:357
  48.8 0.0 collective-permute-start.9
  48.8 19.3 %collective-permute-done.8 = bf16[8,32,1280]{2,1,0:T(8,128)(2,1)S(1)} collective-permute-done((bf16[8,32,1280]{2,1,0:T(8,128)(2,1)S(1)}, bf16[8,32,1280]{2,1,0:T(8,128)(2,1)S(1)}, u32[]{:S(2)}, u32[]{:S(2)}) %collective-permute-start.8) | collective-permute-done | bytes 655392 | tf_op jit(solution)/shard_map/ppermute | solution.py:357
  68.1 21.9 %collective-permute-done.9 = bf16[8,32,1280]{2,1,0:T(8,128)(2,1)S(1)} collective-permute-done((bf16[8,32,1280]{2,1,0:T(8,128)(2,1)}, bf16[8,32,1280]{2,1,0:T(8,128)(2,1)S(1)}, u32[]{:S(2)}, u32[]{:S(2)}) %collective-permute-start.9) | collective-permute-done | bytes 655392 | tf_op jit(solution)/shard_map/ppermute | solution.py:358
  90.0 0.0 collective-permute-done.6.near_a.near0_a
  90.0 0.0 collective-permute-done.7.zed.zed_b.zed0_b.zed1_b
  90.0 0.0 copy-start.1
  90.0 0.1 collective-permute-start.10
  90.1 2.1 collective-permute-start.11
  92.2 8.2 %collective-permute-start.12 = (bf16[8,32,1280]{2,1,0:T(8,128)(2,1)}, bf16[8,32,1280]{2,1,0:T(8,128)(2,1)S(1)}, u32[]{:S(2)}, u32[]{:S(2)}) collective-permute-start(bf16[8,32,1280]{2,1,0:T(8,128)(2,1)} %get-tuple-element.25), channel_id=1, source_target_pairs={{0,16},{16,0},{32,48},{48,32},{64,80},{80,64},{96,112},{112,96},{1... | collective-permute-start | bytes 1966088 | tf_op jit(solution)/shard_map/ppermute | solution.py:357
  100.3 0.0 collective-permute-start.13
  100.3 0.0 copy-done.1
  100.3 6.7 %turn.1 = (bf16[8,32,1280]{2,1,0:T(8,128)(2,1)}, bf16[8,32,1280]{2,1,0:T(8,128)(2,1)}) custom-call(s32[2]{0:T(128)} %pad_add_fusion.1.meta, bf16[1280,1024]{1,0:T(8,128)(2,1)} %copy-done.1), custom_call_target="tpu_custom_call" | custom-call | flops 1024 | bytes 1024 | tf_op jit(solution)/shard_map/turn/pallas_call | solution.py:157
  107.1 0.0 collective-permute-done.10.near_b.near0_b
  107.1 0.0 copy-done.6
  107.1 0.0 copy-done.7
  107.1 1.0 copy-done.5
  108.1 7.4 %early.1 = f32[8,96,512]{2,1,0:T(8,128)} custom-call(s32[2]{0:T(128)} %pad_add_fusion.1.meta, bf16[256,1280]{1,0:T(8,128)(2,1)} %bitcast.22, bf16[256,1280]{1,0:T(8,128)(2,1)} %bitcast.25, bf16[256,1280]{1,0:T(8,128)(2,1)} %bitcast.31, bf16[256,1280]{1,0:T(8,128)(2,1)} %bitcast.33, bf16[256,1280]{1,0:T(8,128)(2,1)} %bitcast.27, bf16[256,1280]{1,0:T(8,128)(2,1)} %bitcast.29, ...), custom_call_target="tpu_custom_call" | custom-call | flops 1024 | bytes 1024 | tf_op jit(solution)/shard_map/early/pallas_call | solution.py:190
  115.5 4.0 %all-to-all-start = ((f32[8,96,512]{2,1,0:T(8,128)}), f32[8,96,512]{2,1,0:T(8,128)S(1)}, u32[]{:S(2)}, u32[]{:S(2)}) async-start(f32[8,96,512]{2,1,0:T(8,128)} %early.1), calls=%async_computation | async-start | bytes 3145728 | tf_op jit(solution)/shard_map/all_to_all | solution.py:373
  119.5 1.1 collective-permute-done.12
  120.6 26.6 %collective-permute-done.13 = bf16[8,32,1280]{2,1,0:T(8,128)(2,1)} collective-permute-done((bf16[8,32,1280]{2,1,0:T(8,128)(2,1)}, bf16[8,32,1280]{2,1,0:T(8,128)(2,1)}, u32[]{:S(2)}, u32[]{:S(2)}) %collective-permute-start.13) | collective-permute-done | bytes 655392 | tf_op jit(solution)/shard_map/ppermute | solution.py:358
  147.2 0.0 collective-permute-done.11.near1_a
  147.2 0.1 collective-permute-start.14
  147.3 3.1 %collective-permute-done.14.near1_b = bf16[1280,512]{1,0:T(8,128)(2,1)S(1)} collective-permute-done((bf16[1280,512]{1,0:T(8,128)(2,1)}, bf16[1280,512]{1,0:T(8,128)(2,1)S(1)}, u32[]{:S(2)}, u32[]{:S(2)}) %collective-permute-start.14) | collective-permute-done | bytes 1310752 | tf_op jit(solution)/shard_map/ppermute | solution.py:359
  150.4 1.1 copy-done.9
  151.5 10.5 %late.1 = f32[8,160,512]{2,1,0:T(8,128)} custom-call(s32[2]{0:T(128)} %pad_add_fusion.1.meta, bf16[256,1280]{1,0:T(8,128)(2,1)} %bitcast.23, bf16[256,1280]{1,0:T(8,128)(2,1)} %bitcast.26, bf16[256,1280]{1,0:T(8,128)(2,1)} %bitcast.32, bf16[256,1280]{1,0:T(8,128)(2,1)} %bitcast.34, bf16[256,1280]{1,0:T(8,128)(2,1)} %bitcast.28, bf16[256,1280]{1,0:T(8,128)(2,1)} %bitcast.30, ...), custom_call_target="tpu_custom_call" | custom-call | flops 1024 | bytes 1024 | tf_op jit(solution)/shard_map/late/pallas_call | solution.py:241
  161.9 0.0 all-to-all-done.early
  162.0 37.6 %all_to_all.15.late = f32[8,160,512]{2,1,0:T(8,128)} all-to-all(f32[8,160,512]{2,1,0:T(8,128)} %late.1), channel_id=1, replica_groups=mesh['z'=8,'yh'=2,'yl'=2,'x'=4,'core'=2] {'yl','x'}, dimensions={0} | all-to-all | bytes 5242880 | tf_op jit(solution)/shard_map/all_to_all | solution.py:377
  199.6 4.3 %gather.7 = (f32[64,1024]{1,0:T(8,128)}, f32[64,1024]{1,0:T(8,128)}, f32[16,64,128]{2,1,0:T(8,128)}) custom-call(s32[2]{0:T(128)} %pad_add_fusion.1.meta, f32[8,96,512]{2,1,0:T(8,128)} %copy-done.2, f32[8,160,512]{2,1,0:T(8,128)} %all_to_all.15.late), custom_call_target="tpu_custom_call" | custom-call | flops 1024 | bytes 1024 | tf_op jit(solution)/shard_map/gather/pallas_call | solution.py:274
  203.9 3.6 %all-to-all-start.2 = ((f32[16,64,128]{2,1,0:T(8,128)}), f32[16,64,128]{2,1,0:T(8,128)S(1)}, u32[]{:S(2)}, u32[]{:S(2)}) async-start(f32[16,64,128]{2,1,0:T(8,128)} %get-tuple-element.40), calls=%async_computation.2 | async-start | bytes 1048576 | tf_op jit(solution)/shard_map/all_to_all | solution.py:380
  207.5 0.0 copy-done
  207.5 0.6 dynamic_slice.3
  208.1 10.2 %all-to-all-done.2 = f32[16,64,128]{2,1,0:T(8,128)S(1)} async-done(((f32[16,64,128]{2,1,0:T(8,128)}), f32[16,64,128]{2,1,0:T(8,128)S(1)}, u32[]{:S(2)}, u32[]{:S(2)}) %all-to-all-start.2) | async-done | bytes 524320 | tf_op jit(solution)/shard_map/all_to_all | solution.py:380
  218.3 2.8 %collective-permute-start.15 = (f32[1024,128]{1,0:T(8,128)S(1)}, f32[1024,128]{1,0:T(8,128)S(1)}, u32[]{:S(2)}, u32[]{:S(2)}) collective-permute-start(f32[1024,128]{1,0:T(8,128)S(1)} %bitcast.35), channel_id=1, source_target_pairs={{0,32},{32,64},{64,96},{96,128},{128,160},{160,192},{192,224},{48,... | collective-permute-start | bytes 1572872 | tf_op jit(solution)/shard_map/ppermute | solution.py:381
  221.2 0.6 gather_fusion
  221.8 2.3 collective-permute-start.16
  224.2 0.6 and_convert_fusion
  224.8 0.6 pad_add_fusion.flags
  225.4 5.6 %collective-permute-done.16.beside = f32[64,1024]{1,0:T(8,128)S(1)} collective-permute-done((f32[64,1024]{1,0:T(8,128)}, f32[64,1024]{1,0:T(8,128)S(1)}, u32[]{:S(2)}, u32[]{:S(2)}) %collective-permute-start.16) | collective-permute-done | bytes 262176 | tf_op jit(solution)/shard_map/ppermute | solution.py:379
  231.0 2.5 %collective-permute-done.15.far = f32[1024,128]{1,0:T(8,128)S(1)} collective-permute-done((f32[1024,128]{1,0:T(8,128)S(1)}, f32[1024,128]{1,0:T(8,128)S(1)}, u32[]{:S(2)}, u32[]{:S(2)}) %collective-permute-start.15) | collective-permute-done | bytes 524320 | tf_op jit(solution)/shard_map/ppermute | solution.py:381
  233.5 0.8 copy-done.11
  234.3 3.5 %assemble.1 = f32[64,5120]{1,0:T(8,128)} custom-call(s32[6]{0:T(128)} %pad_add_fusion.flags, f32[1024,128]{1,0:T(8,128)} %copy-done.11, f32[1024,128]{1,0:T(8,128)} %bitcast.36, f32[64,1024]{1,0:T(8,128)} %get-tuple-element.41.rows2, f32[64,1024]{1,0:T(8,128)} %copy-done.12, f32[64,1024]{1,0:T(8,128)} %reduce-scatter.2.cloned.1.call-done.rows0), custom_call_target="tpu_custom_call" | custom-call | flops 1024 | bytes 1024 | tf_op jit(solution)/shard_map/assemble/pallas_call | solution.py:311
  (24 shorter events, 0.1 us)
Async XLA Ops:
  6.5 227.0 %reduce-scatter.2.cloned.1.call-start = ((), (), s32[]{:S(2)}) async-start(), calls=%async_computation.4 | async-start | bytes 4456448 | tf_op jit(solution)/shard_map/reduce_scatter | solution.py:367
  11.2 2.0 collective-permute-start
  11.3 3.8 %collective-permute-start.1 = (f32[3,1024]{1,0:T(4,128)S(1)}, f32[3,1024]{1,0:T(4,128)S(1)}, u32[]{:S(2)}, u32[]{:S(2)}) collective-permute-start(f32[3,1024]{1,0:T(4,128)S(1)} %pad_maximum_fusion), channel_id=1, source_target_pairs={{0,8},{1,9},{8,0},{9,1},{2,10},{3,11},{10,2},{11,3},{4,12},{5,13},... | collective-permute-start | bytes 36872 | tf_op jit(solution)/shard_map/ppermute | solution.py:34
  13.0 3.2 %collective-permute-start.2 = (f32[3,1024]{1,0:T(4,128)S(1)}, f32[3,1024]{1,0:T(4,128)S(1)}, u32[]{:S(2)}, u32[]{:S(2)}) collective-permute-start(f32[3,1024]{1,0:T(4,128)S(1)} %pad_maximum_fusion), channel_id=1, source_target_pairs={{0,9},{1,8},{8,1},{9,0},{2,11},{3,10},{10,3},{11,2},{4,13},{5,12},... | collective-permute-start | bytes 36872 | tf_op jit(solution)/shard_map/ppermute | solution.py:34
  16.2 6.3 %collective-permute-start.3 = (f32[3,1024]{1,0:T(4,128)S(1)}, f32[3,1024]{1,0:T(4,128)S(1)}, u32[]{:S(2)}, u32[]{:S(2)}) collective-permute-start(f32[3,1024]{1,0:T(4,128)S(1)} %add_add_fusion.1), channel_id=1, source_target_pairs={{0,2},{2,4},{4,6},{6,0},{1,3},{3,5},{5,7},{7,1},{8,10},{10,12},{12... | collective-permute-start | bytes 36872 | tf_op jit(solution)/shard_map/ppermute | solution.py:38
  17.7 5.2 %collective-permute-start.4 = (f32[3,1024]{1,0:T(4,128)S(1)}, f32[3,1024]{1,0:T(4,128)S(1)}, u32[]{:S(2)}, u32[]{:S(2)}) collective-permute-start(f32[3,1024]{1,0:T(4,128)S(1)} %add_add_fusion.1), channel_id=1, source_target_pairs={{0,4},{2,6},{4,0},{6,2},{1,5},{3,7},{5,1},{7,3},{8,12},{10,14},{12... | collective-permute-start | bytes 36872 | tf_op jit(solution)/shard_map/ppermute | solution.py:38
  20.5 3.7 %collective-permute-start.5 = (f32[3,1024]{1,0:T(4,128)S(1)}, f32[3,1024]{1,0:T(4,128)S(1)}, u32[]{:S(2)}, u32[]{:S(2)}) collective-permute-start(f32[3,1024]{1,0:T(4,128)S(1)} %add_add_fusion.1), channel_id=1, source_target_pairs={{0,6},{2,0},{4,2},{6,4},{1,7},{3,1},{5,3},{7,5},{8,14},{10,8},{12,... | collective-permute-start | bytes 36872 | tf_op jit(solution)/shard_map/ppermute | solution.py:38
  34.1 55.9 %collective-permute-start.7 = (bf16[1280,1024]{1,0:T(8,128)(2,1)}, bf16[1280,1024]{1,0:T(8,128)(2,1)S(1)}, u32[]{:S(2)}, u32[]{:S(2)}) collective-permute-start(bf16[1280,1024]{1,0:T(8,128)(2,1)} %get-tuple-element.27.zed_a.zed0_a.zed1_a.right), channel_id=1, source_target_pairs={{0,1},{1,0},{2,3},{3,2},{4,5},{5,4},{6,7},{7,6},{8,9},{9,8},{10,11... | collective-permute-start | bytes 7864328 | tf_op jit(solution)/shard_map/ppermute | solution.py:359
  41.8 2.2 copy-start.3
  41.9 48.1 %collective-permute-start.6 = (bf16[1280,512]{1,0:T(8,128)(2,1)}, bf16[1280,512]{1,0:T(8,128)(2,1)S(1)}, u32[]{:S(2)}, u32[]{:S(2)}) collective-permute-start(bf16[1280,512]{1,0:T(8,128)(2,1)} %get-tuple-element.26), channel_id=1, source_target_pairs={{32,0},{64,32},{96,64},{128,96},{160,128},{192,160},{224,192},{16,... | collective-permute-start | bytes 3932168 | tf_op jit(solution)/shard_map/ppermute | solution.py:356
  44.0 24.1 %collective-permute-start.8 = (bf16[8,32,1280]{2,1,0:T(8,128)(2,1)S(1)}, bf16[8,32,1280]{2,1,0:T(8,128)(2,1)S(1)}, u32[]{:S(2)}, u32[]{:S(2)}) collective-permute-start(bf16[8,32,1280]{2,1,0:T(8,128)(2,1)S(1)} %copy-done.3), channel_id=1, source_target_pairs={{0,16},{16,0},{32,48},{48,32},{64,80},{80,64},{96,112},{112,96},{1... | collective-permute-start | bytes 1966088 | tf_op jit(solution)/shard_map/ppermute | solution.py:357
  48.8 41.2 %collective-permute-start.9 = (bf16[8,32,1280]{2,1,0:T(8,128)(2,1)}, bf16[8,32,1280]{2,1,0:T(8,128)(2,1)S(1)}, u32[]{:S(2)}, u32[]{:S(2)}) collective-permute-start(bf16[8,32,1280]{2,1,0:T(8,128)(2,1)} %get-tuple-element.28), channel_id=1, source_target_pairs={{0,17},{1,16},{16,1},{17,0},{2,19},{3,18},{18,3},{19,2},{4,21},{5,... | collective-permute-start | bytes 1966088 | tf_op jit(solution)/shard_map/ppermute | solution.py:358
  68.1 39.0 %copy-start.6 = (bf16[8,32,1280]{2,1,0:T(8,128)(2,1)}, bf16[8,32,1280]{2,1,0:T(8,128)(2,1)S(1)}, u32[]{:S(2)}) copy-start(bf16[8,32,1280]{2,1,0:T(8,128)(2,1)S(1)} %collective-permute-done.8) | copy-start | bytes 1966084
  90.0 17.1 %copy-start.7 = (bf16[8,32,1280]{2,1,0:T(8,128)(2,1)}, bf16[8,32,1280]{2,1,0:T(8,128)(2,1)S(1)}, u32[]{:S(2)}) copy-start(bf16[8,32,1280]{2,1,0:T(8,128)(2,1)S(1)} %collective-permute-done.9) | copy-start | bytes 1966084
  90.0 17.1 %copy-start.4 = (bf16[1280,512]{1,0:T(8,128)(2,1)}, bf16[1280,512]{1,0:T(8,128)(2,1)S(1)}, u32[]{:S(2)}) copy-start(bf16[1280,512]{1,0:T(8,128)(2,1)S(1)} %collective-permute-done.6.near_a.near0_a) | copy-start | bytes 3932164
  90.0 10.3 %copy-start.1 = (bf16[1280,1024]{1,0:T(8,128)(2,1)}, bf16[1280,1024]{1,0:T(8,128)(2,1)S(1)}, u32[]{:S(2)}) copy-start(bf16[1280,1024]{1,0:T(8,128)(2,1)S(1)} %collective-permute-done.7.zed.zed_b.zed0_b.zed1_b) | copy-start | bytes 7864324
  90.0 17.1 %collective-permute-start.10 = (bf16[1280,512]{1,0:T(8,128)(2,1)S(1)}, bf16[1280,512]{1,0:T(8,128)(2,1)S(1)}, u32[]{:S(2)}, u32[]{:S(2)}) collective-permute-start(bf16[1280,512]{1,0:T(8,128)(2,1)S(1)} %collective-permute-done.6.near_a.near0_a), channel_id=1, source_target_pairs={{0,1},{1,0},{2,3},{3,2},{4,5},{5,4},{6,7},{7,6},{8,9},{9,8},{10,11... | collective-permute-start | bytes 3932168 | tf_op jit(solution)/shard_map/ppermute | solution.py:359
  90.1 57.1 %collective-permute-start.11 = (bf16[1280,512]{1,0:T(8,128)(2,1)}, bf16[1280,512]{1,0:T(8,128)(2,1)}, u32[]{:S(2)}, u32[]{:S(2)}) collective-permute-start(bf16[1280,512]{1,0:T(8,128)(2,1)} %get-tuple-element.35), channel_id=1, source_target_pairs={{32,0},{64,32},{96,64},{128,96},{160,128},{192,160},{224,192},{16,... | collective-permute-start | bytes 3932168 | tf_op jit(solution)/shard_map/ppermute | solution.py:356
  92.2 28.4 %collective-permute-start.12 = (bf16[8,32,1280]{2,1,0:T(8,128)(2,1)}, bf16[8,32,1280]{2,1,0:T(8,128)(2,1)S(1)}, u32[]{:S(2)}, u32[]{:S(2)}) collective-permute-start(bf16[8,32,1280]{2,1,0:T(8,128)(2,1)} %get-tuple-element.25), channel_id=1, source_target_pairs={{0,16},{16,0},{32,48},{48,32},{64,80},{80,64},{96,112},{112,96},{1... | collective-permute-start | bytes 1966088 | tf_op jit(solution)/shard_map/ppermute | solution.py:357
  100.3 46.8 %collective-permute-start.13 = (bf16[8,32,1280]{2,1,0:T(8,128)(2,1)}, bf16[8,32,1280]{2,1,0:T(8,128)(2,1)}, u32[]{:S(2)}, u32[]{:S(2)}) collective-permute-start(bf16[8,32,1280]{2,1,0:T(8,128)(2,1)} %get-tuple-element.36), channel_id=1, source_target_pairs={{0,17},{1,16},{16,1},{17,0},{2,19},{3,18},{18,3},{19,2},{4,21},{5,... | collective-permute-start | bytes 1966088 | tf_op jit(solution)/shard_map/ppermute | solution.py:358
  107.1 1.1 copy-start.5
  115.5 46.4 %all-to-all-start = ((f32[8,96,512]{2,1,0:T(8,128)}), f32[8,96,512]{2,1,0:T(8,128)S(1)}, u32[]{:S(2)}, u32[]{:S(2)}) async-start(f32[8,96,512]{2,1,0:T(8,128)} %early.1), calls=%async_computation | async-start | bytes 3145728 | tf_op jit(solution)/shard_map/all_to_all | solution.py:373
  120.6 29.8 %copy-start.10 = (bf16[8,32,1280]{2,1,0:T(8,128)(2,1)}, bf16[8,32,1280]{2,1,0:T(8,128)(2,1)S(1)}, u32[]{:S(2)}) copy-start(bf16[8,32,1280]{2,1,0:T(8,128)(2,1)S(1)} %collective-permute-done.12) | copy-start | bytes 1966084
  147.2 3.2 %collective-permute-start.14 = (bf16[1280,512]{1,0:T(8,128)(2,1)}, bf16[1280,512]{1,0:T(8,128)(2,1)S(1)}, u32[]{:S(2)}, u32[]{:S(2)}) collective-permute-start(bf16[1280,512]{1,0:T(8,128)(2,1)} %collective-permute-done.11.near1_a), channel_id=1, source_target_pairs={{0,1},{1,0},{2,3},{3,2},{4,5},{5,4},{6,7},{7,6},{8,9},{9,8},{10,11... | collective-permute-start | bytes 3932168 | tf_op jit(solution)/shard_map/ppermute | solution.py:359
  150.4 1.1 copy-start.9
  161.9 37.6 %copy-start.2 = (f32[8,96,512]{2,1,0:T(8,128)}, f32[8,96,512]{2,1,0:T(8,128)S(1)}, u32[]{:S(2)}) copy-start(f32[8,96,512]{2,1,0:T(8,128)S(1)} %all-to-all-done.early) | copy-start | bytes 4718596
  199.6 7.9 %copy-start = (s32[16]{0:T(128)S(1)}, s32[16]{0:T(128)}, u32[]{:S(2)}) copy-start(s32[16]{0:T(128)} %param.5) | copy-start | bytes 196
  203.9 14.4 %all-to-all-start.2 = ((f32[16,64,128]{2,1,0:T(8,128)}), f32[16,64,128]{2,1,0:T(8,128)S(1)}, u32[]{:S(2)}, u32[]{:S(2)}) async-start(f32[16,64,128]{2,1,0:T(8,128)} %get-tuple-element.40), calls=%async_computation.2 | async-start | bytes 1048576 | tf_op jit(solution)/shard_map/all_to_all | solution.py:380
  218.3 15.2 %copy-start.8 = (f32[16,64,128]{2,1,0:T(8,128)}, f32[16,64,128]{2,1,0:T(8,128)S(1)}, u32[]{:S(2)}) copy-start(f32[16,64,128]{2,1,0:T(8,128)S(1)} %all-to-all-done.2) | copy-start | bytes 1572868
  218.3 15.2 %collective-permute-start.15 = (f32[1024,128]{1,0:T(8,128)S(1)}, f32[1024,128]{1,0:T(8,128)S(1)}, u32[]{:S(2)}, u32[]{:S(2)}) collective-permute-start(f32[1024,128]{1,0:T(8,128)S(1)} %bitcast.35), channel_id=1, source_target_pairs={{0,32},{32,64},{64,96},{96,128},{128,160},{160,192},{192,224},{48,... | collective-permute-start | bytes 1572872 | tf_op jit(solution)/shard_map/ppermute | solution.py:381
  221.8 9.2 %collective-permute-start.16 = (f32[64,1024]{1,0:T(8,128)}, f32[64,1024]{1,0:T(8,128)S(1)}, u32[]{:S(2)}, u32[]{:S(2)}) collective-permute-start(f32[64,1024]{1,0:T(8,128)} %get-tuple-element.42), channel_id=1, source_target_pairs={{0,16},{16,0},{32,48},{48,32},{64,80},{80,64},{96,112},{112,96},{1... | collective-permute-start | bytes 786440 | tf_op jit(solution)/shard_map/ppermute | solution.py:379
  231.0 2.5 %copy-start.12 = (f32[64,1024]{1,0:T(8,128)}, f32[64,1024]{1,0:T(8,128)S(1)}, u32[]{:S(2)}) copy-start(f32[64,1024]{1,0:T(8,128)S(1)} %collective-permute-done.16.beside) | copy-start | bytes 786436
  233.5 0.8 copy-start.11
Sparse Core Ops, SparseCore 0:
  42.0 71.8 reduce-scatter.1

commit v2 on v1

--- a/solution.py
+++ b/solution.py
@@ -12,7 +12,6 @@
 SIZES = (8, 2, 2, 4, 2)
 SNP = ("z", "yh")
 SAMP = ("yl", "x", "core")
-CHIP = ("yl", "x")
 NSNP = 16
 B = 1024
 DEPTH = 1280
@@ -40,6 +39,10 @@
     return x + parts[0] + parts[1] + parts[2]
 
 
+def chip_of(piece):
+    return piece // 2 + 4 * (piece % 2)
+
+
 def params():
     return pltpu.CompilerParams(vmem_limit_bytes=56 << 20)
 
@@ -74,10 +77,10 @@
     turned = z.T
 
     def store(*outs):
-        for c in range(PIECES):
+        for p in range(PIECES):
             for k, out in enumerate(outs):
-                at = 2 * ROWS * c + TURN * k
-                out[c] = turned[at : at + TURN]
+                at = 2 * ROWS * chip_of(p) + TURN * k
+                out[p] = turned[at : at + TURN]
 
     pl.when(meta[0] == 0)(lambda: store(kept0, kept1, sent0, sent1))
     pl.when(meta[0] != 0)(lambda: store(sent0, sent1, kept0, kept1))
@@ -110,37 +113,6 @@
     return [t.reshape(LEFT) for t in turned]
 
 
-def own_kernel(meta, kept0, kept1, sent0, sent1, right, out):
-    core = meta[0]
-    r = right[...]
-    for left, half, at in (
-        (kept0, core, 0),
-        (kept1, core, TURN),
-        (sent0, 1 - core, 0),
-        (sent1, 1 - core, TURN),
-    ):
-        acc = matmul(left[...], r)
-        for c in range(PIECES):
-            out[c, half, at : at + TURN] = acc[TURN * c : TURN * (c + 1)]
-
-
-def own_product(meta, turned, zed):
-    out = pl.pallas_call(
-        own_kernel,
-        name="own",
-        out_shape=f32(PIECES, 2, ROWS, B),
-        grid_spec=pltpu.PrefetchScalarGridSpec(
-            num_scalar_prefetch=1,
-            grid=(B // STEP,),
-            in_specs=[whole(LEFT)] * 4 + [pl.BlockSpec((DEPTH, STEP), lambda j, m: (0, j))],
-            out_specs=pl.BlockSpec((PIECES, 2, ROWS, STEP), lambda j, m: (0, 0, 0, j)),
-        ),
-        compiler_params=params(),
-        cost_estimate=cost(2 * DEPTH * B * B, 4 * DEPTH * B + 4 * B * B),
-    )(meta, *flat(*turned), zed)
-    return out.reshape(B, B)
-
-
 def turn_kernel(meta, zed, out0, out1):
     turned = zed[...].T
 
@@ -161,7 +133,7 @@
         grid_spec=pltpu.PrefetchScalarGridSpec(
             num_scalar_prefetch=1,
             grid=(PIECES,),
-            in_specs=[pl.BlockSpec((DEPTH, 2 * ROWS), lambda c, m: (0, c))],
+            in_specs=[pl.BlockSpec((DEPTH, 2 * ROWS), lambda p, m: (0, p // 2 + 4 * (p % 2)))],
             out_specs=(out, out),
         ),
         compiler_params=params(),
@@ -172,6 +144,58 @@
 def store_pieces(out, at, left_a, left_b, right_a, right_b):
     acc = matmul(left_a[...], right_a[...]) + matmul(left_b[...], right_b[...])
     out[:, at : at + TURN] = acc.reshape(PIECES, TURN, STEP)
+
+
+def own_kernel(meta, own0_a, own1_a, own0_b, own1_b, zed_a, zed_b, out):
+    store_pieces(out, 0, own0_a, own0_b, zed_a, zed_b)
+    store_pieces(out, TURN, own1_a, own1_b, zed_a, zed_b)
+
+
+def own_product(meta, own_a, own_b, zed):
+    right = pl.BlockSpec((DEPTH, STEP), lambda j, m: (0, j))
+    return pl.pallas_call(
+        own_kernel,
+        name="own",
+        out_shape=f32(PIECES, ROWS, B),
+        grid_spec=pltpu.PrefetchScalarGridSpec(
+            num_scalar_prefetch=1,
+            grid=(B // STEP,),
+            in_specs=[whole(LEFT)] * 4 + [right] * 2,
+            out_specs=pl.BlockSpec((PIECES, ROWS, STEP), lambda j, m: (0, 0, j)),
+        ),
+        compiler_params=params(),
+        cost_estimate=cost(2 * DEPTH * B * B, 4 * DEPTH * B + 4 * B * B),
+    )(meta, *flat(*own_a, *own_b), *zed)
+
+
+def fold_kernel(meta, parts, keep, send):
+    mine = meta[2]
+    for out, half in ((keep, mine), (send, 1 - mine)):
+        out[...] = parts[0, half] + parts[1, half] + parts[2, half] + parts[3, half]
+
+
+def after(value, *others):
+    return lax.optimization_barrier((value, *others))[0]
+
+
+def fold(meta, parts, *others):
+    _, rows, columns = parts.shape
+    parts = after(lax.all_to_all(parts.reshape(4, 2, rows, columns), "x", 0, 0), *others)
+    out = pl.BlockSpec((rows, STEP), lambda j, m: (0, j))
+    keep, send = pl.pallas_call(
+        fold_kernel,
+        name="fold",
+        out_shape=(f32(rows, columns),) * 2,
+        grid_spec=pltpu.PrefetchScalarGridSpec(
+            num_scalar_prefetch=1,
+            grid=(columns // STEP,),
+            in_specs=[pl.BlockSpec((4, 2, rows, STEP), lambda j, m: (0, 0, 0, j))],
+            out_specs=(out, out),
+        ),
+        compiler_params=params(),
+        cost_estimate=cost(6 * rows * columns, 40 * rows * columns),
+    )(meta, parts)
+    return keep, lax.ppermute(send, "yl", SWAP)
 
 
 def early_kernel(
@@ -253,12 +277,9 @@
     )(meta, *flat(*own_a, *own_b, *other0, *other1), *near0, *near1, *zed, *zed)
 
 
-def gather_kernel(meta, early, late, rows2, rows1, both):
-    a = early[0]
-    b = late[0]
-    for r in range(1, PIECES):
-        a = a + early[r]
-        b = b + late[r]
+def gather_kernel(meta, early_a, early_b, late_a, late_b, rows2, rows1, both):
+    a = early_a[...] + early_b[...]
+    b = late_a[...] + late_b[...]
     rows2[:, :HALF] = a[:ROWS]
     rows2[:, HALF:] = b[:ROWS]
     rows1[:TURN, :HALF] = a[ROWS:]
@@ -278,7 +299,7 @@
         grid_spec=pltpu.PrefetchScalarGridSpec(
             num_scalar_prefetch=1,
             grid=(1,),
-            in_specs=[whole(early.shape), whole(late.shape)],
+            in_specs=[whole(early[0].shape)] * 2 + [whole(late[0].shape)] * 2,
             out_specs=(
                 whole((ROWS, B)),
                 whole((ROWS, B)),
@@ -287,10 +308,10 @@
         ),
         compiler_params=params(),
         cost_estimate=cost(PIECES * ROWS * 2 * B, 4 * PIECES * ROWS * 2 * B),
-    )(meta, early, late)
-
-
-def assemble_kernel(flags, far, here, rows2, beside, rows0, out):
+    )(meta, *early, *late)
+
+
+def assemble_kernel(flags, far, here, rows2, beside, rows0_a, rows0_b, out):
     even = flags[5] == 0
     far_turned = far[...].T
     near = jnp.where(even, far_turned[ROWS:], here[...].T[ROWS:])
@@ -299,7 +320,7 @@
     blocks = (
         jnp.where(even, far2, mine2),
         near,
-        rows0[...],
+        rows0_a[...] + rows0_b[...],
         beside[...],
         jnp.where(even, mine2, far2),
     )
@@ -315,12 +336,12 @@
         grid_spec=pltpu.PrefetchScalarGridSpec(
             num_scalar_prefetch=1,
             grid=(1,),
-            in_specs=[whole((B, 2 * ROWS))] * 2 + [whole((ROWS, B))] * 3,
+            in_specs=[whole((B, 2 * ROWS))] * 2 + [whole((ROWS, B))] * 4,
             out_specs=whole((ROWS, 5 * B)),
         ),
         compiler_params=params(),
         cost_estimate=cost(ROWS * 5 * B, 40 * ROWS * B),
-    )(flags, far, here, rows2, beside, rows0)
+    )(flags, far, here, rows2, beside, *rows0)
 
 
 def kept_flags(band, mine):
@@ -336,7 +357,7 @@
     mine = lax.axis_index(SNP)
     odd = lax.axis_index("yh").reshape(1)
     core = lax.axis_index("core").reshape(1)
-    meta = jnp.concatenate([core, odd]).astype(jnp.int32)
+    meta = jnp.concatenate([core, odd, lax.axis_index("yl").reshape(1)]).astype(jnp.int32)
 
     weight = observed.astype(jnp.float32)
     values = dosage.astype(jnp.float32)
@@ -360,21 +381,22 @@
     zed_b = swap(zed)
     near0 = along(zed0)
     other0 = (across(kept0), athwart(sent0))
-    near1 = along(zed1)
-    other1 = (across(kept1), athwart(sent1))
-
-    own = own_product(meta, (kept0, kept1, sent0, sent1), zed)
-    rows0 = lax.psum_scatter(own, SAMP, scatter_dimension=0, tiled=True)
-    near0, zed_b, other0 = lax.optimization_barrier((near0, zed_b, other0))
+
     own_a = (kept0, kept1)
     own_b = turn(meta, zed_b)
+    rows0 = own_product(meta, own_a, own_b, (zed, zed_b))
+    near0, other0 = after((near0, other0), rows0)
+    near1 = along(after(zed1, near0, other0))
+    other1 = (across(after(kept1, near0, other0)), athwart(after(sent1, near0, other0)))
     near0 = (near0, swap(near0))
     early = early_product(meta, own_a, own_b, other0, near0, (zed, zed_b))
-    early = lax.all_to_all(early, CHIP, 0, 0)
-    near1, other1 = lax.optimization_barrier((near1, other1))
+    rows0 = fold(meta, rows0, early)
+    early = after(early, rows0[0])
+    near1, other1 = after((near1, other1), early)
     near1 = (near1, swap(near1))
     late = late_product(meta, own_a, own_b, other0, other1, near0, near1, (zed, zed_b))
-    late = lax.all_to_all(late, CHIP, 0, 0)
+    early = fold(meta, early, late)
+    late = fold(meta, after(late, early[0]))
     rows2, rows1, both = gather_pieces(meta, early, late)
     beside = lax.ppermute(rows1, SNP, TO_OTHER)
     here = lax.all_to_all(both, SAMP, 0, 0).reshape(B, 2 * ROWS)

time: 246 us -> 224 us (0.911)
  waiting for transfers between devices: 94.9 us -> 71.5 us
  between operations: 13.6 us -> 0.22 us
  Pallas kernels: 49.3 us -> 58.4 us
  local copies, waits for them, and re-layouts: 4.19 us -> 9.11 us
    ppermute x2, waiting for transfers between devices: 48.5 us -> 13.3 us  [on_device(): lax.ppermute(t, ('yh', 'core'), [(i, 3 - i) for i in range(4)])]
    ppermute x0 -> x3, waiting for transfers between devices: none -> 17.1 us  [fold(): return (keep, lax.ppermute(send, 'yl', SWAP))]
    pallas_call x1 -> x4, Pallas kernels: 7.66 us -> 18.1 us  [the longest x3 10.3 us: fold(): pl.pallas_call(fold_kernel, name='fold', out_shape=(f32(rows, columns),)...]
    all_to_all x1 -> x2, waiting for transfers between devices: 0.01 us -> 9.81 us  [fold(): lax.all_to_all(parts.reshape(4, 2, rows, columns), 'x', 0, 0)]
    ppermute x2, waiting for transfers between devices: 20.3 us -> 11 us  [on_device(): across = lambda t: lax.ppermute(t, SNP, TO_OTHER)]
    ppermute x2, starting transfers between devices: 12.9 us -> 6.83 us  [on_device(): across = lambda t: lax.ppermute(t, SNP, TO_OTHER)]
    unnamed x26 -> x32, local copies, waits for them, and re-layouts: 2.94 us -> 7.86 us
    ppermute x2, starting transfers between devices: 0.01 us -> 4.61 us  [on_device(): lax.ppermute(t, ('yh', 'core'), [(i, 3 - i) for i in range(4)])]
  transfers between devices with their start and end apart: 20 -> 23, of which waited for: 12 -> 13; matrix products, arithmetic and copies ran while one was open for 1% -> 1% of each run, Pallas kernels for 15% -> 16%
where the time goes in v2:
time: 224 us; the launch traced here: 223 us
  waiting for transfers between devices  71.5 us (32%)
  Pallas kernels  58.4 us (26%)
  starting transfers between devices  40.1 us (18%)
  blocking collectives  36.4 us (16%)
  local copies, waits for them, and re-layouts  9.11 us (4%)
  other arithmetic  7.27 us (3%)
    all_to_all x1, blocking collectives, fold(): lax.all_to_all(parts.reshape(4, 2, rows, columns), 'x', 0, 0)  36.4 us
    ppermute x3, waiting for transfers between devices, fold(): return (keep, lax.ppermute(send, 'yl', SWAP))  17.1 us
    ppermute x2, waiting for transfers between devices, on_device(): lax.ppermute(t, ('yh', 'core'), [(i, 3 - i) for i in range(4)])  13.3 us
    ppermute x2, waiting for transfers between devices, on_device(): across = lambda t: lax.ppermute(t, SNP, TO_OTHER)  11 us
    pallas_call x1, Pallas kernels, late_product(): pl.pallas_call(late_kernel, name='late', out_shape=f32(PIECES, rows, HALF...  10.5 us
    pallas_call x3, Pallas kernels, fold(): pl.pallas_call(fold_kernel, name='fold', out_shape=(f32(rows, columns),)...  10.3 us
    all_to_all x1, waiting for transfers between devices, on_device(): here = lax.all_to_all(both, SAMP, 0, 0).reshape(B, 2 * ROWS)  10.2 us
    all_to_all x2, waiting for transfers between devices, fold(): lax.all_to_all(parts.reshape(4, 2, rows, columns), 'x', 0, 0)  9.81 us
  transfers between devices with their start and end apart: 23, of which 13 were waited for; matrix products, arithmetic and copies ran while one was open for 1% of the time, Pallas kernels for 16%

profile of v2, /device:TPU:64, one launch (start us, length us, event | category | flops | bytes accessed | tf_op | source)
XLA Modules:
  0.0 223.0 jit_solution(1538969937947766714)
XLA Ops:
  0.0 4.7 %fusion.1 = (f32[1024]{0:T(1024)S(1)}, f32[1024]{0:T(1024)S(1)}, f32[1024]{0:T(1024)S(1)}) fusion(bf16[1280,1024]{1,0:T(8,128)(2,1)} %dosage.1, s32[1280,1024]{1,0:T(8,128)} %observed.1), kind=kLoop, calls=%fused_computation.5 | loop fusion | flops 9171968 | bytes 7876608 | tf_op jit(solution)/shard_map/reduce_sum | solution.py:367
  4.7 1.7 collective-permute-start.1
  6.3 0.0 collective-permute-start.2
  6.3 0.6 collective-permute-start
  6.9 1.6 collective-permute-done.1
  8.5 1.0 collective-permute-done.2
  9.5 0.0 collective-permute-done
  9.5 2.8 %collective-permute-start.5 = (f32[3,1024]{1,0:T(4,128)S(1)}, f32[3,1024]{1,0:T(4,128)S(1)}, u32[]{:S(2)}, u32[]{:S(2)}) collective-permute-start(f32[3,1024]{1,0:T(4,128)S(1)} %add_add_fusion.1), channel_id=1, source_target_pairs={{0,6},{2,0},{4,2},{6,4},{1,7},{3,1},{5,3},{7,5},{8,14},{10,8},{12,... | collective-permute-start | bytes 36872 | tf_op jit(solution)/shard_map/ppermute | solution.py:37
  12.4 0.8 collective-permute-start.4
  13.2 0.9 collective-permute-start.3
  14.1 0.7 pad_add_fusion.1.meta
  14.7 0.0 collective-permute-done.5
  14.7 2.9 %collective-permute-done.4 = f32[3,1024]{1,0:T(4,128)S(1)} collective-permute-done((f32[3,1024]{1,0:T(4,128)S(1)}, f32[3,1024]{1,0:T(4,128)S(1)}, u32[]{:S(2)}, u32[]{:S(2)}) %collective-permute-start.4) | collective-permute-done | bytes 12320 | tf_op jit(solution)/shard_map/ppermute | solution.py:37
  17.6 0.5 collective-permute-done.3
  18.2 0.6 pad_maximum_fusion.1.stats
  18.8 9.2 %standardize.1 = (bf16[1280,1024]{1,0:T(8,128)(2,1)}, bf16[1280,512]{1,0:T(8,128)(2,1)}, bf16[1280,512]{1,0:T(8,128)(2,1)}, bf16[8,32,1280]{2,1,0:T(8,128)(2,1)}...) custom-call(s32[3]{0:T(128)} %pad_add_fusion.1.meta, ...), custom_call_target="tpu_custom_call" | custom-call | flops 1024 | bytes 1024 | tf_op jit(solution)/shard_map/standardize/pallas_call | solution.py:93
  28.0 0.1 collective-permute-start.6
  28.1 2.0 collective-permute-start.7
  30.1 4.6 %collective-permute-start.9 = (bf16[8,32,1280]{2,1,0:T(8,128)(2,1)}, bf16[8,32,1280]{2,1,0:T(8,128)(2,1)S(1)}, u32[]{:S(2)}, u32[]{:S(2)}) collective-permute-start(bf16[8,32,1280]{2,1,0:T(8,128)(2,1)} %get-tuple-element.42), channel_id=1, source_target_pairs={{0,17},{1,16},{16,1},{17,0},{2,19},{3,18},{18,3},{19,2},{4,21},{5,... | collective-permute-start | bytes 1966088 | tf_op jit(solution)/shard_map/ppermute | solution.py:379
  34.7 0.3 collective-permute-start.8
  35.0 0.0 collective-permute-done.6.zed.zed_b.zed0_b.zed1_b
  35.0 1.5 copy-done.1
  36.5 6.7 %turn.1 = (bf16[8,32,1280]{2,1,0:T(8,128)(2,1)}, bf16[8,32,1280]{2,1,0:T(8,128)(2,1)}) custom-call(s32[3]{0:T(128)} %pad_add_fusion.1.meta, bf16[1280,1024]{1,0:T(8,128)(2,1)} %copy-done.1), custom_call_target="tpu_custom_call" | custom-call | flops 1024 | bytes 1024 | tf_op jit(solution)/shard_map/turn/pallas_call | solution.py:129
  43.3 7.8 %own.1 = f32[8,64,1024]{2,1,0:T(8,128)} custom-call(s32[3]{0:T(128)} %pad_add_fusion.1.meta, bf16[256,1280]{1,0:T(8,128)(2,1)} %bitcast.24, bf16[256,1280]{1,0:T(8,128)(2,1)} %bitcast.27, bf16[256,1280]{1,0:T(8,128)(2,1)} %bitcast.30, bf16[256,1280]{1,0:T(8,128)(2,1)} %bitcast.33, bf16[1280,1024]{1,0:T(8,128)(2,1)} %get-tuple-element.38.zed_a.zed0_a.zed1_a, ...), custom_call_target="tpu_custom_call" | custom-call | flops 1024 | bytes 1024 | tf_op jit(solution)/shard_map/own/pallas_call | solution.py:156
  51.1 3.7 %all-to-all-start = ((f32[4,2,64,1024]{3,2,1,0:T(8,128)}), f32[4,2,64,1024]{3,2,1,0:T(8,128)S(1)}, u32[]{:S(2)}, u32[]{:S(2)}) async-start(f32[4,2,64,1024]{3,2,1,0:T(8,128)} %bitcast.22), calls=%async_computation | async-start | bytes 4194304 | tf_op jit(solution)/shard_map/all_to_all | solution.py:183
  54.9 9.5 %collective-permute-done.8 = bf16[8,32,1280]{2,1,0:T(8,128)(2,1)} collective-permute-done((bf16[8,32,1280]{2,1,0:T(8,128)(2,1)}, bf16[8,32,1280]{2,1,0:T(8,128)(2,1)}, u32[]{:S(2)}, u32[]{:S(2)}) %collective-permute-start.8) | collective-permute-done | bytes 655392 | tf_op jit(solution)/shard_map/ppermute | solution.py:378
  64.4 2.0 collective-permute-start.11
  66.4 6.5 %collective-permute-start.12 = (bf16[8,32,1280]{2,1,0:T(8,128)(2,1)S(1)}, bf16[8,32,1280]{2,1,0:T(8,128)(2,1)}, u32[]{:S(2)}, u32[]{:S(2)}) collective-permute-start(bf16[8,32,1280]{2,1,0:T(8,128)(2,1)S(1)} %copy-done.4), channel_id=1, source_target_pairs={{0,16},{16,0},{32,48},{48,32},{64,80},{80,64},{96,112},{112,96},{1... | collective-permute-start | bytes 1966088 | tf_op jit(solution)/shard_map/ppermute | solution.py:378
  73.0 1.0 copy-done.5
  74.0 7.4 %early.1 = f32[8,96,512]{2,1,0:T(8,128)} custom-call(s32[3]{0:T(128)} %pad_add_fusion.1.meta, bf16[256,1280]{1,0:T(8,128)(2,1)} %bitcast.25, bf16[256,1280]{1,0:T(8,128)(2,1)} %bitcast.28, bf16[256,1280]{1,0:T(8,128)(2,1)} %bitcast.31, bf16[256,1280]{1,0:T(8,128)(2,1)} %bitcast.34, bf16[256,1280]{1,0:T(8,128)(2,1)} %bitcast.12.other_a.other0_a, ...), custom_call_target="tpu_custom_call" | custom-call | flops 1024 | bytes 1024 | tf_op jit(solution)/shard_map/early/pallas_call | solution.py:214
  81.4 0.2 all-to-all-done.parts
  81.6 1.3 copy-done.2
  82.9 4.2 %fold.3 = (f32[64,1024]{1,0:T(8,128)}, f32[64,1024]{1,0:T(8,128)}) custom-call(s32[3]{0:T(128)} %pad_add_fusion.1.meta, f32[4,2,64,1024]{3,2,1,0:T(8,128)} %copy-done.2), custom_call_target="tpu_custom_call" | custom-call | flops 1024 | bytes 1024 | tf_op jit(solution)/shard_map/fold/pallas_call | solution.py:185
  87.1 1.5 collective-permute-done.12
  88.6 13.3 %collective-permute-done.13 = bf16[8,32,1280]{2,1,0:T(8,128)(2,1)} collective-permute-done((bf16[8,32,1280]{2,1,0:T(8,128)(2,1)}, bf16[8,32,1280]{2,1,0:T(8,128)(2,1)}, u32[]{:S(2)}, u32[]{:S(2)}) %collective-permute-start.13) | collective-permute-done | bytes 655392 | tf_op jit(solution)/shard_map/ppermute | solution.py:379
  101.8 0.2 collective-permute-start.14
  102.1 3.7 %all-to-all-start.1 = ((f32[4,2,96,512]{3,2,1,0:T(8,128)}), f32[4,2,96,512]{3,2,1,0:T(8,128)S(1)}, u32[]{:S(2)}, u32[]{:S(2)}) async-start(f32[4,2,96,512]{3,2,1,0:T(8,128)} %bitcast.23), calls=%async_computation.1 | async-start | bytes 3145728 | tf_op jit(solution)/shard_map/all_to_all | solution.py:183
  105.8 1.1 copy-done.8
  106.9 10.5 %late.1 = f32[8,160,512]{2,1,0:T(8,128)} custom-call(s32[3]{0:T(128)} %pad_add_fusion.1.meta, bf16[256,1280]{1,0:T(8,128)(2,1)} %bitcast.26, bf16[256,1280]{1,0:T(8,128)(2,1)} %bitcast.29, bf16[256,1280]{1,0:T(8,128)(2,1)} %bitcast.32, bf16[256,1280]{1,0:T(8,128)(2,1)} %bitcast.35, bf16[256,1280]{1,0:T(8,128)(2,1)} %bitcast.12.other_a.other0_a, ...), custom_call_target="tpu_custom_call" | custom-call | flops 1024 | bytes 1024 | tf_op jit(solution)/shard_map/late/pallas_call | solution.py:265
  117.4 9.6 %all-to-all-done.1.parts = f32[4,2,96,512]{3,2,1,0:T(8,128)S(1)} async-done(((f32[4,2,96,512]{3,2,1,0:T(8,128)}), f32[4,2,96,512]{3,2,1,0:T(8,128)S(1)}, u32[]{:S(2)}, u32[]{:S(2)}) %all-to-all-start.1) | async-done | bytes 1572896 | tf_op jit(solution)/shard_map/all_to_all | solution.py:183
  127.1 1.2 copy-done.3
  128.2 2.8 %fold.4 = (f32[96,512]{1,0:T(8,128)}, f32[96,512]{1,0:T(8,128)}) custom-call(s32[3]{0:T(128)} %pad_add_fusion.1.meta, f32[4,2,96,512]{3,2,1,0:T(8,128)} %copy-done.3), custom_call_target="tpu_custom_call" | custom-call | flops 1024 | bytes 1024 | tf_op jit(solution)/shard_map/fold/pallas_call | solution.py:185
  131.0 36.4 %all_to_all.20.parts = f32[4,2,160,512]{3,2,1,0:T(8,128)} all-to-all(f32[4,2,160,512]{3,2,1,0:T(8,128)} %bitcast.21), channel_id=1, replica_groups=mesh['z'=8,'yh'=2,'yl'=2,'x'=4,'core'=2] {'x'}, dimensions={0} | all-to-all | bytes 5242880 | tf_op jit(solution)/shard_map/all_to_all | solution.py:183
  167.4 3.3 %fold.5 = (f32[160,512]{1,0:T(8,128)}, f32[160,512]{1,0:T(8,128)}) custom-call(s32[3]{0:T(128)} %pad_add_fusion.1.meta, f32[4,2,160,512]{3,2,1,0:T(8,128)} %all_to_all.20.parts), custom_call_target="tpu_custom_call" | custom-call | flops 1024 | bytes 1024 | tf_op jit(solution)/shard_map/fold/pallas_call | solution.py:185
  170.7 0.3 collective-permute-start.16
  171.0 1.7 collective-permute-start.15
  172.7 10.6 %collective-permute-done.15.early_b = f32[96,512]{1,0:T(8,128)S(1)} collective-permute-done((f32[96,512]{1,0:T(8,128)S(1)}, f32[96,512]{1,0:T(8,128)S(1)}, u32[]{:S(2)}, u32[]{:S(2)}) %collective-permute-start.15) | collective-permute-done | bytes 196640 | tf_op jit(solution)/shard_map/ppermute | solution.py:198
  183.3 0.7 copy-done.13
  184.0 0.1 copy-done.10
  184.1 3.0 %gather.7 = (f32[64,1024]{1,0:T(8,128)}, f32[64,1024]{1,0:T(8,128)}, f32[16,64,128]{2,1,0:T(8,128)}) custom-call(s32[3]{0:T(128)} %pad_add_fusion.1.meta, f32[96,512]{1,0:T(8,128)} %get-tuple-element.58.early_a, f32[96,512]{1,0:T(8,128)} %copy-done.13, f32[160,512]{1,0:T(8,128)} %get-tuple-element.61.late_a, f32[160,512]{1,0:T(8,128)} %copy-done.10), custom_call_target="tpu_custom_call" | custom-call | flops 1024 | bytes 1024 | tf_op jit(solution)/shard_map/gather/pallas_call | solution.py:295
  187.1 3.6 %all-to-all-start.3 = ((f32[16,64,128]{2,1,0:T(8,128)}), f32[16,64,128]{2,1,0:T(8,128)S(1)}, u32[]{:S(2)}, u32[]{:S(2)}) async-start(f32[16,64,128]{2,1,0:T(8,128)} %get-tuple-element.63), calls=%async_computation.3 | async-start | bytes 1048576 | tf_op jit(solution)/shard_map/all_to_all | solution.py:402
  190.7 0.6 dynamic_slice.3
  191.3 10.2 %all-to-all-done.3 = f32[16,64,128]{2,1,0:T(8,128)S(1)} async-done(((f32[16,64,128]{2,1,0:T(8,128)}), f32[16,64,128]{2,1,0:T(8,128)S(1)}, u32[]{:S(2)}, u32[]{:S(2)}) %all-to-all-start.3) | async-done | bytes 524320 | tf_op jit(solution)/shard_map/all_to_all | solution.py:402
  201.5 2.9 %collective-permute-start.17 = (f32[1024,128]{1,0:T(8,128)S(1)}, f32[1024,128]{1,0:T(8,128)S(1)}, u32[]{:S(2)}, u32[]{:S(2)}) collective-permute-start(f32[1024,128]{1,0:T(8,128)S(1)} %bitcast.38), channel_id=1, source_target_pairs={{0,32},{32,64},{64,96},{96,128},{128,160},{160,192},{192,224},{48,... | collective-permute-start | bytes 1572872 | tf_op jit(solution)/shard_map/ppermute | solution.py:403
  204.4 0.6 gather_fusion
  205.1 0.6 collective-permute-start.19
  205.7 1.0 collective-permute-start.18
  206.6 0.6 and_convert_fusion
  207.3 0.7 pad_add_fusion.flags
  207.9 6.5 %collective-permute-done.19.rows0_b = f32[64,1024]{1,0:T(8,128)S(1)} collective-permute-done((f32[64,1024]{1,0:T(8,128)S(1)}, f32[64,1024]{1,0:T(8,128)S(1)}, u32[]{:S(2)}, u32[]{:S(2)}) %collective-permute-start.19) | collective-permute-done | bytes 262176 | tf_op jit(solution)/shard_map/ppermute | solution.py:198
  214.4 4.1 %collective-permute-done.18.beside = f32[64,1024]{1,0:T(8,128)S(1)} collective-permute-done((f32[64,1024]{1,0:T(8,128)}, f32[64,1024]{1,0:T(8,128)S(1)}, u32[]{:S(2)}, u32[]{:S(2)}) %collective-permute-start.18) | collective-permute-done | bytes 262176 | tf_op jit(solution)/shard_map/ppermute | solution.py:401
  218.6 0.7 copy-done.12
  219.2 0.2 copy-done.9
  219.4 3.6 %assemble.1 = f32[64,5120]{1,0:T(8,128)} custom-call(s32[6]{0:T(128)} %pad_add_fusion.flags, f32[1024,128]{1,0:T(8,128)} %copy-done.9, f32[1024,128]{1,0:T(8,128)} %bitcast.39, f32[64,1024]{1,0:T(8,128)} %get-tuple-element.64.rows2, f32[64,1024]{1,0:T(8,128)} %copy-done.12, f32[64,1024]{1,0:T(8,128)} %get-tuple-element.47.rows0_a, f32[64,1024]{1,0:T(8,128)} %copy-done.11), custom_call_target="tpu_custom_call" | custom-call | flops 1024 | bytes 1024 | tf_op jit(solution)/shard_map/assemble/pallas_call | solution.py:332
  (38 shorter events, 0.2 us)
Async XLA Ops:
  4.7 3.8 %collective-permute-start.1 = (f32[3,1024]{1,0:T(4,128)S(1)}, f32[3,1024]{1,0:T(4,128)S(1)}, u32[]{:S(2)}, u32[]{:S(2)}) collective-permute-start(f32[3,1024]{1,0:T(4,128)S(1)} %pad_maximum_fusion), channel_id=1, source_target_pairs={{0,8},{1,9},{8,0},{9,1},{2,10},{3,11},{10,2},{11,3},{4,12},{5,13},... | collective-permute-start | bytes 36872 | tf_op jit(solution)/shard_map/ppermute | solution.py:33
  6.3 3.2 %collective-permute-start.2 = (f32[3,1024]{1,0:T(4,128)S(1)}, f32[3,1024]{1,0:T(4,128)S(1)}, u32[]{:S(2)}, u32[]{:S(2)}) collective-permute-start(f32[3,1024]{1,0:T(4,128)S(1)} %pad_maximum_fusion), channel_id=1, source_target_pairs={{0,9},{1,8},{8,1},{9,0},{2,11},{3,10},{10,3},{11,2},{4,13},{5,12},... | collective-permute-start | bytes 36872 | tf_op jit(solution)/shard_map/ppermute | solution.py:33
  6.3 3.2 %collective-permute-start = (f32[3,1024]{1,0:T(4,128)S(1)}, f32[3,1024]{1,0:T(4,128)S(1)}, u32[]{:S(2)}, u32[]{:S(2)}) collective-permute-start(f32[3,1024]{1,0:T(4,128)S(1)} %pad_maximum_fusion), channel_id=1, source_target_pairs={{0,1},{1,0},{8,9},{9,8},{2,3},{3,2},{10,11},{11,10},{4,5},{5,4},{1... | collective-permute-start | bytes 36872 | tf_op jit(solution)/shard_map/ppermute | solution.py:33
  9.5 5.2 %collective-permute-start.5 = (f32[3,1024]{1,0:T(4,128)S(1)}, f32[3,1024]{1,0:T(4,128)S(1)}, u32[]{:S(2)}, u32[]{:S(2)}) collective-permute-start(f32[3,1024]{1,0:T(4,128)S(1)} %add_add_fusion.1), channel_id=1, source_target_pairs={{0,6},{2,0},{4,2},{6,4},{1,7},{3,1},{5,3},{7,5},{8,14},{10,8},{12,... | collective-permute-start | bytes 36872 | tf_op jit(solution)/shard_map/ppermute | solution.py:37
  12.4 5.2 %collective-permute-start.4 = (f32[3,1024]{1,0:T(4,128)S(1)}, f32[3,1024]{1,0:T(4,128)S(1)}, u32[]{:S(2)}, u32[]{:S(2)}) collective-permute-start(f32[3,1024]{1,0:T(4,128)S(1)} %add_add_fusion.1), channel_id=1, source_target_pairs={{0,4},{2,6},{4,0},{6,2},{1,5},{3,7},{5,1},{7,3},{8,12},{10,14},{12... | collective-permute-start | bytes 36872 | tf_op jit(solution)/shard_map/ppermute | solution.py:37
  13.2 4.9 %collective-permute-start.3 = (f32[3,1024]{1,0:T(4,128)S(1)}, f32[3,1024]{1,0:T(4,128)S(1)}, u32[]{:S(2)}, u32[]{:S(2)}) collective-permute-start(f32[3,1024]{1,0:T(4,128)S(1)} %add_add_fusion.1), channel_id=1, source_target_pairs={{0,2},{2,4},{4,6},{6,0},{1,3},{3,5},{5,7},{7,1},{8,10},{10,12},{12... | collective-permute-start | bytes 36872 | tf_op jit(solution)/shard_map/ppermute | solution.py:37
  28.0 7.0 %collective-permute-start.6 = (bf16[1280,1024]{1,0:T(8,128)(2,1)}, bf16[1280,1024]{1,0:T(8,128)(2,1)S(1)}, u32[]{:S(2)}, u32[]{:S(2)}) collective-permute-start(bf16[1280,1024]{1,0:T(8,128)(2,1)} %get-tuple-element.38.zed_a.zed0_a.zed1_a), channel_id=1, source_target_pairs={{0,1},{1,0},{2,3},{3,2},{4,5},{5,4},{6,7},{7,6},{8,9},{9,8},{10,11... | collective-permute-start | bytes 7864328 | tf_op jit(solution)/shard_map/ppermute | solution.py:380
  28.1 36.3 %collective-permute-start.7 = (bf16[1280,512]{1,0:T(8,128)(2,1)}, bf16[1280,512]{1,0:T(8,128)(2,1)}, u32[]{:S(2)}, u32[]{:S(2)}) collective-permute-start(bf16[1280,512]{1,0:T(8,128)(2,1)} %get-tuple-element.41), channel_id=1, source_target_pairs={{32,0},{64,32},{96,64},{128,96},{160,128},{192,160},{224,192},{16,... | collective-permute-start | bytes 3932168 | tf_op jit(solution)/shard_map/ppermute | solution.py:377
  30.1 24.7 %collective-permute-start.9 = (bf16[8,32,1280]{2,1,0:T(8,128)(2,1)}, bf16[8,32,1280]{2,1,0:T(8,128)(2,1)S(1)}, u32[]{:S(2)}, u32[]{:S(2)}) collective-permute-start(bf16[8,32,1280]{2,1,0:T(8,128)(2,1)} %get-tuple-element.42), channel_id=1, source_target_pairs={{0,17},{1,16},{16,1},{17,0},{2,19},{3,18},{18,3},{19,2},{4,21},{5,... | collective-permute-start | bytes 1966088 | tf_op jit(solution)/shard_map/ppermute | solution.py:379
  34.7 29.7 %collective-permute-start.8 = (bf16[8,32,1280]{2,1,0:T(8,128)(2,1)}, bf16[8,32,1280]{2,1,0:T(8,128)(2,1)}, u32[]{:S(2)}, u32[]{:S(2)}) collective-permute-start(bf16[8,32,1280]{2,1,0:T(8,128)(2,1)} %get-tuple-element.36), channel_id=1, source_target_pairs={{0,16},{16,0},{32,48},{48,32},{64,80},{80,64},{96,112},{112,96},{1... | collective-permute-start | bytes 1966088 | tf_op jit(solution)/shard_map/ppermute | solution.py:378
  35.0 1.5 copy-start.1
  51.1 15.3 %copy-start.4 = (bf16[8,32,1280]{2,1,0:T(8,128)(2,1)S(1)}, bf16[8,32,1280]{2,1,0:T(8,128)(2,1)}, u32[]{:S(2)}) copy-start(bf16[8,32,1280]{2,1,0:T(8,128)(2,1)} %get-tuple-element.51) | copy-start | bytes 1966084
  51.1 30.5 %all-to-all-start = ((f32[4,2,64,1024]{3,2,1,0:T(8,128)}), f32[4,2,64,1024]{3,2,1,0:T(8,128)S(1)}, u32[]{:S(2)}, u32[]{:S(2)}) async-start(f32[4,2,64,1024]{3,2,1,0:T(8,128)} %bitcast.22), calls=%async_computation | async-start | bytes 4194304 | tf_op jit(solution)/shard_map/all_to_all | solution.py:183
  54.8 18.1 %copy-start.6 = (bf16[8,32,1280]{2,1,0:T(8,128)(2,1)}, bf16[8,32,1280]{2,1,0:T(8,128)(2,1)S(1)}, u32[]{:S(2)}) copy-start(bf16[8,32,1280]{2,1,0:T(8,128)(2,1)S(1)} %collective-permute-done.9) | copy-start | bytes 1966084
  64.4 8.6 %collective-permute-start.10 = (bf16[1280,512]{1,0:T(8,128)(2,1)}, bf16[1280,512]{1,0:T(8,128)(2,1)S(1)}, u32[]{:S(2)}, u32[]{:S(2)}) collective-permute-start(bf16[1280,512]{1,0:T(8,128)(2,1)} %collective-permute-done.7.near_a.near0_a), channel_id=1, source_target_pairs={{0,1},{1,0},{2,3},{3,2},{4,5},{5,4},{6,7},{7,6},{8,9},{9,8},{10,11... | collective-permute-start | bytes 3932168 | tf_op jit(solution)/shard_map/ppermute | solution.py:380
  64.4 37.5 %collective-permute-start.11 = (bf16[1280,512]{1,0:T(8,128)(2,1)}, bf16[1280,512]{1,0:T(8,128)(2,1)}, u32[]{:S(2)}, u32[]{:S(2)}) collective-permute-start(bf16[1280,512]{1,0:T(8,128)(2,1)} %get-tuple-element.50), channel_id=1, source_target_pairs={{32,0},{64,32},{96,64},{128,96},{160,128},{192,160},{224,192},{16,... | collective-permute-start | bytes 3932168 | tf_op jit(solution)/shard_map/ppermute | solution.py:377
  66.4 22.2 %collective-permute-start.12 = (bf16[8,32,1280]{2,1,0:T(8,128)(2,1)S(1)}, bf16[8,32,1280]{2,1,0:T(8,128)(2,1)}, u32[]{:S(2)}, u32[]{:S(2)}) collective-permute-start(bf16[8,32,1280]{2,1,0:T(8,128)(2,1)S(1)} %copy-done.4), channel_id=1, source_target_pairs={{0,16},{16,0},{32,48},{48,32},{64,80},{80,64},{96,112},{112,96},{1... | collective-permute-start | bytes 1966088 | tf_op jit(solution)/shard_map/ppermute | solution.py:378
  73.0 28.9 %collective-permute-start.13 = (bf16[8,32,1280]{2,1,0:T(8,128)(2,1)}, bf16[8,32,1280]{2,1,0:T(8,128)(2,1)}, u32[]{:S(2)}, u32[]{:S(2)}) collective-permute-start(bf16[8,32,1280]{2,1,0:T(8,128)(2,1)} %get-tuple-element.53), channel_id=1, source_target_pairs={{0,17},{1,16},{16,1},{17,0},{2,19},{3,18},{18,3},{19,2},{4,21},{5,... | collective-permute-start | bytes 1966088 | tf_op jit(solution)/shard_map/ppermute | solution.py:379
  73.0 1.1 copy-start.5
  81.6 1.3 copy-start.2
  101.8 4.0 %collective-permute-start.14 = (bf16[1280,512]{1,0:T(8,128)(2,1)}, bf16[1280,512]{1,0:T(8,128)(2,1)S(1)}, u32[]{:S(2)}, u32[]{:S(2)}) collective-permute-start(bf16[1280,512]{1,0:T(8,128)(2,1)} %collective-permute-done.11.near1_a), channel_id=1, source_target_pairs={{0,1},{1,0},{2,3},{3,2},{4,5},{5,4},{6,7},{7,6},{8,9},{9,8},{10,11... | collective-permute-start | bytes 3932168 | tf_op jit(solution)/shard_map/ppermute | solution.py:380
  102.1 25.0 %all-to-all-start.1 = ((f32[4,2,96,512]{3,2,1,0:T(8,128)}), f32[4,2,96,512]{3,2,1,0:T(8,128)S(1)}, u32[]{:S(2)}, u32[]{:S(2)}) async-start(f32[4,2,96,512]{3,2,1,0:T(8,128)} %bitcast.23), calls=%async_computation.1 | async-start | bytes 3145728 | tf_op jit(solution)/shard_map/all_to_all | solution.py:183
  105.8 1.1 copy-start.8
  127.0 1.2 copy-start.3
  167.4 3.6 %copy-start.15 = (f32[96,512]{1,0:T(8,128)S(1)}, f32[96,512]{1,0:T(8,128)}, u32[]{:S(2)}) copy-start(f32[96,512]{1,0:T(8,128)} %get-tuple-element.59) | copy-start | bytes 589828
  167.4 23.3 %copy-start = (s32[16]{0:T(128)S(1)}, s32[16]{0:T(128)}, u32[]{:S(2)}) copy-start(s32[16]{0:T(128)} %param.5) | copy-start | bytes 196
  167.4 37.7 %copy-start.14 = (f32[64,1024]{1,0:T(8,128)S(1)}, f32[64,1024]{1,0:T(8,128)}, u32[]{:S(2)}) copy-start(f32[64,1024]{1,0:T(8,128)} %get-tuple-element.66) | copy-start | bytes 786436
  170.7 12.6 %collective-permute-start.16 = (f32[160,512]{1,0:T(8,128)}, f32[160,512]{1,0:T(8,128)S(1)}, u32[]{:S(2)}, u32[]{:S(2)}) collective-permute-start(f32[160,512]{1,0:T(8,128)} %get-tuple-element.62), channel_id=1, source_target_pairs={{0,8},{8,0},{1,9},{9,1},{2,10},{10,2},{3,11},{11,3},{4,12},{12,4},... | collective-permute-start | bytes 983048 | tf_op jit(solution)/shard_map/ppermute | solution.py:198
  171.0 12.3 %collective-permute-start.15 = (f32[96,512]{1,0:T(8,128)S(1)}, f32[96,512]{1,0:T(8,128)S(1)}, u32[]{:S(2)}, u32[]{:S(2)}) collective-permute-start(f32[96,512]{1,0:T(8,128)S(1)} %copy-done.15), channel_id=1, source_target_pairs={{0,8},{8,0},{1,9},{9,1},{2,10},{10,2},{3,11},{11,3},{4,12},{12,4},... | collective-permute-start | bytes 589832 | tf_op jit(solution)/shard_map/ppermute | solution.py:198
  183.3 0.7 copy-start.13
  183.3 0.8 copy-start.10
  187.1 14.4 %all-to-all-start.3 = ((f32[16,64,128]{2,1,0:T(8,128)}), f32[16,64,128]{2,1,0:T(8,128)S(1)}, u32[]{:S(2)}, u32[]{:S(2)}) async-start(f32[16,64,128]{2,1,0:T(8,128)} %get-tuple-element.63), calls=%async_computation.3 | async-start | bytes 1048576 | tf_op jit(solution)/shard_map/all_to_all | solution.py:402
  201.5 17.1 %copy-start.7 = (f32[16,64,128]{2,1,0:T(8,128)}, f32[16,64,128]{2,1,0:T(8,128)S(1)}, u32[]{:S(2)}) copy-start(f32[16,64,128]{2,1,0:T(8,128)S(1)} %all-to-all-done.3) | copy-start | bytes 1572868
  201.5 17.1 %collective-permute-start.17 = (f32[1024,128]{1,0:T(8,128)S(1)}, f32[1024,128]{1,0:T(8,128)S(1)}, u32[]{:S(2)}, u32[]{:S(2)}) collective-permute-start(f32[1024,128]{1,0:T(8,128)S(1)} %bitcast.38), channel_id=1, source_target_pairs={{0,32},{32,64},{64,96},{96,128},{128,160},{160,192},{192,224},{48,... | collective-permute-start | bytes 1572872 | tf_op jit(solution)/shard_map/ppermute | solution.py:403
  205.1 9.3 %collective-permute-start.19 = (f32[64,1024]{1,0:T(8,128)S(1)}, f32[64,1024]{1,0:T(8,128)S(1)}, u32[]{:S(2)}, u32[]{:S(2)}) collective-permute-start(f32[64,1024]{1,0:T(8,128)S(1)} %copy-done.14), channel_id=1, source_target_pairs={{0,8},{8,0},{1,9},{9,1},{2,10},{10,2},{3,11},{11,3},{4,12},{12,4},... | collective-permute-start | bytes 786440 | tf_op jit(solution)/shard_map/ppermute | solution.py:198
  205.7 12.9 %collective-permute-start.18 = (f32[64,1024]{1,0:T(8,128)}, f32[64,1024]{1,0:T(8,128)S(1)}, u32[]{:S(2)}, u32[]{:S(2)}) collective-permute-start(f32[64,1024]{1,0:T(8,128)} %get-tuple-element.65), channel_id=1, source_target_pairs={{0,16},{16,0},{32,48},{48,32},{64,80},{80,64},{96,112},{112,96},{1... | collective-permute-start | bytes 786440 | tf_op jit(solution)/shard_map/ppermute | solution.py:401
  214.4 4.2 %copy-start.11 = (f32[64,1024]{1,0:T(8,128)}, f32[64,1024]{1,0:T(8,128)S(1)}, u32[]{:S(2)}) copy-start(f32[64,1024]{1,0:T(8,128)S(1)} %collective-permute-done.19.rows0_b) | copy-start | bytes 786436
  218.5 0.7 copy-start.12
  218.5 0.9 copy-start.9

commit v3 on v2

v3 whole, which is shorter than its diff:
```python
import jax
import jax.numpy as jnp
from jax import lax
from jax.experimental import pallas as pl
from jax.experimental.pallas import tpu as pltpu
from jax.sharding import Mesh
from jax.sharding import PartitionSpec as P

eps = 1e-05

AXES = ("z", "yh", "yl", "x", "core")
SIZES = (8, 2, 2, 4, 2)
SNP = ("z", "yh")
SAMP = ("yl", "x", "core")
NSNP = 16
B = 1024
DEPTH = 1280
HALF = B // 2
STEP = 256
PIECES = 8
ROWS = 64
TURN = 32
SWAP = [(0, 1), (1, 0)]
TO_OTHER = [(i, i ^ 1) for i in range(NSNP)]
EVEN_DOWN = [(i + 2, i) for i in range(0, NSNP - 2, 2)]
ODD_UP = [(i, i + 2) for i in range(1, NSNP - 2, 2)]
EVEN_UP = [(i, i + 2) for i in range(0, NSNP - 2, 2)]
ODD_DOWN = [(i + 2, i) for i in range(1, NSNP - 2, 2)]


def sum_over_samples(x):
    parts = [
        lax.ppermute(x, ("yl", "core"), [(i, i ^ k) for i in range(4)]) for k in (1, 2, 3)
    ]
    x = x + parts[0] + parts[1] + parts[2]
    parts = [
        lax.ppermute(x, "x", [(i, (i + k) % 4) for i in range(4)]) for k in (1, 2, 3)
    ]
    return x + parts[0] + parts[1] + parts[2]


def chip_of(piece):
    return piece // 2 + 4 * (piece % 2)


def params():
    return pltpu.CompilerParams(vmem_limit_bytes=56 << 20)


def cost(flops, moved):
    return pl.CostEstimate(flops=1024, bytes_accessed=1024, transcendentals=0)


def whole(shape):
    return pl.BlockSpec(shape, lambda j, m: (0,) * len(shape))


def f32(*shape):
    return jax.ShapeDtypeStruct(shape, jnp.float32)


def bf16(*shape):
    return jax.ShapeDtypeStruct(shape, jnp.bfloat16)


def matmul(left, right):
    return jnp.dot(left, right, preferred_element_type=jnp.float32)


def standard_kernel(meta, dosage, observed, stats, zed, zed0, zed1, kept0, kept1, sent0, sent1):
    weight = observed[...].astype(jnp.float32)
    values = dosage[...].astype(jnp.float32)
    z = (weight * (values - stats[0:1, :]) * stats[1:2, :]).astype(jnp.bfloat16)
    zed[...] = z
    zed0[...] = z[:, :HALF]
    zed1[...] = z[:, HALF:]
    turned = z.T

    def store(*outs):
        for p in range(PIECES):
            for k, out in enumerate(outs):
                at = 2 * ROWS * chip_of(p) + TURN * k
                out[p] = turned[at : at + TURN]

    pl.when(meta[0] == 0)(lambda: store(kept0, kept1, sent0, sent1))
    pl.when(meta[0] != 0)(lambda: store(sent0, sent1, kept0, kept1))


def standardize(meta, dosage, observed, stats):
    rows = 256
    block = lambda width: pl.BlockSpec((rows, width), lambda i, m: (i, 0))
    turned = pl.BlockSpec((PIECES, TURN, rows), lambda i, m: (0, 0, i))
    return pl.pallas_call(
        standard_kernel,
        name="standardize",
        out_shape=(bf16(DEPTH, B), bf16(DEPTH, HALF), bf16(DEPTH, HALF))
        + (bf16(PIECES, TURN, DEPTH),) * 4,
        grid_spec=pltpu.PrefetchScalarGridSpec(
            num_scalar_prefetch=1,
            grid=(DEPTH // rows,),
            in_specs=[block(B), block(B), whole((2, B))],
            out_specs=(block(B), block(HALF), block(HALF)) + (turned,) * 4,
        ),
        compiler_params=params(),
        cost_estimate=cost(4 * DEPTH * B, 12 * DEPTH * B),
    )(meta, dosage, observed, stats)


LEFT = (PIECES * TURN, DEPTH)


def flat(*turned):
    return [t.reshape(LEFT) for t in turned]


def turn_kernel(meta, zed, out0, out1):
    turned = zed[...].T

    def store(at):
        out0[0] = turned[at : at + TURN]
        out1[0] = turned[at + TURN : at + ROWS]

    pl.when(meta[0] == 0)(lambda: store(0))
    pl.when(meta[0] != 0)(lambda: store(ROWS))


def turn(meta, zed):
    out = pl.BlockSpec((1, TURN, DEPTH), lambda c, m: (c, 0, 0))
    return pl.pallas_call(
        turn_kernel,
        name="turn",
        out_shape=(bf16(PIECES, TURN, DEPTH),) * 2,
        grid_spec=pltpu.PrefetchScalarGridSpec(
            num_scalar_prefetch=1,
            grid=(PIECES,),
            in_specs=[pl.BlockSpec((DEPTH, 2 * ROWS), lambda p, m: (0, p // 2 + 4 * (p % 2)))],
            out_specs=(out, out),
        ),
        compiler_params=params(),
        cost_estimate=cost(DEPTH * B, 3 * DEPTH * B),
    )(meta, zed)


def store_pieces(out, at, left_a, left_b, right_a, right_b):
    acc = matmul(left_a[...], right_a[...]) + matmul(left_b[...], right_b[...])
    out[:, at : at + TURN] = acc.reshape(PIECES, TURN, STEP)


def product_kernel(meta, own0_a, own1_a, own0_b, own1_b, right_a, right_b, out):
    store_pieces(out, 0, own0_a, own0_b, right_a, right_b)
    store_pieces(out, TURN, own1_a, own1_b, right_a, right_b)


def product(meta, own_a, own_b, right, name):
    columns = right[0].shape[1]
    block = pl.BlockSpec((DEPTH, STEP), lambda j, m: (0, j))
    return pl.pallas_call(
        product_kernel,
        name=name,
        out_shape=f32(PIECES, ROWS, columns),
        grid_spec=pltpu.PrefetchScalarGridSpec(
            num_scalar_prefetch=1,
            grid=(columns // STEP,),
            in_specs=[whole(LEFT)] * 4 + [block] * 2,
            out_specs=pl.BlockSpec((PIECES, ROWS, STEP), lambda j, m: (0, 0, j)),
        ),
        compiler_params=params(),
        cost_estimate=cost(2 * DEPTH * B * columns, 4 * DEPTH * B + 4 * B * columns),
    )(meta, *flat(*own_a, *own_b), *right)


def across_kernel(
    meta, other0_a, other1_a, other0_b, other1_b, near0_a, near0_b, near1_a, near1_b, zed_a, zed_b, *rest
):
    outs, right = rest[:4], rest[4]
    j = pl.program_id(0)
    odd = meta[1] == 1

    def take(a, b):
        right[:DEPTH] = a[...]
        right[DEPTH:] = b[...]

    pl.when(odd)(lambda: take(zed_a, zed_b))
    pl.when(~odd & (j < 2))(lambda: take(near0_a, near0_b))
    pl.when(~odd & (j >= 2))(lambda: take(near1_a, near1_b))

    for at, left_a, left_b in ((0, other0_a, other0_b), (TURN, other1_a, other1_b)):
        acc = matmul(left_a[...], right[:DEPTH]) + matmul(left_b[...], right[DEPTH:])
        acc = acc.reshape(4, 2, TURN, STEP)
        for x in range(4):

            @pl.when(meta[3] == x)
            def _():
                for k in range(4):
                    outs[k][:, at : at + TURN] = acc[(x + k) % 4]


def across_product(meta, other0, other1, near0, near1, zed):
    first = pl.BlockSpec((DEPTH, STEP), lambda j, m: (0, jnp.clip(j, 0, 1)))
    second = pl.BlockSpec((DEPTH, STEP), lambda j, m: (0, jnp.clip(j - 2, 0, 1)))
    block = pl.BlockSpec((DEPTH, STEP), lambda j, m: (0, j))
    left = (other0[0], other1[0], other0[1], other1[1])
    return pl.pallas_call(
        across_kernel,
        name="across",
        out_shape=(f32(2, ROWS, B),) * 4,
        grid_spec=pltpu.PrefetchScalarGridSpec(
            num_scalar_prefetch=1,
            grid=(B // STEP,),
            in_specs=[whole(LEFT)] * 4 + [first] * 2 + [second] * 2 + [block] * 2,
            out_specs=(pl.BlockSpec((2, ROWS, STEP), lambda j, m: (0, 0, j)),) * 4,
            scratch_shapes=[pltpu.VMEM((2 * DEPTH, STEP), jnp.bfloat16)],
        ),
        compiler_params=params(),
        cost_estimate=cost(2 * DEPTH * B * B, 12 * DEPTH * B + 4 * B * B),
    )(meta, *flat(*left), *near0, *near1, *zed)


def after(value, *others):
    return lax.optimization_barrier((value, *others))[0]


def add_kernel(meta, *refs):
    parts, (keep, send) = refs[:-2], refs[-2:]
    mine = meta[2]
    for out, half in ((keep, mine), (send, 1 - mine)):
        out[...] = parts[0][half] + parts[1][half] + parts[2][half] + parts[3][half]


def add(meta, parts, specs, rows, columns):
    out = pl.BlockSpec((rows, STEP), lambda j, m: (0, j))
    keep, send = pl.pallas_call(
        add_kernel,
        name="add",
        out_shape=(f32(rows, columns),) * 2,
        grid_spec=pltpu.PrefetchScalarGridSpec(
            num_scalar_prefetch=1,
            grid=(columns // STEP,),
            in_specs=specs,
            out_specs=(out, out),
        ),
        compiler_params=params(),
        cost_estimate=cost(6 * rows * columns, 40 * rows * columns),
    )(meta, *parts)
    return keep, lax.ppermute(send, "yl", SWAP)


def fold(meta, parts, *others):
    _, rows, columns = parts.shape
    parts = after(lax.all_to_all(parts.reshape(4, 2, rows, columns), "x", 0, 0), *others)
    specs = [
        pl.BlockSpec((pl.Squeezed(), 2, rows, STEP), lambda j, m, k=k: (k, 0, 0, j)) for k in range(4)
    ]
    return add(meta, [parts] * 4, specs, rows, columns)


def fold_pieces(meta, parts, *others):
    _, rows, columns = parts[0].shape
    parts = [parts[0]] + [
        lax.ppermute(parts[k], "x", [(i, (i + k) % 4) for i in range(4)]) for k in (1, 2, 3)
    ]
    parts = after(parts, *others)
    specs = [pl.BlockSpec((2, rows, STEP), lambda j, m: (0, 0, j))] * 4
    return add(meta, parts, specs, rows, columns)


def gather_kernel(meta, *refs):
    pairs, (rows, packed) = refs[:-2], refs[-2:]
    begin = 0
    for a, b in zip(pairs[::2], pairs[1::2]):
        rows[:, begin : begin + a.shape[1]] = a[...] + b[...]
        begin += a.shape[1]
    for s in range(2 * PIECES):
        packed[s, :, :ROWS] = rows[:TURN, ROWS * s : ROWS * (s + 1)]
        packed[s, :, ROWS:] = rows[TURN:, ROWS * s : ROWS * (s + 1)]


def gather(meta, *pairs):
    flat_pairs = [t for pair in pairs for t in pair]
    packed = (2 * PIECES, TURN, 2 * ROWS)
    rows, packed = pl.pallas_call(
        gather_kernel,
        name="gather",
        out_shape=(f32(ROWS, B), f32(*packed)),
        grid_spec=pltpu.PrefetchScalarGridSpec(
            num_scalar_prefetch=1,
            grid=(1,),
            in_specs=[whole(t.shape) for t in flat_pairs],
            out_specs=(whole((ROWS, B)), whole(packed)),
        ),
        compiler_params=params(),
        cost_estimate=cost(ROWS * B, 16 * ROWS * B),
    )(meta, *flat_pairs)
    return rows, lax.all_to_all(packed, SAMP, 0, 0).reshape(HALF, 2 * ROWS)


def unpack(out, packed):
    turned = packed[...].T
    for s in range(2 * PIECES):
        out[:, ROWS * s : ROWS * s + TURN] = turned[:ROWS, TURN * s : TURN * (s + 1)]
        out[:, ROWS * s + TURN : ROWS * (s + 1)] = turned[ROWS:, TURN * s : TURN * (s + 1)]


def assemble_kernel(flags, far, near, here, rows2, beside, rows0_a, rows0_b, out, far_t, near_t):
    even = flags[5] == 0
    unpack(far_t, far)
    pl.when(even)(lambda: unpack(near_t, near))
    pl.when(~even)(lambda: unpack(near_t, here))
    turned, mine = far_t[...], rows2[...]
    blocks = (
        jnp.where(even, turned, mine),
        near_t[...],
        rows0_a[...] + rows0_b[...],
        beside[...],
        jnp.where(even, mine, turned),
    )
    for d, block in enumerate(blocks):
        out[:, B * d : B * (d + 1)] = jnp.where(flags[d] > 0, block, 0.0)


def assemble(flags, far, near, here, rows2, beside, rows0):
    return pl.pallas_call(
        assemble_kernel,
        name="assemble",
        out_shape=f32(ROWS, 5 * B),
        grid_spec=pltpu.PrefetchScalarGridSpec(
            num_scalar_prefetch=1,
            grid=(1,),
            in_specs=[whole((HALF, 2 * ROWS))] * 3 + [whole((ROWS, B))] * 4,
            out_specs=whole((ROWS, 5 * B)),
            scratch_shapes=[pltpu.VMEM((ROWS, B), jnp.float32)] * 2,
        ),
        compiler_params=params(),
        cost_estimate=cost(ROWS * 5 * B, 40 * ROWS * B),
    )(flags, far, near, here, rows2, beside, *rows0)


def kept_flags(band, mine):
    total = band.shape[0]
    offsets = jnp.arange(5, dtype=jnp.int32) - 2
    other = mine + offsets
    inside = (other >= 0) & (other < total)
    reach = jnp.minimum(band[mine], band[jnp.clip(other, 0, total - 1)])
    return (inside & (jnp.abs(offsets) <= reach)).astype(jnp.int32)


def on_device(dosage, observed, band):
    mine = lax.axis_index(SNP)
    odd = lax.axis_index("yh").reshape(1)
    core = lax.axis_index("core").reshape(1)
    meta = jnp.concatenate([core, odd, lax.axis_index("yl").reshape(1), lax.axis_index("x").reshape(1)]).astype(jnp.int32)

    weight = observed.astype(jnp.float32)
    values = dosage.astype(jnp.float32)
    sums = jnp.stack(
        [
            jnp.sum(weight, axis=0),
            jnp.sum(weight * values, axis=0),
            jnp.sum(weight * values * values, axis=0),
        ]
    )
    cnt, first, second = sum_over_samples(sums)
    mean = first / cnt
    spread = second - first * mean
    stats = jnp.stack([mean, lax.rsqrt(spread + eps * cnt)])

    zed, zed0, zed1, kept0, kept1, sent0, sent1 = standardize(meta, dosage, observed, stats)
    along = lambda t: lax.ppermute(t, SNP, EVEN_DOWN + ODD_UP)
    across = lambda t: lax.ppermute(t, SNP, TO_OTHER)
    athwart = lambda t: lax.ppermute(t, ("yh", "core"), [(i, 3 - i) for i in range(4)])
    swap = lambda t: lax.ppermute(t, "core", SWAP)
    zed_b = swap(zed)
    near0 = along(zed0)
    other0 = (across(kept0), athwart(sent0))

    own_a = (kept0, kept1)
    own_b = turn(meta, zed_b)
    rows0 = product(meta, own_a, own_b, (zed, zed_b), "own")
    near0, other0 = after((near0, other0), rows0)
    near1 = along(after(zed1, near0, other0))
    other1 = (across(after(kept1, near0, other0)), athwart(after(sent1, near0, other0)))
    near0 = (near0, swap(near0))
    first = product(meta, own_a, own_b, near0, "first")
    rows0 = fold(meta, rows0, first)
    near1, other1 = after((near1, other1), first, rows0[0])
    near1 = (near1, swap(near1))
    second = product(meta, own_a, own_b, near1, "second")
    first = fold(meta, after(first, rows0[0]), second)
    pieces = across_product(meta, after(other0, first[0]), other1, near0, near1, (zed, zed_b))
    second = fold(meta, second, pieces[0])
    rows2, turned2 = gather(meta, first, second)
    rows1 = fold_pieces(meta, pieces, rows2)

    far = lax.ppermute(turned2, SNP, EVEN_UP + ODD_DOWN)
    rows1, turned1 = gather(meta, rows1)
    beside = lax.ppermute(rows1, SNP, TO_OTHER)
    near = lax.ppermute(turned1, SNP, EVEN_UP)
    flags = jnp.concatenate([kept_flags(band, mine), odd]).astype(jnp.int32)
    return assemble(flags, far, near, turned1, rows2, beside, rows0)


def solution(mesh):
    whole_mesh = Mesh(mesh.devices.reshape(SIZES), AXES)
    return jax.shard_map(
        on_device,
        mesh=whole_mesh,
        in_specs=(P(SAMP, SNP), P(SAMP, SNP), P()),
        out_specs=P(AXES, None),
        check_vma=False,
    )
```

time: 224 us -> 216 us (0.964)
  blocking collectives: 36.4 us -> 0 us
  starting transfers between devices: 40.1 us -> 60.9 us
  Pallas kernels: 58.4 us -> 69.5 us
  waiting for transfers between devices: 71.5 us -> 64.9 us
    all_to_all x1 -> x0, blocking collectives: 36.4 us -> none  [fold(): lax.all_to_all(parts.reshape(4, 2, rows, columns), 'x', 0, 0)]
    ppermute x4 -> x9, starting transfers between devices: 5.54 us -> 17.2 us  [the longest x3 6.08 us: fold_pieces(): lax.ppermute(parts[k], 'x', [(i, (i + k) % 4) for i in range(4)])]
    pallas_call x7 -> x10, Pallas kernels: 38.9 us -> 49.5 us  [the longest x3 18.4 us: product(): pl.pallas_call(product_kernel, name=name, out_shape=f32(PIECES, ROWS, col...]
    all_to_all x1 -> x2, waiting for transfers between devices: 10.2 us -> 3.11 us  [gather(): return (rows, lax.all_to_all(packed, SAMP, 0, 0).reshape(HALF, 2 * ROWS))]
    all_to_all x1 -> x2, starting transfers between devices: 3.57 us -> 8.54 us  [gather(): return (rows, lax.all_to_all(packed, SAMP, 0, 0).reshape(HALF, 2 * ROWS))]
    all_to_all x2 -> x3, starting transfers between devices: 7.48 us -> 10.9 us  [fold(): lax.all_to_all(parts.reshape(4, 2, rows, columns), 'x', 0, 0)]
    ppermute x4 -> x9, waiting for transfers between devices: 17.1 us -> 14.7 us  [the longest x3 8.53 us: fold_pieces(): lax.ppermute(parts[k], 'x', [(i, (i + k) % 4) for i in range(4)])]
    all_to_all x2 -> x3, waiting for transfers between devices: 9.81 us -> 11.7 us  [fold(): lax.all_to_all(parts.reshape(4, 2, rows, columns), 'x', 0, 0)]
  transfers between devices with their start and end apart: 23 -> 30, of which waited for: 13 -> 15; matrix products, arithmetic and copies ran while one was open for 1% -> 1% of each run, Pallas kernels for 16% -> 24%
where the time goes in v3:
time: 216 us; the launch traced here: 214 us
  Pallas kernels  69.5 us (32%)
  waiting for transfers between devices  64.9 us (30%)
  starting transfers between devices  60.9 us (28%)
  local copies, waits for them, and re-layouts  10.9 us (5%)
  other arithmetic  7.25 us (3%)
    pallas_call x3, Pallas kernels, product(): pl.pallas_call(product_kernel, name=name, out_shape=f32(PIECES, ROWS, col...  18.4 us
    pallas_call x4, Pallas kernels, add(): pl.pallas_call(add_kernel, name='add', out_shape=(f32(rows, columns),) *...  13.8 us
    ppermute x2, waiting for transfers between devices, on_device(): lax.ppermute(t, ('yh', 'core'), [(i, 3 - i) for i in range(4)])  13.3 us
    pallas_call x1, Pallas kernels, across_product(): pl.pallas_call(across_kernel, name='across', out_shape=(f32(2, ROWS, B),)...  12.2 us
    all_to_all x3, waiting for transfers between devices, fold(): lax.all_to_all(parts.reshape(4, 2, rows, columns), 'x', 0, 0)  11.7 us
    all_to_all x3, starting transfers between devices, fold(): lax.all_to_all(parts.reshape(4, 2, rows, columns), 'x', 0, 0)  10.9 us
    ppermute x2, waiting for transfers between devices, on_device(): across = lambda t: lax.ppermute(t, SNP, TO_OTHER)  10.9 us
    unnamed x44, local copies, waits for them, and re-layouts  9.71 us
  transfers between devices with their start and end apart: 30, of which 15 were waited for; matrix products, arithmetic and copies ran while one was open for 1% of the time, Pallas kernels for 24%

profile of v3, /device:TPU:64, one launch (start us, length us, event | category | flops | bytes accessed | tf_op | source)
XLA Modules:
  0.0 213.9 jit_solution(7163009486313797772)
XLA Ops:
  0.0 4.7 %fusion.1 = (f32[1024]{0:T(1024)S(1)}, f32[1024]{0:T(1024)S(1)}, f32[1024]{0:T(1024)S(1)}) fusion(bf16[1280,1024]{1,0:T(8,128)(2,1)} %dosage.1, s32[1280,1024]{1,0:T(8,128)} %observed.1), kind=kLoop, calls=%fused_computation.5 | loop fusion | flops 9171968 | bytes 7876608 | tf_op jit(solution)/shard_map/reduce_sum | solution.py:358
  4.7 1.7 collective-permute-start.1
  6.9 1.6 collective-permute-done.1
  8.5 1.0 collective-permute-done.2
  9.5 2.8 %collective-permute-start.5 = (f32[3,1024]{1,0:T(4,128)S(1)}, f32[3,1024]{1,0:T(4,128)S(1)}, u32[]{:S(2)}, u32[]{:S(2)}) collective-permute-start(f32[3,1024]{1,0:T(4,128)S(1)} %add_add_fusion.1), channel_id=1, source_target_pairs={{0,6},{2,0},{4,2},{6,4},{1,7},{3,1},{5,3},{7,5},{8,14},{10,8},{12,... | collective-permute-start | bytes 36872 | tf_op jit(solution)/shard_map/ppermute | solution.py:37
  12.4 0.8 collective-permute-start.4
  13.2 0.9 collective-permute-start.3
  14.6 3.0 %collective-permute-done.4 = f32[3,1024]{1,0:T(4,128)S(1)} collective-permute-done((f32[3,1024]{1,0:T(4,128)S(1)}, f32[3,1024]{1,0:T(4,128)S(1)}, u32[]{:S(2)}, u32[]{:S(2)}) %collective-permute-start.4) | collective-permute-done | bytes 12320 | tf_op jit(solution)/shard_map/ppermute | solution.py:37
  18.2 0.6 pad_maximum_fusion.1.stats
  18.8 9.3 %standardize.1 = (bf16[1280,1024]{1,0:T(8,128)(2,1)}, bf16[1280,512]{1,0:T(8,128)(2,1)}, bf16[1280,512]{1,0:T(8,128)(2,1)}, bf16[8,32,1280]{2,1,0:T(8,128)(2,1)}...) custom-call(s32[4]{0:T(128)} %pad_add_fusion.1.meta, ...), custom_call_target="tpu_custom_call" | custom-call | flops 1024 | bytes 1024 | tf_op jit(solution)/shard_map/standardize/pallas_call | solution.py:93
  28.1 2.0 collective-permute-start.7
  30.1 4.6 %collective-permute-start.9 = (bf16[8,32,1280]{2,1,0:T(8,128)(2,1)}, bf16[8,32,1280]{2,1,0:T(8,128)(2,1)S(1)}, u32[]{:S(2)}, u32[]{:S(2)}) collective-permute-start(bf16[8,32,1280]{2,1,0:T(8,128)(2,1)} %get-tuple-element.55), channel_id=1, source_target_pairs={{0,17},{1,16},{16,1},{17,0},{2,19},{3,18},{18,3},{19,2},{4,21},{5,... | collective-permute-start | bytes 1966088 | tf_op jit(solution)/shard_map/ppermute | solution.py:370
  35.0 1.5 copy-done.4
  36.5 6.8 %turn.1 = (bf16[8,32,1280]{2,1,0:T(8,128)(2,1)}, bf16[8,32,1280]{2,1,0:T(8,128)(2,1)}) custom-call(s32[4]{0:T(128)} %pad_add_fusion.1.meta, bf16[1280,1024]{1,0:T(8,128)(2,1)} %copy-done.4), custom_call_target="tpu_custom_call" | custom-call | flops 1024 | bytes 1024 | tf_op jit(solution)/shard_map/turn/pallas_call | solution.py:129
  43.3 7.8 %own.1 = f32[8,64,1024]{2,1,0:T(8,128)} custom-call(s32[4]{0:T(128)} %pad_add_fusion.1.meta, bf16[256,1280]{1,0:T(8,128)(2,1)} %bitcast.24, bf16[256,1280]{1,0:T(8,128)(2,1)} %bitcast.27, bf16[256,1280]{1,0:T(8,128)(2,1)} %bitcast.30, bf16[256,1280]{1,0:T(8,128)(2,1)} %bitcast.33, bf16[1280,1024]{1,0:T(8,128)(2,1)} %get-tuple-element.51.right_a.zed_a, ...), custom_call_target="tpu_custom_call" | custom-call | flops 1024 | bytes 1024 | tf_op jit(solution)/shard_map/own/pallas_call | solution.py:157
  51.1 3.7 %all-to-all-start = ((f32[4,2,64,1024]{3,2,1,0:T(8,128)}), f32[4,2,64,1024]{3,2,1,0:T(8,128)S(1)}, u32[]{:S(2)}, u32[]{:S(2)}) async-start(f32[4,2,64,1024]{3,2,1,0:T(8,128)} %bitcast.23), calls=%async_computation | async-start | bytes 4194304 | tf_op jit(solution)/shard_map/all_to_all | solution.py:250
  54.9 9.5 %collective-permute-done.8 = bf16[8,32,1280]{2,1,0:T(8,128)(2,1)} collective-permute-done((bf16[8,32,1280]{2,1,0:T(8,128)(2,1)}, bf16[8,32,1280]{2,1,0:T(8,128)(2,1)}, u32[]{:S(2)}, u32[]{:S(2)}) %collective-permute-start.8) | collective-permute-done | bytes 655392 | tf_op jit(solution)/shard_map/ppermute | solution.py:369
  64.4 2.0 collective-permute-start.11
  66.4 6.5 %collective-permute-start.12 = (bf16[8,32,1280]{2,1,0:T(8,128)(2,1)S(1)}, bf16[8,32,1280]{2,1,0:T(8,128)(2,1)}, u32[]{:S(2)}, u32[]{:S(2)}) collective-permute-start(bf16[8,32,1280]{2,1,0:T(8,128)(2,1)S(1)} %copy-done.5), channel_id=1, source_target_pairs={{0,16},{16,0},{32,48},{48,32},{64,80},{80,64},{96,112},{112,96},{1... | collective-permute-start | bytes 1966088 | tf_op jit(solution)/shard_map/ppermute | solution.py:369
  73.0 1.1 copy-done.6
  74.0 5.3 %first.1 = f32[8,64,512]{2,1,0:T(8,128)} custom-call(s32[4]{0:T(128)} %pad_add_fusion.1.meta, bf16[256,1280]{1,0:T(8,128)(2,1)} %bitcast.25, bf16[256,1280]{1,0:T(8,128)(2,1)} %bitcast.28, bf16[256,1280]{1,0:T(8,128)(2,1)} %bitcast.31, bf16[256,1280]{1,0:T(8,128)(2,1)} %bitcast.34, bf16[1280,512]{1,0:T(8,128)(2,1)} %collective-permute-done.7.right_a.near0_a, ...), custom_call_target="tpu_custom_call" | custom-call | flops 1024 | bytes 1024 | tf_op jit(solution)/shard_map/first/pallas_call | solution.py:157
  79.3 2.3 %all-to-all-done.refs_0_.refs_1_.refs_2_.refs_3_ = f32[4,2,64,1024]{3,2,1,0:T(8,128)S(1)} async-done(((f32[4,2,64,1024]{3,2,1,0:T(8,128)}), f32[4,2,64,1024]{3,2,1,0:T(8,128)S(1)}, u32[]{:S(2)}, u32[]{:S(2)}) %all-to-all-start) | async-done | bytes 2097184 | tf_op jit(solution)/shard_map/all_to_all | solution.py:250
  81.6 1.3 copy-done.1
  83.0 4.2 %add.105 = (f32[64,1024]{1,0:T(8,128)}, f32[64,1024]{1,0:T(8,128)}) custom-call(s32[4]{0:T(128)} %pad_add_fusion.1.meta, f32[4,2,64,1024]{3,2,1,0:T(8,128)} %copy-done.1, f32[4,2,64,1024]{3,2,1,0:T(8,128)} %copy-done.1, f32[4,2,64,1024]{3,2,1,0:T(8,128)} %copy-done.1, f32[4,2,64,1024]{3,2,1,0:T(8,128)} %copy-done.1), custom_call_target="tpu_custom_call" | custom-call | flops 1024 | bytes 1024 | tf_op jit(solution)/shard_map/add/pallas_call | solution.py:232
  87.2 1.4 collective-permute-done.12
  88.6 13.3 %collective-permute-done.13 = bf16[8,32,1280]{2,1,0:T(8,128)(2,1)} collective-permute-done((bf16[8,32,1280]{2,1,0:T(8,128)(2,1)}, bf16[8,32,1280]{2,1,0:T(8,128)(2,1)}, u32[]{:S(2)}, u32[]{:S(2)}) %collective-permute-start.13) | collective-permute-done | bytes 655392 | tf_op jit(solution)/shard_map/ppermute | solution.py:370
  102.1 3.5 %all-to-all-start.1 = ((f32[4,2,64,512]{3,2,1,0:T(8,128)}), f32[4,2,64,512]{3,2,1,0:T(8,128)S(1)}, u32[]{:S(2)}, u32[]{:S(2)}) async-start(f32[4,2,64,512]{3,2,1,0:T(8,128)} %bitcast.37), calls=%async_computation.1 | async-start | bytes 2097152 | tf_op jit(solution)/shard_map/all_to_all | solution.py:250
  105.6 1.1 copy-done.7
  106.7 5.3 %second.1 = f32[8,64,512]{2,1,0:T(8,128)} custom-call(s32[4]{0:T(128)} %pad_add_fusion.1.meta, bf16[256,1280]{1,0:T(8,128)(2,1)} %bitcast.26, bf16[256,1280]{1,0:T(8,128)(2,1)} %bitcast.29, bf16[256,1280]{1,0:T(8,128)(2,1)} %bitcast.32, bf16[256,1280]{1,0:T(8,128)(2,1)} %bitcast.35, bf16[1280,512]{1,0:T(8,128)(2,1)} %collective-permute-done.11.right_a.near1_a, ...), custom_call_target="tpu_custom_call" | custom-call | flops 1024 | bytes 1024 | tf_op jit(solution)/shard_map/second/pallas_call | solution.py:157
  112.0 9.4 %all-to-all-done.1.refs_0_.refs_1_.refs_2_.refs_3_ = f32[4,2,64,512]{3,2,1,0:T(8,128)S(1)} async-done(((f32[4,2,64,512]{3,2,1,0:T(8,128)}), f32[4,2,64,512]{3,2,1,0:T(8,128)S(1)}, u32[]{:S(2)}, u32[]{:S(2)}) %all-to-all-start.1) | async-done | bytes 1048608 | tf_op jit(solution)/shard_map/all_to_all | solution.py:250
  121.4 3.7 %all-to-all-start.2 = ((f32[4,2,64,512]{3,2,1,0:T(8,128)}), f32[4,2,64,512]{3,2,1,0:T(8,128)S(1)}, u32[]{:S(2)}, u32[]{:S(2)}) async-start(f32[4,2,64,512]{3,2,1,0:T(8,128)} %bitcast.36), calls=%async_computation.2 | async-start | bytes 2097152 | tf_op jit(solution)/shard_map/all_to_all | solution.py:250
  125.1 2.7 %add.106 = (f32[64,512]{1,0:T(8,128)}, f32[64,512]{1,0:T(8,128)}) custom-call(s32[4]{0:T(128)} %pad_add_fusion.1.meta, f32[4,2,64,512]{3,2,1,0:T(8,128)} %copy-done.3, f32[4,2,64,512]{3,2,1,0:T(8,128)} %copy-done.3, f32[4,2,64,512]{3,2,1,0:T(8,128)} %copy-done.3, f32[4,2,64,512]{3,2,1,0:T(8,128)} %copy-done.3), custom_call_target="tpu_custom_call" | custom-call | flops 1024 | bytes 1024 | tf_op jit(solution)/shard_map/add/pallas_call | solution.py:232
  127.8 12.2 %across.1 = (f32[2,64,1024]{2,1,0:T(8,128)}, f32[2,64,1024]{2,1,0:T(8,128)}, f32[2,64,1024]{2,1,0:T(8,128)}, f32[2,64,1024]{2,1,0:T(8,128)}) custom-call(s32[4]{0:T(128)} %pad_add_fusion.1.meta, bf16[256,1280]{1,0:T(8,128)(2,1)} %bitcast.16.other0_a, bf16[256,1280]{1,0:T(8,128)(2,1)} %bitcast.17.other1_a, bf16[256,1280]{1,0:T(8,128)(2,1)} %bitcast.40, ...), custom_call_target="tpu_custom_call" | custom-call | flops 1024 | bytes 1024 | tf_op jit(solution)/shard_map/across/pallas_call | solution.py:203
  140.0 2.0 collective-permute-start.18
  142.0 2.6 %collective-permute-start.19 = (f32[2,64,1024]{2,1,0:T(8,128)}, f32[2,64,1024]{2,1,0:T(8,128)S(1)}, u32[]{:S(2)}, u32[]{:S(2)}) collective-permute-start(f32[2,64,1024]{2,1,0:T(8,128)} %get-tuple-element.81), channel_id=1, source_target_pairs={{0,4},{2,6},{4,0},{6,2},{1,5},{3,7},{5,1},{7,3},{8,12},{10,14},{12... | collective-permute-start | bytes 1572872 | tf_op jit(solution)/shard_map/ppermute | solution.py:260
  144.6 1.5 collective-permute-start.20
  146.4 1.0 copy-done.2
  147.3 2.7 %add.107 = (f32[64,512]{1,0:T(8,128)}, f32[64,512]{1,0:T(8,128)}) custom-call(s32[4]{0:T(128)} %pad_add_fusion.1.meta, f32[4,2,64,512]{3,2,1,0:T(8,128)} %copy-done.2, f32[4,2,64,512]{3,2,1,0:T(8,128)} %copy-done.2, f32[4,2,64,512]{3,2,1,0:T(8,128)} %copy-done.2, f32[4,2,64,512]{3,2,1,0:T(8,128)} %copy-done.2), custom_call_target="tpu_custom_call" | custom-call | flops 1024 | bytes 1024 | tf_op jit(solution)/shard_map/add/pallas_call | solution.py:232
  150.0 1.8 collective-permute-start.16
  151.8 3.5 %collective-permute-done.16.refs_3_ = f32[64,512]{1,0:T(8,128)S(1)} collective-permute-done((f32[64,512]{1,0:T(8,128)}, f32[64,512]{1,0:T(8,128)S(1)}, u32[]{:S(2)}, u32[]{:S(2)}) %collective-permute-start.16) | collective-permute-done | bytes 131104 | tf_op jit(solution)/shard_map/ppermute | solution.py:245
  155.3 0.6 copy-done.19
  155.9 2.6 %gather.8 = (f32[64,1024]{1,0:T(8,128)}, f32[16,32,128]{2,1,0:T(8,128)}) custom-call(s32[4]{0:T(128)} %pad_add_fusion.1.meta, f32[64,512]{1,0:T(8,128)} %get-tuple-element.69.refs_0_, f32[64,512]{1,0:T(8,128)} %copy-done.18, f32[64,512]{1,0:T(8,128)} %get-tuple-element.77.refs_2_, f32[64,512]{1,0:T(8,128)} %copy-done.19), custom_call_target="tpu_custom_call" | custom-call | flops 1024 | bytes 1024 | tf_op jit(solution)/shard_map/gather/pallas_call | solution.py:281
  158.5 8.5 %collective-permute-done.19.refs_2_ = f32[2,64,1024]{2,1,0:T(8,128)S(1)} collective-permute-done((f32[2,64,1024]{2,1,0:T(8,128)}, f32[2,64,1024]{2,1,0:T(8,128)S(1)}, u32[]{:S(2)}, u32[]{:S(2)}) %collective-permute-start.19) | collective-permute-done | bytes 524320 | tf_op jit(solution)/shard_map/ppermute | solution.py:260
  167.1 0.8 copy-done.11
  168.1 4.3 %add.108 = (f32[64,1024]{1,0:T(8,128)}, f32[64,1024]{1,0:T(8,128)}) custom-call(s32[4]{0:T(128)} %pad_add_fusion.1.meta, f32[2,64,1024]{2,1,0:T(8,128)} %get-tuple-element.84.refs_0_, f32[2,64,1024]{2,1,0:T(8,128)} %copy-done.10, f32[2,64,1024]{2,1,0:T(8,128)} %copy-done.11, f32[2,64,1024]{2,1,0:T(8,128)} %copy-done.12), custom_call_target="tpu_custom_call" | custom-call | flops 1024 | bytes 1024 | tf_op jit(solution)/shard_map/add/pallas_call | solution.py:232
  172.6 5.0 %all-to-all-start.3 = ((f32[16,32,128]{2,1,0:T(8,128)}), f32[16,32,128]{2,1,0:T(8,128)S(1)}, u32[]{:S(2)}, u32[]{:S(2)}) async-start(f32[16,32,128]{2,1,0:T(8,128)} %get-tuple-element.79), calls=%async_computation.3 | async-start | bytes 524288 | tf_op jit(solution)/shard_map/all_to_all | solution.py:294
  177.7 1.5 collective-permute-done.21.refs_1_
  179.2 0.7 copy-done.13
  179.9 2.5 %gather.9 = (f32[64,1024]{1,0:T(8,128)}, f32[16,32,128]{2,1,0:T(8,128)}) custom-call(s32[4]{0:T(128)} %pad_add_fusion.1.meta, f32[64,1024]{1,0:T(8,128)} %get-tuple-element.88.refs_0_, f32[64,1024]{1,0:T(8,128)} %copy-done.13), custom_call_target="tpu_custom_call" | custom-call | flops 1024 | bytes 1024 | tf_op jit(solution)/shard_map/gather/pallas_call | solution.py:281
  182.4 3.1 %all-to-all-done.3 = f32[16,32,128]{2,1,0:T(8,128)S(1)} async-done(((f32[16,32,128]{2,1,0:T(8,128)}), f32[16,32,128]{2,1,0:T(8,128)S(1)}, u32[]{:S(2)}, u32[]{:S(2)}) %all-to-all-start.3) | async-done | bytes 262176 | tf_op jit(solution)/shard_map/all_to_all | solution.py:294
  185.5 3.5 %all-to-all-start.4 = ((f32[16,32,128]{2,1,0:T(8,128)}), f32[16,32,128]{2,1,0:T(8,128)S(1)}, u32[]{:S(2)}, u32[]{:S(2)}) async-start(f32[16,32,128]{2,1,0:T(8,128)} %get-tuple-element.90), calls=%async_computation.4 | async-start | bytes 524288 | tf_op jit(solution)/shard_map/all_to_all | solution.py:294
  189.1 0.6 dynamic_slice.3
  189.7 0.6 gather_fusion
  190.3 1.9 collective-permute-start.24
  192.3 2.9 %collective-permute-start.17 = (f32[512,128]{1,0:T(8,128)S(1)}, f32[512,128]{1,0:T(8,128)S(1)}, u32[]{:S(2)}, u32[]{:S(2)}) collective-permute-start(f32[512,128]{1,0:T(8,128)S(1)} %bitcast.41), channel_id=1, source_target_pairs={{0,32},{32,64},{64,96},{96,128},{128,160},{160,192},{192,224},{48,... | collective-permute-start | bytes 786440 | tf_op jit(solution)/shard_map/ppermute | solution.py:394
  195.2 1.7 collective-permute-start.23
  196.9 3.9 %collective-permute-start.22 = (f32[512,128]{1,0:T(8,128)S(1)}, f32[512,128]{1,0:T(8,128)S(1)}, u32[]{:S(2)}, u32[]{:S(2)}) collective-permute-start(f32[512,128]{1,0:T(8,128)S(1)} %bitcast.38), channel_id=1, source_target_pairs={{0,32},{32,64},{64,96},{96,128},{128,160},{160,192},{192,224},{1,3... | collective-permute-start | bytes 786440 | tf_op jit(solution)/shard_map/ppermute | solution.py:397
  200.8 0.7 and_convert_fusion
  201.5 0.7 pad_add_fusion.flags
  202.2 1.2 collective-permute-done.17.far
  203.3 5.2 %collective-permute-done.23.beside = f32[64,1024]{1,0:T(8,128)S(1)} collective-permute-done((f32[64,1024]{1,0:T(8,128)}, f32[64,1024]{1,0:T(8,128)S(1)}, u32[]{:S(2)}, u32[]{:S(2)}) %collective-permute-start.23) | collective-permute-done | bytes 262176 | tf_op jit(solution)/shard_map/ppermute | solution.py:396
  208.5 0.7 copy-done.16
  209.2 0.7 copy-done.17
  209.9 3.9 %assemble.1 = f32[64,5120]{1,0:T(8,128)} custom-call(s32[6]{0:T(128)} %pad_add_fusion.flags, f32[512,128]{1,0:T(8,128)} %copy-done.15, f32[512,128]{1,0:T(8,128)} %copy-done.17, f32[512,128]{1,0:T(8,128)} %bitcast.39, f32[64,1024]{1,0:T(8,128)} %get-tuple-element.83.rows2, f32[64,1024]{1,0:T(8,128)} %copy-done.16, f32[64,1024]{1,0:T(8,128)} %get-tuple-element.58.rows0_a, ...), custom_call_target="tpu_custom_call" | custom-call | flops 1024 | bytes 1024 | tf_op jit(solution)/shard_map/assemble/pallas_call | solution.py:322
  (66 shorter events, 3.2 us)
Async XLA Ops:
  4.7 3.8 %collective-permute-start.1 = (f32[3,1024]{1,0:T(4,128)S(1)}, f32[3,1024]{1,0:T(4,128)S(1)}, u32[]{:S(2)}, u32[]{:S(2)}) collective-permute-start(f32[3,1024]{1,0:T(4,128)S(1)} %pad_maximum_fusion), channel_id=1, source_target_pairs={{0,8},{1,9},{8,0},{9,1},{2,10},{3,11},{10,2},{11,3},{4,12},{5,13},... | collective-permute-start | bytes 36872 | tf_op jit(solution)/shard_map/ppermute | solution.py:33
  6.3 3.2 %collective-permute-start.2 = (f32[3,1024]{1,0:T(4,128)S(1)}, f32[3,1024]{1,0:T(4,128)S(1)}, u32[]{:S(2)}, u32[]{:S(2)}) collective-permute-start(f32[3,1024]{1,0:T(4,128)S(1)} %pad_maximum_fusion), channel_id=1, source_target_pairs={{0,9},{1,8},{8,1},{9,0},{2,11},{3,10},{10,3},{11,2},{4,13},{5,12},... | collective-permute-start | bytes 36872 | tf_op jit(solution)/shard_map/ppermute | solution.py:33
  6.3 3.2 %collective-permute-start = (f32[3,1024]{1,0:T(4,128)S(1)}, f32[3,1024]{1,0:T(4,128)S(1)}, u32[]{:S(2)}, u32[]{:S(2)}) collective-permute-start(f32[3,1024]{1,0:T(4,128)S(1)} %pad_maximum_fusion), channel_id=1, source_target_pairs={{0,1},{1,0},{8,9},{9,8},{2,3},{3,2},{10,11},{11,10},{4,5},{5,4},{1... | collective-permute-start | bytes 36872 | tf_op jit(solution)/shard_map/ppermute | solution.py:33
  9.5 5.1 %collective-permute-start.5 = (f32[3,1024]{1,0:T(4,128)S(1)}, f32[3,1024]{1,0:T(4,128)S(1)}, u32[]{:S(2)}, u32[]{:S(2)}) collective-permute-start(f32[3,1024]{1,0:T(4,128)S(1)} %add_add_fusion.1), channel_id=1, source_target_pairs={{0,6},{2,0},{4,2},{6,4},{1,7},{3,1},{5,3},{7,5},{8,14},{10,8},{12,... | collective-permute-start | bytes 36872 | tf_op jit(solution)/shard_map/ppermute | solution.py:37
  12.4 5.2 %collective-permute-start.4 = (f32[3,1024]{1,0:T(4,128)S(1)}, f32[3,1024]{1,0:T(4,128)S(1)}, u32[]{:S(2)}, u32[]{:S(2)}) collective-permute-start(f32[3,1024]{1,0:T(4,128)S(1)} %add_add_fusion.1), channel_id=1, source_target_pairs={{0,4},{2,6},{4,0},{6,2},{1,5},{3,7},{5,1},{7,3},{8,12},{10,14},{12... | collective-permute-start | bytes 36872 | tf_op jit(solution)/shard_map/ppermute | solution.py:37
  13.2 4.9 %collective-permute-start.3 = (f32[3,1024]{1,0:T(4,128)S(1)}, f32[3,1024]{1,0:T(4,128)S(1)}, u32[]{:S(2)}, u32[]{:S(2)}) collective-permute-start(f32[3,1024]{1,0:T(4,128)S(1)} %add_add_fusion.1), channel_id=1, source_target_pairs={{0,2},{2,4},{4,6},{6,0},{1,3},{3,5},{5,7},{7,1},{8,10},{10,12},{12... | collective-permute-start | bytes 36872 | tf_op jit(solution)/shard_map/ppermute | solution.py:37
  28.1 7.0 %collective-permute-start.6 = (bf16[1280,1024]{1,0:T(8,128)(2,1)}, bf16[1280,1024]{1,0:T(8,128)(2,1)S(1)}, u32[]{:S(2)}, u32[]{:S(2)}) collective-permute-start(bf16[1280,1024]{1,0:T(8,128)(2,1)} %get-tuple-element.51.right_a.zed_a), channel_id=1, source_target_pairs={{0,1},{1,0},{2,3},{3,2},{4,5},{5,4},{6,7},{7,6},{8,9},{9,8},{10,11... | collective-permute-start | bytes 7864328 | tf_op jit(solution)/shard_map/ppermute | solution.py:371
  28.1 36.3 %collective-permute-start.7 = (bf16[1280,512]{1,0:T(8,128)(2,1)}, bf16[1280,512]{1,0:T(8,128)(2,1)}, u32[]{:S(2)}, u32[]{:S(2)}) collective-permute-start(bf16[1280,512]{1,0:T(8,128)(2,1)} %get-tuple-element.54), channel_id=1, source_target_pairs={{32,0},{64,32},{96,64},{128,96},{160,128},{192,160},{224,192},{16,... | collective-permute-start | bytes 3932168 | tf_op jit(solution)/shard_map/ppermute | solution.py:368
  30.1 24.7 %collective-permute-start.9 = (bf16[8,32,1280]{2,1,0:T(8,128)(2,1)}, bf16[8,32,1280]{2,1,0:T(8,128)(2,1)S(1)}, u32[]{:S(2)}, u32[]{:S(2)}) collective-permute-start(bf16[8,32,1280]{2,1,0:T(8,128)(2,1)} %get-tuple-element.55), channel_id=1, source_target_pairs={{0,17},{1,16},{16,1},{17,0},{2,19},{3,18},{18,3},{19,2},{4,21},{5,... | collective-permute-start | bytes 1966088 | tf_op jit(solution)/shard_map/ppermute | solution.py:370
  34.7 29.7 %collective-permute-start.8 = (bf16[8,32,1280]{2,1,0:T(8,128)(2,1)}, bf16[8,32,1280]{2,1,0:T(8,128)(2,1)}, u32[]{:S(2)}, u32[]{:S(2)}) collective-permute-start(bf16[8,32,1280]{2,1,0:T(8,128)(2,1)} %get-tuple-element.49), channel_id=1, source_target_pairs={{0,16},{16,0},{32,48},{48,32},{64,80},{80,64},{96,112},{112,96},{1... | collective-permute-start | bytes 1966088 | tf_op jit(solution)/shard_map/ppermute | solution.py:369
  35.0 1.5 copy-start.4
  51.1 15.3 %copy-start.5 = (bf16[8,32,1280]{2,1,0:T(8,128)(2,1)S(1)}, bf16[8,32,1280]{2,1,0:T(8,128)(2,1)}, u32[]{:S(2)}) copy-start(bf16[8,32,1280]{2,1,0:T(8,128)(2,1)} %get-tuple-element.64) | copy-start | bytes 1966084
  51.1 30.5 %all-to-all-start = ((f32[4,2,64,1024]{3,2,1,0:T(8,128)}), f32[4,2,64,1024]{3,2,1,0:T(8,128)S(1)}, u32[]{:S(2)}, u32[]{:S(2)}) async-start(f32[4,2,64,1024]{3,2,1,0:T(8,128)} %bitcast.23), calls=%async_computation | async-start | bytes 4194304 | tf_op jit(solution)/shard_map/all_to_all | solution.py:250
  54.9 47.0 %copy-start.9 = (bf16[8,32,1280]{2,1,0:T(8,128)(2,1)}, bf16[8,32,1280]{2,1,0:T(8,128)(2,1)S(1)}, u32[]{:S(2)}) copy-start(bf16[8,32,1280]{2,1,0:T(8,128)(2,1)S(1)} %collective-permute-done.9) | copy-start | bytes 1966084
  64.4 8.6 %collective-permute-start.10 = (bf16[1280,512]{1,0:T(8,128)(2,1)}, bf16[1280,512]{1,0:T(8,128)(2,1)S(1)}, u32[]{:S(2)}, u32[]{:S(2)}) collective-permute-start(bf16[1280,512]{1,0:T(8,128)(2,1)} %collective-permute-done.7.right_a.near0_a), channel_id=1, source_target_pairs={{0,1},{1,0},{2,3},{3,2},{4,5},{5,4},{6,7},{7,6},{8,9},{9,8},{10,11... | collective-permute-start | bytes 3932168 | tf_op jit(solution)/shard_map/ppermute | solution.py:371
  64.4 37.5 %collective-permute-start.11 = (bf16[1280,512]{1,0:T(8,128)(2,1)}, bf16[1280,512]{1,0:T(8,128)(2,1)}, u32[]{:S(2)}, u32[]{:S(2)}) collective-permute-start(bf16[1280,512]{1,0:T(8,128)(2,1)} %get-tuple-element.63), channel_id=1, source_target_pairs={{32,0},{64,32},{96,64},{128,96},{160,128},{192,160},{224,192},{16,... | collective-permute-start | bytes 3932168 | tf_op jit(solution)/shard_map/ppermute | solution.py:368
  66.4 22.2 %collective-permute-start.12 = (bf16[8,32,1280]{2,1,0:T(8,128)(2,1)S(1)}, bf16[8,32,1280]{2,1,0:T(8,128)(2,1)}, u32[]{:S(2)}, u32[]{:S(2)}) collective-permute-start(bf16[8,32,1280]{2,1,0:T(8,128)(2,1)S(1)} %copy-done.5), channel_id=1, source_target_pairs={{0,16},{16,0},{32,48},{48,32},{64,80},{80,64},{96,112},{112,96},{1... | collective-permute-start | bytes 1966088 | tf_op jit(solution)/shard_map/ppermute | solution.py:369
  73.0 28.9 %collective-permute-start.13 = (bf16[8,32,1280]{2,1,0:T(8,128)(2,1)}, bf16[8,32,1280]{2,1,0:T(8,128)(2,1)}, u32[]{:S(2)}, u32[]{:S(2)}) collective-permute-start(bf16[8,32,1280]{2,1,0:T(8,128)(2,1)} %get-tuple-element.66), channel_id=1, source_target_pairs={{0,17},{1,16},{16,1},{17,0},{2,19},{3,18},{18,3},{19,2},{4,21},{5,... | collective-permute-start | bytes 1966088 | tf_op jit(solution)/shard_map/ppermute | solution.py:370
  73.0 1.1 copy-start.6
  81.6 1.3 copy-start.1
  101.9 3.7 %collective-permute-start.14 = (bf16[1280,512]{1,0:T(8,128)(2,1)}, bf16[1280,512]{1,0:T(8,128)(2,1)S(1)}, u32[]{:S(2)}, u32[]{:S(2)}) collective-permute-start(bf16[1280,512]{1,0:T(8,128)(2,1)} %collective-permute-done.11.right_a.near1_a), channel_id=1, source_target_pairs={{0,1},{1,0},{2,3},{3,2},{4,5},{5,4},{6,7},{7,6},{8,9},{9,8},{10,11... | collective-permute-start | bytes 3932168 | tf_op jit(solution)/shard_map/ppermute | solution.py:371
  102.1 19.3 %all-to-all-start.1 = ((f32[4,2,64,512]{3,2,1,0:T(8,128)}), f32[4,2,64,512]{3,2,1,0:T(8,128)S(1)}, u32[]{:S(2)}, u32[]{:S(2)}) async-start(f32[4,2,64,512]{3,2,1,0:T(8,128)} %bitcast.37), calls=%async_computation.1 | async-start | bytes 2097152 | tf_op jit(solution)/shard_map/all_to_all | solution.py:250
  105.6 1.1 copy-start.7
  121.4 3.7 %copy-start.3 = (f32[4,2,64,512]{3,2,1,0:T(8,128)}, f32[4,2,64,512]{3,2,1,0:T(8,128)S(1)}, u32[]{:S(2)}) copy-start(f32[4,2,64,512]{3,2,1,0:T(8,128)S(1)} %all-to-all-done.1.refs_0_.refs_1_.refs_2_.refs_3_) | copy-start | bytes 3145732
  121.4 25.0 %all-to-all-start.2 = ((f32[4,2,64,512]{3,2,1,0:T(8,128)}), f32[4,2,64,512]{3,2,1,0:T(8,128)S(1)}, u32[]{:S(2)}, u32[]{:S(2)}) async-start(f32[4,2,64,512]{3,2,1,0:T(8,128)} %bitcast.36), calls=%async_computation.2 | async-start | bytes 2097152 | tf_op jit(solution)/shard_map/all_to_all | solution.py:250
  127.8 18.3 %copy-start.21 = (f32[64,512]{1,0:T(8,128)S(1)}, f32[64,512]{1,0:T(8,128)}, u32[]{:S(2)}) copy-start(f32[64,512]{1,0:T(8,128)} %get-tuple-element.70) | copy-start | bytes 393220
  140.0 18.5 %collective-permute-start.18 = (f32[2,64,1024]{2,1,0:T(8,128)}, f32[2,64,1024]{2,1,0:T(8,128)S(1)}, u32[]{:S(2)}, u32[]{:S(2)}) collective-permute-start(f32[2,64,1024]{2,1,0:T(8,128)} %get-tuple-element.80), channel_id=1, source_target_pairs={{0,2},{2,4},{4,6},{6,0},{1,3},{3,5},{5,7},{7,1},{8,10},{10,12},{12... | collective-permute-start | bytes 1572872 | tf_op jit(solution)/shard_map/ppermute | solution.py:260
  142.0 25.1 %collective-permute-start.19 = (f32[2,64,1024]{2,1,0:T(8,128)}, f32[2,64,1024]{2,1,0:T(8,128)S(1)}, u32[]{:S(2)}, u32[]{:S(2)}) collective-permute-start(f32[2,64,1024]{2,1,0:T(8,128)} %get-tuple-element.81), channel_id=1, source_target_pairs={{0,4},{2,6},{4,0},{6,2},{1,5},{3,7},{5,1},{7,3},{8,12},{10,14},{12... | collective-permute-start | bytes 1572872 | tf_op jit(solution)/shard_map/ppermute | solution.py:260
  144.6 22.5 %collective-permute-start.20 = (f32[2,64,1024]{2,1,0:T(8,128)}, f32[2,64,1024]{2,1,0:T(8,128)S(1)}, u32[]{:S(2)}, u32[]{:S(2)}) collective-permute-start(f32[2,64,1024]{2,1,0:T(8,128)} %get-tuple-element.82), channel_id=1, source_target_pairs={{0,6},{2,0},{4,2},{6,4},{1,7},{3,1},{5,3},{7,5},{8,14},{10,8},{12,... | collective-permute-start | bytes 1572872 | tf_op jit(solution)/shard_map/ppermute | solution.py:260
  146.1 5.8 %collective-permute-start.15 = (f32[64,512]{1,0:T(8,128)S(1)}, f32[64,512]{1,0:T(8,128)S(1)}, u32[]{:S(2)}, u32[]{:S(2)}) collective-permute-start(f32[64,512]{1,0:T(8,128)S(1)} %copy-done.21), channel_id=1, source_target_pairs={{0,8},{8,0},{1,9},{9,1},{2,10},{10,2},{3,11},{11,3},{4,12},{12,4},... | collective-permute-start | bytes 393224 | tf_op jit(solution)/shard_map/ppermute | solution.py:245
  146.4 1.0 copy-start.2
  150.0 39.1 %copy-start = (s32[16]{0:T(128)S(1)}, s32[16]{0:T(128)}, u32[]{:S(2)}) copy-start(s32[16]{0:T(128)} %param.5) | copy-start | bytes 196
  150.0 40.3 %copy-start.20 = (f32[64,1024]{1,0:T(8,128)S(1)}, f32[64,1024]{1,0:T(8,128)}, u32[]{:S(2)}) copy-start(f32[64,1024]{1,0:T(8,128)} %get-tuple-element.92) | copy-start | bytes 786436
  150.0 5.3 %collective-permute-start.16 = (f32[64,512]{1,0:T(8,128)}, f32[64,512]{1,0:T(8,128)S(1)}, u32[]{:S(2)}, u32[]{:S(2)}) collective-permute-start(f32[64,512]{1,0:T(8,128)} %get-tuple-element.78), channel_id=1, source_target_pairs={{0,8},{8,0},{1,9},{9,1},{2,10},{10,2},{3,11},{11,3},{4,12},{12,4},... | collective-permute-start | bytes 393224 | tf_op jit(solution)/shard_map/ppermute | solution.py:245
  151.8 3.5 %copy-start.18 = (f32[64,512]{1,0:T(8,128)}, f32[64,512]{1,0:T(8,128)S(1)}, u32[]{:S(2)}) copy-start(f32[64,512]{1,0:T(8,128)S(1)} %collective-permute-done.15.refs_1_) | copy-start | bytes 393220
  155.3 0.7 copy-start.19
  158.5 8.5 %copy-start.10 = (f32[2,64,1024]{2,1,0:T(8,128)}, f32[2,64,1024]{2,1,0:T(8,128)S(1)}, u32[]{:S(2)}) copy-start(f32[2,64,1024]{2,1,0:T(8,128)S(1)} %collective-permute-done.18.refs_1_) | copy-start | bytes 1572868
  167.0 0.8 copy-start.11
  167.1 1.0 copy-start.12
  172.3 6.9 %collective-permute-start.21 = (f32[64,1024]{1,0:T(8,128)}, f32[64,1024]{1,0:T(8,128)S(1)}, u32[]{:S(2)}, u32[]{:S(2)}) collective-permute-start(f32[64,1024]{1,0:T(8,128)} %get-tuple-element.89), channel_id=1, source_target_pairs={{0,8},{8,0},{1,9},{9,1},{2,10},{10,2},{3,11},{11,3},{4,12},{12,4},... | collective-permute-start | bytes 786440 | tf_op jit(solution)/shard_map/ppermute | solution.py:245
  172.6 12.9 %all-to-all-start.3 = ((f32[16,32,128]{2,1,0:T(8,128)}), f32[16,32,128]{2,1,0:T(8,128)S(1)}, u32[]{:S(2)}, u32[]{:S(2)}) async-start(f32[16,32,128]{2,1,0:T(8,128)} %get-tuple-element.79), calls=%async_computation.3 | async-start | bytes 524288 | tf_op jit(solution)/shard_map/all_to_all | solution.py:294
  179.2 0.7 copy-start.13
  185.5 11.4 %all-to-all-start.4 = ((f32[16,32,128]{2,1,0:T(8,128)}), f32[16,32,128]{2,1,0:T(8,128)S(1)}, u32[]{:S(2)}, u32[]{:S(2)}) async-start(f32[16,32,128]{2,1,0:T(8,128)} %get-tuple-element.90), calls=%async_computation.4 | async-start | bytes 524288 | tf_op jit(solution)/shard_map/all_to_all | solution.py:294
  190.3 11.8 %collective-permute-start.24 = (f32[64,1024]{1,0:T(8,128)S(1)}, f32[64,1024]{1,0:T(8,128)S(1)}, u32[]{:S(2)}, u32[]{:S(2)}) collective-permute-start(f32[64,1024]{1,0:T(8,128)S(1)} %copy-done.20), channel_id=1, source_target_pairs={{0,8},{8,0},{1,9},{9,1},{2,10},{10,2},{3,11},{11,3},{4,12},{12,4},... | collective-permute-start | bytes 786440 | tf_op jit(solution)/shard_map/ppermute | solution.py:245
  192.3 11.1 %collective-permute-start.17 = (f32[512,128]{1,0:T(8,128)S(1)}, f32[512,128]{1,0:T(8,128)S(1)}, u32[]{:S(2)}, u32[]{:S(2)}) collective-permute-start(f32[512,128]{1,0:T(8,128)S(1)} %bitcast.41), channel_id=1, source_target_pairs={{0,32},{32,64},{64,96},{96,128},{128,160},{160,192},{192,224},{48,... | collective-permute-start | bytes 786440 | tf_op jit(solution)/shard_map/ppermute | solution.py:394
  195.2 13.3 %collective-permute-start.23 = (f32[64,1024]{1,0:T(8,128)}, f32[64,1024]{1,0:T(8,128)S(1)}, u32[]{:S(2)}, u32[]{:S(2)}) collective-permute-start(f32[64,1024]{1,0:T(8,128)} %get-tuple-element.91), channel_id=1, source_target_pairs={{0,16},{16,0},{32,48},{48,32},{64,80},{80,64},{96,112},{112,96},{1... | collective-permute-start | bytes 786440 | tf_op jit(solution)/shard_map/ppermute | solution.py:396
  196.9 11.6 %copy-start.8 = (f32[16,32,128]{2,1,0:T(8,128)}, f32[16,32,128]{2,1,0:T(8,128)S(1)}, u32[]{:S(2)}) copy-start(f32[16,32,128]{2,1,0:T(8,128)S(1)} %all-to-all-done.4) | copy-start | bytes 786436
  196.9 11.6 %collective-permute-start.22 = (f32[512,128]{1,0:T(8,128)S(1)}, f32[512,128]{1,0:T(8,128)S(1)}, u32[]{:S(2)}, u32[]{:S(2)}) collective-permute-start(f32[512,128]{1,0:T(8,128)S(1)} %bitcast.38), channel_id=1, source_target_pairs={{0,32},{32,64},{64,96},{96,128},{128,160},{160,192},{192,224},{1,3... | collective-permute-start | bytes 786440 | tf_op jit(solution)/shard_map/ppermute | solution.py:397
  202.2 6.3 %copy-start.14 = (f32[64,1024]{1,0:T(8,128)}, f32[64,1024]{1,0:T(8,128)S(1)}, u32[]{:S(2)}) copy-start(f32[64,1024]{1,0:T(8,128)S(1)} %collective-permute-done.24.rows0_b) | copy-start | bytes 786436
  203.3 5.2 %copy-start.15 = (f32[512,128]{1,0:T(8,128)}, f32[512,128]{1,0:T(8,128)S(1)}, u32[]{:S(2)}) copy-start(f32[512,128]{1,0:T(8,128)S(1)} %collective-permute-done.17.far) | copy-start | bytes 786436
  208.5 0.7 copy-start.16
  209.2 0.7 copy-start.17

commit v4 on v3

--- a/solution.py
+++ b/solution.py
@@ -67,91 +67,81 @@
     return jnp.dot(left, right, preferred_element_type=jnp.float32)
 
 
-def standard_kernel(meta, dosage, observed, stats, zed, zed0, zed1, kept0, kept1, sent0, sent1):
+def standard_kernel(meta, dosage, observed, stats, zed, kept, sent):
     weight = observed[...].astype(jnp.float32)
     values = dosage[...].astype(jnp.float32)
     z = (weight * (values - stats[0:1, :]) * stats[1:2, :]).astype(jnp.bfloat16)
     zed[...] = z
-    zed0[...] = z[:, :HALF]
-    zed1[...] = z[:, HALF:]
     turned = z.T
 
     def store(*outs):
         for p in range(PIECES):
             for k, out in enumerate(outs):
-                at = 2 * ROWS * chip_of(p) + TURN * k
-                out[p] = turned[at : at + TURN]
-
-    pl.when(meta[0] == 0)(lambda: store(kept0, kept1, sent0, sent1))
-    pl.when(meta[0] != 0)(lambda: store(sent0, sent1, kept0, kept1))
+                at = 2 * ROWS * chip_of(p) + ROWS * k
+                out[p] = turned[at : at + ROWS]
+
+    pl.when(meta[0] == 0)(lambda: store(kept, sent))
+    pl.when(meta[0] != 0)(lambda: store(sent, kept))
 
 
 def standardize(meta, dosage, observed, stats):
     rows = 256
     block = lambda width: pl.BlockSpec((rows, width), lambda i, m: (i, 0))
-    turned = pl.BlockSpec((PIECES, TURN, rows), lambda i, m: (0, 0, i))
+    turned = pl.BlockSpec((PIECES, ROWS, rows), lambda i, m: (0, 0, i))
     return pl.pallas_call(
         standard_kernel,
         name="standardize",
-        out_shape=(bf16(DEPTH, B), bf16(DEPTH, HALF), bf16(DEPTH, HALF))
-        + (bf16(PIECES, TURN, DEPTH),) * 4,
+        out_shape=(bf16(DEPTH, B),) + (bf16(PIECES, ROWS, DEPTH),) * 2,
         grid_spec=pltpu.PrefetchScalarGridSpec(
             num_scalar_prefetch=1,
             grid=(DEPTH // rows,),
             in_specs=[block(B), block(B), whole((2, B))],
-            out_specs=(block(B), block(HALF), block(HALF)) + (turned,) * 4,
+            out_specs=(block(B), turned, turned),
         ),
         compiler_params=params(),
         cost_estimate=cost(4 * DEPTH * B, 12 * DEPTH * B),
     )(meta, dosage, observed, stats)
 
 
-LEFT = (PIECES * TURN, DEPTH)
+LEFT = (PIECES * ROWS, DEPTH)
 
 
 def flat(*turned):
     return [t.reshape(LEFT) for t in turned]
 
 
-def turn_kernel(meta, zed, out0, out1):
+def turn_kernel(meta, zed, out):
     turned = zed[...].T
 
-    def store(at):
-        out0[0] = turned[at : at + TURN]
-        out1[0] = turned[at + TURN : at + ROWS]
+    def store(part):
+        out[0] = turned[ROWS * part : ROWS * (part + 1)]
 
     pl.when(meta[0] == 0)(lambda: store(0))
-    pl.when(meta[0] != 0)(lambda: store(ROWS))
+    pl.when(meta[0] != 0)(lambda: store(1))
 
 
 def turn(meta, zed):
-    out = pl.BlockSpec((1, TURN, DEPTH), lambda c, m: (c, 0, 0))
     return pl.pallas_call(
         turn_kernel,
         name="turn",
-        out_shape=(bf16(PIECES, TURN, DEPTH),) * 2,
+        out_shape=bf16(PIECES, ROWS, DEPTH),
         grid_spec=pltpu.PrefetchScalarGridSpec(
             num_scalar_prefetch=1,
             grid=(PIECES,),
             in_specs=[pl.BlockSpec((DEPTH, 2 * ROWS), lambda p, m: (0, p // 2 + 4 * (p % 2)))],
-            out_specs=(out, out),
+            out_specs=pl.BlockSpec((1, ROWS, DEPTH), lambda p, m: (p, 0, 0)),
         ),
         compiler_params=params(),
         cost_estimate=cost(DEPTH * B, 3 * DEPTH * B),
     )(meta, zed)
 
 
-def store_pieces(out, at, left_a, left_b, right_a, right_b):
+def product_kernel(meta, left_a, left_b, right_a, right_b, out):
     acc = matmul(left_a[...], right_a[...]) + matmul(left_b[...], right_b[...])
-    out[:, at : at + TURN] = acc.reshape(PIECES, TURN, STEP)
-
-
-def product_kernel(meta, own0_a, own1_a, own0_b, own1_b, right_a, right_b, out):
-    store_pieces(out, 0, own0_a, own0_b, right_a, right_b)
-    store_pieces(out, TURN, own1_a, own1_b, right_a, right_b)
-
-
-def product(meta, own_a, own_b, right, name):
+    out[...] = acc.reshape(PIECES, ROWS, STEP)
+
+
+def product(meta, left, right, name):
     columns = right[0].shape[1]
     block = pl.BlockSpec((DEPTH, STEP), lambda j, m: (0, j))
     return pl.pallas_call(
@@ -161,19 +151,16 @@
         grid_spec=pltpu.PrefetchScalarGridSpec(
             num_scalar_prefetch=1,
             grid=(columns // STEP,),
-            in_specs=[whole(LEFT)] * 4 + [block] * 2,
+            in_specs=[whole(LEFT)] * 2 + [block] * 2,
             out_specs=pl.BlockSpec((PIECES, ROWS, STEP), lambda j, m: (0, 0, j)),
         ),
         compiler_params=params(),
         cost_estimate=cost(2 * DEPTH * B * columns, 4 * DEPTH * B + 4 * B * columns),
-    )(meta, *flat(*own_a, *own_b), *right)
-
-
-def across_kernel(
-    meta, other0_a, other1_a, other0_b, other1_b, near0_a, near0_b, near1_a, near1_b, zed_a, zed_b, *rest
-):
+    )(meta, *flat(*left), *right)
+
+
+def across_kernel(meta, left_a, left_b, near_a, near_b, zed_a, zed_b, *rest):
     outs, right = rest[:4], rest[4]
-    j = pl.program_id(0)
     odd = meta[1] == 1
 
     def take(a, b):
@@ -181,25 +168,19 @@
         right[DEPTH:] = b[...]
 
     pl.when(odd)(lambda: take(zed_a, zed_b))
-    pl.when(~odd & (j < 2))(lambda: take(near0_a, near0_b))
-    pl.when(~odd & (j >= 2))(lambda: take(near1_a, near1_b))
-
-    for at, left_a, left_b in ((0, other0_a, other0_b), (TURN, other1_a, other1_b)):
-        acc = matmul(left_a[...], right[:DEPTH]) + matmul(left_b[...], right[DEPTH:])
-        acc = acc.reshape(4, 2, TURN, STEP)
-        for x in range(4):
-
-            @pl.when(meta[3] == x)
-            def _():
-                for k in range(4):
-                    outs[k][:, at : at + TURN] = acc[(x + k) % 4]
-
-
-def across_product(meta, other0, other1, near0, near1, zed):
-    first = pl.BlockSpec((DEPTH, STEP), lambda j, m: (0, jnp.clip(j, 0, 1)))
-    second = pl.BlockSpec((DEPTH, STEP), lambda j, m: (0, jnp.clip(j - 2, 0, 1)))
+    pl.when(~odd)(lambda: take(near_a, near_b))
+    acc = matmul(left_a[...], right[:DEPTH]) + matmul(left_b[...], right[DEPTH:])
+    acc = acc.reshape(4, 2, ROWS, STEP)
+    for x in range(4):
+
+        @pl.when(meta[3] == x)
+        def _():
+            for k in range(4):
+                outs[k][...] = acc[(x + k) % 4]
+
+
+def across_product(meta, left, near, zed):
     block = pl.BlockSpec((DEPTH, STEP), lambda j, m: (0, j))
-    left = (other0[0], other1[0], other0[1], other1[1])
     return pl.pallas_call(
         across_kernel,
         name="across",
@@ -207,13 +188,13 @@
         grid_spec=pltpu.PrefetchScalarGridSpec(
             num_scalar_prefetch=1,
             grid=(B // STEP,),
-            in_specs=[whole(LEFT)] * 4 + [first] * 2 + [second] * 2 + [block] * 2,
+            in_specs=[whole(LEFT)] * 2 + [block] * 4,
             out_specs=(pl.BlockSpec((2, ROWS, STEP), lambda j, m: (0, 0, j)),) * 4,
             scratch_shapes=[pltpu.VMEM((2 * DEPTH, STEP), jnp.bfloat16)],
         ),
         compiler_params=params(),
         cost_estimate=cost(2 * DEPTH * B * B, 12 * DEPTH * B + 4 * B * B),
-    )(meta, *flat(*left), *near0, *near1, *zed)
+    )(meta, *flat(*left), *near, *zed)
 
 
 def after(value, *others):
@@ -247,7 +228,8 @@
 
 def fold(meta, parts, *others):
     _, rows, columns = parts.shape
-    parts = after(lax.all_to_all(parts.reshape(4, 2, rows, columns), "x", 0, 0), *others)
+    parts = lax.all_to_all(parts.reshape(4, 2, rows, columns), "x", 0, 0)
+    parts = after(parts, *others)
     specs = [
         pl.BlockSpec((pl.Squeezed(), 2, rows, STEP), lambda j, m, k=k: (k, 0, 0, j)) for k in range(4)
     ]
@@ -364,34 +346,25 @@
     spread = second - first * mean
     stats = jnp.stack([mean, lax.rsqrt(spread + eps * cnt)])
 
-    zed, zed0, zed1, kept0, kept1, sent0, sent1 = standardize(meta, dosage, observed, stats)
+    zed, kept, sent = standardize(meta, dosage, observed, stats)
     along = lambda t: lax.ppermute(t, SNP, EVEN_DOWN + ODD_UP)
     across = lambda t: lax.ppermute(t, SNP, TO_OTHER)
     athwart = lambda t: lax.ppermute(t, ("yh", "core"), [(i, 3 - i) for i in range(4)])
     swap = lambda t: lax.ppermute(t, "core", SWAP)
+    other = across(kept)
+    other = (other, athwart(after(sent, other)))
+    near = along(zed)
     zed_b = swap(zed)
-    near0 = along(zed0)
-    other0 = (across(kept0), athwart(sent0))
-
-    own_a = (kept0, kept1)
-    own_b = turn(meta, zed_b)
-    rows0 = product(meta, own_a, own_b, (zed, zed_b), "own")
-    near0, other0 = after((near0, other0), rows0)
-    near1 = along(after(zed1, near0, other0))
-    other1 = (across(after(kept1, near0, other0)), athwart(after(sent1, near0, other0)))
-    near0 = (near0, swap(near0))
-    first = product(meta, own_a, own_b, near0, "first")
-    rows0 = fold(meta, rows0, first)
-    near1, other1 = after((near1, other1), first, rows0[0])
-    near1 = (near1, swap(near1))
-    second = product(meta, own_a, own_b, near1, "second")
-    first = fold(meta, after(first, rows0[0]), second)
-    pieces = across_product(meta, after(other0, first[0]), other1, near0, near1, (zed, zed_b))
-    second = fold(meta, second, pieces[0])
-    rows2, turned2 = gather(meta, first, second)
-    rows1 = fold_pieces(meta, pieces, rows2)
-
+    own = (kept, turn(meta, zed_b))
+    rows0 = fold(meta, product(meta, own, (zed, zed_b), "own"), other)
+    near, other = after((near, other), rows0[0])
+    near = (near, swap(near))
+    rows2 = product(meta, own, near, "along")
+    pieces = across_product(meta, after(other, rows2), near, (zed, zed_b))
+    rows2 = fold(meta, rows2, pieces[0])
+    rows2, turned2 = gather(meta, rows2)
     far = lax.ppermute(turned2, SNP, EVEN_UP + ODD_DOWN)
+    rows1 = fold_pieces(meta, pieces, turned2)
     rows1, turned1 = gather(meta, rows1)
     beside = lax.ppermute(rows1, SNP, TO_OTHER)
     near = lax.ppermute(turned1, SNP, EVEN_UP)

time: 216 us -> 217 us (level)
  waiting for transfers between devices: 64.9 us -> 90.1 us
  starting transfers between devices: 60.9 us -> 46.5 us
  Pallas kernels: 69.5 us -> 61.8 us
    ppermute x2 -> x1, waiting for transfers between devices: 13.3 us -> 30.7 us  [on_device(): lax.ppermute(t, ('yh', 'core'), [(i, 3 - i) for i in range(4)])]
    ppermute x4 -> x3, waiting for transfers between devices: 5 us -> 14 us  [add(): return (keep, lax.ppermute(send, 'yl', SWAP))]
    ppermute x3, waiting for transfers between devices: 8.53 us -> 2.24 us  [fold_pieces(): lax.ppermute(parts[k], 'x', [(i, (i + k) % 4) for i in range(4)])]
    ppermute x3 -> x2, waiting for transfers between devices: 0.01 us -> 5.21 us  [on_device(): swap = lambda t: lax.ppermute(t, 'core', SWAP)]
    ppermute x2 -> x1, starting transfers between devices: 6.83 us -> 2.95 us  [on_device(): across = lambda t: lax.ppermute(t, SNP, TO_OTHER)]
    all_to_all x3 -> x2, starting transfers between devices: 10.9 us -> 7.21 us  [fold(): parts = lax.all_to_all(parts.reshape(4, 2, rows, columns), 'x', 0, 0)]
    pallas_call x1, Pallas kernels: 12.2 us -> 9.35 us  [across_product(): pl.pallas_call(across_kernel, name='across', out_shape=(f32(2, ROWS, B),)...]
    pallas_call x3 -> x2, Pallas kernels: 18.4 us -> 15.6 us  [product(): pl.pallas_call(product_kernel, name=name, out_shape=f32(PIECES, ROWS, col...]
  transfers between devices with their start and end apart: 30 -> 24, of which waited for: 15 -> 15; matrix products, arithmetic and copies ran while one was open for 1% -> 2% of each run, Pallas kernels for 24% -> 16%
where the time goes in v4:
time: 217 us; the launch traced here: 215 us
  waiting for transfers between devices  90.1 us (42%)
  Pallas kernels  61.8 us (28%)
  starting transfers between devices  46.5 us (21%)
  local copies, waits for them, and re-layouts  9.24 us (4%)
  other arithmetic  7.35 us (3%)
    ppermute x1, waiting for transfers between devices, on_device(): lax.ppermute(t, ('yh', 'core'), [(i, 3 - i) for i in range(4)])  30.7 us
    pallas_call x2, Pallas kernels, product(): pl.pallas_call(product_kernel, name=name, out_shape=f32(PIECES, ROWS, col...  15.6 us
    ppermute x3, waiting for transfers between devices, add(): return (keep, lax.ppermute(send, 'yl', SWAP))  14 us
    pallas_call x3, Pallas kernels, add(): pl.pallas_call(add_kernel, name='add', out_shape=(f32(rows, columns),) *...  12.7 us
    all_to_all x2, waiting for transfers between devices, fold(): parts = lax.all_to_all(parts.reshape(4, 2, rows, columns), 'x', 0, 0)  12.2 us
    pallas_call x1, Pallas kernels, across_product(): pl.pallas_call(across_kernel, name='across', out_shape=(f32(2, ROWS, B),)...  9.35 us
    pallas_call x1, Pallas kernels, standardize(): pl.pallas_call(standard_kernel, name='standardize', out_shape=(bf16(DEPTH...  8.37 us
    ppermute x1, waiting for transfers between devices, on_device(): across = lambda t: lax.ppermute(t, SNP, TO_OTHER)  8.11 us
  transfers between devices with their start and end apart: 24, of which 15 were waited for; matrix products, arithmetic and copies ran while one was open for 2% of the time, Pallas kernels for 16%

profile of v4, /device:TPU:64, one launch (start us, length us, event | category | flops | bytes accessed | tf_op | source)
XLA Modules:
  0.0 215.2 jit_solution(15949877069932649813)
XLA Ops:
  0.0 4.7 %fusion.1 = (f32[1024]{0:T(1024)S(1)}, f32[1024]{0:T(1024)S(1)}, f32[1024]{0:T(1024)S(1)}) fusion(bf16[1280,1024]{1,0:T(8,128)(2,1)} %dosage.1, s32[1280,1024]{1,0:T(8,128)} %observed.1), kind=kLoop, calls=%fused_computation.5 | loop fusion | flops 9171968 | bytes 7876608 | tf_op jit(solution)/shard_map/reduce_sum | solution.py:340
  4.7 1.7 collective-permute-start.1
  6.3 0.6 collective-permute-start
  6.9 1.6 collective-permute-done.1
  8.5 1.0 collective-permute-done.2
  9.5 0.0 collective-permute-done
  9.5 2.8 %collective-permute-start.5 = (f32[3,1024]{1,0:T(4,128)S(1)}, f32[3,1024]{1,0:T(4,128)S(1)}, u32[]{:S(2)}, u32[]{:S(2)}) collective-permute-start(f32[3,1024]{1,0:T(4,128)S(1)} %add_add_fusion.1), channel_id=1, source_target_pairs={{0,6},{2,0},{4,2},{6,4},{1,7},{3,1},{5,3},{7,5},{8,14},{10,8},{12,... | collective-permute-start | bytes 36872 | tf_op jit(solution)/shard_map/ppermute | solution.py:37
  12.4 0.8 collective-permute-start.4
  13.2 0.9 collective-permute-start.3
  14.1 0.7 pad_add_fusion.1.meta
  14.7 2.9 %collective-permute-done.4 = f32[3,1024]{1,0:T(4,128)S(1)} collective-permute-done((f32[3,1024]{1,0:T(4,128)S(1)}, f32[3,1024]{1,0:T(4,128)S(1)}, u32[]{:S(2)}, u32[]{:S(2)}) %collective-permute-start.4) | collective-permute-done | bytes 12320 | tf_op jit(solution)/shard_map/ppermute | solution.py:37
  17.6 0.5 collective-permute-done.3
  18.2 0.6 pad_maximum_fusion.1.stats
  18.8 8.4 %standardize.1 = (bf16[1280,1024]{1,0:T(8,128)(2,1)}, bf16[8,64,1280]{2,1,0:T(8,128)(2,1)}, bf16[8,64,1280]{2,1,0:T(8,128)(2,1)}) custom-call(s32[4]{0:T(128)} %pad_add_fusion.1.meta, bf16[1280,1024]{1,0:T(8,128)(2,1)} %dosage.1, s32[1280,1024]{1,0:T(8,128)} %observed.1, f32[2,1024]{1,0:T(2,128)} %pad_maximum_fusion.1.stats), custom_call_target="tpu_custom_call" | custom-call | flops 1024 | bytes 1024 | tf_op jit(solution)/shard_map/standardize/pallas_call | solution.py:91
  27.2 2.9 %collective-permute-start.8 = (bf16[8,64,1280]{2,1,0:T(8,128)(2,1)}, bf16[8,64,1280]{2,1,0:T(8,128)(2,1)S(1)}, u32[]{:S(2)}, u32[]{:S(2)}) collective-permute-start(bf16[8,64,1280]{2,1,0:T(8,128)(2,1)} %get-tuple-element.34), channel_id=1, source_target_pairs={{0,16},{16,0},{32,48},{48,32},{64,80},{80,64},{96,112},{112,96},{1... | collective-permute-start | bytes 3932168 | tf_op jit(solution)/shard_map/ppermute | solution.py:351
  30.1 2.0 collective-permute-start.7
  32.1 0.2 collective-permute-done.6.zed.right_b.zed_b
  32.3 1.5 copy-done.3
  33.8 6.7 %turn.1 = bf16[8,64,1280]{2,1,0:T(8,128)(2,1)} custom-call(s32[4]{0:T(128)} %pad_add_fusion.1.meta, bf16[1280,1024]{1,0:T(8,128)(2,1)} %copy-done.3), custom_call_target="tpu_custom_call" | custom-call | flops 1024 | bytes 1024 | tf_op jit(solution)/shard_map/turn/pallas_call | solution.py:124
  40.5 7.8 %own.1 = f32[8,64,1024]{2,1,0:T(8,128)} custom-call(s32[4]{0:T(128)} %pad_add_fusion.1.meta, bf16[512,1280]{1,0:T(8,128)(2,1)} %bitcast.22, bf16[512,1280]{1,0:T(8,128)(2,1)} %bitcast.18, bf16[1280,1024]{1,0:T(8,128)(2,1)} %get-tuple-element.35.right_a.zed_a, bf16[1280,1024]{1,0:T(8,128)(2,1)} %copy-done.3), custom_call_target="tpu_custom_call" | custom-call | flops 1024 | bytes 1024 | tf_op jit(solution)/shard_map/own/pallas_call | solution.py:147
  48.3 3.6 %all-to-all-start = ((f32[4,2,64,1024]{3,2,1,0:T(8,128)}), f32[4,2,64,1024]{3,2,1,0:T(8,128)S(1)}, u32[]{:S(2)}, u32[]{:S(2)}) async-start(f32[4,2,64,1024]{3,2,1,0:T(8,128)} %bitcast.21), calls=%async_computation | async-start | bytes 4194304 | tf_op jit(solution)/shard_map/all_to_all | solution.py:231
  52.0 8.1 %collective-permute-done.8 = bf16[8,64,1280]{2,1,0:T(8,128)(2,1)S(1)} collective-permute-done((bf16[8,64,1280]{2,1,0:T(8,128)(2,1)}, bf16[8,64,1280]{2,1,0:T(8,128)(2,1)S(1)}, u32[]{:S(2)}, u32[]{:S(2)}) %collective-permute-start.8) | collective-permute-done | bytes 1310752 | tf_op jit(solution)/shard_map/ppermute | solution.py:351
  60.1 2.2 %collective-permute-start.9 = (bf16[8,64,1280]{2,1,0:T(8,128)(2,1)}, bf16[8,64,1280]{2,1,0:T(8,128)(2,1)}, u32[]{:S(2)}, u32[]{:S(2)}) collective-permute-start(bf16[8,64,1280]{2,1,0:T(8,128)(2,1)} %get-tuple-element.37), channel_id=1, source_target_pairs={{0,17},{1,16},{16,1},{17,0},{2,19},{3,18},{18,3},{19,2},{4,21},{5,... | collective-permute-start | bytes 3932168 | tf_op jit(solution)/shard_map/ppermute | solution.py:352
  62.2 30.7 %collective-permute-done.9 = bf16[8,64,1280]{2,1,0:T(8,128)(2,1)} collective-permute-done((bf16[8,64,1280]{2,1,0:T(8,128)(2,1)}, bf16[8,64,1280]{2,1,0:T(8,128)(2,1)}, u32[]{:S(2)}, u32[]{:S(2)}) %collective-permute-start.9) | collective-permute-done | bytes 1310752 | tf_op jit(solution)/shard_map/ppermute | solution.py:352
  92.9 1.4 copy-done.2
  94.3 4.3 %add.104 = (f32[64,1024]{1,0:T(8,128)}, f32[64,1024]{1,0:T(8,128)}) custom-call(s32[4]{0:T(128)} %pad_add_fusion.1.meta, f32[4,2,64,1024]{3,2,1,0:T(8,128)} %copy-done.2, f32[4,2,64,1024]{3,2,1,0:T(8,128)} %copy-done.2, f32[4,2,64,1024]{3,2,1,0:T(8,128)} %copy-done.2, f32[4,2,64,1024]{3,2,1,0:T(8,128)} %copy-done.2), custom_call_target="tpu_custom_call" | custom-call | flops 1024 | bytes 1024 | tf_op jit(solution)/shard_map/add/pallas_call | solution.py:213
  98.5 0.1 collective-permute-start.10
  98.7 5.1 %collective-permute-done.10.right_b.near_b = bf16[1280,1024]{1,0:T(8,128)(2,1)S(1)} collective-permute-done((bf16[1280,1024]{1,0:T(8,128)(2,1)}, bf16[1280,1024]{1,0:T(8,128)(2,1)S(1)}, u32[]{:S(2)}, u32[]{:S(2)}) %collective-permute-start.10) | collective-permute-done | bytes 2621472 | tf_op jit(solution)/shard_map/ppermute | solution.py:353
  103.7 1.6 copy-done.4
  105.3 7.8 %along.1 = f32[8,64,1024]{2,1,0:T(8,128)} custom-call(s32[4]{0:T(128)} %pad_add_fusion.1.meta, bf16[512,1280]{1,0:T(8,128)(2,1)} %bitcast.23, bf16[512,1280]{1,0:T(8,128)(2,1)} %bitcast.19, bf16[1280,1024]{1,0:T(8,128)(2,1)} %collective-permute-done.7.right_a.near_a, bf16[1280,1024]{1,0:T(8,128)(2,1)} %copy-done.4), custom_call_target="tpu_custom_call" | custom-call | flops 1024 | bytes 1024 | tf_op jit(solution)/shard_map/along/pallas_call | solution.py:147
  113.1 3.6 %all-to-all-start.1 = ((f32[4,2,64,1024]{3,2,1,0:T(8,128)}), f32[4,2,64,1024]{3,2,1,0:T(8,128)S(1)}, u32[]{:S(2)}, u32[]{:S(2)}) async-start(f32[4,2,64,1024]{3,2,1,0:T(8,128)} %bitcast.20), calls=%async_computation.1 | async-start | bytes 4194304 | tf_op jit(solution)/shard_map/all_to_all | solution.py:231
  116.7 9.3 %across.1 = (f32[2,64,1024]{2,1,0:T(8,128)}, f32[2,64,1024]{2,1,0:T(8,128)}, f32[2,64,1024]{2,1,0:T(8,128)}, f32[2,64,1024]{2,1,0:T(8,128)}) custom-call(s32[4]{0:T(128)} %pad_add_fusion.1.meta, bf16[512,1280]{1,0:T(8,128)(2,1)} %bitcast.24, bf16[512,1280]{1,0:T(8,128)(2,1)} %bitcast.14.left_b, bf16[1280,1024]{1,0:T(8,128)(2,1)} %collective-permute-done.7.right_a.near_a, ...), custom_call_target="tpu_custom_call" | custom-call | flops 1024 | bytes 1024 | tf_op jit(solution)/shard_map/across/pallas_call | solution.py:184
  126.1 2.1 collective-permute-start.13
  128.2 2.7 %collective-permute-start.14 = (f32[2,64,1024]{2,1,0:T(8,128)}, f32[2,64,1024]{2,1,0:T(8,128)S(1)}, u32[]{:S(2)}, u32[]{:S(2)}) collective-permute-start(f32[2,64,1024]{2,1,0:T(8,128)} %get-tuple-element.51), channel_id=1, source_target_pairs={{0,4},{2,6},{4,0},{6,2},{1,5},{3,7},{5,1},{7,3},{8,12},{10,14},{12... | collective-permute-start | bytes 1572872 | tf_op jit(solution)/shard_map/ppermute | solution.py:242
  130.8 1.5 collective-permute-start.15
  132.3 12.2 %all-to-all-done.1.refs_0_.refs_1_.refs_2_.refs_3_ = f32[4,2,64,1024]{3,2,1,0:T(8,128)S(1)} async-done(((f32[4,2,64,1024]{3,2,1,0:T(8,128)}), f32[4,2,64,1024]{3,2,1,0:T(8,128)S(1)}, u32[]{:S(2)}, u32[]{:S(2)}) %all-to-all-start.1) | async-done | bytes 2097184 | tf_op jit(solution)/shard_map/all_to_all | solution.py:231
  144.5 1.4 copy-done.1
  145.8 4.2 %add.105 = (f32[64,1024]{1,0:T(8,128)}, f32[64,1024]{1,0:T(8,128)}) custom-call(s32[4]{0:T(128)} %pad_add_fusion.1.meta, f32[4,2,64,1024]{3,2,1,0:T(8,128)} %copy-done.1, f32[4,2,64,1024]{3,2,1,0:T(8,128)} %copy-done.1, f32[4,2,64,1024]{3,2,1,0:T(8,128)} %copy-done.1, f32[4,2,64,1024]{3,2,1,0:T(8,128)} %copy-done.1), custom_call_target="tpu_custom_call" | custom-call | flops 1024 | bytes 1024 | tf_op jit(solution)/shard_map/add/pallas_call | solution.py:213
  150.1 0.6 collective-permute-start.11
  150.7 6.4 %collective-permute-done.11.refs_1_ = f32[64,1024]{1,0:T(8,128)S(1)} collective-permute-done((f32[64,1024]{1,0:T(8,128)}, f32[64,1024]{1,0:T(8,128)S(1)}, u32[]{:S(2)}, u32[]{:S(2)}) %collective-permute-start.11) | collective-permute-done | bytes 262176 | tf_op jit(solution)/shard_map/ppermute | solution.py:226
  157.1 0.7 copy-done.10
  157.8 2.5 %gather.8 = (f32[64,1024]{1,0:T(8,128)}, f32[16,32,128]{2,1,0:T(8,128)}) custom-call(s32[4]{0:T(128)} %pad_add_fusion.1.meta, f32[64,1024]{1,0:T(8,128)} %get-tuple-element.47.refs_0_, f32[64,1024]{1,0:T(8,128)} %copy-done.10), custom_call_target="tpu_custom_call" | custom-call | flops 1024 | bytes 1024 | tf_op jit(solution)/shard_map/gather/pallas_call | solution.py:263
  160.3 3.5 %all-to-all-start.2 = ((f32[16,32,128]{2,1,0:T(8,128)}), f32[16,32,128]{2,1,0:T(8,128)S(1)}, u32[]{:S(2)}, u32[]{:S(2)}) async-start(f32[16,32,128]{2,1,0:T(8,128)} %get-tuple-element.49), calls=%async_computation.2 | async-start | bytes 524288 | tf_op jit(solution)/shard_map/all_to_all | solution.py:276
  163.9 2.2 %collective-permute-done.14.refs_2_ = f32[2,64,1024]{2,1,0:T(8,128)S(1)} collective-permute-done((f32[2,64,1024]{2,1,0:T(8,128)}, f32[2,64,1024]{2,1,0:T(8,128)S(1)}, u32[]{:S(2)}, u32[]{:S(2)}) %collective-permute-start.14) | collective-permute-done | bytes 524320 | tf_op jit(solution)/shard_map/ppermute | solution.py:242
  166.1 5.6 %all-to-all-done.2 = f32[16,32,128]{2,1,0:T(8,128)S(1)} async-done(((f32[16,32,128]{2,1,0:T(8,128)}), f32[16,32,128]{2,1,0:T(8,128)S(1)}, u32[]{:S(2)}, u32[]{:S(2)}) %all-to-all-start.2) | async-done | bytes 262176 | tf_op jit(solution)/shard_map/all_to_all | solution.py:276
  171.7 4.2 %add.106 = (f32[64,1024]{1,0:T(8,128)}, f32[64,1024]{1,0:T(8,128)}) custom-call(s32[4]{0:T(128)} %pad_add_fusion.1.meta, f32[2,64,1024]{2,1,0:T(8,128)} %get-tuple-element.53.refs_0_, f32[2,64,1024]{2,1,0:T(8,128)} %copy-done.7, f32[2,64,1024]{2,1,0:T(8,128)} %copy-done.8, f32[2,64,1024]{2,1,0:T(8,128)} %collective-permute-done.15.refs_3_), custom_call_target="tpu_custom_call" | custom-call | flops 1024 | bytes 1024 | tf_op jit(solution)/shard_map/add/pallas_call | solution.py:213
  175.9 0.5 collective-permute-start.16
  176.5 7.6 %collective-permute-done.16.refs_1_ = f32[64,1024]{1,0:T(8,128)S(1)} collective-permute-done((f32[64,1024]{1,0:T(8,128)}, f32[64,1024]{1,0:T(8,128)S(1)}, u32[]{:S(2)}, u32[]{:S(2)}) %collective-permute-start.16) | collective-permute-done | bytes 262176 | tf_op jit(solution)/shard_map/ppermute | solution.py:226
  184.1 0.7 copy-done.9
  184.8 2.6 %gather.9 = (f32[64,1024]{1,0:T(8,128)}, f32[16,32,128]{2,1,0:T(8,128)}) custom-call(s32[4]{0:T(128)} %pad_add_fusion.1.meta, f32[64,1024]{1,0:T(8,128)} %get-tuple-element.57.refs_0_, f32[64,1024]{1,0:T(8,128)} %copy-done.9), custom_call_target="tpu_custom_call" | custom-call | flops 1024 | bytes 1024 | tf_op jit(solution)/shard_map/gather/pallas_call | solution.py:263
  187.3 3.5 %all-to-all-start.3 = ((f32[16,32,128]{2,1,0:T(8,128)}), f32[16,32,128]{2,1,0:T(8,128)S(1)}, u32[]{:S(2)}, u32[]{:S(2)}) async-start(f32[16,32,128]{2,1,0:T(8,128)} %get-tuple-element.59), calls=%async_computation.3 | async-start | bytes 524288 | tf_op jit(solution)/shard_map/all_to_all | solution.py:276
  190.9 0.6 dynamic_slice.3
  191.5 0.6 gather_fusion
  192.1 1.9 collective-permute-start.19
  194.1 3.8 %collective-permute-start.12 = (f32[512,128]{1,0:T(8,128)S(1)}, f32[512,128]{1,0:T(8,128)S(1)}, u32[]{:S(2)}, u32[]{:S(2)}) collective-permute-start(f32[512,128]{1,0:T(8,128)S(1)} %bitcast.27), channel_id=1, source_target_pairs={{0,32},{32,64},{64,96},{96,128},{128,160},{160,192},{192,224},{48,... | collective-permute-start | bytes 786440 | tf_op jit(solution)/shard_map/ppermute | solution.py:366
  197.9 1.1 collective-permute-start.18
  199.0 4.1 %collective-permute-start.17 = (f32[512,128]{1,0:T(8,128)S(1)}, f32[512,128]{1,0:T(8,128)S(1)}, u32[]{:S(2)}, u32[]{:S(2)}) collective-permute-start(f32[512,128]{1,0:T(8,128)S(1)} %bitcast.25), channel_id=1, source_target_pairs={{0,32},{32,64},{64,96},{96,128},{128,160},{160,192},{192,224},{1,3... | collective-permute-start | bytes 786440 | tf_op jit(solution)/shard_map/ppermute | solution.py:370
  203.0 0.7 and_convert_fusion
  203.7 0.7 pad_add_fusion.flags
  204.4 0.6 collective-permute-done.12.far
  205.0 5.4 %collective-permute-done.18.beside = f32[64,1024]{1,0:T(8,128)S(1)} collective-permute-done((f32[64,1024]{1,0:T(8,128)}, f32[64,1024]{1,0:T(8,128)S(1)}, u32[]{:S(2)}, u32[]{:S(2)}) %collective-permute-start.18) | collective-permute-done | bytes 262176 | tf_op jit(solution)/shard_map/ppermute | solution.py:369
  210.5 0.7 copy-done.13
  211.2 0.1 copy-done.14
  211.3 3.9 %assemble.1 = f32[64,5120]{1,0:T(8,128)} custom-call(s32[6]{0:T(128)} %pad_add_fusion.flags, f32[512,128]{1,0:T(8,128)} %copy-done.12, f32[512,128]{1,0:T(8,128)} %copy-done.14, f32[512,128]{1,0:T(8,128)} %bitcast.26, f32[64,1024]{1,0:T(8,128)} %get-tuple-element.60.rows2, f32[64,1024]{1,0:T(8,128)} %copy-done.13, f32[64,1024]{1,0:T(8,128)} %get-tuple-element.39.rows0_a, ...), custom_call_target="tpu_custom_call" | custom-call | flops 1024 | bytes 1024 | tf_op jit(solution)/shard_map/assemble/pallas_call | solution.py:304
  (40 shorter events, 0.2 us)
Async XLA Ops:
  4.7 3.8 %collective-permute-start.1 = (f32[3,1024]{1,0:T(4,128)S(1)}, f32[3,1024]{1,0:T(4,128)S(1)}, u32[]{:S(2)}, u32[]{:S(2)}) collective-permute-start(f32[3,1024]{1,0:T(4,128)S(1)} %pad_maximum_fusion), channel_id=1, source_target_pairs={{0,8},{1,9},{8,0},{9,1},{2,10},{3,11},{10,2},{11,3},{4,12},{5,13},... | collective-permute-start | bytes 36872 | tf_op jit(solution)/shard_map/ppermute | solution.py:33
  6.3 3.2 %collective-permute-start.2 = (f32[3,1024]{1,0:T(4,128)S(1)}, f32[3,1024]{1,0:T(4,128)S(1)}, u32[]{:S(2)}, u32[]{:S(2)}) collective-permute-start(f32[3,1024]{1,0:T(4,128)S(1)} %pad_maximum_fusion), channel_id=1, source_target_pairs={{0,9},{1,8},{8,1},{9,0},{2,11},{3,10},{10,3},{11,2},{4,13},{5,12},... | collective-permute-start | bytes 36872 | tf_op jit(solution)/shard_map/ppermute | solution.py:33
  6.3 3.2 %collective-permute-start = (f32[3,1024]{1,0:T(4,128)S(1)}, f32[3,1024]{1,0:T(4,128)S(1)}, u32[]{:S(2)}, u32[]{:S(2)}) collective-permute-start(f32[3,1024]{1,0:T(4,128)S(1)} %pad_maximum_fusion), channel_id=1, source_target_pairs={{0,1},{1,0},{8,9},{9,8},{2,3},{3,2},{10,11},{11,10},{4,5},{5,4},{1... | collective-permute-start | bytes 36872 | tf_op jit(solution)/shard_map/ppermute | solution.py:33
  9.5 5.2 %collective-permute-start.5 = (f32[3,1024]{1,0:T(4,128)S(1)}, f32[3,1024]{1,0:T(4,128)S(1)}, u32[]{:S(2)}, u32[]{:S(2)}) collective-permute-start(f32[3,1024]{1,0:T(4,128)S(1)} %add_add_fusion.1), channel_id=1, source_target_pairs={{0,6},{2,0},{4,2},{6,4},{1,7},{3,1},{5,3},{7,5},{8,14},{10,8},{12,... | collective-permute-start | bytes 36872 | tf_op jit(solution)/shard_map/ppermute | solution.py:37
  12.4 5.2 %collective-permute-start.4 = (f32[3,1024]{1,0:T(4,128)S(1)}, f32[3,1024]{1,0:T(4,128)S(1)}, u32[]{:S(2)}, u32[]{:S(2)}) collective-permute-start(f32[3,1024]{1,0:T(4,128)S(1)} %add_add_fusion.1), channel_id=1, source_target_pairs={{0,4},{2,6},{4,0},{6,2},{1,5},{3,7},{5,1},{7,3},{8,12},{10,14},{12... | collective-permute-start | bytes 36872 | tf_op jit(solution)/shard_map/ppermute | solution.py:37
  13.2 4.9 %collective-permute-start.3 = (f32[3,1024]{1,0:T(4,128)S(1)}, f32[3,1024]{1,0:T(4,128)S(1)}, u32[]{:S(2)}, u32[]{:S(2)}) collective-permute-start(f32[3,1024]{1,0:T(4,128)S(1)} %add_add_fusion.1), channel_id=1, source_target_pairs={{0,2},{2,4},{4,6},{6,0},{1,3},{3,5},{5,7},{7,1},{8,10},{10,12},{12... | collective-permute-start | bytes 36872 | tf_op jit(solution)/shard_map/ppermute | solution.py:37
  27.2 5.1 %collective-permute-start.6 = (bf16[1280,1024]{1,0:T(8,128)(2,1)}, bf16[1280,1024]{1,0:T(8,128)(2,1)S(1)}, u32[]{:S(2)}, u32[]{:S(2)}) collective-permute-start(bf16[1280,1024]{1,0:T(8,128)(2,1)} %get-tuple-element.35.right_a.zed_a), channel_id=1, source_target_pairs={{0,1},{1,0},{2,3},{3,2},{4,5},{5,4},{6,7},{7,6},{8,9},{9,8},{10,11... | collective-permute-start | bytes 7864328 | tf_op jit(solution)/shard_map/ppermute | solution.py:353
  27.2 32.9 %collective-permute-start.8 = (bf16[8,64,1280]{2,1,0:T(8,128)(2,1)}, bf16[8,64,1280]{2,1,0:T(8,128)(2,1)S(1)}, u32[]{:S(2)}, u32[]{:S(2)}) collective-permute-start(bf16[8,64,1280]{2,1,0:T(8,128)(2,1)} %get-tuple-element.34), channel_id=1, source_target_pairs={{0,16},{16,0},{32,48},{48,32},{64,80},{80,64},{96,112},{112,96},{1... | collective-permute-start | bytes 3932168 | tf_op jit(solution)/shard_map/ppermute | solution.py:351
  30.1 68.4 %collective-permute-start.7 = (bf16[1280,1024]{1,0:T(8,128)(2,1)}, bf16[1280,1024]{1,0:T(8,128)(2,1)}, u32[]{:S(2)}, u32[]{:S(2)}) collective-permute-start(bf16[1280,1024]{1,0:T(8,128)(2,1)} %get-tuple-element.35.right_a.zed_a), channel_id=1, source_target_pairs={{32,0},{64,32},{96,64},{128,96},{160,128},{192,160},{224,192},{16,... | collective-permute-start | bytes 7864328 | tf_op jit(solution)/shard_map/ppermute | solution.py:350
  32.3 1.5 copy-start.3
  48.3 44.6 %all-to-all-start = ((f32[4,2,64,1024]{3,2,1,0:T(8,128)}), f32[4,2,64,1024]{3,2,1,0:T(8,128)S(1)}, u32[]{:S(2)}, u32[]{:S(2)}) async-start(f32[4,2,64,1024]{3,2,1,0:T(8,128)} %bitcast.21), calls=%async_computation | async-start | bytes 4194304 | tf_op jit(solution)/shard_map/all_to_all | solution.py:231
  60.1 53.1 %copy-start.5 = (bf16[8,64,1280]{2,1,0:T(8,128)(2,1)}, bf16[8,64,1280]{2,1,0:T(8,128)(2,1)S(1)}, u32[]{:S(2)}) copy-start(bf16[8,64,1280]{2,1,0:T(8,128)(2,1)S(1)} %collective-permute-done.8) | copy-start | bytes 3932164
  60.1 32.8 %collective-permute-start.9 = (bf16[8,64,1280]{2,1,0:T(8,128)(2,1)}, bf16[8,64,1280]{2,1,0:T(8,128)(2,1)}, u32[]{:S(2)}, u32[]{:S(2)}) collective-permute-start(bf16[8,64,1280]{2,1,0:T(8,128)(2,1)} %get-tuple-element.37), channel_id=1, source_target_pairs={{0,17},{1,16},{16,1},{17,0},{2,19},{3,18},{18,3},{19,2},{4,21},{5,... | collective-permute-start | bytes 3932168 | tf_op jit(solution)/shard_map/ppermute | solution.py:352
  92.9 1.4 copy-start.2
  98.5 5.2 %collective-permute-start.10 = (bf16[1280,1024]{1,0:T(8,128)(2,1)}, bf16[1280,1024]{1,0:T(8,128)(2,1)S(1)}, u32[]{:S(2)}, u32[]{:S(2)}) collective-permute-start(bf16[1280,1024]{1,0:T(8,128)(2,1)} %collective-permute-done.7.right_a.near_a), channel_id=1, source_target_pairs={{0,1},{1,0},{2,3},{3,2},{4,5},{5,4},{6,7},{7,6},{8,9},{9,8},{10,11... | collective-permute-start | bytes 7864328 | tf_op jit(solution)/shard_map/ppermute | solution.py:353
  103.7 1.6 copy-start.4
  113.1 31.3 %all-to-all-start.1 = ((f32[4,2,64,1024]{3,2,1,0:T(8,128)}), f32[4,2,64,1024]{3,2,1,0:T(8,128)S(1)}, u32[]{:S(2)}, u32[]{:S(2)}) async-start(f32[4,2,64,1024]{3,2,1,0:T(8,128)} %bitcast.20), calls=%async_computation.1 | async-start | bytes 4194304 | tf_op jit(solution)/shard_map/all_to_all | solution.py:231
  126.1 37.8 %collective-permute-start.13 = (f32[2,64,1024]{2,1,0:T(8,128)}, f32[2,64,1024]{2,1,0:T(8,128)S(1)}, u32[]{:S(2)}, u32[]{:S(2)}) collective-permute-start(f32[2,64,1024]{2,1,0:T(8,128)} %get-tuple-element.50), channel_id=1, source_target_pairs={{0,2},{2,4},{4,6},{6,0},{1,3},{3,5},{5,7},{7,1},{8,10},{10,12},{12... | collective-permute-start | bytes 1572872 | tf_op jit(solution)/shard_map/ppermute | solution.py:242
  128.2 38.0 %collective-permute-start.14 = (f32[2,64,1024]{2,1,0:T(8,128)}, f32[2,64,1024]{2,1,0:T(8,128)S(1)}, u32[]{:S(2)}, u32[]{:S(2)}) collective-permute-start(f32[2,64,1024]{2,1,0:T(8,128)} %get-tuple-element.51), channel_id=1, source_target_pairs={{0,4},{2,6},{4,0},{6,2},{1,5},{3,7},{5,1},{7,3},{8,12},{10,14},{12... | collective-permute-start | bytes 1572872 | tf_op jit(solution)/shard_map/ppermute | solution.py:242
  130.8 35.3 %collective-permute-start.15 = (f32[2,64,1024]{2,1,0:T(8,128)}, f32[2,64,1024]{2,1,0:T(8,128)}, u32[]{:S(2)}, u32[]{:S(2)}) collective-permute-start(f32[2,64,1024]{2,1,0:T(8,128)} %get-tuple-element.52), channel_id=1, source_target_pairs={{0,6},{2,0},{4,2},{6,4},{1,7},{3,1},{5,3},{7,5},{8,14},{10,8},{12,... | collective-permute-start | bytes 1572872 | tf_op jit(solution)/shard_map/ppermute | solution.py:242
  144.5 1.4 copy-start.1
  150.1 40.8 %copy-start = (s32[16]{0:T(128)S(1)}, s32[16]{0:T(128)}, u32[]{:S(2)}) copy-start(s32[16]{0:T(128)} %param.5) | copy-start | bytes 196
  150.1 42.0 %copy-start.15 = (f32[64,1024]{1,0:T(8,128)S(1)}, f32[64,1024]{1,0:T(8,128)}, u32[]{:S(2)}) copy-start(f32[64,1024]{1,0:T(8,128)} %get-tuple-element.62) | copy-start | bytes 786436
  150.1 7.0 %collective-permute-start.11 = (f32[64,1024]{1,0:T(8,128)}, f32[64,1024]{1,0:T(8,128)S(1)}, u32[]{:S(2)}, u32[]{:S(2)}) collective-permute-start(f32[64,1024]{1,0:T(8,128)} %get-tuple-element.48), channel_id=1, source_target_pairs={{0,8},{8,0},{1,9},{9,1},{2,10},{10,2},{3,11},{11,3},{4,12},{12,4},... | collective-permute-start | bytes 786440 | tf_op jit(solution)/shard_map/ppermute | solution.py:226
  157.1 0.7 copy-start.10
  160.3 11.4 %all-to-all-start.2 = ((f32[16,32,128]{2,1,0:T(8,128)}), f32[16,32,128]{2,1,0:T(8,128)S(1)}, u32[]{:S(2)}, u32[]{:S(2)}) async-start(f32[16,32,128]{2,1,0:T(8,128)} %get-tuple-element.49), calls=%async_computation.2 | async-start | bytes 524288 | tf_op jit(solution)/shard_map/all_to_all | solution.py:276
  163.9 7.8 %copy-start.7 = (f32[2,64,1024]{2,1,0:T(8,128)}, f32[2,64,1024]{2,1,0:T(8,128)S(1)}, u32[]{:S(2)}) copy-start(f32[2,64,1024]{2,1,0:T(8,128)S(1)} %collective-permute-done.13.refs_1_) | copy-start | bytes 1572868
  166.1 5.6 %copy-start.8 = (f32[2,64,1024]{2,1,0:T(8,128)}, f32[2,64,1024]{2,1,0:T(8,128)S(1)}, u32[]{:S(2)}) copy-start(f32[2,64,1024]{2,1,0:T(8,128)S(1)} %collective-permute-done.14.refs_2_) | copy-start | bytes 1572868
  175.9 8.1 %collective-permute-start.16 = (f32[64,1024]{1,0:T(8,128)}, f32[64,1024]{1,0:T(8,128)S(1)}, u32[]{:S(2)}, u32[]{:S(2)}) collective-permute-start(f32[64,1024]{1,0:T(8,128)} %get-tuple-element.58), channel_id=1, source_target_pairs={{0,8},{8,0},{1,9},{9,1},{2,10},{10,2},{3,11},{11,3},{4,12},{12,4},... | collective-permute-start | bytes 786440 | tf_op jit(solution)/shard_map/ppermute | solution.py:226
  184.1 0.7 copy-start.9
  187.3 11.6 %all-to-all-start.3 = ((f32[16,32,128]{2,1,0:T(8,128)}), f32[16,32,128]{2,1,0:T(8,128)S(1)}, u32[]{:S(2)}, u32[]{:S(2)}) async-start(f32[16,32,128]{2,1,0:T(8,128)} %get-tuple-element.59), calls=%async_computation.3 | async-start | bytes 524288 | tf_op jit(solution)/shard_map/all_to_all | solution.py:276
  192.1 12.2 %collective-permute-start.19 = (f32[64,1024]{1,0:T(8,128)S(1)}, f32[64,1024]{1,0:T(8,128)S(1)}, u32[]{:S(2)}, u32[]{:S(2)}) collective-permute-start(f32[64,1024]{1,0:T(8,128)S(1)} %copy-done.15), channel_id=1, source_target_pairs={{0,8},{8,0},{1,9},{9,1},{2,10},{10,2},{3,11},{11,3},{4,12},{12,4},... | collective-permute-start | bytes 786440 | tf_op jit(solution)/shard_map/ppermute | solution.py:226
  194.1 11.0 %collective-permute-start.12 = (f32[512,128]{1,0:T(8,128)S(1)}, f32[512,128]{1,0:T(8,128)S(1)}, u32[]{:S(2)}, u32[]{:S(2)}) collective-permute-start(f32[512,128]{1,0:T(8,128)S(1)} %bitcast.27), channel_id=1, source_target_pairs={{0,32},{32,64},{64,96},{96,128},{128,160},{160,192},{192,224},{48,... | collective-permute-start | bytes 786440 | tf_op jit(solution)/shard_map/ppermute | solution.py:366
  197.9 12.6 %collective-permute-start.18 = (f32[64,1024]{1,0:T(8,128)}, f32[64,1024]{1,0:T(8,128)S(1)}, u32[]{:S(2)}, u32[]{:S(2)}) collective-permute-start(f32[64,1024]{1,0:T(8,128)} %get-tuple-element.61), channel_id=1, source_target_pairs={{0,16},{16,0},{32,48},{48,32},{64,80},{80,64},{96,112},{112,96},{1... | collective-permute-start | bytes 786440 | tf_op jit(solution)/shard_map/ppermute | solution.py:369
  199.0 11.5 %copy-start.6 = (f32[16,32,128]{2,1,0:T(8,128)}, f32[16,32,128]{2,1,0:T(8,128)S(1)}, u32[]{:S(2)}) copy-start(f32[16,32,128]{2,1,0:T(8,128)S(1)} %all-to-all-done.3) | copy-start | bytes 786436
  199.0 11.5 %collective-permute-start.17 = (f32[512,128]{1,0:T(8,128)S(1)}, f32[512,128]{1,0:T(8,128)S(1)}, u32[]{:S(2)}, u32[]{:S(2)}) collective-permute-start(f32[512,128]{1,0:T(8,128)S(1)} %bitcast.25), channel_id=1, source_target_pairs={{0,32},{32,64},{64,96},{96,128},{128,160},{160,192},{192,224},{1,3... | collective-permute-start | bytes 786440 | tf_op jit(solution)/shard_map/ppermute | solution.py:370
  204.4 6.1 %copy-start.11 = (f32[64,1024]{1,0:T(8,128)}, f32[64,1024]{1,0:T(8,128)S(1)}, u32[]{:S(2)}) copy-start(f32[64,1024]{1,0:T(8,128)S(1)} %collective-permute-done.19.rows0_b) | copy-start | bytes 786436
  205.0 5.5 %copy-start.12 = (f32[512,128]{1,0:T(8,128)}, f32[512,128]{1,0:T(8,128)S(1)}, u32[]{:S(2)}) copy-start(f32[512,128]{1,0:T(8,128)S(1)} %collective-permute-done.12.far) | copy-start | bytes 786436
  210.5 0.7 copy-start.13
  210.5 0.8 copy-start.14

commit v5 on v4

--- a/solution.py
+++ b/solution.py
@@ -1,3 +1,5 @@
+import functools
+
 import jax
 import jax.numpy as jnp
 from jax import lax
@@ -12,6 +14,7 @@
 SIZES = (8, 2, 2, 4, 2)
 SNP = ("z", "yh")
 SAMP = ("yl", "x", "core")
+CHIP = ("yl", "x")
 NSNP = 16
 B = 1024
 DEPTH = 1280
@@ -43,6 +46,10 @@
     return piece // 2 + 4 * (piece % 2)
 
 
+def piece_at(place, r):
+    return (place // 2 + r // 2) % 4 * 2 + (place % 2 ^ r % 2)
+
+
 def params():
     return pltpu.CompilerParams(vmem_limit_bytes=56 << 20)
 
@@ -67,11 +74,13 @@
     return jnp.dot(left, right, preferred_element_type=jnp.float32)
 
 
-def standard_kernel(meta, dosage, observed, stats, zed, kept, sent):
+def standard_kernel(meta, dosage, observed, stats, zed, zed0, zed1, kept, sent):
     weight = observed[...].astype(jnp.float32)
     values = dosage[...].astype(jnp.float32)
     z = (weight * (values - stats[0:1, :]) * stats[1:2, :]).astype(jnp.bfloat16)
     zed[...] = z
+    zed0[...] = z[:, :HALF]
+    zed1[...] = z[:, HALF:]
     turned = z.T
 
     def store(*outs):
@@ -91,12 +100,13 @@
     return pl.pallas_call(
         standard_kernel,
         name="standardize",
-        out_shape=(bf16(DEPTH, B),) + (bf16(PIECES, ROWS, DEPTH),) * 2,
+        out_shape=(bf16(DEPTH, B), bf16(DEPTH, HALF), bf16(DEPTH, HALF))
+        + (bf16(PIECES, ROWS, DEPTH),) * 2,
         grid_spec=pltpu.PrefetchScalarGridSpec(
             num_scalar_prefetch=1,
             grid=(DEPTH // rows,),
             in_specs=[block(B), block(B), whole((2, B))],
-            out_specs=(block(B), turned, turned),
+            out_specs=(block(B), block(HALF), block(HALF), turned, turned),
         ),
         compiler_params=params(),
         cost_estimate=cost(4 * DEPTH * B, 12 * DEPTH * B),
@@ -136,143 +146,146 @@
     )(meta, zed)
 
 
-def product_kernel(meta, left_a, left_b, right_a, right_b, out):
+def product_kernel(place_of, meta, left_a, left_b, right_a, right_b, *rest):
     acc = matmul(left_a[...], right_a[...]) + matmul(left_b[...], right_b[...])
-    out[...] = acc.reshape(PIECES, ROWS, STEP)
-
-
-def product(meta, left, right, name):
+    for p in range(PIECES):
+        rest[-1][place_of(p)] = acc[ROWS * p : ROWS * (p + 1)]
+
+
+def product(meta, left, right, place_of, name, first=0, before=()):
     columns = right[0].shape[1]
     block = pl.BlockSpec((DEPTH, STEP), lambda j, m: (0, j))
     return pl.pallas_call(
-        product_kernel,
+        functools.partial(product_kernel, place_of),
         name=name,
-        out_shape=f32(PIECES, ROWS, columns),
+        out_shape=f32(PIECES, ROWS, B),
         grid_spec=pltpu.PrefetchScalarGridSpec(
             num_scalar_prefetch=1,
             grid=(columns // STEP,),
-            in_specs=[whole(LEFT)] * 2 + [block] * 2,
-            out_specs=pl.BlockSpec((PIECES, ROWS, STEP), lambda j, m: (0, 0, j)),
-        ),
+            in_specs=[whole(LEFT)] * 2
+            + [block] * 2
+            + [pl.BlockSpec(memory_space=pl.ANY)] * len(before),
+            out_specs=pl.BlockSpec((PIECES, ROWS, STEP), lambda j, m: (0, 0, j + first // STEP)),
+        ),
+        input_output_aliases={5: 0} if before else {},
         compiler_params=params(),
         cost_estimate=cost(2 * DEPTH * B * columns, 4 * DEPTH * B + 4 * B * columns),
-    )(meta, *flat(*left), *right)
-
-
-def across_kernel(meta, left_a, left_b, near_a, near_b, zed_a, zed_b, *rest):
-    outs, right = rest[:4], rest[4]
+    )(meta, *flat(*left), *right, *before)
+
+
+def across_kernel(
+    meta, left_a, left_b, near0_a, near0_b, near1_a, near1_b, zed_a, zed_b, *rest
+):
+    outs, right = rest[:PIECES], rest[PIECES]
     odd = meta[1] == 1
+    early = pl.program_id(0) < HALF // STEP
 
     def take(a, b):
         right[:DEPTH] = a[...]
         right[DEPTH:] = b[...]
 
     pl.when(odd)(lambda: take(zed_a, zed_b))
-    pl.when(~odd)(lambda: take(near_a, near_b))
+    pl.when(~odd & early)(lambda: take(near0_a, near0_b))
+    pl.when(~odd & ~early)(lambda: take(near1_a, near1_b))
     acc = matmul(left_a[...], right[:DEPTH]) + matmul(left_b[...], right[DEPTH:])
     acc = acc.reshape(4, 2, ROWS, STEP)
     for x in range(4):
-
-        @pl.when(meta[3] == x)
-        def _():
-            for k in range(4):
-                outs[k][...] = acc[(x + k) % 4]
-
-
-def across_product(meta, left, near, zed):
+        for y in range(2):
+
+            @pl.when((meta[3] == x) & (meta[2] == y))
+            def _():
+                for r in range(PIECES):
+                    outs[r][...] = acc[(x + r // 2) % 4, y ^ (r % 2)]
+
+
+def across_product(meta, left, near0, near1, zed):
+    half = HALF // STEP
+    first = pl.BlockSpec((DEPTH, STEP), lambda j, m: (0, jnp.minimum(j, half - 1)))
+    second = pl.BlockSpec((DEPTH, STEP), lambda j, m: (0, jnp.maximum(j - half, 0)))
     block = pl.BlockSpec((DEPTH, STEP), lambda j, m: (0, j))
     return pl.pallas_call(
         across_kernel,
         name="across",
-        out_shape=(f32(2, ROWS, B),) * 4,
+        out_shape=(f32(ROWS, B),) * PIECES,
         grid_spec=pltpu.PrefetchScalarGridSpec(
             num_scalar_prefetch=1,
             grid=(B // STEP,),
-            in_specs=[whole(LEFT)] * 2 + [block] * 4,
-            out_specs=(pl.BlockSpec((2, ROWS, STEP), lambda j, m: (0, 0, j)),) * 4,
+            in_specs=[whole(LEFT)] * 2 + [first] * 2 + [second] * 2 + [block] * 2,
+            out_specs=(pl.BlockSpec((ROWS, STEP), lambda j, m: (0, j)),) * PIECES,
             scratch_shapes=[pltpu.VMEM((2 * DEPTH, STEP), jnp.bfloat16)],
         ),
         compiler_params=params(),
         cost_estimate=cost(2 * DEPTH * B * B, 12 * DEPTH * B + 4 * B * B),
-    )(meta, *flat(*left), *near, *zed)
+    )(meta, *flat(*left), *near0, *near1, *zed)
 
 
 def after(value, *others):
     return lax.optimization_barrier((value, *others))[0]
 
 
-def add_kernel(meta, *refs):
-    parts, (keep, send) = refs[:-2], refs[-2:]
+def add_kernel(meta, parts, keep, send):
     mine = meta[2]
     for out, half in ((keep, mine), (send, 1 - mine)):
-        out[...] = parts[0][half] + parts[1][half] + parts[2][half] + parts[3][half]
-
-
-def add(meta, parts, specs, rows, columns):
-    out = pl.BlockSpec((rows, STEP), lambda j, m: (0, j))
+        out[...] = parts[0, half] + parts[1, half] + parts[2, half] + parts[3, half]
+
+
+def fold(meta, parts, *others):
+    _, rows, columns = parts.shape
+    parts = lax.all_to_all(parts.reshape(4, 2, rows, columns), "x", 0, 0)
+    parts = after(parts, *others)
+    step = 2 * STEP
+    out = pl.BlockSpec((rows, step), lambda j, m: (0, j))
     keep, send = pl.pallas_call(
         add_kernel,
         name="add",
         out_shape=(f32(rows, columns),) * 2,
         grid_spec=pltpu.PrefetchScalarGridSpec(
             num_scalar_prefetch=1,
-            grid=(columns // STEP,),
-            in_specs=specs,
+            grid=(columns // step,),
+            in_specs=[pl.BlockSpec((4, 2, rows, step), lambda j, m: (0, 0, 0, j))],
             out_specs=(out, out),
         ),
         compiler_params=params(),
         cost_estimate=cost(6 * rows * columns, 40 * rows * columns),
-    )(meta, *parts)
+    )(meta, parts)
     return keep, lax.ppermute(send, "yl", SWAP)
 
 
-def fold(meta, parts, *others):
-    _, rows, columns = parts.shape
-    parts = lax.all_to_all(parts.reshape(4, 2, rows, columns), "x", 0, 0)
-    parts = after(parts, *others)
-    specs = [
-        pl.BlockSpec((pl.Squeezed(), 2, rows, STEP), lambda j, m, k=k: (k, 0, 0, j)) for k in range(4)
-    ]
-    return add(meta, [parts] * 4, specs, rows, columns)
-
-
-def fold_pieces(meta, parts, *others):
-    _, rows, columns = parts[0].shape
-    parts = [parts[0]] + [
-        lax.ppermute(parts[k], "x", [(i, (i + k) % 4) for i in range(4)]) for k in (1, 2, 3)
-    ]
-    parts = after(parts, *others)
-    specs = [pl.BlockSpec((2, rows, STEP), lambda j, m: (0, 0, j))] * 4
-    return add(meta, parts, specs, rows, columns)
-
-
 def gather_kernel(meta, *refs):
-    pairs, (rows, packed) = refs[:-2], refs[-2:]
-    begin = 0
-    for a, b in zip(pairs[::2], pairs[1::2]):
-        rows[:, begin : begin + a.shape[1]] = a[...] + b[...]
-        begin += a.shape[1]
-    for s in range(2 * PIECES):
-        packed[s, :, :ROWS] = rows[:TURN, ROWS * s : ROWS * (s + 1)]
-        packed[s, :, ROWS:] = rows[TURN:, ROWS * s : ROWS * (s + 1)]
-
-
-def gather(meta, *pairs):
-    flat_pairs = [t for pair in pairs for t in pair]
+    parts, (rows, packed) = refs[:-2], refs[-2:]
+    if len(parts) == 1:
+        parts = [parts[0].at[r] for r in range(PIECES)]
+    total = parts[0][...]
+    for part in parts[1:]:
+        total = total + part[...]
+    rows[...] = total
+    for s in range(2 * STEP // ROWS):
+        packed[s, :, :ROWS] = total[:TURN, ROWS * s : ROWS * (s + 1)]
+        packed[s, :, ROWS:] = total[TURN:, ROWS * s : ROWS * (s + 1)]
+
+
+def gather(meta, *parts):
+    step = 2 * STEP
     packed = (2 * PIECES, TURN, 2 * ROWS)
+    spec = lambda t: pl.BlockSpec(
+        t.shape[:-1] + (step,), lambda j, m: (0,) * (t.ndim - 1) + (j,)
+    )
     rows, packed = pl.pallas_call(
         gather_kernel,
         name="gather",
         out_shape=(f32(ROWS, B), f32(*packed)),
         grid_spec=pltpu.PrefetchScalarGridSpec(
             num_scalar_prefetch=1,
-            grid=(1,),
-            in_specs=[whole(t.shape) for t in flat_pairs],
-            out_specs=(whole((ROWS, B)), whole(packed)),
+            grid=(B // step,),
+            in_specs=[spec(t) for t in parts],
+            out_specs=(
+                pl.BlockSpec((ROWS, step), lambda j, m: (0, j)),
+                pl.BlockSpec((step // ROWS, TURN, 2 * ROWS), lambda j, m: (j, 0, 0)),
+            ),
         ),
         compiler_params=params(),
         cost_estimate=cost(ROWS * B, 16 * ROWS * B),
-    )(meta, *flat_pairs)
+    )(meta, *parts)
     return rows, lax.all_to_all(packed, SAMP, 0, 0).reshape(HALF, 2 * ROWS)
 
 
@@ -346,28 +359,38 @@
     spread = second - first * mean
     stats = jnp.stack([mean, lax.rsqrt(spread + eps * cnt)])
 
-    zed, kept, sent = standardize(meta, dosage, observed, stats)
+    zed, zed0, zed1, kept, sent = standardize(meta, dosage, observed, stats)
     along = lambda t: lax.ppermute(t, SNP, EVEN_DOWN + ODD_UP)
     across = lambda t: lax.ppermute(t, SNP, TO_OTHER)
     athwart = lambda t: lax.ppermute(t, ("yh", "core"), [(i, 3 - i) for i in range(4)])
     swap = lambda t: lax.ppermute(t, "core", SWAP)
-    other = across(kept)
-    other = (other, athwart(after(sent, other)))
-    near = along(zed)
+    other0 = across(kept)
+    near0 = along(zed0)
     zed_b = swap(zed)
     own = (kept, turn(meta, zed_b))
-    rows0 = fold(meta, product(meta, own, (zed, zed_b), "own"), other)
-    near, other = after((near, other), rows0[0])
-    near = (near, swap(near))
-    rows2 = product(meta, own, near, "along")
-    pieces = across_product(meta, after(other, rows2), near, (zed, zed_b))
-    rows2 = fold(meta, rows2, pieces[0])
-    rows2, turned2 = gather(meta, rows2)
+    rows0 = product(meta, own, (zed, zed_b), lambda p: p, "own")
+    near0, other0 = after((near0, other0), rows0)
+    other1 = athwart(after(sent, near0, other0))
+    near1 = along(after(zed1, near0, other0))
+    near0 = (near0, swap(near0))
+    rows2 = product(meta, own, near0, chip_of, "first")
+    rows0 = fold(meta, rows0, rows2)
+    near1, other1 = after((near1, other1), rows2, rows0[0])
+    near1 = (near1, swap(near1))
+    rows2 = product(meta, own, near1, chip_of, "second", HALF, (rows2,))
+    pieces = across_product(meta, (other0, other1), near0, near1, (zed, zed_b))
+    rows2 = lax.all_to_all(after(rows2, rows0[0]), CHIP, 0, 0)
+    rows2, turned2 = gather(meta, after(rows2, pieces[0]))
+    pieces = [pieces[0]] + [
+        lax.ppermute(
+            pieces[r], CHIP, [(chip_of(i), chip_of(piece_at(i, r))) for i in range(PIECES)]
+        )
+        for r in range(1, PIECES)
+    ]
+    rows1, turned1 = gather(meta, *after(pieces, turned2, rows0[1]))
     far = lax.ppermute(turned2, SNP, EVEN_UP + ODD_DOWN)
-    rows1 = fold_pieces(meta, pieces, turned2)
-    rows1, turned1 = gather(meta, rows1)
     beside = lax.ppermute(rows1, SNP, TO_OTHER)
-    near = lax.ppermute(turned1, SNP, EVEN_UP)
+    near = lax.ppermute(after(turned1, far, beside), SNP, EVEN_UP)
     flags = jnp.concatenate([kept_flags(band, mine), odd]).astype(jnp.int32)
     return assemble(flags, far, near, turned1, rows2, beside, rows0)
 

time: 217 us -> 220 us (1.014)
  starting transfers between devices: 46.5 us -> 65.4 us
  waiting for transfers between devices: 90.1 us -> 77.7 us
  Pallas kernels: 61.8 us -> 57.3 us
    ppermute x1, waiting for transfers between devices: 30.7 us -> 2.05 us  [on_device(): lax.ppermute(t, ('yh', 'core'), [(i, 3 - i) for i in range(4)])]
    ppermute x1 -> x2, waiting for transfers between devices: 0.01 us -> 20.7 us  [on_device(): along = lambda t: lax.ppermute(t, SNP, EVEN_DOWN + ODD_UP)]
    ppermute x7 -> x9, waiting for transfers between devices: 16.2 us -> 26.9 us  [the longest x1 13.8 us: fold(): return (keep, lax.ppermute(send, 'yl', SWAP))]
    all_to_all x2 -> x1, waiting for transfers between devices: 12.2 us -> 2.34 us  [fold(): parts = lax.all_to_all(parts.reshape(4, 2, rows, columns), 'x', 0, 0)]
    ppermute x7 -> x9, starting transfers between devices: 13.3 us -> 22.7 us  [the longest x7 16.8 us: on_device(): lax.ppermute(pieces[r], CHIP, [(chip_of(i), chip_of(piece_at(i, r))) for...]
    all_to_all x2, waiting for transfers between devices: 5.58 us -> 14.4 us  [gather(): return (rows, lax.all_to_all(packed, SAMP, 0, 0).reshape(HALF, 2 * ROWS))]
    pallas_call x6 -> x5, Pallas kernels: 37.7 us -> 31.3 us  [the longest x3 18.6 us: product(): pl.pallas_call(functools.partial(product_kernel, place_of), name=name, ou...]
    ppermute x1, waiting for transfers between devices: 8.11 us -> 2.62 us  [on_device(): across = lambda t: lax.ppermute(t, SNP, TO_OTHER)]
  transfers between devices with their start and end apart: 24 -> 28, of which waited for: 15 -> 15; matrix products, arithmetic and copies ran while one was open for 2% -> 1% of each run, Pallas kernels for 16% -> 18%
where the time goes in v5:
time: 220 us; the launch traced here: 218 us
  waiting for transfers between devices  77.7 us (35%)
  starting transfers between devices  65.4 us (30%)
  Pallas kernels  57.3 us (26%)
  local copies, waits for them, and re-layouts  10.2 us (5%)
  other arithmetic  7.22 us (3%)
    ppermute x2, waiting for transfers between devices, on_device(): along = lambda t: lax.ppermute(t, SNP, EVEN_DOWN + ODD_UP)  20.7 us
    pallas_call x3, Pallas kernels, product(): pl.pallas_call(functools.partial(product_kernel, place_of), name=name, ou...  18.6 us
    ppermute x7, starting transfers between devices, on_device(): lax.ppermute(pieces[r], CHIP, [(chip_of(i), chip_of(piece_at(i, r))) for...  16.8 us
    all_to_all x2, waiting for transfers between devices, gather(): return (rows, lax.all_to_all(packed, SAMP, 0, 0).reshape(HALF, 2 * ROWS))  14.4 us
    ppermute x1, waiting for transfers between devices, fold(): return (keep, lax.ppermute(send, 'yl', SWAP))  13.8 us
    pallas_call x1, Pallas kernels, across_product(): pl.pallas_call(across_kernel, name='across', out_shape=(f32(ROWS, B),) *...  9.75 us
    pallas_call x1, Pallas kernels, standardize(): pl.pallas_call(standard_kernel, name='standardize', out_shape=(bf16(DEPTH...  9.27 us
    unnamed x38, local copies, waits for them, and re-layouts  9.01 us
  transfers between devices with their start and end apart: 28, of which 15 were waited for; matrix products, arithmetic and copies ran while one was open for 1% of the time, Pallas kernels for 18%

profile of v5, /device:TPU:64, one launch (start us, length us, event | category | flops | bytes accessed | tf_op | source)
XLA Modules:
  0.0 218.1 jit_solution(16061643955106262626)
XLA Ops:
  0.0 4.7 %fusion.1 = (f32[1024]{0:T(1024)S(1)}, f32[1024]{0:T(1024)S(1)}, f32[1024]{0:T(1024)S(1)}) fusion(bf16[1280,1024]{1,0:T(8,128)(2,1)} %dosage.1, s32[1280,1024]{1,0:T(8,128)} %observed.1), kind=kLoop, calls=%fused_computation.5 | loop fusion | flops 9171968 | bytes 7876608 | tf_op jit(solution)/shard_map/reduce_sum | solution.py:353
  4.7 1.7 collective-permute-start.1
  6.3 0.6 collective-permute-start
  6.9 1.6 collective-permute-done.1
  8.5 1.0 collective-permute-done.2
  9.5 2.8 %collective-permute-start.5 = (f32[3,1024]{1,0:T(4,128)S(1)}, f32[3,1024]{1,0:T(4,128)S(1)}, u32[]{:S(2)}, u32[]{:S(2)}) collective-permute-start(f32[3,1024]{1,0:T(4,128)S(1)} %add_add_fusion.1), channel_id=1, source_target_pairs={{0,6},{2,0},{4,2},{6,4},{1,7},{3,1},{5,3},{7,5},{8,14},{10,8},{12,... | collective-permute-start | bytes 36872 | tf_op jit(solution)/shard_map/ppermute | solution.py:40
  12.4 0.8 collective-permute-start.4
  13.2 0.9 collective-permute-start.3
  14.1 0.6 pad_add_fusion.1.meta
  14.7 2.9 %collective-permute-done.4 = f32[3,1024]{1,0:T(4,128)S(1)} collective-permute-done((f32[3,1024]{1,0:T(4,128)S(1)}, f32[3,1024]{1,0:T(4,128)S(1)}, u32[]{:S(2)}, u32[]{:S(2)}) %collective-permute-start.4) | collective-permute-done | bytes 12320 | tf_op jit(solution)/shard_map/ppermute | solution.py:40
  17.6 0.5 collective-permute-done.3
  18.2 0.6 pad_maximum_fusion.1.stats
  18.8 9.3 %standardize.1 = (bf16[1280,1024]{1,0:T(8,128)(2,1)}, bf16[1280,512]{1,0:T(8,128)(2,1)}, bf16[1280,512]{1,0:T(8,128)(2,1)}, bf16[8,64,1280]{2,1,0:T(8,128)(2,1)}, bf16[8,64,1280]{2,1,0:T(8,128)(2,1)}) custom-call(s32[4]{0:T(128)} %pad_add_fusion.1.meta, bf16[1280,1024]{1,0:T(8,128)(2,1)} %dosage.1, s32[1280,1024]{1,0:T(8,128)} %observed.1, ...), custom_call_target="tpu_custom_call" | custom-call | flops 1024 | bytes 1024 | tf_op jit(solution)/shard_map/standardize/pallas_call | solution.py:100
  28.1 2.0 collective-permute-start.7
  30.1 4.8 %collective-permute-start.8 = (bf16[8,64,1280]{2,1,0:T(8,128)(2,1)}, bf16[8,64,1280]{2,1,0:T(8,128)(2,1)S(1)}, u32[]{:S(2)}, u32[]{:S(2)}) collective-permute-start(bf16[8,64,1280]{2,1,0:T(8,128)(2,1)} %get-tuple-element.42), channel_id=1, source_target_pairs={{0,16},{16,0},{32,48},{48,32},{64,80},{80,64},{96,112},{112,96},{1... | collective-permute-start | bytes 3932168 | tf_op jit(solution)/shard_map/ppermute | solution.py:364
  34.9 1.5 copy-done.1
  36.4 6.7 %turn.1 = bf16[8,64,1280]{2,1,0:T(8,128)(2,1)} custom-call(s32[4]{0:T(128)} %pad_add_fusion.1.meta, bf16[1280,1024]{1,0:T(8,128)(2,1)} %copy-done.1), custom_call_target="tpu_custom_call" | custom-call | flops 1024 | bytes 1024 | tf_op jit(solution)/shard_map/turn/pallas_call | solution.py:134
  43.1 7.8 %own.1 = f32[8,64,1024]{2,1,0:T(8,128)} custom-call(s32[4]{0:T(128)} %pad_add_fusion.1.meta, bf16[512,1280]{1,0:T(8,128)(2,1)} %bitcast.20, bf16[512,1280]{1,0:T(8,128)(2,1)} %bitcast.17, bf16[1280,1024]{1,0:T(8,128)(2,1)} %get-tuple-element.43.right_a.zed_a, bf16[1280,1024]{1,0:T(8,128)(2,1)} %copy-done.1), custom_call_target="tpu_custom_call" | custom-call | flops 1024 | bytes 1024 | tf_op jit(solution)/shard_map/own/pallas_call | solution.py:158
  50.9 3.6 %all-to-all-start = ((f32[4,2,64,1024]{3,2,1,0:T(8,128)}), f32[4,2,64,1024]{3,2,1,0:T(8,128)S(1)}, u32[]{:S(2)}, u32[]{:S(2)}) async-start(f32[4,2,64,1024]{3,2,1,0:T(8,128)} %bitcast.23), calls=%async_computation | async-start | bytes 4194304 | tf_op jit(solution)/shard_map/all_to_all | solution.py:234
  54.5 7.1 %collective-permute-done.7.right_a.near0_a = bf16[1280,512]{1,0:T(8,128)(2,1)} collective-permute-done((bf16[1280,512]{1,0:T(8,128)(2,1)}, bf16[1280,512]{1,0:T(8,128)(2,1)}, u32[]{:S(2)}, u32[]{:S(2)}) %collective-permute-start.7) | collective-permute-done | bytes 1310752 | tf_op jit(solution)/shard_map/ppermute | solution.py:363
  61.6 2.6 %collective-permute-done.8 = bf16[8,64,1280]{2,1,0:T(8,128)(2,1)S(1)} collective-permute-done((bf16[8,64,1280]{2,1,0:T(8,128)(2,1)}, bf16[8,64,1280]{2,1,0:T(8,128)(2,1)S(1)}, u32[]{:S(2)}, u32[]{:S(2)}) %collective-permute-start.8) | collective-permute-done | bytes 1310752 | tf_op jit(solution)/shard_map/ppermute | solution.py:364
  64.2 1.1 copy-done.7
  65.3 2.0 collective-permute-start.9
  67.4 5.1 %collective-permute-start.10 = (bf16[8,64,1280]{2,1,0:T(8,128)(2,1)}, bf16[8,64,1280]{2,1,0:T(8,128)(2,1)}, u32[]{:S(2)}, u32[]{:S(2)}) collective-permute-start(bf16[8,64,1280]{2,1,0:T(8,128)(2,1)} %get-tuple-element.50), channel_id=1, source_target_pairs={{0,17},{1,16},{16,1},{17,0},{2,19},{3,18},{18,3},{19,2},{4,21},{5,... | collective-permute-start | bytes 3932168 | tf_op jit(solution)/shard_map/ppermute | solution.py:365
  72.5 1.1 copy-done.6
  73.5 5.3 %first.1.rest_0_ = f32[8,64,1024]{2,1,0:T(8,128)} custom-call(s32[4]{0:T(128)} %pad_add_fusion.1.meta, bf16[512,1280]{1,0:T(8,128)(2,1)} %bitcast.21, bf16[512,1280]{1,0:T(8,128)(2,1)} %bitcast.18, bf16[1280,512]{1,0:T(8,128)(2,1)} %collective-permute-done.7.right_a.near0_a, bf16[1280,512]{1,0:T(8,128)(2,1)} %copy-done.6), custom_call_target="tpu_custom_call" | custom-call | flops 1024 | bytes 1024 | tf_op jit(solution)/shard_map/first/pallas_call | solution.py:158
  78.9 2.3 %all-to-all-done.parts = f32[4,2,64,1024]{3,2,1,0:T(8,128)S(1)} async-done(((f32[4,2,64,1024]{3,2,1,0:T(8,128)}), f32[4,2,64,1024]{3,2,1,0:T(8,128)S(1)}, u32[]{:S(2)}, u32[]{:S(2)}) %all-to-all-start) | async-done | bytes 2097184 | tf_op jit(solution)/shard_map/all_to_all | solution.py:234
  81.2 1.4 copy-done.3
  82.6 3.0 %add.102 = (f32[64,1024]{1,0:T(8,128)}, f32[64,1024]{1,0:T(8,128)}) custom-call(s32[4]{0:T(128)} %pad_add_fusion.1.meta, f32[4,2,64,1024]{3,2,1,0:T(8,128)} %copy-done.3), custom_call_target="tpu_custom_call" | custom-call | flops 1024 | bytes 1024 | tf_op jit(solution)/shard_map/add/pallas_call | solution.py:238
  85.6 13.6 %collective-permute-done.9.right_a.near1_a = bf16[1280,512]{1,0:T(8,128)(2,1)S(1)} collective-permute-done((bf16[1280,512]{1,0:T(8,128)(2,1)}, bf16[1280,512]{1,0:T(8,128)(2,1)S(1)}, u32[]{:S(2)}, u32[]{:S(2)}) %collective-permute-start.9) | collective-permute-done | bytes 1310752 | tf_op jit(solution)/shard_map/ppermute | solution.py:363
  99.2 2.0 collective-permute-done.10
  101.3 0.8 collective-permute-start.12
  102.0 2.7 %collective-permute-done.12.right_b.near1_b = bf16[1280,512]{1,0:T(8,128)(2,1)S(1)} collective-permute-done((bf16[1280,512]{1,0:T(8,128)(2,1)S(1)}, bf16[1280,512]{1,0:T(8,128)(2,1)S(1)}, u32[]{:S(2)}, u32[]{:S(2)}) %collective-permute-start.12) | collective-permute-done | bytes 1310752 | tf_op jit(solution)/shard_map/ppermute | solution.py:366
  104.7 1.1 copy-done.5
  105.9 5.4 %second.1 = f32[8,64,1024]{2,1,0:T(8,128)} custom-call(s32[4]{0:T(128)} %pad_add_fusion.1.meta, bf16[512,1280]{1,0:T(8,128)(2,1)} %bitcast.22, bf16[512,1280]{1,0:T(8,128)(2,1)} %bitcast.19, bf16[1280,512]{1,0:T(8,128)(2,1)} %copy-done.4, bf16[1280,512]{1,0:T(8,128)(2,1)} %copy-done.5, f32[8,64,1024]{2,1,0:T(8,128)} %first.1.rest_0_), custom_call_target="tpu_custom_call", output_to_operand_aliasing={{}: (5, {})} | custom-call | flops 1024 | bytes 1024 | tf_op jit(solution)/shard_map/second/pallas_call | solution.py:158
  111.3 3.7 %all-to-all-start.1 = ((f32[8,64,1024]{2,1,0:T(8,128)}), f32[8,64,1024]{2,1,0:T(8,128)S(1)}, u32[]{:S(2)}, u32[]{:S(2)}) async-start(f32[8,64,1024]{2,1,0:T(8,128)} %second.1), calls=%async_computation.1 | async-start | bytes 4194304 | tf_op jit(solution)/shard_map/all_to_all | solution.py:382
  115.0 1.9 collective-permute-start.21
  117.0 9.8 %across.1 = (f32[64,1024]{1,0:T(8,128)}, f32[64,1024]{1,0:T(8,128)}, f32[64,1024]{1,0:T(8,128)}, f32[64,1024]{1,0:T(8,128)}, f32[64,1024]{1,0:T(8,128)}, /*index...) custom-call(s32[4]{0:T(128)} %pad_add_fusion.1.meta, bf16[512,1280]{1,0:T(8,128)(2,1)} %bitcast.24, ...), custom_call_target="tpu_custom_call" | custom-call | flops 1024 | bytes 1024 | tf_op jit(solution)/shard_map/across/pallas_call | solution.py:206
  126.7 0.5 collective-permute-start.14
  127.2 1.6 collective-permute-start.15
  128.9 2.4 %collective-permute-start.16 = (f32[64,1024]{1,0:T(8,128)}, f32[64,1024]{1,0:T(8,128)S(1)}, u32[]{:S(2)}, u32[]{:S(2)}) collective-permute-start(f32[64,1024]{1,0:T(8,128)} %get-tuple-element.61), channel_id=1, source_target_pairs={{0,10},{8,2},{2,12},{10,4},{4,14},{12,6},{6,8},{14,0},{1,11},{9,3}... | collective-permute-start | bytes 786440 | tf_op jit(solution)/shard_map/ppermute | solution.py:385
  131.3 1.7 collective-permute-start.17
  133.0 13.8 %collective-permute-done.21.rows0_b = f32[64,1024]{1,0:T(8,128)S(1)} collective-permute-done((f32[64,1024]{1,0:T(8,128)S(1)}, f32[64,1024]{1,0:T(8,128)S(1)}, u32[]{:S(2)}, u32[]{:S(2)}) %collective-permute-start.21) | collective-permute-done | bytes 262176 | tf_op jit(solution)/shard_map/ppermute | solution.py:251
  146.7 2.2 %collective-permute-start.18 = (f32[64,1024]{1,0:T(8,128)}, f32[64,1024]{1,0:T(8,128)S(1)}, u32[]{:S(2)}, u32[]{:S(2)}) collective-permute-start(f32[64,1024]{1,0:T(8,128)} %get-tuple-element.63), channel_id=1, source_target_pairs={{0,12},{8,4},{2,14},{10,6},{4,8},{12,0},{6,10},{14,2},{1,13},{9,5}... | collective-permute-start | bytes 786440 | tf_op jit(solution)/shard_map/ppermute | solution.py:385
  149.0 8.4 %collective-permute-done.14.refs_1_ = f32[64,1024]{1,0:T(8,128)S(1)} collective-permute-done((f32[64,1024]{1,0:T(8,128)}, f32[64,1024]{1,0:T(8,128)S(1)}, u32[]{:S(2)}, u32[]{:S(2)}) %collective-permute-start.14) | collective-permute-done | bytes 262176 | tf_op jit(solution)/shard_map/ppermute | solution.py:385
  157.4 8.3 %collective-permute-start.19 = (f32[64,1024]{1,0:T(8,128)}, f32[64,1024]{1,0:T(8,128)}, u32[]{:S(2)}, u32[]{:S(2)}) collective-permute-start(f32[64,1024]{1,0:T(8,128)} %get-tuple-element.64), channel_id=1, source_target_pairs={{0,6},{8,14},{2,0},{10,8},{4,2},{12,10},{6,4},{14,12},{1,7},{9,15}... | collective-permute-start | bytes 786440 | tf_op jit(solution)/shard_map/ppermute | solution.py:385
  165.8 1.3 copy-done.2
  167.2 3.0 %gather.8 = (f32[64,1024]{1,0:T(8,128)}, f32[16,32,128]{2,1,0:T(8,128)}) custom-call(s32[4]{0:T(128)} %pad_add_fusion.1.meta, f32[8,64,1024]{2,1,0:T(8,128)} %copy-done.2), custom_call_target="tpu_custom_call" | custom-call | flops 1024 | bytes 1024 | tf_op jit(solution)/shard_map/gather/pallas_call | solution.py:273
  170.2 4.4 %all-to-all-start.2 = ((f32[16,32,128]{2,1,0:T(8,128)}), f32[16,32,128]{2,1,0:T(8,128)S(1)}, u32[]{:S(2)}, u32[]{:S(2)}) async-start(f32[16,32,128]{2,1,0:T(8,128)} %get-tuple-element.58), calls=%async_computation.2 | async-start | bytes 524288 | tf_op jit(solution)/shard_map/all_to_all | solution.py:289
  174.6 7.9 %all-to-all-done.2 = f32[16,32,128]{2,1,0:T(8,128)S(1)} async-done(((f32[16,32,128]{2,1,0:T(8,128)}), f32[16,32,128]{2,1,0:T(8,128)S(1)}, u32[]{:S(2)}, u32[]{:S(2)}) %all-to-all-start.2) | async-done | bytes 262176 | tf_op jit(solution)/shard_map/all_to_all | solution.py:289
  182.5 3.0 %collective-permute-start.13 = (f32[512,128]{1,0:T(8,128)S(1)}, f32[512,128]{1,0:T(8,128)S(1)}, u32[]{:S(2)}, u32[]{:S(2)}) collective-permute-start(f32[512,128]{1,0:T(8,128)S(1)} %bitcast.27), channel_id=1, source_target_pairs={{0,32},{32,64},{64,96},{96,128},{128,160},{160,192},{192,224},{48,... | collective-permute-start | bytes 786440 | tf_op jit(solution)/shard_map/ppermute | solution.py:391
  185.6 0.6 copy-done.12
  186.3 3.1 %gather.9 = (f32[64,1024]{1,0:T(8,128)}, f32[16,32,128]{2,1,0:T(8,128)}) custom-call(s32[4]{0:T(128)} %pad_add_fusion.1.meta, f32[64,1024]{1,0:T(8,128)} %get-tuple-element.67.refs_0_, f32[64,1024]{1,0:T(8,128)} %copy-done.9, f32[64,1024]{1,0:T(8,128)} %copy-done.10, f32[64,1024]{1,0:T(8,128)} %copy-done.11, f32[64,1024]{1,0:T(8,128)} %copy-done.12, ...), custom_call_target="tpu_custom_call" | custom-call | flops 1024 | bytes 1024 | tf_op jit(solution)/shard_map/gather/pallas_call | solution.py:273
  189.4 2.9 %collective-permute-start.22 = (f32[64,1024]{1,0:T(8,128)}, f32[64,1024]{1,0:T(8,128)S(1)}, u32[]{:S(2)}, u32[]{:S(2)}) collective-permute-start(f32[64,1024]{1,0:T(8,128)} %get-tuple-element.76), channel_id=1, source_target_pairs={{0,16},{16,0},{32,48},{48,32},{64,80},{80,64},{96,112},{112,96},{1... | collective-permute-start | bytes 786440 | tf_op jit(solution)/shard_map/ppermute | solution.py:392
  192.3 3.5 %all-to-all-start.3 = ((f32[16,32,128]{2,1,0:T(8,128)}), f32[16,32,128]{2,1,0:T(8,128)S(1)}, u32[]{:S(2)}, u32[]{:S(2)}) async-start(f32[16,32,128]{2,1,0:T(8,128)} %get-tuple-element.75), calls=%async_computation.3 | async-start | bytes 524288 | tf_op jit(solution)/shard_map/all_to_all | solution.py:289
  195.9 0.6 dynamic_slice.3
  196.5 0.6 gather_fusion
  197.1 6.6 %all-to-all-done.3 = f32[16,32,128]{2,1,0:T(8,128)S(1)} async-done(((f32[16,32,128]{2,1,0:T(8,128)}), f32[16,32,128]{2,1,0:T(8,128)S(1)}, u32[]{:S(2)}, u32[]{:S(2)}) %all-to-all-start.3) | async-done | bytes 262176 | tf_op jit(solution)/shard_map/all_to_all | solution.py:289
  203.7 3.9 %collective-permute-start.23 = (f32[512,128]{1,0:T(8,128)S(1)}, f32[512,128]{1,0:T(8,128)S(1)}, u32[]{:S(2)}, u32[]{:S(2)}) collective-permute-start(f32[512,128]{1,0:T(8,128)S(1)} %bitcast.25), channel_id=1, source_target_pairs={{0,32},{32,64},{64,96},{96,128},{128,160},{160,192},{192,224},{1,3... | collective-permute-start | bytes 786440 | tf_op jit(solution)/shard_map/ppermute | solution.py:393
  207.6 0.7 and_convert_fusion
  208.3 0.6 pad_add_fusion.flags
  208.9 4.6 %collective-permute-done.23.near = f32[512,128]{1,0:T(8,128)S(1)} collective-permute-done((f32[512,128]{1,0:T(8,128)S(1)}, f32[512,128]{1,0:T(8,128)S(1)}, u32[]{:S(2)}, u32[]{:S(2)}) %collective-permute-start.23) | collective-permute-done | bytes 262176 | tf_op jit(solution)/shard_map/ppermute | solution.py:393
  213.5 0.7 copy-done.17
  214.2 3.9 %assemble.1 = f32[64,5120]{1,0:T(8,128)} custom-call(s32[6]{0:T(128)} %pad_add_fusion.flags, f32[512,128]{1,0:T(8,128)} %copy-done.15, f32[512,128]{1,0:T(8,128)} %copy-done.17, f32[512,128]{1,0:T(8,128)} %bitcast.26, f32[64,1024]{1,0:T(8,128)} %get-tuple-element.78.rows2, f32[64,1024]{1,0:T(8,128)} %copy-done.16, f32[64,1024]{1,0:T(8,128)} %get-tuple-element.52.rows0_a, ...), custom_call_target="tpu_custom_call" | custom-call | flops 1024 | bytes 1024 | tf_op jit(solution)/shard_map/assemble/pallas_call | solution.py:317
  (53 shorter events, 0.4 us)
Async XLA Ops:
  4.7 3.8 %collective-permute-start.1 = (f32[3,1024]{1,0:T(4,128)S(1)}, f32[3,1024]{1,0:T(4,128)S(1)}, u32[]{:S(2)}, u32[]{:S(2)}) collective-permute-start(f32[3,1024]{1,0:T(4,128)S(1)} %pad_maximum_fusion), channel_id=1, source_target_pairs={{0,8},{1,9},{8,0},{9,1},{2,10},{3,11},{10,2},{11,3},{4,12},{5,13},... | collective-permute-start | bytes 36872 | tf_op jit(solution)/shard_map/ppermute | solution.py:36
  6.3 3.2 %collective-permute-start.2 = (f32[3,1024]{1,0:T(4,128)S(1)}, f32[3,1024]{1,0:T(4,128)S(1)}, u32[]{:S(2)}, u32[]{:S(2)}) collective-permute-start(f32[3,1024]{1,0:T(4,128)S(1)} %pad_maximum_fusion), channel_id=1, source_target_pairs={{0,9},{1,8},{8,1},{9,0},{2,11},{3,10},{10,3},{11,2},{4,13},{5,12},... | collective-permute-start | bytes 36872 | tf_op jit(solution)/shard_map/ppermute | solution.py:36
  6.3 3.2 %collective-permute-start = (f32[3,1024]{1,0:T(4,128)S(1)}, f32[3,1024]{1,0:T(4,128)S(1)}, u32[]{:S(2)}, u32[]{:S(2)}) collective-permute-start(f32[3,1024]{1,0:T(4,128)S(1)} %pad_maximum_fusion), channel_id=1, source_target_pairs={{0,1},{1,0},{8,9},{9,8},{2,3},{3,2},{10,11},{11,10},{4,5},{5,4},{1... | collective-permute-start | bytes 36872 | tf_op jit(solution)/shard_map/ppermute | solution.py:36
  9.5 5.2 %collective-permute-start.5 = (f32[3,1024]{1,0:T(4,128)S(1)}, f32[3,1024]{1,0:T(4,128)S(1)}, u32[]{:S(2)}, u32[]{:S(2)}) collective-permute-start(f32[3,1024]{1,0:T(4,128)S(1)} %add_add_fusion.1), channel_id=1, source_target_pairs={{0,6},{2,0},{4,2},{6,4},{1,7},{3,1},{5,3},{7,5},{8,14},{10,8},{12,... | collective-permute-start | bytes 36872 | tf_op jit(solution)/shard_map/ppermute | solution.py:40
  12.4 5.2 %collective-permute-start.4 = (f32[3,1024]{1,0:T(4,128)S(1)}, f32[3,1024]{1,0:T(4,128)S(1)}, u32[]{:S(2)}, u32[]{:S(2)}) collective-permute-start(f32[3,1024]{1,0:T(4,128)S(1)} %add_add_fusion.1), channel_id=1, source_target_pairs={{0,4},{2,6},{4,0},{6,2},{1,5},{3,7},{5,1},{7,3},{8,12},{10,14},{12... | collective-permute-start | bytes 36872 | tf_op jit(solution)/shard_map/ppermute | solution.py:40
  13.2 4.9 %collective-permute-start.3 = (f32[3,1024]{1,0:T(4,128)S(1)}, f32[3,1024]{1,0:T(4,128)S(1)}, u32[]{:S(2)}, u32[]{:S(2)}) collective-permute-start(f32[3,1024]{1,0:T(4,128)S(1)} %add_add_fusion.1), channel_id=1, source_target_pairs={{0,2},{2,4},{4,6},{6,0},{1,3},{3,5},{5,7},{7,1},{8,10},{10,12},{12... | collective-permute-start | bytes 36872 | tf_op jit(solution)/shard_map/ppermute | solution.py:40
  28.0 6.8 %collective-permute-start.6 = (bf16[1280,1024]{1,0:T(8,128)(2,1)}, bf16[1280,1024]{1,0:T(8,128)(2,1)S(1)}, u32[]{:S(2)}, u32[]{:S(2)}) collective-permute-start(bf16[1280,1024]{1,0:T(8,128)(2,1)} %get-tuple-element.43.right_a.zed_a), channel_id=1, source_target_pairs={{0,1},{1,0},{2,3},{3,2},{4,5},{5,4},{6,7},{7,6},{8,9},{9,8},{10,11... | collective-permute-start | bytes 7864328 | tf_op jit(solution)/shard_map/ppermute | solution.py:366
  28.1 33.6 %collective-permute-start.7 = (bf16[1280,512]{1,0:T(8,128)(2,1)}, bf16[1280,512]{1,0:T(8,128)(2,1)}, u32[]{:S(2)}, u32[]{:S(2)}) collective-permute-start(bf16[1280,512]{1,0:T(8,128)(2,1)} %get-tuple-element.45), channel_id=1, source_target_pairs={{32,0},{64,32},{96,64},{128,96},{160,128},{192,160},{224,192},{16,... | collective-permute-start | bytes 3932168 | tf_op jit(solution)/shard_map/ppermute | solution.py:363
  30.1 34.2 %collective-permute-start.8 = (bf16[8,64,1280]{2,1,0:T(8,128)(2,1)}, bf16[8,64,1280]{2,1,0:T(8,128)(2,1)S(1)}, u32[]{:S(2)}, u32[]{:S(2)}) collective-permute-start(bf16[8,64,1280]{2,1,0:T(8,128)(2,1)} %get-tuple-element.42), channel_id=1, source_target_pairs={{0,16},{16,0},{32,48},{48,32},{64,80},{80,64},{96,112},{112,96},{1... | collective-permute-start | bytes 3932168 | tf_op jit(solution)/shard_map/ppermute | solution.py:364
  34.9 1.5 copy-start.1
  50.9 30.3 %all-to-all-start = ((f32[4,2,64,1024]{3,2,1,0:T(8,128)}), f32[4,2,64,1024]{3,2,1,0:T(8,128)S(1)}, u32[]{:S(2)}, u32[]{:S(2)}) async-start(f32[4,2,64,1024]{3,2,1,0:T(8,128)} %bitcast.23), calls=%async_computation | async-start | bytes 4194304 | tf_op jit(solution)/shard_map/all_to_all | solution.py:234
  64.2 1.1 copy-start.7
  64.2 8.2 %collective-permute-start.11 = (bf16[1280,512]{1,0:T(8,128)(2,1)}, bf16[1280,512]{1,0:T(8,128)(2,1)S(1)}, u32[]{:S(2)}, u32[]{:S(2)}) collective-permute-start(bf16[1280,512]{1,0:T(8,128)(2,1)} %collective-permute-done.7.right_a.near0_a), channel_id=1, source_target_pairs={{0,1},{1,0},{2,3},{3,2},{4,5},{5,4},{6,7},{7,6},{8,9},{9,8},{10,11... | collective-permute-start | bytes 3932168 | tf_op jit(solution)/shard_map/ppermute | solution.py:366
  65.3 33.9 %collective-permute-start.9 = (bf16[1280,512]{1,0:T(8,128)(2,1)}, bf16[1280,512]{1,0:T(8,128)(2,1)S(1)}, u32[]{:S(2)}, u32[]{:S(2)}) collective-permute-start(bf16[1280,512]{1,0:T(8,128)(2,1)} %get-tuple-element.48), channel_id=1, source_target_pairs={{32,0},{64,32},{96,64},{128,96},{160,128},{192,160},{224,192},{16,... | collective-permute-start | bytes 3932168 | tf_op jit(solution)/shard_map/ppermute | solution.py:363
  67.4 33.9 %collective-permute-start.10 = (bf16[8,64,1280]{2,1,0:T(8,128)(2,1)}, bf16[8,64,1280]{2,1,0:T(8,128)(2,1)}, u32[]{:S(2)}, u32[]{:S(2)}) collective-permute-start(bf16[8,64,1280]{2,1,0:T(8,128)(2,1)} %get-tuple-element.50), channel_id=1, source_target_pairs={{0,17},{1,16},{16,1},{17,0},{2,19},{3,18},{18,3},{19,2},{4,21},{5,... | collective-permute-start | bytes 3932168 | tf_op jit(solution)/shard_map/ppermute | solution.py:365
  72.4 1.1 copy-start.6
  81.2 1.4 copy-start.3
  99.2 5.5 %copy-start.4 = (bf16[1280,512]{1,0:T(8,128)(2,1)}, bf16[1280,512]{1,0:T(8,128)(2,1)S(1)}, u32[]{:S(2)}) copy-start(bf16[1280,512]{1,0:T(8,128)(2,1)S(1)} %collective-permute-done.9.right_a.near1_a) | copy-start | bytes 3932164
  101.3 3.4 %collective-permute-start.12 = (bf16[1280,512]{1,0:T(8,128)(2,1)S(1)}, bf16[1280,512]{1,0:T(8,128)(2,1)S(1)}, u32[]{:S(2)}, u32[]{:S(2)}) collective-permute-start(bf16[1280,512]{1,0:T(8,128)(2,1)S(1)} %collective-permute-done.9.right_a.near1_a), channel_id=1, source_target_pairs={{0,1},{1,0},{2,3},{3,2},{4,5},{5,4},{6,7},{7,6},{8,9},{9,8},{10,11... | collective-permute-start | bytes 3932168 | tf_op jit(solution)/shard_map/ppermute | solution.py:366
  104.7 1.1 copy-start.5
  111.3 3.7 %copy-start.18 = (f32[64,1024]{1,0:T(8,128)S(1)}, f32[64,1024]{1,0:T(8,128)}, u32[]{:S(2)}) copy-start(f32[64,1024]{1,0:T(8,128)} %get-tuple-element.66) | copy-start | bytes 786436
  111.3 54.5 %all-to-all-start.1 = ((f32[8,64,1024]{2,1,0:T(8,128)}), f32[8,64,1024]{2,1,0:T(8,128)S(1)}, u32[]{:S(2)}, u32[]{:S(2)}) async-start(f32[8,64,1024]{2,1,0:T(8,128)} %second.1), calls=%async_computation.1 | async-start | bytes 4194304 | tf_op jit(solution)/shard_map/all_to_all | solution.py:382
  115.0 31.7 %collective-permute-start.21 = (f32[64,1024]{1,0:T(8,128)S(1)}, f32[64,1024]{1,0:T(8,128)S(1)}, u32[]{:S(2)}, u32[]{:S(2)}) collective-permute-start(f32[64,1024]{1,0:T(8,128)S(1)} %copy-done.18), channel_id=1, source_target_pairs={{0,8},{8,0},{1,9},{9,1},{2,10},{10,2},{3,11},{11,3},{4,12},{12,4},... | collective-permute-start | bytes 786440 | tf_op jit(solution)/shard_map/ppermute | solution.py:251
  126.7 30.7 %collective-permute-start.14 = (f32[64,1024]{1,0:T(8,128)}, f32[64,1024]{1,0:T(8,128)S(1)}, u32[]{:S(2)}, u32[]{:S(2)}) collective-permute-start(f32[64,1024]{1,0:T(8,128)} %get-tuple-element.59), channel_id=1, source_target_pairs={{0,8},{8,0},{2,10},{10,2},{4,12},{12,4},{6,14},{14,6},{1,9},{9,1},... | collective-permute-start | bytes 786440 | tf_op jit(solution)/shard_map/ppermute | solution.py:385
  127.2 38.5 %collective-permute-start.15 = (f32[64,1024]{1,0:T(8,128)}, f32[64,1024]{1,0:T(8,128)S(1)}, u32[]{:S(2)}, u32[]{:S(2)}) collective-permute-start(f32[64,1024]{1,0:T(8,128)} %get-tuple-element.60), channel_id=1, source_target_pairs={{0,2},{8,10},{2,4},{10,12},{4,6},{12,14},{6,0},{14,8},{1,3},{9,11}... | collective-permute-start | bytes 786440 | tf_op jit(solution)/shard_map/ppermute | solution.py:385
  128.9 45.7 %collective-permute-start.16 = (f32[64,1024]{1,0:T(8,128)}, f32[64,1024]{1,0:T(8,128)S(1)}, u32[]{:S(2)}, u32[]{:S(2)}) collective-permute-start(f32[64,1024]{1,0:T(8,128)} %get-tuple-element.61), channel_id=1, source_target_pairs={{0,10},{8,2},{2,12},{10,4},{4,14},{12,6},{6,8},{14,0},{1,11},{9,3}... | collective-permute-start | bytes 786440 | tf_op jit(solution)/shard_map/ppermute | solution.py:385
  131.3 54.3 %collective-permute-start.17 = (f32[64,1024]{1,0:T(8,128)}, f32[64,1024]{1,0:T(8,128)S(1)}, u32[]{:S(2)}, u32[]{:S(2)}) collective-permute-start(f32[64,1024]{1,0:T(8,128)} %get-tuple-element.62), channel_id=1, source_target_pairs={{0,4},{8,12},{2,6},{10,14},{4,0},{12,8},{6,2},{14,10},{1,5},{9,13}... | collective-permute-start | bytes 786440 | tf_op jit(solution)/shard_map/ppermute | solution.py:385
  146.7 19.0 %copy-start.14 = (f32[64,1024]{1,0:T(8,128)}, f32[64,1024]{1,0:T(8,128)S(1)}, u32[]{:S(2)}) copy-start(f32[64,1024]{1,0:T(8,128)S(1)} %collective-permute-done.21.rows0_b) | copy-start | bytes 786436
  146.7 38.8 %collective-permute-start.18 = (f32[64,1024]{1,0:T(8,128)}, f32[64,1024]{1,0:T(8,128)S(1)}, u32[]{:S(2)}, u32[]{:S(2)}) collective-permute-start(f32[64,1024]{1,0:T(8,128)} %get-tuple-element.63), channel_id=1, source_target_pairs={{0,12},{8,4},{2,14},{10,6},{4,8},{12,0},{6,10},{14,2},{1,13},{9,5}... | collective-permute-start | bytes 786440 | tf_op jit(solution)/shard_map/ppermute | solution.py:385
  157.4 28.2 %copy-start.9 = (f32[64,1024]{1,0:T(8,128)}, f32[64,1024]{1,0:T(8,128)S(1)}, u32[]{:S(2)}) copy-start(f32[64,1024]{1,0:T(8,128)S(1)} %collective-permute-done.14.refs_1_) | copy-start | bytes 786436
  157.4 28.1 %collective-permute-start.19 = (f32[64,1024]{1,0:T(8,128)}, f32[64,1024]{1,0:T(8,128)}, u32[]{:S(2)}, u32[]{:S(2)}) collective-permute-start(f32[64,1024]{1,0:T(8,128)} %get-tuple-element.64), channel_id=1, source_target_pairs={{0,6},{8,14},{2,0},{10,8},{4,2},{12,10},{6,4},{14,12},{1,7},{9,15}... | collective-permute-start | bytes 786440 | tf_op jit(solution)/shard_map/ppermute | solution.py:385
  165.7 19.9 %copy-start.10 = (f32[64,1024]{1,0:T(8,128)}, f32[64,1024]{1,0:T(8,128)S(1)}, u32[]{:S(2)}) copy-start(f32[64,1024]{1,0:T(8,128)S(1)} %collective-permute-done.15.refs_2_) | copy-start | bytes 786436
  165.7 19.8 %collective-permute-start.20 = (f32[64,1024]{1,0:T(8,128)}, f32[64,1024]{1,0:T(8,128)}, u32[]{:S(2)}, u32[]{:S(2)}) collective-permute-start(f32[64,1024]{1,0:T(8,128)} %get-tuple-element.65), channel_id=1, source_target_pairs={{0,14},{8,6},{2,8},{10,0},{4,10},{12,2},{6,12},{14,4},{1,15},{9,7}... | collective-permute-start | bytes 786440 | tf_op jit(solution)/shard_map/ppermute | solution.py:385
  165.8 1.3 copy-start.2
  170.2 25.7 %copy-start = (s32[16]{0:T(128)S(1)}, s32[16]{0:T(128)}, u32[]{:S(2)}) copy-start(s32[16]{0:T(128)} %param.5) | copy-start | bytes 196
  170.2 12.3 %all-to-all-start.2 = ((f32[16,32,128]{2,1,0:T(8,128)}), f32[16,32,128]{2,1,0:T(8,128)S(1)}, u32[]{:S(2)}, u32[]{:S(2)}) async-start(f32[16,32,128]{2,1,0:T(8,128)} %get-tuple-element.58), calls=%async_computation.2 | async-start | bytes 524288 | tf_op jit(solution)/shard_map/all_to_all | solution.py:289
  174.6 11.0 %copy-start.11 = (f32[64,1024]{1,0:T(8,128)}, f32[64,1024]{1,0:T(8,128)S(1)}, u32[]{:S(2)}) copy-start(f32[64,1024]{1,0:T(8,128)S(1)} %collective-permute-done.16.refs_3_) | copy-start | bytes 786436
  182.5 21.2 %collective-permute-start.13 = (f32[512,128]{1,0:T(8,128)S(1)}, f32[512,128]{1,0:T(8,128)S(1)}, u32[]{:S(2)}, u32[]{:S(2)}) collective-permute-start(f32[512,128]{1,0:T(8,128)S(1)} %bitcast.27), channel_id=1, source_target_pairs={{0,32},{32,64},{64,96},{96,128},{128,160},{160,192},{192,224},{48,... | collective-permute-start | bytes 786440 | tf_op jit(solution)/shard_map/ppermute | solution.py:391
  185.5 0.7 copy-start.12
  185.5 0.8 copy-start.13
  189.4 14.3 %collective-permute-start.22 = (f32[64,1024]{1,0:T(8,128)}, f32[64,1024]{1,0:T(8,128)S(1)}, u32[]{:S(2)}, u32[]{:S(2)}) collective-permute-start(f32[64,1024]{1,0:T(8,128)} %get-tuple-element.76), channel_id=1, source_target_pairs={{0,16},{16,0},{32,48},{48,32},{64,80},{80,64},{96,112},{112,96},{1... | collective-permute-start | bytes 786440 | tf_op jit(solution)/shard_map/ppermute | solution.py:392
  192.3 11.4 %all-to-all-start.3 = ((f32[16,32,128]{2,1,0:T(8,128)}), f32[16,32,128]{2,1,0:T(8,128)S(1)}, u32[]{:S(2)}, u32[]{:S(2)}) async-start(f32[16,32,128]{2,1,0:T(8,128)} %get-tuple-element.75), calls=%async_computation.3 | async-start | bytes 524288 | tf_op jit(solution)/shard_map/all_to_all | solution.py:289
  203.7 9.8 %copy-start.8 = (f32[16,32,128]{2,1,0:T(8,128)}, f32[16,32,128]{2,1,0:T(8,128)S(1)}, u32[]{:S(2)}) copy-start(f32[16,32,128]{2,1,0:T(8,128)S(1)} %all-to-all-done.3) | copy-start | bytes 786436
  203.7 9.8 %copy-start.15 = (f32[512,128]{1,0:T(8,128)}, f32[512,128]{1,0:T(8,128)S(1)}, u32[]{:S(2)}) copy-start(f32[512,128]{1,0:T(8,128)S(1)} %collective-permute-done.13.far) | copy-start | bytes 786436
  203.7 9.8 %copy-start.16 = (f32[64,1024]{1,0:T(8,128)}, f32[64,1024]{1,0:T(8,128)S(1)}, u32[]{:S(2)}) copy-start(f32[64,1024]{1,0:T(8,128)S(1)} %collective-permute-done.22.beside) | copy-start | bytes 786436
  203.7 9.8 %collective-permute-start.23 = (f32[512,128]{1,0:T(8,128)S(1)}, f32[512,128]{1,0:T(8,128)S(1)}, u32[]{:S(2)}, u32[]{:S(2)}) collective-permute-start(f32[512,128]{1,0:T(8,128)S(1)} %bitcast.25), channel_id=1, source_target_pairs={{0,32},{32,64},{64,96},{96,128},{128,160},{160,192},{192,224},{1,3... | collective-permute-start | bytes 786440 | tf_op jit(solution)/shard_map/ppermute | solution.py:393
  213.5 0.7 copy-start.17

commit v6 on v5

--- a/solution.py
+++ b/solution.py
@@ -1,5 +1,3 @@
-import functools
-
 import jax
 import jax.numpy as jnp
 from jax import lax
@@ -19,6 +17,8 @@
 B = 1024
 DEPTH = 1280
 HALF = B // 2
+FIRST = 768
+REST = B - FIRST
 STEP = 256
 PIECES = 8
 ROWS = 64
@@ -74,39 +74,34 @@
     return jnp.dot(left, right, preferred_element_type=jnp.float32)
 
 
-def standard_kernel(meta, dosage, observed, stats, zed, zed0, zed1, kept, sent):
+def standard_kernel(meta, dosage, observed, stats, zed, zed0, zed1, turned):
     weight = observed[...].astype(jnp.float32)
     values = dosage[...].astype(jnp.float32)
     z = (weight * (values - stats[0:1, :]) * stats[1:2, :]).astype(jnp.bfloat16)
     zed[...] = z
-    zed0[...] = z[:, :HALF]
-    zed1[...] = z[:, HALF:]
-    turned = z.T
-
-    def store(*outs):
-        for p in range(PIECES):
-            for k, out in enumerate(outs):
-                at = 2 * ROWS * chip_of(p) + ROWS * k
-                out[p] = turned[at : at + ROWS]
-
-    pl.when(meta[0] == 0)(lambda: store(kept, sent))
-    pl.when(meta[0] != 0)(lambda: store(sent, kept))
+    zed0[...] = z[:, :FIRST]
+    zed1[...] = z[:, FIRST:]
+    columns = z.T
+    for p in range(PIECES):
+        for k in range(2):
+            at = 2 * ROWS * chip_of(p) + ROWS * k
+            turned[meta[0] ^ k, p] = columns[at : at + ROWS]
 
 
 def standardize(meta, dosage, observed, stats):
     rows = 256
     block = lambda width: pl.BlockSpec((rows, width), lambda i, m: (i, 0))
-    turned = pl.BlockSpec((PIECES, ROWS, rows), lambda i, m: (0, 0, i))
+    turned = pl.BlockSpec((2, PIECES, ROWS, rows), lambda i, m: (0, 0, 0, i))
     return pl.pallas_call(
         standard_kernel,
         name="standardize",
-        out_shape=(bf16(DEPTH, B), bf16(DEPTH, HALF), bf16(DEPTH, HALF))
-        + (bf16(PIECES, ROWS, DEPTH),) * 2,
+        out_shape=(bf16(DEPTH, B), bf16(DEPTH, FIRST), bf16(DEPTH, REST))
+        + (bf16(2, PIECES, ROWS, DEPTH),),
         grid_spec=pltpu.PrefetchScalarGridSpec(
             num_scalar_prefetch=1,
             grid=(DEPTH // rows,),
             in_specs=[block(B), block(B), whole((2, B))],
-            out_specs=(block(B), block(HALF), block(HALF), turned, turned),
+            out_specs=(block(B), block(FIRST), block(REST), turned),
         ),
         compiler_params=params(),
         cost_estimate=cost(4 * DEPTH * B, 12 * DEPTH * B),
@@ -117,7 +112,7 @@
 
 
 def flat(*turned):
-    return [t.reshape(LEFT) for t in turned]
+    return [t.reshape(-1, DEPTH) for t in turned]
 
 
 def turn_kernel(meta, zed, out):
@@ -146,28 +141,61 @@
     )(meta, zed)
 
 
-def product_kernel(place_of, meta, left_a, left_b, right_a, right_b, *rest):
+def own_kernel(meta, left_a, left_b, right_a, right_b, out):
     acc = matmul(left_a[...], right_a[...]) + matmul(left_b[...], right_b[...])
-    for p in range(PIECES):
-        rest[-1][place_of(p)] = acc[ROWS * p : ROWS * (p + 1)]
-
-
-def product(meta, left, right, place_of, name, first=0, before=()):
+    out[...] = acc.reshape(PIECES, ROWS, STEP)
+
+
+def own_product(meta, left, right):
+    block = pl.BlockSpec((DEPTH, STEP), lambda j, m: (0, j))
+    return pl.pallas_call(
+        own_kernel,
+        name="own",
+        out_shape=f32(PIECES, ROWS, B),
+        grid_spec=pltpu.PrefetchScalarGridSpec(
+            num_scalar_prefetch=1,
+            grid=(B // STEP,),
+            in_specs=[whole(LEFT)] * 2 + [block] * 2,
+            out_specs=pl.BlockSpec((PIECES, ROWS, STEP), lambda j, m: (0, 0, j)),
+        ),
+        compiler_params=params(),
+        cost_estimate=cost(2 * DEPTH * B * B, 8 * DEPTH * B + 4 * B * B),
+    )(meta, *flat(*left), *right)
+
+
+def store_relative(meta, outs, acc):
+    acc = acc.reshape(4, 2, ROWS, STEP)
+    for x in range(4):
+        for y in range(2):
+
+            @pl.when((meta[3] == x) & (meta[2] == y))
+            def _():
+                for r in range(PIECES):
+                    outs[r][...] = acc[(x + r // 2) % 4, y ^ (r % 2)]
+
+
+def along_kernel(meta, left_a, left_b, right_a, right_b, *rest):
+    acc = matmul(left_a[...], right_a[...]) + matmul(left_b[...], right_b[...])
+    store_relative(meta, rest[-PIECES:], acc)
+
+
+def along_product(meta, left, right, first=0, before=()):
     columns = right[0].shape[1]
     block = pl.BlockSpec((DEPTH, STEP), lambda j, m: (0, j))
-    return pl.pallas_call(
-        functools.partial(product_kernel, place_of),
-        name=name,
-        out_shape=f32(PIECES, ROWS, B),
+    out = pl.BlockSpec((ROWS, STEP), lambda j, m: (0, j + first // STEP))
+    return pl.pallas_call(
+        along_kernel,
+        name="along",
+        out_shape=(f32(ROWS, B),) * PIECES,
         grid_spec=pltpu.PrefetchScalarGridSpec(
             num_scalar_prefetch=1,
             grid=(columns // STEP,),
             in_specs=[whole(LEFT)] * 2
             + [block] * 2
             + [pl.BlockSpec(memory_space=pl.ANY)] * len(before),
-            out_specs=pl.BlockSpec((PIECES, ROWS, STEP), lambda j, m: (0, 0, j + first // STEP)),
-        ),
-        input_output_aliases={5: 0} if before else {},
+            out_specs=(out,) * PIECES,
+        ),
+        input_output_aliases={5 + r: r for r in range(len(before))},
         compiler_params=params(),
         cost_estimate=cost(2 * DEPTH * B * columns, 4 * DEPTH * B + 4 * B * columns),
     )(meta, *flat(*left), *right, *before)
@@ -178,7 +206,7 @@
 ):
     outs, right = rest[:PIECES], rest[PIECES]
     odd = meta[1] == 1
-    early = pl.program_id(0) < HALF // STEP
+    early = pl.program_id(0) < FIRST // STEP
 
     def take(a, b):
         right[:DEPTH] = a[...]
@@ -188,18 +216,11 @@
     pl.when(~odd & early)(lambda: take(near0_a, near0_b))
     pl.when(~odd & ~early)(lambda: take(near1_a, near1_b))
     acc = matmul(left_a[...], right[:DEPTH]) + matmul(left_b[...], right[DEPTH:])
-    acc = acc.reshape(4, 2, ROWS, STEP)
-    for x in range(4):
-        for y in range(2):
-
-            @pl.when((meta[3] == x) & (meta[2] == y))
-            def _():
-                for r in range(PIECES):
-                    outs[r][...] = acc[(x + r // 2) % 4, y ^ (r % 2)]
+    store_relative(meta, outs, acc)
 
 
 def across_product(meta, left, near0, near1, zed):
-    half = HALF // STEP
+    half = FIRST // STEP
     first = pl.BlockSpec((DEPTH, STEP), lambda j, m: (0, jnp.minimum(j, half - 1)))
     second = pl.BlockSpec((DEPTH, STEP), lambda j, m: (0, jnp.maximum(j - half, 0)))
     block = pl.BlockSpec((DEPTH, STEP), lambda j, m: (0, j))
@@ -287,6 +308,11 @@
         cost_estimate=cost(ROWS * B, 16 * ROWS * B),
     )(meta, *parts)
     return rows, lax.all_to_all(packed, SAMP, 0, 0).reshape(HALF, 2 * ROWS)
+
+
+def send_pieces(pieces):
+    pairs = lambda r: [(chip_of(i), chip_of(piece_at(i, r))) for i in range(PIECES)]
+    return [pieces[0]] + [lax.ppermute(pieces[r], CHIP, pairs(r)) for r in range(1, PIECES)]
 
 
 def unpack(out, packed):
@@ -359,38 +385,30 @@
     spread = second - first * mean
     stats = jnp.stack([mean, lax.rsqrt(spread + eps * cnt)])
 
-    zed, zed0, zed1, kept, sent = standardize(meta, dosage, observed, stats)
+    zed, zed0, zed1, turned = standardize(meta, dosage, observed, stats)
     along = lambda t: lax.ppermute(t, SNP, EVEN_DOWN + ODD_UP)
-    across = lambda t: lax.ppermute(t, SNP, TO_OTHER)
-    athwart = lambda t: lax.ppermute(t, ("yh", "core"), [(i, 3 - i) for i in range(4)])
     swap = lambda t: lax.ppermute(t, "core", SWAP)
-    other0 = across(kept)
+    other = lax.ppermute(turned, SNP, TO_OTHER)
     near0 = along(zed0)
     zed_b = swap(zed)
-    own = (kept, turn(meta, zed_b))
-    rows0 = product(meta, own, (zed, zed_b), lambda p: p, "own")
-    near0, other0 = after((near0, other0), rows0)
-    other1 = athwart(after(sent, near0, other0))
-    near1 = along(after(zed1, near0, other0))
+    own = (turned, turn(meta, zed_b))
+    rows0 = own_product(meta, own, (zed, zed_b))
+    near0 = after(near0, rows0)
+    near1 = along(after(zed1, near0))
     near0 = (near0, swap(near0))
-    rows2 = product(meta, own, near0, chip_of, "first")
-    rows0 = fold(meta, rows0, rows2)
-    near1, other1 = after((near1, other1), rows2, rows0[0])
+    rows2 = along_product(meta, own, near0)
+    rows0 = fold(meta, rows0, rows2[0])
+    near1, other = after((near1, other), rows2[0], rows0[0])
     near1 = (near1, swap(near1))
-    rows2 = product(meta, own, near1, chip_of, "second", HALF, (rows2,))
-    pieces = across_product(meta, (other0, other1), near0, near1, (zed, zed_b))
-    rows2 = lax.all_to_all(after(rows2, rows0[0]), CHIP, 0, 0)
-    rows2, turned2 = gather(meta, after(rows2, pieces[0]))
-    pieces = [pieces[0]] + [
-        lax.ppermute(
-            pieces[r], CHIP, [(chip_of(i), chip_of(piece_at(i, r))) for i in range(PIECES)]
-        )
-        for r in range(1, PIECES)
-    ]
-    rows1, turned1 = gather(meta, *after(pieces, turned2, rows0[1]))
-    far = lax.ppermute(turned2, SNP, EVEN_UP + ODD_DOWN)
+    other = (other, swap(other[1]))
+    pieces = across_product(meta, other, near0, near1, (zed, zed_b))
+    near1 = after(near1, pieces[0])
+    rows2 = along_product(meta, own, near1, FIRST, rows2)
+    rows1, turned1 = gather(meta, *after(send_pieces(pieces), rows2[0]))
     beside = lax.ppermute(rows1, SNP, TO_OTHER)
-    near = lax.ppermute(after(turned1, far, beside), SNP, EVEN_UP)
+    near = lax.ppermute(turned1, SNP, EVEN_UP)
+    rows2, turned2 = gather(meta, *after(send_pieces(rows2), rows1))
+    far = lax.ppermute(after(turned2, near, beside, rows0[1]), SNP, EVEN_UP + ODD_DOWN)
     flags = jnp.concatenate([kept_flags(band, mine), odd]).astype(jnp.int32)
     return assemble(flags, far, near, turned1, rows2, beside, rows0)
 

time: 220 us -> 232 us (1.055)
  waiting for transfers between devices: 77.7 us -> 95.8 us
  starting transfers between devices: 65.4 us -> 60 us
    ppermute x11 -> x17, waiting for transfers between devices: 17.8 us -> 35.7 us  [the longest x14 30.8 us: send_pieces(): lax.ppermute(pieces[r], CHIP, pairs(r))]
    all_to_all x1, waiting for transfers between devices: 2.34 us -> 18.2 us  [fold(): parts = lax.all_to_all(parts.reshape(4, 2, rows, columns), 'x', 0, 0)]
    ppermute x1, waiting for transfers between devices: 13.8 us -> 0.01 us  [fold(): return (keep, lax.ppermute(send, 'yl', SWAP))]
    all_to_all x2, waiting for transfers between devices: 14.4 us -> 7.7 us  [gather(): return (rows, lax.all_to_all(packed, SAMP, 0, 0).reshape(HALF, 2 * ROWS))]
    ppermute x2, waiting for transfers between devices: 20.7 us -> 24.7 us  [on_device(): along = lambda t: lax.ppermute(t, SNP, EVEN_DOWN + ODD_UP)]
    all_to_all x1 -> x0, starting transfers between devices: 3.73 us -> none  [on_device(): rows2 = lax.all_to_all(after(rows2, rows0[0]), CHIP, 0, 0)]
    unnamed x38 -> x68, local copies, waits for them, and re-layouts: 9.01 us -> 6.36 us
    ppermute x11 -> x17, starting transfers between devices: 33.7 us -> 32 us  [the longest x14 18.6 us: send_pieces(): lax.ppermute(pieces[r], CHIP, pairs(r))]
  transfers between devices with their start and end apart: 28 -> 34, of which waited for: 15 -> 18; matrix products, arithmetic and copies ran while one was open for 1% -> 1% of each run, Pallas kernels for 18% -> 13%
where the time goes in v6:
time: 232 us; the launch traced here: 231 us
  waiting for transfers between devices  95.8 us (41%)
  starting transfers between devices  60 us (26%)
  Pallas kernels  58 us (25%)
  local copies, waits for them, and re-layouts  9.24 us (4%)
  other arithmetic  7.22 us (3%)
    ppermute x14, waiting for transfers between devices, send_pieces(): lax.ppermute(pieces[r], CHIP, pairs(r))  30.8 us
    ppermute x2, waiting for transfers between devices, on_device(): along = lambda t: lax.ppermute(t, SNP, EVEN_DOWN + ODD_UP)  24.7 us
    ppermute x14, starting transfers between devices, send_pieces(): lax.ppermute(pieces[r], CHIP, pairs(r))  18.6 us
    all_to_all x1, waiting for transfers between devices, fold(): parts = lax.all_to_all(parts.reshape(4, 2, rows, columns), 'x', 0, 0)  18.2 us
    pallas_call x2, Pallas kernels, along_product(): pl.pallas_call(along_kernel, name='along', out_shape=(f32(ROWS, B),) * PI...  11.7 us
    pallas_call x1, Pallas kernels, across_product(): pl.pallas_call(across_kernel, name='across', out_shape=(f32(ROWS, B),) *...  9.8 us
    all_to_all x2, starting transfers between devices, gather(): return (rows, lax.all_to_all(packed, SAMP, 0, 0).reshape(HALF, 2 * ROWS))  9.65 us
    pallas_call x1, Pallas kernels, standardize(): pl.pallas_call(standard_kernel, name='standardize', out_shape=(bf16(DEPTH...  8.94 us
  transfers between devices with their start and end apart: 34, of which 18 were waited for; matrix products, arithmetic and copies ran while one was open for 1% of the time, Pallas kernels for 13%

profile of v6, /device:TPU:64, one launch (start us, length us, event | category | flops | bytes accessed | tf_op | source)
XLA Modules:
  0.0 230.8 jit_solution(533473293761853737)
XLA Ops:
  0.0 4.7 %fusion.1 = (f32[1024]{0:T(1024)S(1)}, f32[1024]{0:T(1024)S(1)}, f32[1024]{0:T(1024)S(1)}) fusion(bf16[1280,1024]{1,0:T(8,128)(2,1)} %dosage.1, s32[1280,1024]{1,0:T(8,128)} %observed.1), kind=kLoop, calls=%fused_computation.5 | loop fusion | flops 9171968 | bytes 7876608 | tf_op jit(solution)/shard_map/reduce_sum | solution.py:379
  4.7 1.7 collective-permute-start.1
  6.9 1.6 collective-permute-done.1
  8.5 1.0 collective-permute-done.2
  9.5 2.8 %collective-permute-start.5 = (f32[3,1024]{1,0:T(4,128)S(1)}, f32[3,1024]{1,0:T(4,128)S(1)}, u32[]{:S(2)}, u32[]{:S(2)}) collective-permute-start(f32[3,1024]{1,0:T(4,128)S(1)} %add_add_fusion.1), channel_id=1, source_target_pairs={{0,6},{2,0},{4,2},{6,4},{1,7},{3,1},{5,3},{7,5},{8,14},{10,8},{12,... | collective-permute-start | bytes 36872 | tf_op jit(solution)/shard_map/ppermute | solution.py:40
  12.4 0.8 collective-permute-start.4
  13.2 0.9 collective-permute-start.3
  14.1 0.6 pad_add_fusion.1.meta
  14.7 2.9 %collective-permute-done.4 = f32[3,1024]{1,0:T(4,128)S(1)} collective-permute-done((f32[3,1024]{1,0:T(4,128)S(1)}, f32[3,1024]{1,0:T(4,128)S(1)}, u32[]{:S(2)}, u32[]{:S(2)}) %collective-permute-start.4) | collective-permute-done | bytes 12320 | tf_op jit(solution)/shard_map/ppermute | solution.py:40
  18.2 0.6 pad_maximum_fusion.1.stats
  18.8 8.9 %standardize.1 = (bf16[1280,1024]{1,0:T(8,128)(2,1)}, bf16[1280,768]{1,0:T(8,128)(2,1)}, bf16[1280,256]{1,0:T(8,128)(2,1)}, bf16[2,8,64,1280]{3,2,1,0:T(8,128)(2,1)}) custom-call(s32[4]{0:T(128)} %pad_add_fusion.1.meta, bf16[1280,1024]{1,0:T(8,128)(2,1)} %dosage.1, s32[1280,1024]{1,0:T(8,128)} %observed.1, f32[2,1024]{1,0:T(2,128)} %pad_maximum_fusion.1.stats), custom_call_target="tpu_custom_call" | custom-call | flops 1024 | bytes 1024 | tf_op jit(solution)/shard_map/standardize/pallas_call | solution.py:95
  27.7 2.0 collective-permute-start.7
  29.8 4.8 %collective-permute-start.9 = (bf16[2,8,64,1280]{3,2,1,0:T(8,128)(2,1)}, bf16[2,8,64,1280]{3,2,1,0:T(8,128)(2,1)}, u32[]{:S(2)}, u32[]{:S(2)}) collective-permute-start(bf16[2,8,64,1280]{3,2,1,0:T(8,128)(2,1)} %get-tuple-element.63), channel_id=1, source_target_pairs={{0,16},{16,0},{32,48},{48,32},{64,80},{80,64},{96,112},{112,96},{1... | collective-permute-start | bytes 7864328 | tf_op jit(solution)/shard_map/ppermute | solution.py:391
  34.6 1.5 copy-done.1
  36.1 6.7 %turn.1 = bf16[8,64,1280]{2,1,0:T(8,128)(2,1)} custom-call(s32[4]{0:T(128)} %pad_add_fusion.1.meta, bf16[1280,1024]{1,0:T(8,128)(2,1)} %copy-done.1), custom_call_target="tpu_custom_call" | custom-call | flops 1024 | bytes 1024 | tf_op jit(solution)/shard_map/turn/pallas_call | solution.py:129
  42.8 7.8 %own.1 = f32[8,64,1024]{2,1,0:T(8,128)} custom-call(s32[4]{0:T(128)} %pad_add_fusion.1.meta, bf16[1024,1280]{1,0:T(8,128)(2,1)} %bitcast.19, bf16[512,1280]{1,0:T(8,128)(2,1)} %bitcast.22, bf16[1280,1024]{1,0:T(8,128)(2,1)} %get-tuple-element.64.right_a.zed_a, bf16[1280,1024]{1,0:T(8,128)(2,1)} %copy-done.1), custom_call_target="tpu_custom_call" | custom-call | flops 1024 | bytes 1024 | tf_op jit(solution)/shard_map/own/pallas_call | solution.py:151
  50.6 24.7 %collective-permute-done.7.right_a.near0_a = bf16[1280,768]{1,0:T(8,128)(2,1)} collective-permute-done((bf16[1280,768]{1,0:T(8,128)(2,1)}, bf16[1280,768]{1,0:T(8,128)(2,1)}, u32[]{:S(2)}, u32[]{:S(2)}) %collective-permute-start.7) | collective-permute-done | bytes 1966112 | tf_op jit(solution)/shard_map/ppermute | solution.py:389
  75.3 3.6 %all-to-all-start = ((f32[4,2,64,1024]{3,2,1,0:T(8,128)}), f32[4,2,64,1024]{3,2,1,0:T(8,128)S(1)}, u32[]{:S(2)}, u32[]{:S(2)}) async-start(f32[4,2,64,1024]{3,2,1,0:T(8,128)} %bitcast.25), calls=%async_computation | async-start | bytes 4194304 | tf_op jit(solution)/shard_map/all_to_all | solution.py:255
  79.0 2.0 collective-permute-start.8
  81.0 7.0 %along.2 = (f32[64,1024]{1,0:T(8,128)}, f32[64,1024]{1,0:T(8,128)}, f32[64,1024]{1,0:T(8,128)}, f32[64,1024]{1,0:T(8,128)}, f32[64,1024]{1,0:T(8,128)}, /*index=...) custom-call(s32[4]{0:T(128)} %pad_add_fusion.1.meta, bf16[1024,1280]{1,0:T(8,128)(2,1)} %bitcast.20, ...), custom_call_target="tpu_custom_call" | custom-call | flops 1024 | bytes 1024 | tf_op jit(solution)/shard_map/along/pallas_call | solution.py:186
  88.0 18.2 %all-to-all-done.parts = f32[4,2,64,1024]{3,2,1,0:T(8,128)S(1)} async-done(((f32[4,2,64,1024]{3,2,1,0:T(8,128)}), f32[4,2,64,1024]{3,2,1,0:T(8,128)S(1)}, u32[]{:S(2)}, u32[]{:S(2)}) %all-to-all-start) | async-done | bytes 2097184 | tf_op jit(solution)/shard_map/all_to_all | solution.py:255
  106.2 1.3 copy-done.2
  107.6 3.0 %add.102 = (f32[64,1024]{1,0:T(8,128)}, f32[64,1024]{1,0:T(8,128)}) custom-call(s32[4]{0:T(128)} %pad_add_fusion.1.meta, f32[4,2,64,1024]{3,2,1,0:T(8,128)} %copy-done.2), custom_call_target="tpu_custom_call" | custom-call | flops 1024 | bytes 1024 | tf_op jit(solution)/shard_map/add/pallas_call | solution.py:259
  110.6 1.6 slice_bitcast_fusion
  112.8 3.5 %collective-permute-done.11.near1_b.right_b = bf16[1280,256]{1,0:T(8,128)(2,1)S(1)} collective-permute-done((bf16[1280,256]{1,0:T(8,128)(2,1)S(1)}, bf16[1280,256]{1,0:T(8,128)(2,1)S(1)}, u32[]{:S(2)}, u32[]{:S(2)}) %collective-permute-start.11) | collective-permute-done | bytes 655392 | tf_op jit(solution)/shard_map/ppermute | solution.py:390
  116.3 0.9 copy-done.4
  117.7 9.8 %across.1 = (f32[64,1024]{1,0:T(8,128)}, f32[64,1024]{1,0:T(8,128)}, f32[64,1024]{1,0:T(8,128)}, f32[64,1024]{1,0:T(8,128)}, f32[64,1024]{1,0:T(8,128)}, /*index...) custom-call(s32[4]{0:T(128)} %pad_add_fusion.1.meta, bf16[1024,1280]{1,0:T(8,128)(2,1)} %bitcast.12.left_a, ...), custom_call_target="tpu_custom_call" | custom-call | flops 1024 | bytes 1024 | tf_op jit(solution)/shard_map/across/pallas_call | solution.py:227
  127.5 4.7 %along.3 = (f32[64,1024]{1,0:T(8,128)}, f32[64,1024]{1,0:T(8,128)}, f32[64,1024]{1,0:T(8,128)}, f32[64,1024]{1,0:T(8,128)}, f32[64,1024]{1,0:T(8,128)}, /*index=...) custom-call(s32[4]{0:T(128)} %pad_add_fusion.1.meta, ...), custom_call_target="tpu_custom_call", output_to_operand_aliasing={{0}: (5, {}), {1}: (6, {}), {2}: (7, {}), {3}: (8, {}), {4}... | custom-call | flops 1024 | bytes 1024 | tf_op jit(solution)/shard_map/along/pallas_call | solution.py:186
  132.2 0.7 collective-permute-start.13
  133.5 1.4 collective-permute-start.20
  134.9 2.1 collective-permute-start.22
  137.0 4.6 %collective-permute-done.13.refs_1_ = f32[64,1024]{1,0:T(8,128)S(1)} collective-permute-done((f32[64,1024]{1,0:T(8,128)}, f32[64,1024]{1,0:T(8,128)S(1)}, u32[]{:S(2)}, u32[]{:S(2)}) %collective-permute-start.13) | collective-permute-done | bytes 262176 | tf_op jit(solution)/shard_map/ppermute | solution.py:315
  141.6 0.6 collective-permute-start.23
  142.2 1.3 collective-permute-done.14.refs_2_
  143.5 1.8 collective-permute-start.24
  145.3 1.1 collective-permute-done.20.refs_1_
  146.4 1.2 collective-permute-start.25
  147.6 1.5 collective-permute-done.21.refs_2_
  149.1 0.8 collective-permute-start.26
  149.9 4.7 %collective-permute-done.22.refs_3_ = f32[64,1024]{1,0:T(8,128)S(1)} collective-permute-done((f32[64,1024]{1,0:T(8,128)S(1)}, f32[64,1024]{1,0:T(8,128)S(1)}, u32[]{:S(2)}, u32[]{:S(2)}) %collective-permute-start.22) | collective-permute-done | bytes 262176 | tf_op jit(solution)/shard_map/ppermute | solution.py:315
  154.6 3.0 %collective-permute-start.15 = (f32[64,1024]{1,0:T(8,128)}, f32[64,1024]{1,0:T(8,128)S(1)}, u32[]{:S(2)}, u32[]{:S(2)}) collective-permute-start(f32[64,1024]{1,0:T(8,128)} %get-tuple-element.87), channel_id=1, source_target_pairs={{0,10},{8,2},{2,12},{10,4},{4,14},{12,6},{6,8},{14,0},{1,11},{9,3}... | collective-permute-start | bytes 786440 | tf_op jit(solution)/shard_map/ppermute | solution.py:315
  157.6 3.9 %collective-permute-done.23.refs_4_ = f32[64,1024]{1,0:T(8,128)S(1)} collective-permute-done((f32[64,1024]{1,0:T(8,128)S(1)}, f32[64,1024]{1,0:T(8,128)S(1)}, u32[]{:S(2)}, u32[]{:S(2)}) %collective-permute-start.23) | collective-permute-done | bytes 262176 | tf_op jit(solution)/shard_map/ppermute | solution.py:315
  161.5 1.3 collective-permute-start.16
  162.9 6.9 %collective-permute-done.24.refs_5_ = f32[64,1024]{1,0:T(8,128)S(1)} collective-permute-done((f32[64,1024]{1,0:T(8,128)S(1)}, f32[64,1024]{1,0:T(8,128)S(1)}, u32[]{:S(2)}, u32[]{:S(2)}) %collective-permute-start.24) | collective-permute-done | bytes 262176 | tf_op jit(solution)/shard_map/ppermute | solution.py:315
  169.8 4.0 %collective-permute-start.17 = (f32[64,1024]{1,0:T(8,128)}, f32[64,1024]{1,0:T(8,128)S(1)}, u32[]{:S(2)}, u32[]{:S(2)}) collective-permute-start(f32[64,1024]{1,0:T(8,128)} %get-tuple-element.89), channel_id=1, source_target_pairs={{0,12},{8,4},{2,14},{10,6},{4,8},{12,0},{6,10},{14,2},{1,13},{9,5}... | collective-permute-start | bytes 786440 | tf_op jit(solution)/shard_map/ppermute | solution.py:315
  173.7 1.0 collective-permute-start.19
  174.8 3.1 %gather.8 = (f32[64,1024]{1,0:T(8,128)}, f32[16,32,128]{2,1,0:T(8,128)}) custom-call(s32[4]{0:T(128)} %pad_add_fusion.1.meta, f32[64,1024]{1,0:T(8,128)} %get-tuple-element.99.refs_0_, f32[64,1024]{1,0:T(8,128)} %copy-done.11, f32[64,1024]{1,0:T(8,128)} %copy-done.12, f32[64,1024]{1,0:T(8,128)} %copy-done.14, f32[64,1024]{1,0:T(8,128)} %copy-done.16, ...), custom_call_target="tpu_custom_call" | custom-call | flops 1024 | bytes 1024 | tf_op jit(solution)/shard_map/gather/pallas_call | solution.py:294
  177.9 5.5 %all-to-all-start.2 = ((f32[16,32,128]{2,1,0:T(8,128)}), f32[16,32,128]{2,1,0:T(8,128)S(1)}, u32[]{:S(2)}, u32[]{:S(2)}) async-start(f32[16,32,128]{2,1,0:T(8,128)} %get-tuple-element.117), calls=%async_computation.2 | async-start | bytes 524288 | tf_op jit(solution)/shard_map/all_to_all | solution.py:310
  183.4 6.9 %collective-permute-done.15.refs_3_ = f32[64,1024]{1,0:T(8,128)S(1)} collective-permute-done((f32[64,1024]{1,0:T(8,128)}, f32[64,1024]{1,0:T(8,128)S(1)}, u32[]{:S(2)}, u32[]{:S(2)}) %collective-permute-start.15) | collective-permute-done | bytes 262176 | tf_op jit(solution)/shard_map/ppermute | solution.py:315
  190.5 3.2 %collective-permute-start.28 = (f32[64,1024]{1,0:T(8,128)}, f32[64,1024]{1,0:T(8,128)S(1)}, u32[]{:S(2)}, u32[]{:S(2)}) collective-permute-start(f32[64,1024]{1,0:T(8,128)} %get-tuple-element.107), channel_id=1, source_target_pairs={{0,16},{16,0},{32,48},{48,32},{64,80},{80,64},{96,112},{112,96},{1... | collective-permute-start | bytes 786440 | tf_op jit(solution)/shard_map/ppermute | solution.py:408
  193.7 1.1 all-to-all-done.2
  194.8 5.0 %collective-permute-start.27 = (f32[512,128]{1,0:T(8,128)S(1)}, f32[512,128]{1,0:T(8,128)S(1)}, u32[]{:S(2)}, u32[]{:S(2)}) collective-permute-start(f32[512,128]{1,0:T(8,128)S(1)} %bitcast.27), channel_id=1, source_target_pairs={{0,32},{32,64},{64,96},{96,128},{128,160},{160,192},{192,224},{1,3... | collective-permute-start | bytes 786440 | tf_op jit(solution)/shard_map/ppermute | solution.py:409
  199.9 0.6 copy-done.15
  200.5 0.7 copy-done.17
  201.2 3.1 %gather.9 = (f32[64,1024]{1,0:T(8,128)}, f32[16,32,128]{2,1,0:T(8,128)}) custom-call(s32[4]{0:T(128)} %pad_add_fusion.1.meta, f32[64,1024]{1,0:T(8,128)} %get-tuple-element.108.refs_0_, f32[64,1024]{1,0:T(8,128)} %copy-done.7, f32[64,1024]{1,0:T(8,128)} %copy-done.8, f32[64,1024]{1,0:T(8,128)} %copy-done.9, f32[64,1024]{1,0:T(8,128)} %copy-done.10, ...), custom_call_target="tpu_custom_call" | custom-call | flops 1024 | bytes 1024 | tf_op jit(solution)/shard_map/gather/pallas_call | solution.py:294
  204.3 4.1 %all-to-all-start.1 = ((f32[16,32,128]{2,1,0:T(8,128)}), f32[16,32,128]{2,1,0:T(8,128)S(1)}, u32[]{:S(2)}, u32[]{:S(2)}) async-start(f32[16,32,128]{2,1,0:T(8,128)} %get-tuple-element.116), calls=%async_computation.1 | async-start | bytes 524288 | tf_op jit(solution)/shard_map/all_to_all | solution.py:310
  209.0 0.6 gather_fusion
  209.7 6.6 %all-to-all-done.1 = f32[16,32,128]{2,1,0:T(8,128)S(1)} async-done(((f32[16,32,128]{2,1,0:T(8,128)}), f32[16,32,128]{2,1,0:T(8,128)S(1)}, u32[]{:S(2)}, u32[]{:S(2)}) %all-to-all-start.1) | async-done | bytes 262176 | tf_op jit(solution)/shard_map/all_to_all | solution.py:310
  216.3 3.6 %collective-permute-start.30 = (f32[512,128]{1,0:T(8,128)S(1)}, f32[512,128]{1,0:T(8,128)S(1)}, u32[]{:S(2)}, u32[]{:S(2)}) collective-permute-start(f32[512,128]{1,0:T(8,128)S(1)} %bitcast.29), channel_id=1, source_target_pairs={{0,32},{32,64},{64,96},{96,128},{128,160},{160,192},{192,224},{48,... | collective-permute-start | bytes 786440 | tf_op jit(solution)/shard_map/ppermute | solution.py:411
  220.0 0.7 and_convert_fusion
  220.6 0.6 pad_add_fusion.flags
  221.2 4.9 %collective-permute-done.30.far = f32[512,128]{1,0:T(8,128)S(1)} collective-permute-done((f32[512,128]{1,0:T(8,128)S(1)}, f32[512,128]{1,0:T(8,128)S(1)}, u32[]{:S(2)}, u32[]{:S(2)}) %collective-permute-start.30) | collective-permute-done | bytes 262176 | tf_op jit(solution)/shard_map/ppermute | solution.py:411
  226.2 0.7 copy-done.24
  226.8 3.9 %assemble.1 = f32[64,5120]{1,0:T(8,128)} custom-call(s32[6]{0:T(128)} %pad_add_fusion.flags, f32[512,128]{1,0:T(8,128)} %copy-done.24, f32[512,128]{1,0:T(8,128)} %copy-done.23, f32[512,128]{1,0:T(8,128)} %bitcast.28, f32[64,1024]{1,0:T(8,128)} %get-tuple-element.120.rows2, f32[64,1024]{1,0:T(8,128)} %copy-done.22, f32[64,1024]{1,0:T(8,128)} %get-tuple-element.71.rows0_a, ...), custom_call_target="tpu_custom_call" | custom-call | flops 1024 | bytes 1024 | tf_op jit(solution)/shard_map/assemble/pallas_call | solution.py:343
  (96 shorter events, 3.7 us)
Async XLA Ops:
  4.7 3.8 %collective-permute-start.1 = (f32[3,1024]{1,0:T(4,128)S(1)}, f32[3,1024]{1,0:T(4,128)S(1)}, u32[]{:S(2)}, u32[]{:S(2)}) collective-permute-start(f32[3,1024]{1,0:T(4,128)S(1)} %pad_maximum_fusion), channel_id=1, source_target_pairs={{0,8},{1,9},{8,0},{9,1},{2,10},{3,11},{10,2},{11,3},{4,12},{5,13},... | collective-permute-start | bytes 36872 | tf_op jit(solution)/shard_map/ppermute | solution.py:36
  6.3 3.2 %collective-permute-start.2 = (f32[3,1024]{1,0:T(4,128)S(1)}, f32[3,1024]{1,0:T(4,128)S(1)}, u32[]{:S(2)}, u32[]{:S(2)}) collective-permute-start(f32[3,1024]{1,0:T(4,128)S(1)} %pad_maximum_fusion), channel_id=1, source_target_pairs={{0,9},{1,8},{8,1},{9,0},{2,11},{3,10},{10,3},{11,2},{4,13},{5,12},... | collective-permute-start | bytes 36872 | tf_op jit(solution)/shard_map/ppermute | solution.py:36
  6.3 3.2 %collective-permute-start = (f32[3,1024]{1,0:T(4,128)S(1)}, f32[3,1024]{1,0:T(4,128)S(1)}, u32[]{:S(2)}, u32[]{:S(2)}) collective-permute-start(f32[3,1024]{1,0:T(4,128)S(1)} %pad_maximum_fusion), channel_id=1, source_target_pairs={{0,1},{1,0},{8,9},{9,8},{2,3},{3,2},{10,11},{11,10},{4,5},{5,4},{1... | collective-permute-start | bytes 36872 | tf_op jit(solution)/shard_map/ppermute | solution.py:36
  9.5 5.1 %collective-permute-start.5 = (f32[3,1024]{1,0:T(4,128)S(1)}, f32[3,1024]{1,0:T(4,128)S(1)}, u32[]{:S(2)}, u32[]{:S(2)}) collective-permute-start(f32[3,1024]{1,0:T(4,128)S(1)} %add_add_fusion.1), channel_id=1, source_target_pairs={{0,6},{2,0},{4,2},{6,4},{1,7},{3,1},{5,3},{7,5},{8,14},{10,8},{12,... | collective-permute-start | bytes 36872 | tf_op jit(solution)/shard_map/ppermute | solution.py:40
  12.4 5.2 %collective-permute-start.4 = (f32[3,1024]{1,0:T(4,128)S(1)}, f32[3,1024]{1,0:T(4,128)S(1)}, u32[]{:S(2)}, u32[]{:S(2)}) collective-permute-start(f32[3,1024]{1,0:T(4,128)S(1)} %add_add_fusion.1), channel_id=1, source_target_pairs={{0,4},{2,6},{4,0},{6,2},{1,5},{3,7},{5,1},{7,3},{8,12},{10,14},{12... | collective-permute-start | bytes 36872 | tf_op jit(solution)/shard_map/ppermute | solution.py:40
  13.2 4.9 %collective-permute-start.3 = (f32[3,1024]{1,0:T(4,128)S(1)}, f32[3,1024]{1,0:T(4,128)S(1)}, u32[]{:S(2)}, u32[]{:S(2)}) collective-permute-start(f32[3,1024]{1,0:T(4,128)S(1)} %add_add_fusion.1), channel_id=1, source_target_pairs={{0,2},{2,4},{4,6},{6,0},{1,3},{3,5},{5,7},{7,1},{8,10},{10,12},{12... | collective-permute-start | bytes 36872 | tf_op jit(solution)/shard_map/ppermute | solution.py:40
  27.7 6.8 %collective-permute-start.6 = (bf16[1280,1024]{1,0:T(8,128)(2,1)}, bf16[1280,1024]{1,0:T(8,128)(2,1)S(1)}, u32[]{:S(2)}, u32[]{:S(2)}) collective-permute-start(bf16[1280,1024]{1,0:T(8,128)(2,1)} %get-tuple-element.64.right_a.zed_a), channel_id=1, source_target_pairs={{0,1},{1,0},{2,3},{3,2},{4,5},{5,4},{6,7},{7,6},{8,9},{9,8},{10,11... | collective-permute-start | bytes 7864328 | tf_op jit(solution)/shard_map/ppermute | solution.py:390
  27.7 47.6 %collective-permute-start.7 = (bf16[1280,768]{1,0:T(8,128)(2,1)}, bf16[1280,768]{1,0:T(8,128)(2,1)}, u32[]{:S(2)}, u32[]{:S(2)}) collective-permute-start(bf16[1280,768]{1,0:T(8,128)(2,1)} %get-tuple-element.66), channel_id=1, source_target_pairs={{32,0},{64,32},{96,64},{128,96},{160,128},{192,160},{224,192},{16,... | collective-permute-start | bytes 5898248 | tf_op jit(solution)/shard_map/ppermute | solution.py:389
  29.8 80.8 %collective-permute-start.9 = (bf16[2,8,64,1280]{3,2,1,0:T(8,128)(2,1)}, bf16[2,8,64,1280]{3,2,1,0:T(8,128)(2,1)}, u32[]{:S(2)}, u32[]{:S(2)}) collective-permute-start(bf16[2,8,64,1280]{3,2,1,0:T(8,128)(2,1)} %get-tuple-element.63), channel_id=1, source_target_pairs={{0,16},{16,0},{32,48},{48,32},{64,80},{80,64},{96,112},{112,96},{1... | collective-permute-start | bytes 7864328 | tf_op jit(solution)/shard_map/ppermute | solution.py:391
  34.6 1.5 copy-start.1
  50.6 28.3 %copy-start.25 = (bf16[1280,256]{1,0:T(8,128)(2,1)S(1)}, bf16[1280,256]{1,0:T(8,128)(2,1)}, u32[]{:S(2)}) copy-start(bf16[1280,256]{1,0:T(8,128)(2,1)} %get-tuple-element.68) | copy-start | bytes 1966084
  75.3 5.7 %collective-permute-start.10 = (bf16[1280,768]{1,0:T(8,128)(2,1)}, bf16[1280,768]{1,0:T(8,128)(2,1)}, u32[]{:S(2)}, u32[]{:S(2)}) collective-permute-start(bf16[1280,768]{1,0:T(8,128)(2,1)} %collective-permute-done.7.right_a.near0_a), channel_id=1, source_target_pairs={{0,1},{1,0},{2,3},{3,2},{4,5},{5,4},{6,7},{7,6},{8,9},{9,8},{10,11... | collective-permute-start | bytes 5898248 | tf_op jit(solution)/shard_map/ppermute | solution.py:390
  75.3 30.9 %all-to-all-start = ((f32[4,2,64,1024]{3,2,1,0:T(8,128)}), f32[4,2,64,1024]{3,2,1,0:T(8,128)S(1)}, u32[]{:S(2)}, u32[]{:S(2)}) async-start(f32[4,2,64,1024]{3,2,1,0:T(8,128)} %bitcast.25), calls=%async_computation | async-start | bytes 4194304 | tf_op jit(solution)/shard_map/all_to_all | solution.py:255
  79.0 31.6 %collective-permute-start.8 = (bf16[1280,256]{1,0:T(8,128)(2,1)S(1)}, bf16[1280,256]{1,0:T(8,128)(2,1)S(1)}, u32[]{:S(2)}, u32[]{:S(2)}) collective-permute-start(bf16[1280,256]{1,0:T(8,128)(2,1)S(1)} %copy-done.25), channel_id=1, source_target_pairs={{32,0},{64,32},{96,64},{128,96},{160,128},{192,160},{224,192},{16,... | collective-permute-start | bytes 1966088 | tf_op jit(solution)/shard_map/ppermute | solution.py:389
  106.2 1.4 copy-start.2
  110.6 5.7 %copy-start.3 = (bf16[1280,256]{1,0:T(8,128)(2,1)}, bf16[1280,256]{1,0:T(8,128)(2,1)S(1)}, u32[]{:S(2)}) copy-start(bf16[1280,256]{1,0:T(8,128)(2,1)S(1)} %collective-permute-done.8.near1_a.right_a) | copy-start | bytes 1966084
  112.2 4.1 %collective-permute-start.12 = (bf16[8,64,1280]{2,1,0:T(8,128)(2,1)S(1)}, bf16[8,64,1280]{2,1,0:T(8,128)(2,1)S(1)}, u32[]{:S(2)}, u32[]{:S(2)}) collective-permute-start(bf16[8,64,1280]{2,1,0:T(8,128)(2,1)S(1)} %slice_bitcast_fusion), channel_id=1, source_target_pairs={{0,1},{1,0},{2,3},{3,2},{4,5},{5,4},{6,7},{7,6},{8,9},{9,8},{10,11... | collective-permute-start | bytes 3932168 | tf_op jit(solution)/shard_map/ppermute | solution.py:390
  112.3 4.0 %collective-permute-start.11 = (bf16[1280,256]{1,0:T(8,128)(2,1)S(1)}, bf16[1280,256]{1,0:T(8,128)(2,1)S(1)}, u32[]{:S(2)}, u32[]{:S(2)}) collective-permute-start(bf16[1280,256]{1,0:T(8,128)(2,1)S(1)} %collective-permute-done.8.near1_a.right_a), channel_id=1, source_target_pairs={{0,1},{1,0},{2,3},{3,2},{4,5},{5,4},{6,7},{7,6},{8,9},{9,8},{10,11... | collective-permute-start | bytes 1966088 | tf_op jit(solution)/shard_map/ppermute | solution.py:390
  116.3 1.4 copy-start.5
  127.5 6.0 %copy-start.33 = (f32[64,1024]{1,0:T(8,128)S(1)}, f32[64,1024]{1,0:T(8,128)}, u32[]{:S(2)}) copy-start(f32[64,1024]{1,0:T(8,128)} %get-tuple-element.92) | copy-start | bytes 786436
  127.5 7.4 %copy-start.32 = (f32[64,1024]{1,0:T(8,128)S(1)}, f32[64,1024]{1,0:T(8,128)}, u32[]{:S(2)}) copy-start(f32[64,1024]{1,0:T(8,128)} %get-tuple-element.93) | copy-start | bytes 786436
  127.5 7.4 %copy-start.31 = (f32[64,1024]{1,0:T(8,128)S(1)}, f32[64,1024]{1,0:T(8,128)}, u32[]{:S(2)}) copy-start(f32[64,1024]{1,0:T(8,128)} %get-tuple-element.94) | copy-start | bytes 786436
  127.5 14.1 %copy-start.30 = (f32[64,1024]{1,0:T(8,128)S(1)}, f32[64,1024]{1,0:T(8,128)}, u32[]{:S(2)}) copy-start(f32[64,1024]{1,0:T(8,128)} %get-tuple-element.95) | copy-start | bytes 786436
  127.5 16.0 %copy-start.29 = (f32[64,1024]{1,0:T(8,128)S(1)}, f32[64,1024]{1,0:T(8,128)}, u32[]{:S(2)}) copy-start(f32[64,1024]{1,0:T(8,128)} %get-tuple-element.96) | copy-start | bytes 786436
  127.5 18.9 %copy-start.28 = (f32[64,1024]{1,0:T(8,128)S(1)}, f32[64,1024]{1,0:T(8,128)}, u32[]{:S(2)}) copy-start(f32[64,1024]{1,0:T(8,128)} %get-tuple-element.97) | copy-start | bytes 786436
  127.5 21.6 %copy-start.27 = (f32[64,1024]{1,0:T(8,128)S(1)}, f32[64,1024]{1,0:T(8,128)}, u32[]{:S(2)}) copy-start(f32[64,1024]{1,0:T(8,128)} %get-tuple-element.98) | copy-start | bytes 786436
  132.2 58.1 %copy-start.26 = (f32[64,1024]{1,0:T(8,128)S(1)}, f32[64,1024]{1,0:T(8,128)}, u32[]{:S(2)}) copy-start(f32[64,1024]{1,0:T(8,128)} %get-tuple-element.118) | copy-start | bytes 786436
  132.2 9.4 %collective-permute-start.13 = (f32[64,1024]{1,0:T(8,128)}, f32[64,1024]{1,0:T(8,128)S(1)}, u32[]{:S(2)}, u32[]{:S(2)}) collective-permute-start(f32[64,1024]{1,0:T(8,128)} %get-tuple-element.85), channel_id=1, source_target_pairs={{0,8},{8,0},{2,10},{10,2},{4,12},{12,4},{6,14},{14,6},{1,9},{9,1},... | collective-permute-start | bytes 786440 | tf_op jit(solution)/shard_map/ppermute | solution.py:315
  132.9 10.6 %collective-permute-start.14 = (f32[64,1024]{1,0:T(8,128)}, f32[64,1024]{1,0:T(8,128)S(1)}, u32[]{:S(2)}, u32[]{:S(2)}) collective-permute-start(f32[64,1024]{1,0:T(8,128)} %get-tuple-element.86), channel_id=1, source_target_pairs={{0,2},{8,10},{2,4},{10,12},{4,6},{12,14},{6,0},{14,8},{1,3},{9,11}... | collective-permute-start | bytes 786440 | tf_op jit(solution)/shard_map/ppermute | solution.py:315
  133.5 12.9 %collective-permute-start.20 = (f32[64,1024]{1,0:T(8,128)S(1)}, f32[64,1024]{1,0:T(8,128)S(1)}, u32[]{:S(2)}, u32[]{:S(2)}) collective-permute-start(f32[64,1024]{1,0:T(8,128)S(1)} %copy-done.33), channel_id=1, source_target_pairs={{0,8},{8,0},{2,10},{10,2},{4,12},{12,4},{6,14},{14,6},{1,9},{9,1},... | collective-permute-start | bytes 786440 | tf_op jit(solution)/shard_map/ppermute | solution.py:315
  134.9 14.3 %collective-permute-start.21 = (f32[64,1024]{1,0:T(8,128)S(1)}, f32[64,1024]{1,0:T(8,128)S(1)}, u32[]{:S(2)}, u32[]{:S(2)}) collective-permute-start(f32[64,1024]{1,0:T(8,128)S(1)} %copy-done.32), channel_id=1, source_target_pairs={{0,2},{8,10},{2,4},{10,12},{4,6},{12,14},{6,0},{14,8},{1,3},{9,11}... | collective-permute-start | bytes 786440 | tf_op jit(solution)/shard_map/ppermute | solution.py:315
  134.9 19.7 %collective-permute-start.22 = (f32[64,1024]{1,0:T(8,128)S(1)}, f32[64,1024]{1,0:T(8,128)S(1)}, u32[]{:S(2)}, u32[]{:S(2)}) collective-permute-start(f32[64,1024]{1,0:T(8,128)S(1)} %copy-done.31), channel_id=1, source_target_pairs={{0,10},{8,2},{2,12},{10,4},{4,14},{12,6},{6,8},{14,0},{1,11},{9,3}... | collective-permute-start | bytes 786440 | tf_op jit(solution)/shard_map/ppermute | solution.py:315
  141.6 58.3 %copy-start.7 = (f32[64,1024]{1,0:T(8,128)}, f32[64,1024]{1,0:T(8,128)S(1)}, u32[]{:S(2)}) copy-start(f32[64,1024]{1,0:T(8,128)S(1)} %collective-permute-done.13.refs_1_) | copy-start | bytes 786436
  141.6 19.9 %collective-permute-start.23 = (f32[64,1024]{1,0:T(8,128)S(1)}, f32[64,1024]{1,0:T(8,128)S(1)}, u32[]{:S(2)}, u32[]{:S(2)}) collective-permute-start(f32[64,1024]{1,0:T(8,128)S(1)} %copy-done.30), channel_id=1, source_target_pairs={{0,4},{8,12},{2,6},{10,14},{4,0},{12,8},{6,2},{14,10},{1,5},{9,13}... | collective-permute-start | bytes 786440 | tf_op jit(solution)/shard_map/ppermute | solution.py:315
  143.5 56.4 %copy-start.8 = (f32[64,1024]{1,0:T(8,128)}, f32[64,1024]{1,0:T(8,128)S(1)}, u32[]{:S(2)}) copy-start(f32[64,1024]{1,0:T(8,128)S(1)} %collective-permute-done.14.refs_2_) | copy-start | bytes 786436
  143.5 26.2 %collective-permute-start.24 = (f32[64,1024]{1,0:T(8,128)S(1)}, f32[64,1024]{1,0:T(8,128)S(1)}, u32[]{:S(2)}, u32[]{:S(2)}) collective-permute-start(f32[64,1024]{1,0:T(8,128)S(1)} %copy-done.29), channel_id=1, source_target_pairs={{0,12},{8,4},{2,14},{10,6},{4,8},{12,0},{6,10},{14,2},{1,13},{9,5}... | collective-permute-start | bytes 786440 | tf_op jit(solution)/shard_map/ppermute | solution.py:315
  146.4 28.4 %copy-start.11 = (f32[64,1024]{1,0:T(8,128)}, f32[64,1024]{1,0:T(8,128)S(1)}, u32[]{:S(2)}) copy-start(f32[64,1024]{1,0:T(8,128)S(1)} %collective-permute-done.20.refs_1_) | copy-start | bytes 786436
  146.4 27.3 %collective-permute-start.25 = (f32[64,1024]{1,0:T(8,128)S(1)}, f32[64,1024]{1,0:T(8,128)S(1)}, u32[]{:S(2)}, u32[]{:S(2)}) collective-permute-start(f32[64,1024]{1,0:T(8,128)S(1)} %copy-done.28), channel_id=1, source_target_pairs={{0,6},{8,14},{2,0},{10,8},{4,2},{12,10},{6,4},{14,12},{1,7},{9,15}... | collective-permute-start | bytes 786440 | tf_op jit(solution)/shard_map/ppermute | solution.py:315
  149.1 25.6 %copy-start.12 = (f32[64,1024]{1,0:T(8,128)}, f32[64,1024]{1,0:T(8,128)S(1)}, u32[]{:S(2)}) copy-start(f32[64,1024]{1,0:T(8,128)S(1)} %collective-permute-done.21.refs_2_) | copy-start | bytes 786436
  149.1 24.6 %collective-permute-start.26 = (f32[64,1024]{1,0:T(8,128)S(1)}, f32[64,1024]{1,0:T(8,128)S(1)}, u32[]{:S(2)}, u32[]{:S(2)}) collective-permute-start(f32[64,1024]{1,0:T(8,128)S(1)} %copy-done.27), channel_id=1, source_target_pairs={{0,14},{8,6},{2,8},{10,0},{4,10},{12,2},{6,12},{14,4},{1,15},{9,7}... | collective-permute-start | bytes 786440 | tf_op jit(solution)/shard_map/ppermute | solution.py:315
  154.6 20.2 %copy-start.14 = (f32[64,1024]{1,0:T(8,128)}, f32[64,1024]{1,0:T(8,128)S(1)}, u32[]{:S(2)}) copy-start(f32[64,1024]{1,0:T(8,128)S(1)} %collective-permute-done.22.refs_3_) | copy-start | bytes 786436
  154.6 35.7 %collective-permute-start.15 = (f32[64,1024]{1,0:T(8,128)}, f32[64,1024]{1,0:T(8,128)S(1)}, u32[]{:S(2)}, u32[]{:S(2)}) collective-permute-start(f32[64,1024]{1,0:T(8,128)} %get-tuple-element.87), channel_id=1, source_target_pairs={{0,10},{8,2},{2,12},{10,4},{4,14},{12,6},{6,8},{14,0},{1,11},{9,3}... | collective-permute-start | bytes 786440 | tf_op jit(solution)/shard_map/ppermute | solution.py:315
  161.5 13.2 %copy-start.16 = (f32[64,1024]{1,0:T(8,128)}, f32[64,1024]{1,0:T(8,128)S(1)}, u32[]{:S(2)}) copy-start(f32[64,1024]{1,0:T(8,128)S(1)} %collective-permute-done.23.refs_4_) | copy-start | bytes 786436
  161.5 29.0 %collective-permute-start.16 = (f32[64,1024]{1,0:T(8,128)}, f32[64,1024]{1,0:T(8,128)S(1)}, u32[]{:S(2)}, u32[]{:S(2)}) collective-permute-start(f32[64,1024]{1,0:T(8,128)} %get-tuple-element.88), channel_id=1, source_target_pairs={{0,4},{8,12},{2,6},{10,14},{4,0},{12,8},{6,2},{14,10},{1,5},{9,13}... | collective-permute-start | bytes 786440 | tf_op jit(solution)/shard_map/ppermute | solution.py:315
  169.8 5.0 %copy-start.18 = (f32[64,1024]{1,0:T(8,128)}, f32[64,1024]{1,0:T(8,128)S(1)}, u32[]{:S(2)}) copy-start(f32[64,1024]{1,0:T(8,128)S(1)} %collective-permute-done.24.refs_5_) | copy-start | bytes 786436
  169.8 23.9 %collective-permute-start.17 = (f32[64,1024]{1,0:T(8,128)}, f32[64,1024]{1,0:T(8,128)S(1)}, u32[]{:S(2)}, u32[]{:S(2)}) collective-permute-start(f32[64,1024]{1,0:T(8,128)} %get-tuple-element.89), channel_id=1, source_target_pairs={{0,12},{8,4},{2,14},{10,6},{4,8},{12,0},{6,10},{14,2},{1,13},{9,5}... | collective-permute-start | bytes 786440 | tf_op jit(solution)/shard_map/ppermute | solution.py:315
  173.7 1.1 copy-start.19
  173.7 26.1 %collective-permute-start.18 = (f32[64,1024]{1,0:T(8,128)}, f32[64,1024]{1,0:T(8,128)S(1)}, u32[]{:S(2)}, u32[]{:S(2)}) collective-permute-start(f32[64,1024]{1,0:T(8,128)} %get-tuple-element.90), channel_id=1, source_target_pairs={{0,6},{8,14},{2,0},{10,8},{4,2},{12,10},{6,4},{14,12},{1,7},{9,15}... | collective-permute-start | bytes 786440 | tf_op jit(solution)/shard_map/ppermute | solution.py:315
  173.7 1.1 copy-start.20
  173.7 26.1 %collective-permute-start.19 = (f32[64,1024]{1,0:T(8,128)}, f32[64,1024]{1,0:T(8,128)S(1)}, u32[]{:S(2)}, u32[]{:S(2)}) collective-permute-start(f32[64,1024]{1,0:T(8,128)} %get-tuple-element.91), channel_id=1, source_target_pairs={{0,14},{8,6},{2,8},{10,0},{4,10},{12,2},{6,12},{14,4},{1,15},{9,7}... | collective-permute-start | bytes 786440 | tf_op jit(solution)/shard_map/ppermute | solution.py:315
  174.8 33.6 %copy-start = (s32[16]{0:T(128)S(1)}, s32[16]{0:T(128)}, u32[]{:S(2)}) copy-start(s32[16]{0:T(128)} %param.5) | copy-start | bytes 196
  177.9 16.9 %all-to-all-start.2 = ((f32[16,32,128]{2,1,0:T(8,128)}), f32[16,32,128]{2,1,0:T(8,128)S(1)}, u32[]{:S(2)}, u32[]{:S(2)}) async-start(f32[16,32,128]{2,1,0:T(8,128)} %get-tuple-element.117), calls=%async_computation.2 | async-start | bytes 524288 | tf_op jit(solution)/shard_map/all_to_all | solution.py:310
  190.3 9.6 %copy-start.9 = (f32[64,1024]{1,0:T(8,128)}, f32[64,1024]{1,0:T(8,128)S(1)}, u32[]{:S(2)}) copy-start(f32[64,1024]{1,0:T(8,128)S(1)} %collective-permute-done.15.refs_3_) | copy-start | bytes 786436
  190.3 19.4 %collective-permute-start.29 = (f32[64,1024]{1,0:T(8,128)S(1)}, f32[64,1024]{1,0:T(8,128)S(1)}, u32[]{:S(2)}, u32[]{:S(2)}) collective-permute-start(f32[64,1024]{1,0:T(8,128)S(1)} %copy-done.26), channel_id=1, source_target_pairs={{0,8},{8,0},{1,9},{9,1},{2,10},{10,2},{3,11},{11,3},{4,12},{12,4},... | collective-permute-start | bytes 786440 | tf_op jit(solution)/shard_map/ppermute | solution.py:272
  190.5 9.4 %copy-start.10 = (f32[64,1024]{1,0:T(8,128)}, f32[64,1024]{1,0:T(8,128)S(1)}, u32[]{:S(2)}) copy-start(f32[64,1024]{1,0:T(8,128)S(1)} %collective-permute-done.16.refs_4_) | copy-start | bytes 786436
  190.5 25.8 %collective-permute-start.28 = (f32[64,1024]{1,0:T(8,128)}, f32[64,1024]{1,0:T(8,128)S(1)}, u32[]{:S(2)}, u32[]{:S(2)}) collective-permute-start(f32[64,1024]{1,0:T(8,128)} %get-tuple-element.107), channel_id=1, source_target_pairs={{0,16},{16,0},{32,48},{48,32},{64,80},{80,64},{96,112},{112,96},{1... | collective-permute-start | bytes 786440 | tf_op jit(solution)/shard_map/ppermute | solution.py:408
  193.7 6.2 %copy-start.13 = (f32[64,1024]{1,0:T(8,128)}, f32[64,1024]{1,0:T(8,128)S(1)}, u32[]{:S(2)}) copy-start(f32[64,1024]{1,0:T(8,128)S(1)} %collective-permute-done.17.refs_5_) | copy-start | bytes 786436
  194.8 31.4 %copy-start.6 = (f32[16,32,128]{2,1,0:T(8,128)}, f32[16,32,128]{2,1,0:T(8,128)S(1)}, u32[]{:S(2)}) copy-start(f32[16,32,128]{2,1,0:T(8,128)S(1)} %all-to-all-done.2) | copy-start | bytes 786436
  194.8 21.5 %collective-permute-start.27 = (f32[512,128]{1,0:T(8,128)S(1)}, f32[512,128]{1,0:T(8,128)S(1)}, u32[]{:S(2)}, u32[]{:S(2)}) collective-permute-start(f32[512,128]{1,0:T(8,128)S(1)} %bitcast.27), channel_id=1, source_target_pairs={{0,32},{32,64},{64,96},{96,128},{128,160},{160,192},{192,224},{1,3... | collective-permute-start | bytes 786440 | tf_op jit(solution)/shard_map/ppermute | solution.py:409
  204.3 12.0 %all-to-all-start.1 = ((f32[16,32,128]{2,1,0:T(8,128)}), f32[16,32,128]{2,1,0:T(8,128)S(1)}, u32[]{:S(2)}, u32[]{:S(2)}) async-start(f32[16,32,128]{2,1,0:T(8,128)} %get-tuple-element.116), calls=%async_computation.1 | async-start | bytes 524288 | tf_op jit(solution)/shard_map/all_to_all | solution.py:310
  209.7 16.4 %copy-start.21 = (f32[64,1024]{1,0:T(8,128)}, f32[64,1024]{1,0:T(8,128)S(1)}, u32[]{:S(2)}) copy-start(f32[64,1024]{1,0:T(8,128)S(1)} %collective-permute-done.29.rows0_b) | copy-start | bytes 786436
  216.3 9.8 %copy-start.22 = (f32[64,1024]{1,0:T(8,128)}, f32[64,1024]{1,0:T(8,128)S(1)}, u32[]{:S(2)}) copy-start(f32[64,1024]{1,0:T(8,128)S(1)} %collective-permute-done.28.beside) | copy-start | bytes 786436
  216.3 9.8 %copy-start.23 = (f32[512,128]{1,0:T(8,128)}, f32[512,128]{1,0:T(8,128)S(1)}, u32[]{:S(2)}) copy-start(f32[512,128]{1,0:T(8,128)S(1)} %collective-permute-done.27.near) | copy-start | bytes 786436
  216.3 9.8 %collective-permute-start.30 = (f32[512,128]{1,0:T(8,128)S(1)}, f32[512,128]{1,0:T(8,128)S(1)}, u32[]{:S(2)}, u32[]{:S(2)}) collective-permute-start(f32[512,128]{1,0:T(8,128)S(1)} %bitcast.29), channel_id=1, source_target_pairs={{0,32},{32,64},{64,96},{96,128},{128,160},{160,192},{192,224},{48,... | collective-permute-start | bytes 786440 | tf_op jit(solution)/shard_map/ppermute | solution.py:411
  (4 other events, 3.0 us)

commit v7 on v5

--- a/solution.py
+++ b/solution.py
@@ -1,5 +1,3 @@
-import functools
-
 import jax
 import jax.numpy as jnp
 from jax import lax
@@ -14,7 +12,6 @@
 SIZES = (8, 2, 2, 4, 2)
 SNP = ("z", "yh")
 SAMP = ("yl", "x", "core")
-CHIP = ("yl", "x")
 NSNP = 16
 B = 1024
 DEPTH = 1280
@@ -46,10 +43,6 @@
     return piece // 2 + 4 * (piece % 2)
 
 
-def piece_at(place, r):
-    return (place // 2 + r // 2) % 4 * 2 + (place % 2 ^ r % 2)
-
-
 def params():
     return pltpu.CompilerParams(vmem_limit_bytes=56 << 20)
 
@@ -74,39 +67,34 @@
     return jnp.dot(left, right, preferred_element_type=jnp.float32)
 
 
-def standard_kernel(meta, dosage, observed, stats, zed, zed0, zed1, kept, sent):
+def standard_kernel(meta, dosage, observed, stats, zed, zed0, zed1, turned):
     weight = observed[...].astype(jnp.float32)
     values = dosage[...].astype(jnp.float32)
     z = (weight * (values - stats[0:1, :]) * stats[1:2, :]).astype(jnp.bfloat16)
     zed[...] = z
     zed0[...] = z[:, :HALF]
     zed1[...] = z[:, HALF:]
-    turned = z.T
-
-    def store(*outs):
-        for p in range(PIECES):
-            for k, out in enumerate(outs):
-                at = 2 * ROWS * chip_of(p) + ROWS * k
-                out[p] = turned[at : at + ROWS]
-
-    pl.when(meta[0] == 0)(lambda: store(kept, sent))
-    pl.when(meta[0] != 0)(lambda: store(sent, kept))
+    columns = z.T
+    for p in range(PIECES):
+        for k in range(2):
+            at = 2 * ROWS * chip_of(p) + ROWS * k
+            turned[meta[0] ^ k, p] = columns[at : at + ROWS]
 
 
 def standardize(meta, dosage, observed, stats):
     rows = 256
     block = lambda width: pl.BlockSpec((rows, width), lambda i, m: (i, 0))
-    turned = pl.BlockSpec((PIECES, ROWS, rows), lambda i, m: (0, 0, i))
+    turned = pl.BlockSpec((2, PIECES, ROWS, rows), lambda i, m: (0, 0, 0, i))
     return pl.pallas_call(
         standard_kernel,
         name="standardize",
         out_shape=(bf16(DEPTH, B), bf16(DEPTH, HALF), bf16(DEPTH, HALF))
-        + (bf16(PIECES, ROWS, DEPTH),) * 2,
+        + (bf16(2, PIECES, ROWS, DEPTH),),
         grid_spec=pltpu.PrefetchScalarGridSpec(
             num_scalar_prefetch=1,
             grid=(DEPTH // rows,),
             in_specs=[block(B), block(B), whole((2, B))],
-            out_specs=(block(B), block(HALF), block(HALF), turned, turned),
+            out_specs=(block(B), block(HALF), block(HALF), turned),
         ),
         compiler_params=params(),
         cost_estimate=cost(4 * DEPTH * B, 12 * DEPTH * B),
@@ -117,7 +105,7 @@
 
 
 def flat(*turned):
-    return [t.reshape(LEFT) for t in turned]
+    return [t.reshape(-1, DEPTH) for t in turned]
 
 
 def turn_kernel(meta, zed, out):
@@ -146,17 +134,16 @@
     )(meta, zed)
 
 
-def product_kernel(place_of, meta, left_a, left_b, right_a, right_b, *rest):
+def product_kernel(meta, left_a, left_b, right_a, right_b, *rest):
     acc = matmul(left_a[...], right_a[...]) + matmul(left_b[...], right_b[...])
-    for p in range(PIECES):
-        rest[-1][place_of(p)] = acc[ROWS * p : ROWS * (p + 1)]
-
-
-def product(meta, left, right, place_of, name, first=0, before=()):
+    rest[-1][...] = acc.reshape(PIECES, ROWS, STEP)
+
+
+def product(meta, left, right, name, first=0, before=()):
     columns = right[0].shape[1]
     block = pl.BlockSpec((DEPTH, STEP), lambda j, m: (0, j))
     return pl.pallas_call(
-        functools.partial(product_kernel, place_of),
+        product_kernel,
         name=name,
         out_shape=f32(PIECES, ROWS, B),
         grid_spec=pltpu.PrefetchScalarGridSpec(
@@ -176,7 +163,7 @@
 def across_kernel(
     meta, left_a, left_b, near0_a, near0_b, near1_a, near1_b, zed_a, zed_b, *rest
 ):
-    outs, right = rest[:PIECES], rest[PIECES]
+    outs, right = rest[:4], rest[4]
     odd = meta[1] == 1
     early = pl.program_id(0) < HALF // STEP
 
@@ -190,12 +177,11 @@
     acc = matmul(left_a[...], right[:DEPTH]) + matmul(left_b[...], right[DEPTH:])
     acc = acc.reshape(4, 2, ROWS, STEP)
     for x in range(4):
-        for y in range(2):
-
-            @pl.when((meta[3] == x) & (meta[2] == y))
-            def _():
-                for r in range(PIECES):
-                    outs[r][...] = acc[(x + r // 2) % 4, y ^ (r % 2)]
+
+        @pl.when(meta[3] == x)
+        def _():
+            for k in range(4):
+                outs[k][...] = acc[(x + k) % 4]
 
 
 def across_product(meta, left, near0, near1, zed):
@@ -206,12 +192,12 @@
     return pl.pallas_call(
         across_kernel,
         name="across",
-        out_shape=(f32(ROWS, B),) * PIECES,
+        out_shape=(f32(2, ROWS, B),) * 4,
         grid_spec=pltpu.PrefetchScalarGridSpec(
             num_scalar_prefetch=1,
             grid=(B // STEP,),
             in_specs=[whole(LEFT)] * 2 + [first] * 2 + [second] * 2 + [block] * 2,
-            out_specs=(pl.BlockSpec((ROWS, STEP), lambda j, m: (0, j)),) * PIECES,
+            out_specs=(pl.BlockSpec((2, ROWS, STEP), lambda j, m: (0, 0, j)),) * 4,
             scratch_shapes=[pltpu.VMEM((2 * DEPTH, STEP), jnp.bfloat16)],
         ),
         compiler_params=params(),
@@ -223,18 +209,20 @@
     return lax.optimization_barrier((value, *others))[0]
 
 
-def add_kernel(meta, parts, keep, send):
+def add_kernel(meta, *refs):
+    parts, (keep, send) = refs[:-2], refs[-2:]
+    if len(parts) == 1:
+        parts = [parts[0].at[k] for k in range(4)]
     mine = meta[2]
     for out, half in ((keep, mine), (send, 1 - mine)):
-        out[...] = parts[0, half] + parts[1, half] + parts[2, half] + parts[3, half]
-
-
-def fold(meta, parts, *others):
-    _, rows, columns = parts.shape
-    parts = lax.all_to_all(parts.reshape(4, 2, rows, columns), "x", 0, 0)
-    parts = after(parts, *others)
+        out[...] = parts[0][half] + parts[1][half] + parts[2][half] + parts[3][half]
+
+
+def add(meta, *parts):
+    rows, columns = parts[0].shape[-2:]
     step = 2 * STEP
     out = pl.BlockSpec((rows, step), lambda j, m: (0, j))
+    spec = lambda t: pl.BlockSpec(t.shape[:-1] + (step,), lambda j, m: (0,) * (t.ndim - 1) + (j,))
     keep, send = pl.pallas_call(
         add_kernel,
         name="add",
@@ -242,13 +230,26 @@
         grid_spec=pltpu.PrefetchScalarGridSpec(
             num_scalar_prefetch=1,
             grid=(columns // step,),
-            in_specs=[pl.BlockSpec((4, 2, rows, step), lambda j, m: (0, 0, 0, j))],
+            in_specs=[spec(t) for t in parts],
             out_specs=(out, out),
         ),
         compiler_params=params(),
         cost_estimate=cost(6 * rows * columns, 40 * rows * columns),
-    )(meta, parts)
+    )(meta, *parts)
     return keep, lax.ppermute(send, "yl", SWAP)
+
+
+def fold(meta, parts, *others):
+    _, rows, columns = parts.shape
+    parts = lax.all_to_all(parts.reshape(4, 2, rows, columns), "x", 0, 0)
+    return add(meta, after(parts, *others))
+
+
+def fold_pieces(meta, pieces, *others):
+    moved = [
+        lax.ppermute(pieces[k], "x", [(i, (i + k) % 4) for i in range(4)]) for k in (1, 2, 3)
+    ]
+    return add(meta, *after((pieces[0], *moved), *others))
 
 
 def gather_kernel(meta, *refs):
@@ -359,36 +360,31 @@
     spread = second - first * mean
     stats = jnp.stack([mean, lax.rsqrt(spread + eps * cnt)])
 
-    zed, zed0, zed1, kept, sent = standardize(meta, dosage, observed, stats)
+    zed, zed0, zed1, turned = standardize(meta, dosage, observed, stats)
     along = lambda t: lax.ppermute(t, SNP, EVEN_DOWN + ODD_UP)
-    across = lambda t: lax.ppermute(t, SNP, TO_OTHER)
-    athwart = lambda t: lax.ppermute(t, ("yh", "core"), [(i, 3 - i) for i in range(4)])
     swap = lambda t: lax.ppermute(t, "core", SWAP)
-    other0 = across(kept)
+    other = lax.ppermute(turned, SNP, TO_OTHER)
     near0 = along(zed0)
     zed_b = swap(zed)
-    own = (kept, turn(meta, zed_b))
-    rows0 = product(meta, own, (zed, zed_b), lambda p: p, "own")
-    near0, other0 = after((near0, other0), rows0)
-    other1 = athwart(after(sent, near0, other0))
-    near1 = along(after(zed1, near0, other0))
-    near0 = (near0, swap(near0))
-    rows2 = product(meta, own, near0, chip_of, "first")
-    rows0 = fold(meta, rows0, rows2)
-    near1, other1 = after((near1, other1), rows2, rows0[0])
+    own = (turned, turn(meta, zed_b))
+    rows0 = product(meta, own, (zed, zed_b), "own")
+    near0 = after(near0, rows0)
+    near1 = along(after(zed1, near0))
+    rows0 = fold(meta, rows0)
+    near0 = after((near0, swap(near0)), rows0[0])
+    rows2 = product(meta, own, near0, "first")
+    near1, other = after((near1, other), rows2)
     near1 = (near1, swap(near1))
-    rows2 = product(meta, own, near1, chip_of, "second", HALF, (rows2,))
-    pieces = across_product(meta, (other0, other1), near0, near1, (zed, zed_b))
-    rows2 = lax.all_to_all(after(rows2, rows0[0]), CHIP, 0, 0)
-    rows2, turned2 = gather(meta, after(rows2, pieces[0]))
-    pieces = [pieces[0]] + [
-        lax.ppermute(
-            pieces[r], CHIP, [(chip_of(i), chip_of(piece_at(i, r))) for i in range(PIECES)]
-        )
-        for r in range(1, PIECES)
-    ]
-    rows1, turned1 = gather(meta, *after(pieces, turned2, rows0[1]))
+    other = (other, swap(other[1]))
+    near1 = after(near1, other[1])
+    rows2 = product(meta, own, near1, "second", HALF, (rows2,))
+    other = after(other, rows2)
+    pieces = across_product(meta, other, near0, near1, (zed, zed_b))
+    rows2 = fold(meta, rows2, pieces[0])
+    rows2, turned2 = gather(meta, *rows2)
     far = lax.ppermute(turned2, SNP, EVEN_UP + ODD_DOWN)
+    rows1 = fold_pieces(meta, pieces, turned2, rows0[1])
+    rows1, turned1 = gather(meta, *rows1)
     beside = lax.ppermute(rows1, SNP, TO_OTHER)
     near = lax.ppermute(after(turned1, far, beside), SNP, EVEN_UP)
     flags = jnp.concatenate([kept_flags(band, mine), odd]).astype(jnp.int32)

time: 220 us -> 215 us (0.977)
  starting transfers between devices: 65.4 us -> 51.2 us
  Pallas kernels: 57.3 us -> 61.9 us
    all_to_all x1 -> x2, waiting for transfers between devices: 2.34 us -> 29.4 us  [fold(): parts = lax.all_to_all(parts.reshape(4, 2, rows, columns), 'x', 0, 0)]
    ppermute x10 -> x7, starting transfers between devices: 28.7 us -> 13.7 us  [the longest x3 6.4 us: fold_pieces(): lax.ppermute(pieces[k], 'x', [(i, (i + k) % 4) for i in range(4)])]
    ppermute x10 -> x7, waiting for transfers between devices: 26.9 us -> 12.5 us  [the longest x3 10.2 us: add(): return (keep, lax.ppermute(send, 'yl', SWAP))]
    ppermute x2, waiting for transfers between devices: 20.7 us -> 10.8 us  [on_device(): along = lambda t: lax.ppermute(t, SNP, EVEN_DOWN + ODD_UP)]
    pallas_call x5 -> x7, Pallas kernels: 31.3 us -> 37.1 us  [the longest x3 18.5 us: product(): pl.pallas_call(product_kernel, name=name, out_shape=f32(PIECES, ROWS, B),...]
    all_to_all x1 -> x0, starting transfers between devices: 3.73 us -> none  [on_device(): rows2 = lax.all_to_all(after(rows2, rows0[0]), CHIP, 0, 0)]
    all_to_all x1 -> x2, starting transfers between devices: 3.61 us -> 7.21 us  [fold(): parts = lax.all_to_all(parts.reshape(4, 2, rows, columns), 'x', 0, 0)]
    unnamed x38 -> x32, local copies, waits for them, and re-layouts: 9.01 us -> 8.57 us
  transfers between devices with their start and end apart: 28 -> 26, of which waited for: 15 -> 17; matrix products, arithmetic and copies ran while one was open for 1% -> 1% of each run, Pallas kernels for 18% -> 19%
where the time goes in v7:
time: 215 us; the launch traced here: 212 us
  waiting for transfers between devices  79.8 us (37%)
  Pallas kernels  61.9 us (29%)
  starting transfers between devices  51.2 us (24%)
  local copies, waits for them, and re-layouts  11.2 us (5%)
  other arithmetic  7.29 us (3%)
    all_to_all x2, waiting for transfers between devices, fold(): parts = lax.all_to_all(parts.reshape(4, 2, rows, columns), 'x', 0, 0)  29.4 us
    pallas_call x3, Pallas kernels, product(): pl.pallas_call(product_kernel, name=name, out_shape=f32(PIECES, ROWS, B),...  18.5 us
    all_to_all x2, waiting for transfers between devices, gather(): return (rows, lax.all_to_all(packed, SAMP, 0, 0).reshape(HALF, 2 * ROWS))  13.4 us
    ppermute x2, waiting for transfers between devices, on_device(): along = lambda t: lax.ppermute(t, SNP, EVEN_DOWN + ODD_UP)  10.8 us
    ppermute x3, waiting for transfers between devices, add(): return (keep, lax.ppermute(send, 'yl', SWAP))  10.2 us
    pallas_call x1, Pallas kernels, across_product(): pl.pallas_call(across_kernel, name='across', out_shape=(f32(2, ROWS, B),)...  9.66 us
    pallas_call x1, Pallas kernels, standardize(): pl.pallas_call(standard_kernel, name='standardize', out_shape=(bf16(DEPTH...  8.94 us
    pallas_call x3, Pallas kernels, add(): pl.pallas_call(add_kernel, name='add', out_shape=(f32(rows, columns),) *...  8.91 us
  transfers between devices with their start and end apart: 26, of which 17 were waited for; matrix products, arithmetic and copies ran while one was open for 1% of the time, Pallas kernels for 19%

profile of v7, /device:TPU:64, one launch (start us, length us, event | category | flops | bytes accessed | tf_op | source)
XLA Modules:
  0.0 211.7 jit_solution(18276017862349972083)
XLA Ops:
  0.0 4.7 %fusion.1 = (f32[1024]{0:T(1024)S(1)}, f32[1024]{0:T(1024)S(1)}, f32[1024]{0:T(1024)S(1)}) fusion(bf16[1280,1024]{1,0:T(8,128)(2,1)} %dosage.1, s32[1280,1024]{1,0:T(8,128)} %observed.1), kind=kLoop, calls=%fused_computation.5 | loop fusion | flops 9171968 | bytes 7876608 | tf_op jit(solution)/shard_map/reduce_sum | solution.py:354
  4.7 1.7 collective-permute-start.1
  6.3 0.6 collective-permute-start
  6.9 1.6 collective-permute-done.1
  8.5 1.0 collective-permute-done.2
  9.5 2.8 %collective-permute-start.5 = (f32[3,1024]{1,0:T(4,128)S(1)}, f32[3,1024]{1,0:T(4,128)S(1)}, u32[]{:S(2)}, u32[]{:S(2)}) collective-permute-start(f32[3,1024]{1,0:T(4,128)S(1)} %add_add_fusion.1), channel_id=1, source_target_pairs={{0,6},{2,0},{4,2},{6,4},{1,7},{3,1},{5,3},{7,5},{8,14},{10,8},{12,... | collective-permute-start | bytes 36872 | tf_op jit(solution)/shard_map/ppermute | solution.py:37
  12.4 0.8 collective-permute-start.4
  13.2 0.9 collective-permute-start.3
  14.1 0.7 pad_add_fusion.1.meta
  14.7 2.9 %collective-permute-done.4 = f32[3,1024]{1,0:T(4,128)S(1)} collective-permute-done((f32[3,1024]{1,0:T(4,128)S(1)}, f32[3,1024]{1,0:T(4,128)S(1)}, u32[]{:S(2)}, u32[]{:S(2)}) %collective-permute-start.4) | collective-permute-done | bytes 12320 | tf_op jit(solution)/shard_map/ppermute | solution.py:37
  18.2 0.6 pad_maximum_fusion.1.stats
  18.8 8.9 %standardize.1 = (bf16[1280,1024]{1,0:T(8,128)(2,1)}, bf16[1280,512]{1,0:T(8,128)(2,1)}, bf16[1280,512]{1,0:T(8,128)(2,1)}, bf16[2,8,64,1280]{3,2,1,0:T(8,128)(2,1)}) custom-call(s32[4]{0:T(128)} %pad_add_fusion.1.meta, bf16[1280,1024]{1,0:T(8,128)(2,1)} %dosage.1, s32[1280,1024]{1,0:T(8,128)} %observed.1, f32[2,1024]{1,0:T(2,128)} %pad_maximum_fusion.1.stats), custom_call_target="tpu_custom_call" | custom-call | flops 1024 | bytes 1024 | tf_op jit(solution)/shard_map/standardize/pallas_call | solution.py:88
  27.7 2.0 collective-permute-start.7
  29.8 4.8 %collective-permute-start.9 = (bf16[2,8,64,1280]{3,2,1,0:T(8,128)(2,1)}, bf16[2,8,64,1280]{3,2,1,0:T(8,128)(2,1)}, u32[]{:S(2)}, u32[]{:S(2)}) collective-permute-start(bf16[2,8,64,1280]{3,2,1,0:T(8,128)(2,1)} %get-tuple-element.39), channel_id=1, source_target_pairs={{0,16},{16,0},{32,48},{48,32},{64,80},{80,64},{96,112},{112,96},{1... | collective-permute-start | bytes 7864328 | tf_op jit(solution)/shard_map/ppermute | solution.py:366
  34.6 1.5 copy-done.1
  36.1 6.7 %turn.1 = bf16[8,64,1280]{2,1,0:T(8,128)(2,1)} custom-call(s32[4]{0:T(128)} %pad_add_fusion.1.meta, bf16[1280,1024]{1,0:T(8,128)(2,1)} %copy-done.1), custom_call_target="tpu_custom_call" | custom-call | flops 1024 | bytes 1024 | tf_op jit(solution)/shard_map/turn/pallas_call | solution.py:122
  42.8 7.8 %own.1 = f32[8,64,1024]{2,1,0:T(8,128)} custom-call(s32[4]{0:T(128)} %pad_add_fusion.1.meta, bf16[1024,1280]{1,0:T(8,128)(2,1)} %bitcast.20, bf16[512,1280]{1,0:T(8,128)(2,1)} %bitcast.23, bf16[1280,1024]{1,0:T(8,128)(2,1)} %get-tuple-element.40.right_a.zed_a, bf16[1280,1024]{1,0:T(8,128)(2,1)} %copy-done.1), custom_call_target="tpu_custom_call" | custom-call | flops 1024 | bytes 1024 | tf_op jit(solution)/shard_map/own/pallas_call | solution.py:145
  50.6 3.6 %all-to-all-start = ((f32[4,2,64,1024]{3,2,1,0:T(8,128)}), f32[4,2,64,1024]{3,2,1,0:T(8,128)S(1)}, u32[]{:S(2)}, u32[]{:S(2)}) async-start(f32[4,2,64,1024]{3,2,1,0:T(8,128)} %bitcast.27), calls=%async_computation | async-start | bytes 4194304 | tf_op jit(solution)/shard_map/all_to_all | solution.py:244
  54.2 7.0 %collective-permute-done.7.right_a.near0_a = bf16[1280,512]{1,0:T(8,128)(2,1)S(1)} collective-permute-done((bf16[1280,512]{1,0:T(8,128)(2,1)}, bf16[1280,512]{1,0:T(8,128)(2,1)S(1)}, u32[]{:S(2)}, u32[]{:S(2)}) %collective-permute-start.7) | collective-permute-done | bytes 1310752 | tf_op jit(solution)/shard_map/ppermute | solution.py:364
  61.2 2.0 collective-permute-start.8
  63.2 17.7 %all-to-all-done.refs_0_ = f32[4,2,64,1024]{3,2,1,0:T(8,128)S(1)} async-done(((f32[4,2,64,1024]{3,2,1,0:T(8,128)}), f32[4,2,64,1024]{3,2,1,0:T(8,128)S(1)}, u32[]{:S(2)}, u32[]{:S(2)}) %all-to-all-start) | async-done | bytes 2097184 | tf_op jit(solution)/shard_map/all_to_all | solution.py:244
  80.9 1.4 copy-done.3
  82.3 3.0 %add.104 = (f32[64,1024]{1,0:T(8,128)}, f32[64,1024]{1,0:T(8,128)}) custom-call(s32[4]{0:T(128)} %pad_add_fusion.1.meta, f32[4,2,64,1024]{3,2,1,0:T(8,128)} %copy-done.3), custom_call_target="tpu_custom_call" | custom-call | flops 1024 | bytes 1024 | tf_op jit(solution)/shard_map/add/pallas_call | solution.py:226
  85.3 5.4 %first.1.rest_0_ = f32[8,64,1024]{2,1,0:T(8,128)} custom-call(s32[4]{0:T(128)} %pad_add_fusion.1.meta, bf16[1024,1280]{1,0:T(8,128)(2,1)} %bitcast.21, bf16[512,1280]{1,0:T(8,128)(2,1)} %bitcast.24, bf16[1280,512]{1,0:T(8,128)(2,1)} %copy-done.4, bf16[1280,512]{1,0:T(8,128)(2,1)} %collective-permute-done.10.right_b.near0_b), custom_call_target="tpu_custom_call" | custom-call | flops 1024 | bytes 1024 | tf_op jit(solution)/shard_map/first/pallas_call | solution.py:145
  90.7 1.4 collective-permute-done.9
  92.1 3.9 %collective-permute-done.8.right_a.near1_a = bf16[1280,512]{1,0:T(8,128)(2,1)} collective-permute-done((bf16[1280,512]{1,0:T(8,128)(2,1)}, bf16[1280,512]{1,0:T(8,128)(2,1)}, u32[]{:S(2)}, u32[]{:S(2)}) %collective-permute-start.8) | collective-permute-done | bytes 1310752 | tf_op jit(solution)/shard_map/ppermute | solution.py:364
  96.0 1.4 slice_bitcast_fusion
  98.0 3.4 %collective-permute-done.12 = bf16[8,64,1280]{2,1,0:T(8,128)(2,1)S(1)} collective-permute-done((bf16[8,64,1280]{2,1,0:T(8,128)(2,1)S(1)}, bf16[8,64,1280]{2,1,0:T(8,128)(2,1)S(1)}, u32[]{:S(2)}, u32[]{:S(2)}) %collective-permute-start.12) | collective-permute-done | bytes 1310752 | tf_op jit(solution)/shard_map/ppermute | solution.py:365
  101.4 1.1 copy-done.6
  102.6 1.1 copy-done.5
  103.7 5.4 %second.1 = f32[8,64,1024]{2,1,0:T(8,128)} custom-call(s32[4]{0:T(128)} %pad_add_fusion.1.meta, bf16[1024,1280]{1,0:T(8,128)(2,1)} %bitcast.22, bf16[512,1280]{1,0:T(8,128)(2,1)} %bitcast.25, bf16[1280,512]{1,0:T(8,128)(2,1)} %collective-permute-done.8.right_a.near1_a, bf16[1280,512]{1,0:T(8,128)(2,1)} %copy-done.5, ...), custom_call_target="tpu_custom_call", output_to_operand_aliasing={{}: (5, {})} | custom-call | flops 1024 | bytes 1024 | tf_op jit(solution)/shard_map/second/pallas_call | solution.py:145
  109.0 3.6 %all-to-all-start.1 = ((f32[4,2,64,1024]{3,2,1,0:T(8,128)}), f32[4,2,64,1024]{3,2,1,0:T(8,128)S(1)}, u32[]{:S(2)}, u32[]{:S(2)}) async-start(f32[4,2,64,1024]{3,2,1,0:T(8,128)} %bitcast.26), calls=%async_computation.1 | async-start | bytes 4194304 | tf_op jit(solution)/shard_map/all_to_all | solution.py:244
  112.6 9.7 %across.1 = (f32[2,64,1024]{2,1,0:T(8,128)}, f32[2,64,1024]{2,1,0:T(8,128)}, f32[2,64,1024]{2,1,0:T(8,128)}, f32[2,64,1024]{2,1,0:T(8,128)}) custom-call(s32[4]{0:T(128)} %pad_add_fusion.1.meta, bf16[1024,1280]{1,0:T(8,128)(2,1)} %bitcast.14.left_a, bf16[512,1280]{1,0:T(8,128)(2,1)} %bitcast.28, bf16[1280,512]{1,0:T(8,128)(2,1)} %copy-done.4, ...), custom_call_target="tpu_custom_call" | custom-call | flops 1024 | bytes 1024 | tf_op jit(solution)/shard_map/across/pallas_call | solution.py:192
  122.3 2.3 %collective-permute-start.15 = (f32[2,64,1024]{2,1,0:T(8,128)}, f32[2,64,1024]{2,1,0:T(8,128)S(1)}, u32[]{:S(2)}, u32[]{:S(2)}) collective-permute-start(f32[2,64,1024]{2,1,0:T(8,128)} %get-tuple-element.59), channel_id=1, source_target_pairs={{0,2},{2,4},{4,6},{6,0},{1,3},{3,5},{5,7},{7,1},{8,10},{10,12},{12... | collective-permute-start | bytes 1572872 | tf_op jit(solution)/shard_map/ppermute | solution.py:250
  124.6 2.7 %collective-permute-start.16 = (f32[2,64,1024]{2,1,0:T(8,128)}, f32[2,64,1024]{2,1,0:T(8,128)S(1)}, u32[]{:S(2)}, u32[]{:S(2)}) collective-permute-start(f32[2,64,1024]{2,1,0:T(8,128)} %get-tuple-element.60), channel_id=1, source_target_pairs={{0,4},{2,6},{4,0},{6,2},{1,5},{3,7},{5,1},{7,3},{8,12},{10,14},{12... | collective-permute-start | bytes 1572872 | tf_op jit(solution)/shard_map/ppermute | solution.py:250
  127.2 1.5 collective-permute-start.17
  128.7 11.7 %all-to-all-done.1.refs_0_ = f32[4,2,64,1024]{3,2,1,0:T(8,128)S(1)} async-done(((f32[4,2,64,1024]{3,2,1,0:T(8,128)}), f32[4,2,64,1024]{3,2,1,0:T(8,128)S(1)}, u32[]{:S(2)}, u32[]{:S(2)}) %all-to-all-start.1) | async-done | bytes 2097184 | tf_op jit(solution)/shard_map/all_to_all | solution.py:244
  140.4 1.3 copy-done.2
  141.7 3.0 %add.105 = (f32[64,1024]{1,0:T(8,128)}, f32[64,1024]{1,0:T(8,128)}) custom-call(s32[4]{0:T(128)} %pad_add_fusion.1.meta, f32[4,2,64,1024]{3,2,1,0:T(8,128)} %copy-done.2), custom_call_target="tpu_custom_call" | custom-call | flops 1024 | bytes 1024 | tf_op jit(solution)/shard_map/add/pallas_call | solution.py:226
  144.7 0.6 collective-permute-start.13
  145.3 1.4 collective-permute-start.18
  146.7 7.4 %collective-permute-done.13.refs_1_ = f32[64,1024]{1,0:T(8,128)S(1)} collective-permute-done((f32[64,1024]{1,0:T(8,128)}, f32[64,1024]{1,0:T(8,128)S(1)}, u32[]{:S(2)}, u32[]{:S(2)}) %collective-permute-start.13) | collective-permute-done | bytes 262176 | tf_op jit(solution)/shard_map/ppermute | solution.py:239
  154.1 0.7 copy-done.10
  154.9 2.7 %gather.8 = (f32[64,1024]{1,0:T(8,128)}, f32[16,32,128]{2,1,0:T(8,128)}) custom-call(s32[4]{0:T(128)} %pad_add_fusion.1.meta, f32[64,1024]{1,0:T(8,128)} %get-tuple-element.56.refs_0_, f32[64,1024]{1,0:T(8,128)} %copy-done.10), custom_call_target="tpu_custom_call" | custom-call | flops 1024 | bytes 1024 | tf_op jit(solution)/shard_map/gather/pallas_call | solution.py:274
  157.5 3.5 %all-to-all-start.2 = ((f32[16,32,128]{2,1,0:T(8,128)}), f32[16,32,128]{2,1,0:T(8,128)S(1)}, u32[]{:S(2)}, u32[]{:S(2)}) async-start(f32[16,32,128]{2,1,0:T(8,128)} %get-tuple-element.58), calls=%async_computation.2 | async-start | bytes 524288 | tf_op jit(solution)/shard_map/all_to_all | solution.py:290
  161.1 0.9 collective-permute-done.16.refs_2_
  162.0 6.9 %all-to-all-done.2 = f32[16,32,128]{2,1,0:T(8,128)S(1)} async-done(((f32[16,32,128]{2,1,0:T(8,128)}), f32[16,32,128]{2,1,0:T(8,128)S(1)}, u32[]{:S(2)}, u32[]{:S(2)}) %all-to-all-start.2) | async-done | bytes 262176 | tf_op jit(solution)/shard_map/all_to_all | solution.py:290
  168.9 3.0 %add.106 = (f32[64,1024]{1,0:T(8,128)}, f32[64,1024]{1,0:T(8,128)}) custom-call(s32[4]{0:T(128)} %pad_add_fusion.1.meta, f32[2,64,1024]{2,1,0:T(8,128)} %get-tuple-element.63.refs_0_, f32[2,64,1024]{2,1,0:T(8,128)} %copy-done.8, f32[2,64,1024]{2,1,0:T(8,128)} %copy-done.9, f32[2,64,1024]{2,1,0:T(8,128)} %collective-permute-done.17.refs_3_), custom_call_target="tpu_custom_call" | custom-call | flops 1024 | bytes 1024 | tf_op jit(solution)/shard_map/add/pallas_call | solution.py:226
  171.9 0.5 collective-permute-start.19
  172.4 4.8 %collective-permute-start.14 = (f32[512,128]{1,0:T(8,128)S(1)}, f32[512,128]{1,0:T(8,128)S(1)}, u32[]{:S(2)}, u32[]{:S(2)}) collective-permute-start(f32[512,128]{1,0:T(8,128)S(1)} %bitcast.31), channel_id=1, source_target_pairs={{0,32},{32,64},{64,96},{96,128},{128,160},{160,192},{192,224},{48,... | collective-permute-start | bytes 786440 | tf_op jit(solution)/shard_map/ppermute | solution.py:385
  177.2 2.8 %collective-permute-done.19.refs_1_ = f32[64,1024]{1,0:T(8,128)S(1)} collective-permute-done((f32[64,1024]{1,0:T(8,128)}, f32[64,1024]{1,0:T(8,128)S(1)}, u32[]{:S(2)}, u32[]{:S(2)}) %collective-permute-start.19) | collective-permute-done | bytes 262176 | tf_op jit(solution)/shard_map/ppermute | solution.py:239
  180.0 0.7 copy-done.11
  180.7 2.5 %gather.9 = (f32[64,1024]{1,0:T(8,128)}, f32[16,32,128]{2,1,0:T(8,128)}) custom-call(s32[4]{0:T(128)} %pad_add_fusion.1.meta, f32[64,1024]{1,0:T(8,128)} %get-tuple-element.67.refs_0_, f32[64,1024]{1,0:T(8,128)} %copy-done.11), custom_call_target="tpu_custom_call" | custom-call | flops 1024 | bytes 1024 | tf_op jit(solution)/shard_map/gather/pallas_call | solution.py:274
  183.2 1.5 collective-permute-start.20
  184.7 3.5 %all-to-all-start.3 = ((f32[16,32,128]{2,1,0:T(8,128)}), f32[16,32,128]{2,1,0:T(8,128)S(1)}, u32[]{:S(2)}, u32[]{:S(2)}) async-start(f32[16,32,128]{2,1,0:T(8,128)} %get-tuple-element.69), calls=%async_computation.3 | async-start | bytes 524288 | tf_op jit(solution)/shard_map/all_to_all | solution.py:290
  188.3 0.6 dynamic_slice.3
  188.9 0.6 gather_fusion
  189.6 6.6 %all-to-all-done.3 = f32[16,32,128]{2,1,0:T(8,128)S(1)} async-done(((f32[16,32,128]{2,1,0:T(8,128)}), f32[16,32,128]{2,1,0:T(8,128)S(1)}, u32[]{:S(2)}, u32[]{:S(2)}) %all-to-all-start.3) | async-done | bytes 262176 | tf_op jit(solution)/shard_map/all_to_all | solution.py:290
  196.1 5.5 %collective-permute-start.21 = (f32[512,128]{1,0:T(8,128)S(1)}, f32[512,128]{1,0:T(8,128)S(1)}, u32[]{:S(2)}, u32[]{:S(2)}) collective-permute-start(f32[512,128]{1,0:T(8,128)S(1)} %bitcast.29), channel_id=1, source_target_pairs={{0,32},{32,64},{64,96},{96,128},{128,160},{160,192},{192,224},{1,3... | collective-permute-start | bytes 786440 | tf_op jit(solution)/shard_map/ppermute | solution.py:389
  201.6 0.7 and_convert_fusion
  202.3 0.6 pad_add_fusion.flags
  202.9 4.1 %collective-permute-done.21.near = f32[512,128]{1,0:T(8,128)S(1)} collective-permute-done((f32[512,128]{1,0:T(8,128)S(1)}, f32[512,128]{1,0:T(8,128)S(1)}, u32[]{:S(2)}, u32[]{:S(2)}) %collective-permute-start.21) | collective-permute-done | bytes 262176 | tf_op jit(solution)/shard_map/ppermute | solution.py:389
  207.1 0.7 copy-done.15
  207.8 3.9 %assemble.1 = f32[64,5120]{1,0:T(8,128)} custom-call(s32[6]{0:T(128)} %pad_add_fusion.flags, f32[512,128]{1,0:T(8,128)} %copy-done.13, f32[512,128]{1,0:T(8,128)} %copy-done.15, f32[512,128]{1,0:T(8,128)} %bitcast.30, f32[64,1024]{1,0:T(8,128)} %get-tuple-element.72.rows2, f32[64,1024]{1,0:T(8,128)} %copy-done.14, f32[64,1024]{1,0:T(8,128)} %get-tuple-element.45.rows0_a, ...), custom_call_target="tpu_custom_call" | custom-call | flops 1024 | bytes 1024 | tf_op jit(solution)/shard_map/assemble/pallas_call | solution.py:318
  (46 shorter events, 1.4 us)
Async XLA Ops:
  4.7 3.8 %collective-permute-start.1 = (f32[3,1024]{1,0:T(4,128)S(1)}, f32[3,1024]{1,0:T(4,128)S(1)}, u32[]{:S(2)}, u32[]{:S(2)}) collective-permute-start(f32[3,1024]{1,0:T(4,128)S(1)} %pad_maximum_fusion), channel_id=1, source_target_pairs={{0,8},{1,9},{8,0},{9,1},{2,10},{3,11},{10,2},{11,3},{4,12},{5,13},... | collective-permute-start | bytes 36872 | tf_op jit(solution)/shard_map/ppermute | solution.py:33
  6.3 3.2 %collective-permute-start.2 = (f32[3,1024]{1,0:T(4,128)S(1)}, f32[3,1024]{1,0:T(4,128)S(1)}, u32[]{:S(2)}, u32[]{:S(2)}) collective-permute-start(f32[3,1024]{1,0:T(4,128)S(1)} %pad_maximum_fusion), channel_id=1, source_target_pairs={{0,9},{1,8},{8,1},{9,0},{2,11},{3,10},{10,3},{11,2},{4,13},{5,12},... | collective-permute-start | bytes 36872 | tf_op jit(solution)/shard_map/ppermute | solution.py:33
  6.3 3.2 %collective-permute-start = (f32[3,1024]{1,0:T(4,128)S(1)}, f32[3,1024]{1,0:T(4,128)S(1)}, u32[]{:S(2)}, u32[]{:S(2)}) collective-permute-start(f32[3,1024]{1,0:T(4,128)S(1)} %pad_maximum_fusion), channel_id=1, source_target_pairs={{0,1},{1,0},{8,9},{9,8},{2,3},{3,2},{10,11},{11,10},{4,5},{5,4},{1... | collective-permute-start | bytes 36872 | tf_op jit(solution)/shard_map/ppermute | solution.py:33
  9.5 5.2 %collective-permute-start.5 = (f32[3,1024]{1,0:T(4,128)S(1)}, f32[3,1024]{1,0:T(4,128)S(1)}, u32[]{:S(2)}, u32[]{:S(2)}) collective-permute-start(f32[3,1024]{1,0:T(4,128)S(1)} %add_add_fusion.1), channel_id=1, source_target_pairs={{0,6},{2,0},{4,2},{6,4},{1,7},{3,1},{5,3},{7,5},{8,14},{10,8},{12,... | collective-permute-start | bytes 36872 | tf_op jit(solution)/shard_map/ppermute | solution.py:37
  12.4 5.2 %collective-permute-start.4 = (f32[3,1024]{1,0:T(4,128)S(1)}, f32[3,1024]{1,0:T(4,128)S(1)}, u32[]{:S(2)}, u32[]{:S(2)}) collective-permute-start(f32[3,1024]{1,0:T(4,128)S(1)} %add_add_fusion.1), channel_id=1, source_target_pairs={{0,4},{2,6},{4,0},{6,2},{1,5},{3,7},{5,1},{7,3},{8,12},{10,14},{12... | collective-permute-start | bytes 36872 | tf_op jit(solution)/shard_map/ppermute | solution.py:37
  13.2 4.9 %collective-permute-start.3 = (f32[3,1024]{1,0:T(4,128)S(1)}, f32[3,1024]{1,0:T(4,128)S(1)}, u32[]{:S(2)}, u32[]{:S(2)}) collective-permute-start(f32[3,1024]{1,0:T(4,128)S(1)} %add_add_fusion.1), channel_id=1, source_target_pairs={{0,2},{2,4},{4,6},{6,0},{1,3},{3,5},{5,7},{7,1},{8,10},{10,12},{12... | collective-permute-start | bytes 36872 | tf_op jit(solution)/shard_map/ppermute | solution.py:37
  27.7 6.8 %collective-permute-start.6 = (bf16[1280,1024]{1,0:T(8,128)(2,1)}, bf16[1280,1024]{1,0:T(8,128)(2,1)S(1)}, u32[]{:S(2)}, u32[]{:S(2)}) collective-permute-start(bf16[1280,1024]{1,0:T(8,128)(2,1)} %get-tuple-element.40.right_a.zed_a), channel_id=1, source_target_pairs={{0,1},{1,0},{2,3},{3,2},{4,5},{5,4},{6,7},{7,6},{8,9},{9,8},{10,11... | collective-permute-start | bytes 7864328 | tf_op jit(solution)/shard_map/ppermute | solution.py:365
  27.7 33.5 %collective-permute-start.7 = (bf16[1280,512]{1,0:T(8,128)(2,1)}, bf16[1280,512]{1,0:T(8,128)(2,1)S(1)}, u32[]{:S(2)}, u32[]{:S(2)}) collective-permute-start(bf16[1280,512]{1,0:T(8,128)(2,1)} %get-tuple-element.42), channel_id=1, source_target_pairs={{32,0},{64,32},{96,64},{128,96},{160,128},{192,160},{224,192},{16,... | collective-permute-start | bytes 3932168 | tf_op jit(solution)/shard_map/ppermute | solution.py:364
  29.8 62.4 %collective-permute-start.9 = (bf16[2,8,64,1280]{3,2,1,0:T(8,128)(2,1)}, bf16[2,8,64,1280]{3,2,1,0:T(8,128)(2,1)}, u32[]{:S(2)}, u32[]{:S(2)}) collective-permute-start(bf16[2,8,64,1280]{3,2,1,0:T(8,128)(2,1)} %get-tuple-element.39), channel_id=1, source_target_pairs={{0,16},{16,0},{32,48},{48,32},{64,80},{80,64},{96,112},{112,96},{1... | collective-permute-start | bytes 7864328 | tf_op jit(solution)/shard_map/ppermute | solution.py:366
  34.6 1.5 copy-start.1
  50.6 30.3 %all-to-all-start = ((f32[4,2,64,1024]{3,2,1,0:T(8,128)}), f32[4,2,64,1024]{3,2,1,0:T(8,128)S(1)}, u32[]{:S(2)}, u32[]{:S(2)}) async-start(f32[4,2,64,1024]{3,2,1,0:T(8,128)} %bitcast.27), calls=%async_computation | async-start | bytes 4194304 | tf_op jit(solution)/shard_map/all_to_all | solution.py:244
  61.2 24.1 %copy-start.4 = (bf16[1280,512]{1,0:T(8,128)(2,1)}, bf16[1280,512]{1,0:T(8,128)(2,1)S(1)}, u32[]{:S(2)}) copy-start(bf16[1280,512]{1,0:T(8,128)(2,1)S(1)} %collective-permute-done.7.right_a.near0_a) | copy-start | bytes 3932164
  61.2 24.1 %collective-permute-start.10 = (bf16[1280,512]{1,0:T(8,128)(2,1)S(1)}, bf16[1280,512]{1,0:T(8,128)(2,1)}, u32[]{:S(2)}, u32[]{:S(2)}) collective-permute-start(bf16[1280,512]{1,0:T(8,128)(2,1)S(1)} %collective-permute-done.7.right_a.near0_a), channel_id=1, source_target_pairs={{0,1},{1,0},{2,3},{3,2},{4,5},{5,4},{6,7},{7,6},{8,9},{9,8},{10,11... | collective-permute-start | bytes 3932168 | tf_op jit(solution)/shard_map/ppermute | solution.py:365
  61.2 34.8 %collective-permute-start.8 = (bf16[1280,512]{1,0:T(8,128)(2,1)}, bf16[1280,512]{1,0:T(8,128)(2,1)}, u32[]{:S(2)}, u32[]{:S(2)}) collective-permute-start(bf16[1280,512]{1,0:T(8,128)(2,1)} %get-tuple-element.44), channel_id=1, source_target_pairs={{32,0},{64,32},{96,64},{128,96},{160,128},{192,160},{224,192},{16,... | collective-permute-start | bytes 3932168 | tf_op jit(solution)/shard_map/ppermute | solution.py:364
  80.9 1.4 copy-start.3
  97.4 4.0 %collective-permute-start.12 = (bf16[8,64,1280]{2,1,0:T(8,128)(2,1)S(1)}, bf16[8,64,1280]{2,1,0:T(8,128)(2,1)S(1)}, u32[]{:S(2)}, u32[]{:S(2)}) collective-permute-start(bf16[8,64,1280]{2,1,0:T(8,128)(2,1)S(1)} %slice_bitcast_fusion), channel_id=1, source_target_pairs={{0,1},{1,0},{2,3},{3,2},{4,5},{5,4},{6,7},{7,6},{8,9},{9,8},{10,11... | collective-permute-start | bytes 3932168 | tf_op jit(solution)/shard_map/ppermute | solution.py:365
  97.5 5.1 %collective-permute-start.11 = (bf16[1280,512]{1,0:T(8,128)(2,1)}, bf16[1280,512]{1,0:T(8,128)(2,1)S(1)}, u32[]{:S(2)}, u32[]{:S(2)}) collective-permute-start(bf16[1280,512]{1,0:T(8,128)(2,1)} %collective-permute-done.8.right_a.near1_a), channel_id=1, source_target_pairs={{0,1},{1,0},{2,3},{3,2},{4,5},{5,4},{6,7},{7,6},{8,9},{9,8},{10,11... | collective-permute-start | bytes 3932168 | tf_op jit(solution)/shard_map/ppermute | solution.py:365
  101.4 1.1 copy-start.6
  102.6 1.1 copy-start.5
  109.0 31.3 %all-to-all-start.1 = ((f32[4,2,64,1024]{3,2,1,0:T(8,128)}), f32[4,2,64,1024]{3,2,1,0:T(8,128)S(1)}, u32[]{:S(2)}, u32[]{:S(2)}) async-start(f32[4,2,64,1024]{3,2,1,0:T(8,128)} %bitcast.26), calls=%async_computation.1 | async-start | bytes 4194304 | tf_op jit(solution)/shard_map/all_to_all | solution.py:244
  122.3 38.8 %collective-permute-start.15 = (f32[2,64,1024]{2,1,0:T(8,128)}, f32[2,64,1024]{2,1,0:T(8,128)S(1)}, u32[]{:S(2)}, u32[]{:S(2)}) collective-permute-start(f32[2,64,1024]{2,1,0:T(8,128)} %get-tuple-element.59), channel_id=1, source_target_pairs={{0,2},{2,4},{4,6},{6,0},{1,3},{3,5},{5,7},{7,1},{8,10},{10,12},{12... | collective-permute-start | bytes 1572872 | tf_op jit(solution)/shard_map/ppermute | solution.py:250
  124.6 37.5 %collective-permute-start.16 = (f32[2,64,1024]{2,1,0:T(8,128)}, f32[2,64,1024]{2,1,0:T(8,128)S(1)}, u32[]{:S(2)}, u32[]{:S(2)}) collective-permute-start(f32[2,64,1024]{2,1,0:T(8,128)} %get-tuple-element.60), channel_id=1, source_target_pairs={{0,4},{2,6},{4,0},{6,2},{1,5},{3,7},{5,1},{7,3},{8,12},{10,14},{12... | collective-permute-start | bytes 1572872 | tf_op jit(solution)/shard_map/ppermute | solution.py:250
  127.2 34.8 %collective-permute-start.17 = (f32[2,64,1024]{2,1,0:T(8,128)}, f32[2,64,1024]{2,1,0:T(8,128)}, u32[]{:S(2)}, u32[]{:S(2)}) collective-permute-start(f32[2,64,1024]{2,1,0:T(8,128)} %get-tuple-element.61), channel_id=1, source_target_pairs={{0,6},{2,0},{4,2},{6,4},{1,7},{3,1},{5,3},{7,5},{8,14},{10,8},{12,... | collective-permute-start | bytes 1572872 | tf_op jit(solution)/shard_map/ppermute | solution.py:250
  140.4 1.3 copy-start.2
  144.7 9.5 %collective-permute-start.13 = (f32[64,1024]{1,0:T(8,128)}, f32[64,1024]{1,0:T(8,128)S(1)}, u32[]{:S(2)}, u32[]{:S(2)}) collective-permute-start(f32[64,1024]{1,0:T(8,128)} %get-tuple-element.57), channel_id=1, source_target_pairs={{0,8},{8,0},{1,9},{9,1},{2,10},{10,2},{3,11},{11,3},{4,12},{12,4},... | collective-permute-start | bytes 786440 | tf_op jit(solution)/shard_map/ppermute | solution.py:239
  145.3 15.8 %collective-permute-start.18 = (f32[64,1024]{1,0:T(8,128)}, f32[64,1024]{1,0:T(8,128)S(1)}, u32[]{:S(2)}, u32[]{:S(2)}) collective-permute-start(f32[64,1024]{1,0:T(8,128)} %get-tuple-element.62), channel_id=1, source_target_pairs={{0,8},{8,0},{1,9},{9,1},{2,10},{10,2},{3,11},{11,3},{4,12},{12,4},... | collective-permute-start | bytes 786440 | tf_op jit(solution)/shard_map/ppermute | solution.py:239
  154.1 0.7 copy-start.10
  154.8 33.4 %copy-start = (s32[16]{0:T(128)S(1)}, s32[16]{0:T(128)}, u32[]{:S(2)}) copy-start(s32[16]{0:T(128)} %param.5) | copy-start | bytes 196
  157.5 11.4 %all-to-all-start.2 = ((f32[16,32,128]{2,1,0:T(8,128)}), f32[16,32,128]{2,1,0:T(8,128)S(1)}, u32[]{:S(2)}, u32[]{:S(2)}) async-start(f32[16,32,128]{2,1,0:T(8,128)} %get-tuple-element.58), calls=%async_computation.2 | async-start | bytes 524288 | tf_op jit(solution)/shard_map/all_to_all | solution.py:290
  161.1 46.0 %copy-start.12 = (f32[64,1024]{1,0:T(8,128)}, f32[64,1024]{1,0:T(8,128)S(1)}, u32[]{:S(2)}) copy-start(f32[64,1024]{1,0:T(8,128)S(1)} %collective-permute-done.18.rows0_b) | copy-start | bytes 786436
  161.1 7.8 %copy-start.8 = (f32[2,64,1024]{2,1,0:T(8,128)}, f32[2,64,1024]{2,1,0:T(8,128)S(1)}, u32[]{:S(2)}) copy-start(f32[2,64,1024]{2,1,0:T(8,128)S(1)} %collective-permute-done.15.refs_1_) | copy-start | bytes 1572868
  162.0 6.9 %copy-start.9 = (f32[2,64,1024]{2,1,0:T(8,128)}, f32[2,64,1024]{2,1,0:T(8,128)S(1)}, u32[]{:S(2)}) copy-start(f32[2,64,1024]{2,1,0:T(8,128)S(1)} %collective-permute-done.16.refs_2_) | copy-start | bytes 1572868
  171.9 8.1 %collective-permute-start.19 = (f32[64,1024]{1,0:T(8,128)}, f32[64,1024]{1,0:T(8,128)S(1)}, u32[]{:S(2)}, u32[]{:S(2)}) collective-permute-start(f32[64,1024]{1,0:T(8,128)} %get-tuple-element.68), channel_id=1, source_target_pairs={{0,8},{8,0},{1,9},{9,1},{2,10},{10,2},{3,11},{11,3},{4,12},{12,4},... | collective-permute-start | bytes 786440 | tf_op jit(solution)/shard_map/ppermute | solution.py:239
  172.4 17.2 %collective-permute-start.14 = (f32[512,128]{1,0:T(8,128)S(1)}, f32[512,128]{1,0:T(8,128)S(1)}, u32[]{:S(2)}, u32[]{:S(2)}) collective-permute-start(f32[512,128]{1,0:T(8,128)S(1)} %bitcast.31), channel_id=1, source_target_pairs={{0,32},{32,64},{64,96},{96,128},{128,160},{160,192},{192,224},{48,... | collective-permute-start | bytes 786440 | tf_op jit(solution)/shard_map/ppermute | solution.py:385
  180.0 0.7 copy-start.11
  183.2 12.9 %collective-permute-start.20 = (f32[64,1024]{1,0:T(8,128)}, f32[64,1024]{1,0:T(8,128)S(1)}, u32[]{:S(2)}, u32[]{:S(2)}) collective-permute-start(f32[64,1024]{1,0:T(8,128)} %get-tuple-element.70), channel_id=1, source_target_pairs={{0,16},{16,0},{32,48},{48,32},{64,80},{80,64},{96,112},{112,96},{1... | collective-permute-start | bytes 786440 | tf_op jit(solution)/shard_map/ppermute | solution.py:388
  184.7 11.4 %all-to-all-start.3 = ((f32[16,32,128]{2,1,0:T(8,128)}), f32[16,32,128]{2,1,0:T(8,128)S(1)}, u32[]{:S(2)}, u32[]{:S(2)}) async-start(f32[16,32,128]{2,1,0:T(8,128)} %get-tuple-element.69), calls=%async_computation.3 | async-start | bytes 524288 | tf_op jit(solution)/shard_map/all_to_all | solution.py:290
  189.5 17.5 %copy-start.13 = (f32[512,128]{1,0:T(8,128)}, f32[512,128]{1,0:T(8,128)S(1)}, u32[]{:S(2)}) copy-start(f32[512,128]{1,0:T(8,128)S(1)} %collective-permute-done.14.far) | copy-start | bytes 786436
  196.1 10.9 %copy-start.7 = (f32[16,32,128]{2,1,0:T(8,128)}, f32[16,32,128]{2,1,0:T(8,128)S(1)}, u32[]{:S(2)}) copy-start(f32[16,32,128]{2,1,0:T(8,128)S(1)} %all-to-all-done.3) | copy-start | bytes 786436
  196.1 10.9 %copy-start.14 = (f32[64,1024]{1,0:T(8,128)}, f32[64,1024]{1,0:T(8,128)S(1)}, u32[]{:S(2)}) copy-start(f32[64,1024]{1,0:T(8,128)S(1)} %collective-permute-done.20.beside) | copy-start | bytes 786436
  196.1 10.9 %collective-permute-start.21 = (f32[512,128]{1,0:T(8,128)S(1)}, f32[512,128]{1,0:T(8,128)S(1)}, u32[]{:S(2)}, u32[]{:S(2)}) collective-permute-start(f32[512,128]{1,0:T(8,128)S(1)} %bitcast.29), channel_id=1, source_target_pairs={{0,32},{32,64},{64,96},{96,128},{128,160},{160,192},{192,224},{1,3... | collective-permute-start | bytes 786440 | tf_op jit(solution)/shard_map/ppermute | solution.py:389
  207.0 0.7 copy-start.15

commit v8 on v7

--- a/solution.py
+++ b/solution.py
@@ -67,13 +67,11 @@
     return jnp.dot(left, right, preferred_element_type=jnp.float32)
 
 
-def standard_kernel(meta, dosage, observed, stats, zed, zed0, zed1, turned):
+def standard_kernel(meta, dosage, observed, stats, zed, turned):
     weight = observed[...].astype(jnp.float32)
     values = dosage[...].astype(jnp.float32)
     z = (weight * (values - stats[0:1, :]) * stats[1:2, :]).astype(jnp.bfloat16)
     zed[...] = z
-    zed0[...] = z[:, :HALF]
-    zed1[...] = z[:, HALF:]
     columns = z.T
     for p in range(PIECES):
         for k in range(2):
@@ -88,13 +86,13 @@
     return pl.pallas_call(
         standard_kernel,
         name="standardize",
-        out_shape=(bf16(DEPTH, B), bf16(DEPTH, HALF), bf16(DEPTH, HALF))
+        out_shape=(bf16(DEPTH, B),)
         + (bf16(2, PIECES, ROWS, DEPTH),),
         grid_spec=pltpu.PrefetchScalarGridSpec(
             num_scalar_prefetch=1,
             grid=(DEPTH // rows,),
             in_specs=[block(B), block(B), whole((2, B))],
-            out_specs=(block(B), block(HALF), block(HALF), turned),
+            out_specs=(block(B), turned),
         ),
         compiler_params=params(),
         cost_estimate=cost(4 * DEPTH * B, 12 * DEPTH * B),
@@ -134,13 +132,12 @@
     )(meta, zed)
 
 
-def product_kernel(meta, left_a, left_b, right_a, right_b, *rest):
+def product_kernel(meta, left_a, left_b, right_a, right_b, out):
     acc = matmul(left_a[...], right_a[...]) + matmul(left_b[...], right_b[...])
-    rest[-1][...] = acc.reshape(PIECES, ROWS, STEP)
-
-
-def product(meta, left, right, name, first=0, before=()):
-    columns = right[0].shape[1]
+    out[...] = acc.reshape(PIECES, ROWS, STEP)
+
+
+def product(meta, left, right, name):
     block = pl.BlockSpec((DEPTH, STEP), lambda j, m: (0, j))
     return pl.pallas_call(
         product_kernel,
@@ -148,32 +145,25 @@
         out_shape=f32(PIECES, ROWS, B),
         grid_spec=pltpu.PrefetchScalarGridSpec(
             num_scalar_prefetch=1,
-            grid=(columns // STEP,),
-            in_specs=[whole(LEFT)] * 2
-            + [block] * 2
-            + [pl.BlockSpec(memory_space=pl.ANY)] * len(before),
-            out_specs=pl.BlockSpec((PIECES, ROWS, STEP), lambda j, m: (0, 0, j + first // STEP)),
-        ),
-        input_output_aliases={5: 0} if before else {},
-        compiler_params=params(),
-        cost_estimate=cost(2 * DEPTH * B * columns, 4 * DEPTH * B + 4 * B * columns),
-    )(meta, *flat(*left), *right, *before)
-
-
-def across_kernel(
-    meta, left_a, left_b, near0_a, near0_b, near1_a, near1_b, zed_a, zed_b, *rest
-):
+            grid=(B // STEP,),
+            in_specs=[whole(LEFT)] * 2 + [block] * 2,
+            out_specs=pl.BlockSpec((PIECES, ROWS, STEP), lambda j, m: (0, 0, j)),
+        ),
+        compiler_params=params(),
+        cost_estimate=cost(2 * DEPTH * B * B, 8 * DEPTH * B + 4 * B * B),
+    )(meta, *flat(*left), *right)
+
+
+def across_kernel(meta, left_a, left_b, near_a, near_b, zed_a, zed_b, *rest):
     outs, right = rest[:4], rest[4]
     odd = meta[1] == 1
-    early = pl.program_id(0) < HALF // STEP
 
     def take(a, b):
         right[:DEPTH] = a[...]
         right[DEPTH:] = b[...]
 
     pl.when(odd)(lambda: take(zed_a, zed_b))
-    pl.when(~odd & early)(lambda: take(near0_a, near0_b))
-    pl.when(~odd & ~early)(lambda: take(near1_a, near1_b))
+    pl.when(~odd)(lambda: take(near_a, near_b))
     acc = matmul(left_a[...], right[:DEPTH]) + matmul(left_b[...], right[DEPTH:])
     acc = acc.reshape(4, 2, ROWS, STEP)
     for x in range(4):
@@ -184,10 +174,7 @@
                 outs[k][...] = acc[(x + k) % 4]
 
 
-def across_product(meta, left, near0, near1, zed):
-    half = HALF // STEP
-    first = pl.BlockSpec((DEPTH, STEP), lambda j, m: (0, jnp.minimum(j, half - 1)))
-    second = pl.BlockSpec((DEPTH, STEP), lambda j, m: (0, jnp.maximum(j - half, 0)))
+def across_product(meta, left, near, zed):
     block = pl.BlockSpec((DEPTH, STEP), lambda j, m: (0, j))
     return pl.pallas_call(
         across_kernel,
@@ -196,13 +183,13 @@
         grid_spec=pltpu.PrefetchScalarGridSpec(
             num_scalar_prefetch=1,
             grid=(B // STEP,),
-            in_specs=[whole(LEFT)] * 2 + [first] * 2 + [second] * 2 + [block] * 2,
+            in_specs=[whole(LEFT)] * 2 + [block] * 4,
             out_specs=(pl.BlockSpec((2, ROWS, STEP), lambda j, m: (0, 0, j)),) * 4,
             scratch_shapes=[pltpu.VMEM((2 * DEPTH, STEP), jnp.bfloat16)],
         ),
         compiler_params=params(),
         cost_estimate=cost(2 * DEPTH * B * B, 12 * DEPTH * B + 4 * B * B),
-    )(meta, *flat(*left), *near0, *near1, *zed)
+    )(meta, *flat(*left), *near, *zed)
 
 
 def after(value, *others):
@@ -360,31 +347,23 @@
     spread = second - first * mean
     stats = jnp.stack([mean, lax.rsqrt(spread + eps * cnt)])
 
-    zed, zed0, zed1, turned = standardize(meta, dosage, observed, stats)
-    along = lambda t: lax.ppermute(t, SNP, EVEN_DOWN + ODD_UP)
+    zed, turned = standardize(meta, dosage, observed, stats)
     swap = lambda t: lax.ppermute(t, "core", SWAP)
     other = lax.ppermute(turned, SNP, TO_OTHER)
-    near0 = along(zed0)
+    near = lax.ppermute(zed, SNP, EVEN_DOWN + ODD_UP)
     zed_b = swap(zed)
     own = (turned, turn(meta, zed_b))
-    rows0 = product(meta, own, (zed, zed_b), "own")
-    near0 = after(near0, rows0)
-    near1 = along(after(zed1, near0))
-    rows0 = fold(meta, rows0)
-    near0 = after((near0, swap(near0)), rows0[0])
-    rows2 = product(meta, own, near0, "first")
-    near1, other = after((near1, other), rows2)
-    near1 = (near1, swap(near1))
+    rows0 = fold(meta, product(meta, own, (zed, zed_b), "own"))
+    near, other = after((near, other), rows0[0])
+    near = (near, swap(near))
     other = (other, swap(other[1]))
-    near1 = after(near1, other[1])
-    rows2 = product(meta, own, near1, "second", HALF, (rows2,))
-    other = after(other, rows2)
-    pieces = across_product(meta, other, near0, near1, (zed, zed_b))
+    rows2 = product(meta, own, after(near, other[1]), "along")
+    pieces = across_product(meta, after(other, rows2), near, (zed, zed_b))
     rows2 = fold(meta, rows2, pieces[0])
     rows2, turned2 = gather(meta, *rows2)
     far = lax.ppermute(turned2, SNP, EVEN_UP + ODD_DOWN)
-    rows1 = fold_pieces(meta, pieces, turned2, rows0[1])
-    rows1, turned1 = gather(meta, *rows1)
+    rows1 = fold_pieces(meta, pieces, rows2, rows0[1])
+    rows1, turned1 = gather(meta, *after(rows1, turned2))
     beside = lax.ppermute(rows1, SNP, TO_OTHER)
     near = lax.ppermute(after(turned1, far, beside), SNP, EVEN_UP)
     flags = jnp.concatenate([kept_flags(band, mine), odd]).astype(jnp.int32)

time: 215 us -> 213 us (level)
  blocking collectives: 0 us -> 42.8 us
  waiting for transfers between devices: 79.8 us -> 56.5 us
  starting transfers between devices: 51.2 us -> 36.6 us
  Pallas kernels: 61.9 us -> 57.9 us
    all_to_all x0 -> x2, blocking collectives: none -> 42.8 us  [the longest x1 31.4 us: fold(): parts = lax.all_to_all(parts.reshape(4, 2, rows, columns), 'x', 0, 0)]
    all_to_all x2 -> x1, waiting for transfers between devices: 29.4 us -> 12 us  [fold(): parts = lax.all_to_all(parts.reshape(4, 2, rows, columns), 'x', 0, 0)]
    ppermute x2 -> x1, waiting for transfers between devices: 10.8 us -> 3.18 us  [on_device(): near = lax.ppermute(zed, SNP, EVEN_DOWN + ODD_UP)]
    all_to_all x2 -> x1, waiting for transfers between devices: 13.4 us -> 6.55 us  [gather(): return (rows, lax.all_to_all(packed, SAMP, 0, 0).reshape(HALF, 2 * ROWS))]
    ppermute x1, waiting for transfers between devices: 1.44 us -> 5.4 us  [on_device(): other = lax.ppermute(turned, SNP, TO_OTHER)]
    ppermute x3, waiting for transfers between devices: 0.93 us -> 4.61 us  [fold_pieces(): lax.ppermute(pieces[k], 'x', [(i, (i + k) % 4) for i in range(4)])]
    all_to_all x2 -> x1, starting transfers between devices: 7.21 us -> 3.61 us  [fold(): parts = lax.all_to_all(parts.reshape(4, 2, rows, columns), 'x', 0, 0)]
    all_to_all x2 -> x1, starting transfers between devices: 7.06 us -> 3.53 us  [gather(): return (rows, lax.all_to_all(packed, SAMP, 0, 0).reshape(HALF, 2 * ROWS))]
  transfers between devices with their start and end apart: 26 -> 22, of which waited for: 17 -> 13; matrix products, arithmetic and copies ran while one was open for 1% -> 1% of each run, Pallas kernels for 19% -> 17%
where the time goes in v8:
time: 213 us; the launch traced here: 211 us
  Pallas kernels  57.9 us (27%)
  waiting for transfers between devices  56.5 us (27%)
  blocking collectives  42.8 us (20%)
  starting transfers between devices  36.6 us (17%)
  local copies, waits for them, and re-layouts  9.78 us (5%)
  other arithmetic  7.15 us (3%)
    all_to_all x1, blocking collectives, fold(): parts = lax.all_to_all(parts.reshape(4, 2, rows, columns), 'x', 0, 0)  31.4 us
    pallas_call x2, Pallas kernels, product(): pl.pallas_call(product_kernel, name=name, out_shape=f32(PIECES, ROWS, B),...  15.7 us
    all_to_all x1, waiting for transfers between devices, fold(): parts = lax.all_to_all(parts.reshape(4, 2, rows, columns), 'x', 0, 0)  12 us
    all_to_all x1, blocking collectives, gather(): return (rows, lax.all_to_all(packed, SAMP, 0, 0).reshape(HALF, 2 * ROWS))  11.4 us
    pallas_call x1, Pallas kernels, across_product(): pl.pallas_call(across_kernel, name='across', out_shape=(f32(2, ROWS, B),)...  9.48 us
    pallas_call x3, Pallas kernels, add(): pl.pallas_call(add_kernel, name='add', out_shape=(f32(rows, columns),) *...  8.93 us
    unnamed x34, local copies, waits for them, and re-layouts  8.46 us
    pallas_call x1, Pallas kernels, standardize(): pl.pallas_call(standard_kernel, name='standardize', out_shape=(bf16(DEPTH...  8.12 us
  transfers between devices with their start and end apart: 22, of which 13 were waited for; matrix products, arithmetic and copies ran while one was open for 1% of the time, Pallas kernels for 17%

profile of v8, /device:TPU:64, one launch (start us, length us, event | category | flops | bytes accessed | tf_op | source)
XLA Modules:
  0.0 210.9 jit_solution(18433809625090448270)
XLA Ops:
  0.0 4.7 %fusion.1 = (f32[1024]{0:T(1024)S(1)}, f32[1024]{0:T(1024)S(1)}, f32[1024]{0:T(1024)S(1)}) fusion(bf16[1280,1024]{1,0:T(8,128)(2,1)} %dosage.1, s32[1280,1024]{1,0:T(8,128)} %observed.1), kind=kLoop, calls=%fused_computation.5 | loop fusion | flops 9171968 | bytes 7876608 | tf_op jit(solution)/shard_map/reduce_sum | solution.py:341
  4.7 1.7 collective-permute-start.1
  6.3 0.0 collective-permute-start.2
  6.3 0.6 collective-permute-start
  6.9 1.6 collective-permute-done.1
  8.5 1.0 collective-permute-done.2
  9.5 0.0 collective-permute-done
  9.5 2.8 %collective-permute-start.5 = (f32[3,1024]{1,0:T(4,128)S(1)}, f32[3,1024]{1,0:T(4,128)S(1)}, u32[]{:S(2)}, u32[]{:S(2)}) collective-permute-start(f32[3,1024]{1,0:T(4,128)S(1)} %add_add_fusion.1), channel_id=1, source_target_pairs={{0,6},{2,0},{4,2},{6,4},{1,7},{3,1},{5,3},{7,5},{8,14},{10,8},{12,... | collective-permute-start | bytes 36872 | tf_op jit(solution)/shard_map/ppermute | solution.py:37
  12.4 0.8 collective-permute-start.4
  13.2 0.9 collective-permute-start.3
  14.1 0.6 pad_add_fusion.1.meta
  14.6 0.0 collective-permute-done.5
  14.6 3.0 %collective-permute-done.4 = f32[3,1024]{1,0:T(4,128)S(1)} collective-permute-done((f32[3,1024]{1,0:T(4,128)S(1)}, f32[3,1024]{1,0:T(4,128)S(1)}, u32[]{:S(2)}, u32[]{:S(2)}) %collective-permute-start.4) | collective-permute-done | bytes 12320 | tf_op jit(solution)/shard_map/ppermute | solution.py:37
  17.6 0.5 collective-permute-done.3
  18.2 0.6 pad_maximum_fusion.1.stats
  18.8 8.1 %standardize.1 = (bf16[1280,1024]{1,0:T(8,128)(2,1)}, bf16[2,8,64,1280]{3,2,1,0:T(8,128)(2,1)}) custom-call(s32[4]{0:T(128)} %pad_add_fusion.1.meta, bf16[1280,1024]{1,0:T(8,128)(2,1)} %dosage.1, s32[1280,1024]{1,0:T(8,128)} %observed.1, f32[2,1024]{1,0:T(2,128)} %pad_maximum_fusion.1.stats), custom_call_target="tpu_custom_call" | custom-call | flops 1024 | bytes 1024 | tf_op jit(solution)/shard_map/standardize/pallas_call | solution.py:86
  26.9 2.9 %collective-permute-start.8 = (bf16[2,8,64,1280]{3,2,1,0:T(8,128)(2,1)}, bf16[2,8,64,1280]{3,2,1,0:T(8,128)(2,1)S(1)}, u32[]{:S(2)}, u32[]{:S(2)}) collective-permute-start(bf16[2,8,64,1280]{3,2,1,0:T(8,128)(2,1)} %get-tuple-element.35), channel_id=1, source_target_pairs={{0,16},{16,0},{32,48},{48,32},{64,80},{80,64},{96,112},{112,96},{1... | collective-permute-start | bytes 7864328 | tf_op jit(solution)/shard_map/ppermute | solution.py:352
  29.8 2.0 collective-permute-start.7
  31.8 0.2 collective-permute-done.6.zed.right_b.zed_b
  32.0 1.5 copy-done.1
  33.5 6.7 %turn.1 = bf16[8,64,1280]{2,1,0:T(8,128)(2,1)} custom-call(s32[4]{0:T(128)} %pad_add_fusion.1.meta, bf16[1280,1024]{1,0:T(8,128)(2,1)} %copy-done.1), custom_call_target="tpu_custom_call" | custom-call | flops 1024 | bytes 1024 | tf_op jit(solution)/shard_map/turn/pallas_call | solution.py:120
  40.3 7.8 %own.1 = f32[8,64,1024]{2,1,0:T(8,128)} custom-call(s32[4]{0:T(128)} %pad_add_fusion.1.meta, bf16[1024,1280]{1,0:T(8,128)(2,1)} %bitcast.22, bf16[512,1280]{1,0:T(8,128)(2,1)} %bitcast.20, bf16[1280,1024]{1,0:T(8,128)(2,1)} %get-tuple-element.36.right_a.zed_a, bf16[1280,1024]{1,0:T(8,128)(2,1)} %copy-done.1), custom_call_target="tpu_custom_call" | custom-call | flops 1024 | bytes 1024 | tf_op jit(solution)/shard_map/own/pallas_call | solution.py:142
  48.1 31.4 %all_to_all.20.refs_0_ = f32[4,2,64,1024]{3,2,1,0:T(8,128)} all-to-all(f32[4,2,64,1024]{3,2,1,0:T(8,128)} %bitcast.25), channel_id=1, replica_groups=mesh['z'=8,'yh'=2,'yl'=2,'x'=4,'core'=2] {'x'}, dimensions={0} | all-to-all | bytes 4194304 | tf_op jit(solution)/shard_map/all_to_all | solution.py:231
  79.5 3.0 %add.104 = (f32[64,1024]{1,0:T(8,128)}, f32[64,1024]{1,0:T(8,128)}) custom-call(s32[4]{0:T(128)} %pad_add_fusion.1.meta, f32[4,2,64,1024]{3,2,1,0:T(8,128)} %all_to_all.20.refs_0_), custom_call_target="tpu_custom_call" | custom-call | flops 1024 | bytes 1024 | tf_op jit(solution)/shard_map/add/pallas_call | solution.py:213
  82.5 5.4 %collective-permute-done.8 = bf16[2,8,64,1280]{3,2,1,0:T(8,128)(2,1)S(1)} collective-permute-done((bf16[2,8,64,1280]{3,2,1,0:T(8,128)(2,1)}, bf16[2,8,64,1280]{3,2,1,0:T(8,128)(2,1)S(1)}, u32[]{:S(2)}, u32[]{:S(2)}) %collective-permute-start.8) | collective-permute-done | bytes 2621472 | tf_op jit(solution)/shard_map/ppermute | solution.py:352
  87.9 3.2 %collective-permute-done.7.right_a.near_a = bf16[1280,1024]{1,0:T(8,128)(2,1)S(1)} collective-permute-done((bf16[1280,1024]{1,0:T(8,128)(2,1)}, bf16[1280,1024]{1,0:T(8,128)(2,1)S(1)}, u32[]{:S(2)}, u32[]{:S(2)}) %collective-permute-start.7) | collective-permute-done | bytes 2621472 | tf_op jit(solution)/shard_map/ppermute | solution.py:353
  91.1 0.1 slice_bitcast_fusion
  91.2 0.6 collective-permute-start.10
  91.8 6.1 %collective-permute-done.10 = bf16[8,64,1280]{2,1,0:T(8,128)(2,1)S(1)} collective-permute-done((bf16[8,64,1280]{2,1,0:T(8,128)(2,1)S(1)}, bf16[8,64,1280]{2,1,0:T(8,128)(2,1)S(1)}, u32[]{:S(2)}, u32[]{:S(2)}) %collective-permute-start.10) | collective-permute-done | bytes 1310752 | tf_op jit(solution)/shard_map/ppermute | solution.py:351
  97.9 1.1 copy-done.6
  98.9 1.6 copy-done.3
  100.5 7.9 %along.1 = f32[8,64,1024]{2,1,0:T(8,128)} custom-call(s32[4]{0:T(128)} %pad_add_fusion.1.meta, bf16[1024,1280]{1,0:T(8,128)(2,1)} %bitcast.23, bf16[512,1280]{1,0:T(8,128)(2,1)} %bitcast.21, bf16[1280,1024]{1,0:T(8,128)(2,1)} %copy-done.2, bf16[1280,1024]{1,0:T(8,128)(2,1)} %copy-done.3), custom_call_target="tpu_custom_call" | custom-call | flops 1024 | bytes 1024 | tf_op jit(solution)/shard_map/along/pallas_call | solution.py:142
  108.4 3.6 %all-to-all-start.1 = ((f32[4,2,64,1024]{3,2,1,0:T(8,128)}), f32[4,2,64,1024]{3,2,1,0:T(8,128)S(1)}, u32[]{:S(2)}, u32[]{:S(2)}) async-start(f32[4,2,64,1024]{3,2,1,0:T(8,128)} %bitcast.24), calls=%async_computation.1 | async-start | bytes 4194304 | tf_op jit(solution)/shard_map/all_to_all | solution.py:231
  112.0 9.5 %across.1 = (f32[2,64,1024]{2,1,0:T(8,128)}, f32[2,64,1024]{2,1,0:T(8,128)}, f32[2,64,1024]{2,1,0:T(8,128)}, f32[2,64,1024]{2,1,0:T(8,128)}) custom-call(s32[4]{0:T(128)} %pad_add_fusion.1.meta, bf16[1024,1280]{1,0:T(8,128)(2,1)} %bitcast.26, bf16[512,1280]{1,0:T(8,128)(2,1)} %bitcast.27, bf16[1280,1024]{1,0:T(8,128)(2,1)} %copy-done.2, ...), custom_call_target="tpu_custom_call" | custom-call | flops 1024 | bytes 1024 | tf_op jit(solution)/shard_map/across/pallas_call | solution.py:179
  121.5 2.1 collective-permute-start.13
  123.5 2.7 %collective-permute-start.14 = (f32[2,64,1024]{2,1,0:T(8,128)}, f32[2,64,1024]{2,1,0:T(8,128)S(1)}, u32[]{:S(2)}, u32[]{:S(2)}) collective-permute-start(f32[2,64,1024]{2,1,0:T(8,128)} %get-tuple-element.50), channel_id=1, source_target_pairs={{0,4},{2,6},{4,0},{6,2},{1,5},{3,7},{5,1},{7,3},{8,12},{10,14},{12... | collective-permute-start | bytes 1572872 | tf_op jit(solution)/shard_map/ppermute | solution.py:237
  126.2 1.5 collective-permute-start.15
  127.7 12.0 %all-to-all-done.1.refs_0_ = f32[4,2,64,1024]{3,2,1,0:T(8,128)S(1)} async-done(((f32[4,2,64,1024]{3,2,1,0:T(8,128)}), f32[4,2,64,1024]{3,2,1,0:T(8,128)S(1)}, u32[]{:S(2)}, u32[]{:S(2)}) %all-to-all-start.1) | async-done | bytes 2097184 | tf_op jit(solution)/shard_map/all_to_all | solution.py:231
  139.7 1.4 copy-done.4
  141.1 3.0 %add.105 = (f32[64,1024]{1,0:T(8,128)}, f32[64,1024]{1,0:T(8,128)}) custom-call(s32[4]{0:T(128)} %pad_add_fusion.1.meta, f32[4,2,64,1024]{3,2,1,0:T(8,128)} %copy-done.4), custom_call_target="tpu_custom_call" | custom-call | flops 1024 | bytes 1024 | tf_op jit(solution)/shard_map/add/pallas_call | solution.py:213
  144.1 0.3 collective-permute-start.11
  144.4 1.7 collective-permute-start.16
  146.1 7.4 %collective-permute-done.11.refs_1_ = f32[64,1024]{1,0:T(8,128)S(1)} collective-permute-done((f32[64,1024]{1,0:T(8,128)}, f32[64,1024]{1,0:T(8,128)S(1)}, u32[]{:S(2)}, u32[]{:S(2)}) %collective-permute-start.11) | collective-permute-done | bytes 262176 | tf_op jit(solution)/shard_map/ppermute | solution.py:226
  153.5 0.7 copy-done.11
  154.2 2.5 %gather.8 = (f32[64,1024]{1,0:T(8,128)}, f32[16,32,128]{2,1,0:T(8,128)}) custom-call(s32[4]{0:T(128)} %pad_add_fusion.1.meta, f32[64,1024]{1,0:T(8,128)} %get-tuple-element.46.refs_0_, f32[64,1024]{1,0:T(8,128)} %copy-done.11), custom_call_target="tpu_custom_call" | custom-call | flops 1024 | bytes 1024 | tf_op jit(solution)/shard_map/gather/pallas_call | solution.py:261
  156.8 4.6 %collective-permute-done.14.refs_2_ = f32[2,64,1024]{2,1,0:T(8,128)S(1)} collective-permute-done((f32[2,64,1024]{2,1,0:T(8,128)}, f32[2,64,1024]{2,1,0:T(8,128)S(1)}, u32[]{:S(2)}, u32[]{:S(2)}) %collective-permute-start.14) | collective-permute-done | bytes 524320 | tf_op jit(solution)/shard_map/ppermute | solution.py:237
  161.4 0.8 copy-done.9
  162.2 2.9 %add.106 = (f32[64,1024]{1,0:T(8,128)}, f32[64,1024]{1,0:T(8,128)}) custom-call(s32[4]{0:T(128)} %pad_add_fusion.1.meta, f32[2,64,1024]{2,1,0:T(8,128)} %get-tuple-element.54.refs_0_, f32[2,64,1024]{2,1,0:T(8,128)} %copy-done.8, f32[2,64,1024]{2,1,0:T(8,128)} %copy-done.9, f32[2,64,1024]{2,1,0:T(8,128)} %collective-permute-done.15.refs_3_), custom_call_target="tpu_custom_call" | custom-call | flops 1024 | bytes 1024 | tf_op jit(solution)/shard_map/add/pallas_call | solution.py:213
  165.2 0.3 collective-permute-start.17
  165.5 11.4 %all_to_all.21 = f32[16,32,128]{2,1,0:T(8,128)S(1)} all-to-all(f32[16,32,128]{2,1,0:T(8,128)} %get-tuple-element.48), channel_id=1, replica_groups=mesh['z'=8,'yh'=2,'yl'=2,'x'=4,'core'=2] {'yl','x','core'}, dimensions={0} | all-to-all | bytes 524288 | tf_op jit(solution)/shard_map/all_to_all | solution.py:277
  176.8 5.0 %collective-permute-start.12 = (f32[512,128]{1,0:T(8,128)S(1)}, f32[512,128]{1,0:T(8,128)S(1)}, u32[]{:S(2)}, u32[]{:S(2)}) collective-permute-start(f32[512,128]{1,0:T(8,128)S(1)} %bitcast.30), channel_id=1, source_target_pairs={{0,32},{32,64},{64,96},{96,128},{128,160},{160,192},{192,224},{48,... | collective-permute-start | bytes 786440 | tf_op jit(solution)/shard_map/ppermute | solution.py:364
  181.9 0.0 copy-start.10
  181.9 0.7 copy-done.10
  182.6 2.5 %gather.9 = (f32[64,1024]{1,0:T(8,128)}, f32[16,32,128]{2,1,0:T(8,128)}) custom-call(s32[4]{0:T(128)} %pad_add_fusion.1.meta, f32[64,1024]{1,0:T(8,128)} %get-tuple-element.60.refs_0_, f32[64,1024]{1,0:T(8,128)} %copy-done.10), custom_call_target="tpu_custom_call" | custom-call | flops 1024 | bytes 1024 | tf_op jit(solution)/shard_map/gather/pallas_call | solution.py:261
  185.1 3.5 %all-to-all-start.3 = ((f32[16,32,128]{2,1,0:T(8,128)}), f32[16,32,128]{2,1,0:T(8,128)S(1)}, u32[]{:S(2)}, u32[]{:S(2)}) async-start(f32[16,32,128]{2,1,0:T(8,128)} %get-tuple-element.62), calls=%async_computation.3 | async-start | bytes 524288 | tf_op jit(solution)/shard_map/all_to_all | solution.py:277
  188.7 0.6 dynamic_slice.3
  189.3 0.6 gather_fusion
  189.9 6.6 %all-to-all-done.3 = f32[16,32,128]{2,1,0:T(8,128)S(1)} async-done(((f32[16,32,128]{2,1,0:T(8,128)}), f32[16,32,128]{2,1,0:T(8,128)S(1)}, u32[]{:S(2)}, u32[]{:S(2)}) %all-to-all-start.3) | async-done | bytes 262176 | tf_op jit(solution)/shard_map/all_to_all | solution.py:277
  196.5 3.6 %collective-permute-start.19 = (f32[512,128]{1,0:T(8,128)S(1)}, f32[512,128]{1,0:T(8,128)S(1)}, u32[]{:S(2)}, u32[]{:S(2)}) collective-permute-start(f32[512,128]{1,0:T(8,128)S(1)} %bitcast.28), channel_id=1, source_target_pairs={{0,32},{32,64},{64,96},{96,128},{128,160},{160,192},{192,224},{1,3... | collective-permute-start | bytes 786440 | tf_op jit(solution)/shard_map/ppermute | solution.py:368
  200.1 0.7 and_convert_fusion
  200.8 0.6 pad_add_fusion.flags
  201.4 4.9 %collective-permute-done.19.near = f32[512,128]{1,0:T(8,128)S(1)} collective-permute-done((f32[512,128]{1,0:T(8,128)S(1)}, f32[512,128]{1,0:T(8,128)S(1)}, u32[]{:S(2)}, u32[]{:S(2)}) %collective-permute-start.19) | collective-permute-done | bytes 262176 | tf_op jit(solution)/shard_map/ppermute | solution.py:368
  206.3 0.7 copy-done.15
  207.0 3.9 %assemble.1 = f32[64,5120]{1,0:T(8,128)} custom-call(s32[6]{0:T(128)} %pad_add_fusion.flags, f32[512,128]{1,0:T(8,128)} %copy-done.13, f32[512,128]{1,0:T(8,128)} %copy-done.15, f32[512,128]{1,0:T(8,128)} %bitcast.29, f32[64,1024]{1,0:T(8,128)} %get-tuple-element.52.rows2, f32[64,1024]{1,0:T(8,128)} %copy-done.14, f32[64,1024]{1,0:T(8,128)} %get-tuple-element.37.rows0_a, ...), custom_call_target="tpu_custom_call" | custom-call | flops 1024 | bytes 1024 | tf_op jit(solution)/shard_map/assemble/pallas_call | solution.py:305
  (41 shorter events, 0.2 us)
Async XLA Ops:
  4.7 3.8 %collective-permute-start.1 = (f32[3,1024]{1,0:T(4,128)S(1)}, f32[3,1024]{1,0:T(4,128)S(1)}, u32[]{:S(2)}, u32[]{:S(2)}) collective-permute-start(f32[3,1024]{1,0:T(4,128)S(1)} %pad_maximum_fusion), channel_id=1, source_target_pairs={{0,8},{1,9},{8,0},{9,1},{2,10},{3,11},{10,2},{11,3},{4,12},{5,13},... | collective-permute-start | bytes 36872 | tf_op jit(solution)/shard_map/ppermute | solution.py:33
  6.3 3.2 %collective-permute-start.2 = (f32[3,1024]{1,0:T(4,128)S(1)}, f32[3,1024]{1,0:T(4,128)S(1)}, u32[]{:S(2)}, u32[]{:S(2)}) collective-permute-start(f32[3,1024]{1,0:T(4,128)S(1)} %pad_maximum_fusion), channel_id=1, source_target_pairs={{0,9},{1,8},{8,1},{9,0},{2,11},{3,10},{10,3},{11,2},{4,13},{5,12},... | collective-permute-start | bytes 36872 | tf_op jit(solution)/shard_map/ppermute | solution.py:33
  6.3 3.2 %collective-permute-start = (f32[3,1024]{1,0:T(4,128)S(1)}, f32[3,1024]{1,0:T(4,128)S(1)}, u32[]{:S(2)}, u32[]{:S(2)}) collective-permute-start(f32[3,1024]{1,0:T(4,128)S(1)} %pad_maximum_fusion), channel_id=1, source_target_pairs={{0,1},{1,0},{8,9},{9,8},{2,3},{3,2},{10,11},{11,10},{4,5},{5,4},{1... | collective-permute-start | bytes 36872 | tf_op jit(solution)/shard_map/ppermute | solution.py:33
  9.5 5.1 %collective-permute-start.5 = (f32[3,1024]{1,0:T(4,128)S(1)}, f32[3,1024]{1,0:T(4,128)S(1)}, u32[]{:S(2)}, u32[]{:S(2)}) collective-permute-start(f32[3,1024]{1,0:T(4,128)S(1)} %add_add_fusion.1), channel_id=1, source_target_pairs={{0,6},{2,0},{4,2},{6,4},{1,7},{3,1},{5,3},{7,5},{8,14},{10,8},{12,... | collective-permute-start | bytes 36872 | tf_op jit(solution)/shard_map/ppermute | solution.py:37
  12.4 5.2 %collective-permute-start.4 = (f32[3,1024]{1,0:T(4,128)S(1)}, f32[3,1024]{1,0:T(4,128)S(1)}, u32[]{:S(2)}, u32[]{:S(2)}) collective-permute-start(f32[3,1024]{1,0:T(4,128)S(1)} %add_add_fusion.1), channel_id=1, source_target_pairs={{0,4},{2,6},{4,0},{6,2},{1,5},{3,7},{5,1},{7,3},{8,12},{10,14},{12... | collective-permute-start | bytes 36872 | tf_op jit(solution)/shard_map/ppermute | solution.py:37
  13.2 4.9 %collective-permute-start.3 = (f32[3,1024]{1,0:T(4,128)S(1)}, f32[3,1024]{1,0:T(4,128)S(1)}, u32[]{:S(2)}, u32[]{:S(2)}) collective-permute-start(f32[3,1024]{1,0:T(4,128)S(1)} %add_add_fusion.1), channel_id=1, source_target_pairs={{0,2},{2,4},{4,6},{6,0},{1,3},{3,5},{5,7},{7,1},{8,10},{10,12},{12... | collective-permute-start | bytes 36872 | tf_op jit(solution)/shard_map/ppermute | solution.py:37
  26.9 5.1 %collective-permute-start.6 = (bf16[1280,1024]{1,0:T(8,128)(2,1)}, bf16[1280,1024]{1,0:T(8,128)(2,1)S(1)}, u32[]{:S(2)}, u32[]{:S(2)}) collective-permute-start(bf16[1280,1024]{1,0:T(8,128)(2,1)} %get-tuple-element.36.right_a.zed_a), channel_id=1, source_target_pairs={{0,1},{1,0},{2,3},{3,2},{4,5},{5,4},{6,7},{7,6},{8,9},{9,8},{10,11... | collective-permute-start | bytes 7864328 | tf_op jit(solution)/shard_map/ppermute | solution.py:351
  26.9 61.0 %collective-permute-start.8 = (bf16[2,8,64,1280]{3,2,1,0:T(8,128)(2,1)}, bf16[2,8,64,1280]{3,2,1,0:T(8,128)(2,1)S(1)}, u32[]{:S(2)}, u32[]{:S(2)}) collective-permute-start(bf16[2,8,64,1280]{3,2,1,0:T(8,128)(2,1)} %get-tuple-element.35), channel_id=1, source_target_pairs={{0,16},{16,0},{32,48},{48,32},{64,80},{80,64},{96,112},{112,96},{1... | collective-permute-start | bytes 7864328 | tf_op jit(solution)/shard_map/ppermute | solution.py:352
  29.8 61.2 %collective-permute-start.7 = (bf16[1280,1024]{1,0:T(8,128)(2,1)}, bf16[1280,1024]{1,0:T(8,128)(2,1)S(1)}, u32[]{:S(2)}, u32[]{:S(2)}) collective-permute-start(bf16[1280,1024]{1,0:T(8,128)(2,1)} %get-tuple-element.36.right_a.zed_a), channel_id=1, source_target_pairs={{32,0},{64,32},{96,64},{128,96},{160,128},{192,160},{224,192},{16,... | collective-permute-start | bytes 7864328 | tf_op jit(solution)/shard_map/ppermute | solution.py:353
  32.0 1.5 copy-start.1
  87.9 20.5 %copy-start.5 = (bf16[2,8,64,1280]{3,2,1,0:T(8,128)(2,1)}, bf16[2,8,64,1280]{3,2,1,0:T(8,128)(2,1)S(1)}, u32[]{:S(2)}) copy-start(bf16[2,8,64,1280]{3,2,1,0:T(8,128)(2,1)S(1)} %collective-permute-done.8) | copy-start | bytes 7864324
  91.1 7.8 %copy-start.2 = (bf16[1280,1024]{1,0:T(8,128)(2,1)}, bf16[1280,1024]{1,0:T(8,128)(2,1)S(1)}, u32[]{:S(2)}) copy-start(bf16[1280,1024]{1,0:T(8,128)(2,1)S(1)} %collective-permute-done.7.right_a.near_a) | copy-start | bytes 7864324
  91.1 7.8 %collective-permute-start.9 = (bf16[1280,1024]{1,0:T(8,128)(2,1)S(1)}, bf16[1280,1024]{1,0:T(8,128)(2,1)S(1)}, u32[]{:S(2)}, u32[]{:S(2)}) collective-permute-start(bf16[1280,1024]{1,0:T(8,128)(2,1)S(1)} %collective-permute-done.7.right_a.near_a), channel_id=1, source_target_pairs={{0,1},{1,0},{2,3},{3,2},{4,5},{5,4},{6,7},{7,6},{8,9},{9,8},{10,11... | collective-permute-start | bytes 7864328 | tf_op jit(solution)/shard_map/ppermute | solution.py:351
  91.2 6.7 %collective-permute-start.10 = (bf16[8,64,1280]{2,1,0:T(8,128)(2,1)S(1)}, bf16[8,64,1280]{2,1,0:T(8,128)(2,1)S(1)}, u32[]{:S(2)}, u32[]{:S(2)}) collective-permute-start(bf16[8,64,1280]{2,1,0:T(8,128)(2,1)S(1)} %slice_bitcast_fusion), channel_id=1, source_target_pairs={{0,1},{1,0},{2,3},{3,2},{4,5},{5,4},{6,7},{7,6},{8,9},{9,8},{10,11... | collective-permute-start | bytes 3932168 | tf_op jit(solution)/shard_map/ppermute | solution.py:351
  97.9 1.1 copy-start.6
  98.9 1.6 copy-start.3
  108.4 31.3 %all-to-all-start.1 = ((f32[4,2,64,1024]{3,2,1,0:T(8,128)}), f32[4,2,64,1024]{3,2,1,0:T(8,128)S(1)}, u32[]{:S(2)}, u32[]{:S(2)}) async-start(f32[4,2,64,1024]{3,2,1,0:T(8,128)} %bitcast.24), calls=%async_computation.1 | async-start | bytes 4194304 | tf_op jit(solution)/shard_map/all_to_all | solution.py:231
  112.0 32.4 %copy-start.16 = (f32[64,1024]{1,0:T(8,128)S(1)}, f32[64,1024]{1,0:T(8,128)}, u32[]{:S(2)}) copy-start(f32[64,1024]{1,0:T(8,128)} %get-tuple-element.53) | copy-start | bytes 786436
  121.5 35.3 %collective-permute-start.13 = (f32[2,64,1024]{2,1,0:T(8,128)}, f32[2,64,1024]{2,1,0:T(8,128)S(1)}, u32[]{:S(2)}, u32[]{:S(2)}) collective-permute-start(f32[2,64,1024]{2,1,0:T(8,128)} %get-tuple-element.49), channel_id=1, source_target_pairs={{0,2},{2,4},{4,6},{6,0},{1,3},{3,5},{5,7},{7,1},{8,10},{10,12},{12... | collective-permute-start | bytes 1572872 | tf_op jit(solution)/shard_map/ppermute | solution.py:237
  123.5 37.9 %collective-permute-start.14 = (f32[2,64,1024]{2,1,0:T(8,128)}, f32[2,64,1024]{2,1,0:T(8,128)S(1)}, u32[]{:S(2)}, u32[]{:S(2)}) collective-permute-start(f32[2,64,1024]{2,1,0:T(8,128)} %get-tuple-element.50), channel_id=1, source_target_pairs={{0,4},{2,6},{4,0},{6,2},{1,5},{3,7},{5,1},{7,3},{8,12},{10,14},{12... | collective-permute-start | bytes 1572872 | tf_op jit(solution)/shard_map/ppermute | solution.py:237
  126.2 35.2 %collective-permute-start.15 = (f32[2,64,1024]{2,1,0:T(8,128)}, f32[2,64,1024]{2,1,0:T(8,128)}, u32[]{:S(2)}, u32[]{:S(2)}) collective-permute-start(f32[2,64,1024]{2,1,0:T(8,128)} %get-tuple-element.51), channel_id=1, source_target_pairs={{0,6},{2,0},{4,2},{6,4},{1,7},{3,1},{5,3},{7,5},{8,14},{10,8},{12,... | collective-permute-start | bytes 1572872 | tf_op jit(solution)/shard_map/ppermute | solution.py:237
  139.7 1.4 copy-start.4
  144.1 44.6 %copy-start = (s32[16]{0:T(128)S(1)}, s32[16]{0:T(128)}, u32[]{:S(2)}) copy-start(s32[16]{0:T(128)} %param.5) | copy-start | bytes 196
  144.1 9.5 %collective-permute-start.11 = (f32[64,1024]{1,0:T(8,128)}, f32[64,1024]{1,0:T(8,128)S(1)}, u32[]{:S(2)}, u32[]{:S(2)}) collective-permute-start(f32[64,1024]{1,0:T(8,128)} %get-tuple-element.47), channel_id=1, source_target_pairs={{0,8},{8,0},{1,9},{9,1},{2,10},{10,2},{3,11},{11,3},{4,12},{12,4},... | collective-permute-start | bytes 786440 | tf_op jit(solution)/shard_map/ppermute | solution.py:226
  144.4 12.4 %collective-permute-start.16 = (f32[64,1024]{1,0:T(8,128)S(1)}, f32[64,1024]{1,0:T(8,128)S(1)}, u32[]{:S(2)}, u32[]{:S(2)}) collective-permute-start(f32[64,1024]{1,0:T(8,128)S(1)} %copy-done.16), channel_id=1, source_target_pairs={{0,8},{8,0},{1,9},{9,1},{2,10},{10,2},{3,11},{11,3},{4,12},{12,4},... | collective-permute-start | bytes 786440 | tf_op jit(solution)/shard_map/ppermute | solution.py:226
  153.5 0.7 copy-start.11
  156.8 49.5 %copy-start.12 = (f32[64,1024]{1,0:T(8,128)}, f32[64,1024]{1,0:T(8,128)S(1)}, u32[]{:S(2)}) copy-start(f32[64,1024]{1,0:T(8,128)S(1)} %collective-permute-done.16.rows0_b) | copy-start | bytes 786436
  156.8 4.6 %copy-start.8 = (f32[2,64,1024]{2,1,0:T(8,128)}, f32[2,64,1024]{2,1,0:T(8,128)S(1)}, u32[]{:S(2)}) copy-start(f32[2,64,1024]{2,1,0:T(8,128)S(1)} %collective-permute-done.13.refs_1_) | copy-start | bytes 1572868
  161.4 0.8 copy-start.9
  165.2 16.7 %collective-permute-start.17 = (f32[64,1024]{1,0:T(8,128)}, f32[64,1024]{1,0:T(8,128)S(1)}, u32[]{:S(2)}, u32[]{:S(2)}) collective-permute-start(f32[64,1024]{1,0:T(8,128)} %get-tuple-element.59), channel_id=1, source_target_pairs={{0,8},{8,0},{1,9},{9,1},{2,10},{10,2},{3,11},{11,3},{4,12},{12,4},... | collective-permute-start | bytes 786440 | tf_op jit(solution)/shard_map/ppermute | solution.py:226
  176.8 13.1 %collective-permute-start.12 = (f32[512,128]{1,0:T(8,128)S(1)}, f32[512,128]{1,0:T(8,128)S(1)}, u32[]{:S(2)}, u32[]{:S(2)}) collective-permute-start(f32[512,128]{1,0:T(8,128)S(1)} %bitcast.30), channel_id=1, source_target_pairs={{0,32},{32,64},{64,96},{96,128},{128,160},{160,192},{192,224},{48,... | collective-permute-start | bytes 786440 | tf_op jit(solution)/shard_map/ppermute | solution.py:364
  181.9 0.7 copy-start.10
  185.1 11.4 %collective-permute-start.18 = (f32[64,1024]{1,0:T(8,128)}, f32[64,1024]{1,0:T(8,128)S(1)}, u32[]{:S(2)}, u32[]{:S(2)}) collective-permute-start(f32[64,1024]{1,0:T(8,128)} %get-tuple-element.63), channel_id=1, source_target_pairs={{0,16},{16,0},{32,48},{48,32},{64,80},{80,64},{96,112},{112,96},{1... | collective-permute-start | bytes 786440 | tf_op jit(solution)/shard_map/ppermute | solution.py:367
  185.1 11.4 %all-to-all-start.3 = ((f32[16,32,128]{2,1,0:T(8,128)}), f32[16,32,128]{2,1,0:T(8,128)S(1)}, u32[]{:S(2)}, u32[]{:S(2)}) async-start(f32[16,32,128]{2,1,0:T(8,128)} %get-tuple-element.62), calls=%async_computation.3 | async-start | bytes 524288 | tf_op jit(solution)/shard_map/all_to_all | solution.py:277
  189.9 16.4 %copy-start.13 = (f32[512,128]{1,0:T(8,128)}, f32[512,128]{1,0:T(8,128)S(1)}, u32[]{:S(2)}) copy-start(f32[512,128]{1,0:T(8,128)S(1)} %collective-permute-done.12.far) | copy-start | bytes 786436
  196.5 9.8 %copy-start.7 = (f32[16,32,128]{2,1,0:T(8,128)}, f32[16,32,128]{2,1,0:T(8,128)S(1)}, u32[]{:S(2)}) copy-start(f32[16,32,128]{2,1,0:T(8,128)S(1)} %all-to-all-done.3) | copy-start | bytes 786436
  196.5 9.8 %copy-start.14 = (f32[64,1024]{1,0:T(8,128)}, f32[64,1024]{1,0:T(8,128)S(1)}, u32[]{:S(2)}) copy-start(f32[64,1024]{1,0:T(8,128)S(1)} %collective-permute-done.18.beside) | copy-start | bytes 786436
  196.5 9.8 %collective-permute-start.19 = (f32[512,128]{1,0:T(8,128)S(1)}, f32[512,128]{1,0:T(8,128)S(1)}, u32[]{:S(2)}, u32[]{:S(2)}) collective-permute-start(f32[512,128]{1,0:T(8,128)S(1)} %bitcast.28), channel_id=1, source_target_pairs={{0,32},{32,64},{64,96},{96,128},{128,160},{160,192},{192,224},{1,3... | collective-permute-start | bytes 786440 | tf_op jit(solution)/shard_map/ppermute | solution.py:368
  206.3 0.7 copy-start.15

commit v9 on v8

--- a/solution.py
+++ b/solution.py
@@ -154,17 +154,7 @@
     )(meta, *flat(*left), *right)
 
 
-def across_kernel(meta, left_a, left_b, near_a, near_b, zed_a, zed_b, *rest):
-    outs, right = rest[:4], rest[4]
-    odd = meta[1] == 1
-
-    def take(a, b):
-        right[:DEPTH] = a[...]
-        right[DEPTH:] = b[...]
-
-    pl.when(odd)(lambda: take(zed_a, zed_b))
-    pl.when(~odd)(lambda: take(near_a, near_b))
-    acc = matmul(left_a[...], right[:DEPTH]) + matmul(left_b[...], right[DEPTH:])
+def store_relative(meta, outs, acc):
     acc = acc.reshape(4, 2, ROWS, STEP)
     for x in range(4):
 
@@ -172,6 +162,42 @@
         def _():
             for k in range(4):
                 outs[k][...] = acc[(x + k) % 4]
+
+
+def along_kernel(meta, left_a, left_b, right_a, right_b, *outs):
+    acc = matmul(left_a[...], right_a[...]) + matmul(left_b[...], right_b[...])
+    store_relative(meta, outs, acc)
+
+
+def along_product(meta, left, right):
+    block = pl.BlockSpec((DEPTH, STEP), lambda j, m: (0, j))
+    return pl.pallas_call(
+        along_kernel,
+        name="along",
+        out_shape=(f32(2, ROWS, B),) * 4,
+        grid_spec=pltpu.PrefetchScalarGridSpec(
+            num_scalar_prefetch=1,
+            grid=(B // STEP,),
+            in_specs=[whole(LEFT)] * 2 + [block] * 2,
+            out_specs=(pl.BlockSpec((2, ROWS, STEP), lambda j, m: (0, 0, j)),) * 4,
+        ),
+        compiler_params=params(),
+        cost_estimate=cost(2 * DEPTH * B * B, 8 * DEPTH * B + 4 * B * B),
+    )(meta, *flat(*left), *right)
+
+
+def across_kernel(meta, left_a, left_b, near_a, near_b, zed_a, zed_b, *rest):
+    outs, right = rest[:4], rest[4]
+    odd = meta[1] == 1
+
+    def take(a, b):
+        right[:DEPTH] = a[...]
+        right[DEPTH:] = b[...]
+
+    pl.when(odd)(lambda: take(zed_a, zed_b))
+    pl.when(~odd)(lambda: take(near_a, near_b))
+    acc = matmul(left_a[...], right[:DEPTH]) + matmul(left_b[...], right[DEPTH:])
+    store_relative(meta, outs, acc)
 
 
 def across_product(meta, left, near, zed):
@@ -357,13 +383,13 @@
     near, other = after((near, other), rows0[0])
     near = (near, swap(near))
     other = (other, swap(other[1]))
-    rows2 = product(meta, own, after(near, other[1]), "along")
-    pieces = across_product(meta, after(other, rows2), near, (zed, zed_b))
-    rows2 = fold(meta, rows2, pieces[0])
+    rows2 = along_product(meta, own, after(near, other[1]))
+    pieces = across_product(meta, after(other, rows2[0]), near, (zed, zed_b))
+    rows2 = fold_pieces(meta, rows2, pieces[0])
     rows2, turned2 = gather(meta, *rows2)
     far = lax.ppermute(turned2, SNP, EVEN_UP + ODD_DOWN)
-    rows1 = fold_pieces(meta, pieces, rows2, rows0[1])
-    rows1, turned1 = gather(meta, *after(rows1, turned2))
+    rows1 = fold_pieces(meta, pieces, turned2, rows0[1])
+    rows1, turned1 = gather(meta, *rows1)
     beside = lax.ppermute(rows1, SNP, TO_OTHER)
     near = lax.ppermute(after(turned1, far, beside), SNP, EVEN_UP)
     flags = jnp.concatenate([kept_flags(band, mine), odd]).astype(jnp.int32)

time: 213 us -> 210 us (0.986)
  blocking collectives: 42.8 us -> 31.4 us
  waiting for transfers between devices: 56.5 us -> 62 us
  starting transfers between devices: 36.6 us -> 39.6 us
    all_to_all x1 -> x0, waiting for transfers between devices: 12 us -> none  [fold(): parts = lax.all_to_all(parts.reshape(4, 2, rows, columns), 'x', 0, 0)]
    all_to_all x1 -> x0, blocking collectives: 11.4 us -> none  [gather(): return (rows, lax.all_to_all(packed, SAMP, 0, 0).reshape(HALF, 2 * ROWS))]
    ppermute x3 -> x6, waiting for transfers between devices: 4.61 us -> 13.2 us  [fold_pieces(): lax.ppermute(pieces[k], 'x', [(i, (i + k) % 4) for i in range(4)])]
    pallas_call x0 -> x1, Pallas kernels: none -> 7.96 us  [along_product(): pl.pallas_call(along_kernel, name='along', out_shape=(f32(2, ROWS, B),) *...]
    pallas_call x2 -> x1, Pallas kernels: 15.7 us -> 7.81 us  [product(): pl.pallas_call(product_kernel, name=name, out_shape=f32(PIECES, ROWS, B),...]
    all_to_all x1 -> x2, waiting for transfers between devices: 6.55 us -> 13.7 us  [gather(): return (rows, lax.all_to_all(packed, SAMP, 0, 0).reshape(HALF, 2 * ROWS))]
    all_to_all x1 -> x2, starting transfers between devices: 3.53 us -> 7.6 us  [gather(): return (rows, lax.all_to_all(packed, SAMP, 0, 0).reshape(HALF, 2 * ROWS))]
    all_to_all x1 -> x0, starting transfers between devices: 3.61 us -> none  [fold(): parts = lax.all_to_all(parts.reshape(4, 2, rows, columns), 'x', 0, 0)]
  transfers between devices with their start and end apart: 22 -> 25, of which waited for: 13 -> 17; matrix products, arithmetic and copies ran while one was open for 1% -> 2% of each run, Pallas kernels for 17% -> 17%
where the time goes in v9:
time: 210 us; the launch traced here: 207 us
  waiting for transfers between devices  62 us (30%)
  Pallas kernels  58 us (28%)
  starting transfers between devices  39.6 us (19%)
  blocking collectives  31.4 us (15%)
  local copies, waits for them, and re-layouts  8.48 us (4%)
  other arithmetic  7.19 us (3%)
    all_to_all x1, blocking collectives, fold(): parts = lax.all_to_all(parts.reshape(4, 2, rows, columns), 'x', 0, 0)  31.4 us
    all_to_all x2, waiting for transfers between devices, gather(): return (rows, lax.all_to_all(packed, SAMP, 0, 0).reshape(HALF, 2 * ROWS))  13.7 us
    ppermute x6, waiting for transfers between devices, fold_pieces(): lax.ppermute(pieces[k], 'x', [(i, (i + k) % 4) for i in range(4)])  13.2 us
    ppermute x3, waiting for transfers between devices, add(): return (keep, lax.ppermute(send, 'yl', SWAP))  9.97 us
    pallas_call x1, Pallas kernels, across_product(): pl.pallas_call(across_kernel, name='across', out_shape=(f32(2, ROWS, B),)...  9.5 us
    pallas_call x3, Pallas kernels, add(): pl.pallas_call(add_kernel, name='add', out_shape=(f32(rows, columns),) *...  8.89 us
    pallas_call x1, Pallas kernels, standardize(): pl.pallas_call(standard_kernel, name='standardize', out_shape=(bf16(DEPTH...  8.13 us
    pallas_call x1, Pallas kernels, along_product(): pl.pallas_call(along_kernel, name='along', out_shape=(f32(2, ROWS, B),) *...  7.96 us
  transfers between devices with their start and end apart: 25, of which 17 were waited for; matrix products, arithmetic and copies ran while one was open for 2% of the time, Pallas kernels for 17%

profile of v9, /device:TPU:64, one launch (start us, length us, event | category | flops | bytes accessed | tf_op | source)
XLA Modules:
  0.0 206.9 jit_solution(16058783148618918706)
XLA Ops:
  0.0 4.7 %fusion.1 = (f32[1024]{0:T(1024)S(1)}, f32[1024]{0:T(1024)S(1)}, f32[1024]{0:T(1024)S(1)}) fusion(bf16[1280,1024]{1,0:T(8,128)(2,1)} %dosage.1, s32[1280,1024]{1,0:T(8,128)} %observed.1), kind=kLoop, calls=%fused_computation.5 | loop fusion | flops 9171968 | bytes 7876608 | tf_op jit(solution)/shard_map/reduce_sum | solution.py:367
  4.7 1.7 collective-permute-start.1
  6.3 0.6 collective-permute-start
  6.9 1.6 collective-permute-done.1
  8.5 1.0 collective-permute-done.2
  9.5 2.8 %collective-permute-start.5 = (f32[3,1024]{1,0:T(4,128)S(1)}, f32[3,1024]{1,0:T(4,128)S(1)}, u32[]{:S(2)}, u32[]{:S(2)}) collective-permute-start(f32[3,1024]{1,0:T(4,128)S(1)} %add_add_fusion.1), channel_id=1, source_target_pairs={{0,6},{2,0},{4,2},{6,4},{1,7},{3,1},{5,3},{7,5},{8,14},{10,8},{12,... | collective-permute-start | bytes 36872 | tf_op jit(solution)/shard_map/ppermute | solution.py:37
  12.4 0.8 collective-permute-start.4
  13.2 0.9 collective-permute-start.3
  14.1 0.6 pad_add_fusion.1.meta
  14.7 3.0 %collective-permute-done.4 = f32[3,1024]{1,0:T(4,128)S(1)} collective-permute-done((f32[3,1024]{1,0:T(4,128)S(1)}, f32[3,1024]{1,0:T(4,128)S(1)}, u32[]{:S(2)}, u32[]{:S(2)}) %collective-permute-start.4) | collective-permute-done | bytes 12320 | tf_op jit(solution)/shard_map/ppermute | solution.py:37
  17.6 0.5 collective-permute-done.3
  18.2 0.6 pad_maximum_fusion.1.stats
  18.8 8.1 %standardize.1 = (bf16[1280,1024]{1,0:T(8,128)(2,1)}, bf16[2,8,64,1280]{3,2,1,0:T(8,128)(2,1)}) custom-call(s32[4]{0:T(128)} %pad_add_fusion.1.meta, bf16[1280,1024]{1,0:T(8,128)(2,1)} %dosage.1, s32[1280,1024]{1,0:T(8,128)} %observed.1, f32[2,1024]{1,0:T(2,128)} %pad_maximum_fusion.1.stats), custom_call_target="tpu_custom_call" | custom-call | flops 1024 | bytes 1024 | tf_op jit(solution)/shard_map/standardize/pallas_call | solution.py:86
  26.9 2.9 %collective-permute-start.8 = (bf16[2,8,64,1280]{3,2,1,0:T(8,128)(2,1)}, bf16[2,8,64,1280]{3,2,1,0:T(8,128)(2,1)S(1)}, u32[]{:S(2)}, u32[]{:S(2)}) collective-permute-start(bf16[2,8,64,1280]{3,2,1,0:T(8,128)(2,1)} %get-tuple-element.40), channel_id=1, source_target_pairs={{0,16},{16,0},{32,48},{48,32},{64,80},{80,64},{96,112},{112,96},{1... | collective-permute-start | bytes 7864328 | tf_op jit(solution)/shard_map/ppermute | solution.py:378
  29.8 2.0 collective-permute-start.7
  31.9 0.2 collective-permute-done.6.zed.right_b.zed_b
  32.0 1.5 copy-done.1
  33.6 6.7 %turn.1 = bf16[8,64,1280]{2,1,0:T(8,128)(2,1)} custom-call(s32[4]{0:T(128)} %pad_add_fusion.1.meta, bf16[1280,1024]{1,0:T(8,128)(2,1)} %copy-done.1), custom_call_target="tpu_custom_call" | custom-call | flops 1024 | bytes 1024 | tf_op jit(solution)/shard_map/turn/pallas_call | solution.py:120
  40.3 7.8 %own.1 = f32[8,64,1024]{2,1,0:T(8,128)} custom-call(s32[4]{0:T(128)} %pad_add_fusion.1.meta, bf16[1024,1280]{1,0:T(8,128)(2,1)} %bitcast.21, bf16[512,1280]{1,0:T(8,128)(2,1)} %bitcast.19, bf16[1280,1024]{1,0:T(8,128)(2,1)} %get-tuple-element.41.right_a.zed_a, bf16[1280,1024]{1,0:T(8,128)(2,1)} %copy-done.1), custom_call_target="tpu_custom_call" | custom-call | flops 1024 | bytes 1024 | tf_op jit(solution)/shard_map/own/pallas_call | solution.py:142
  48.1 31.4 %all_to_all.15.refs_0_ = f32[4,2,64,1024]{3,2,1,0:T(8,128)} all-to-all(f32[4,2,64,1024]{3,2,1,0:T(8,128)} %bitcast.23), channel_id=1, replica_groups=mesh['z'=8,'yh'=2,'yl'=2,'x'=4,'core'=2] {'x'}, dimensions={0} | all-to-all | bytes 4194304 | tf_op jit(solution)/shard_map/all_to_all | solution.py:257
  79.5 3.0 %add.104 = (f32[64,1024]{1,0:T(8,128)}, f32[64,1024]{1,0:T(8,128)}) custom-call(s32[4]{0:T(128)} %pad_add_fusion.1.meta, f32[4,2,64,1024]{3,2,1,0:T(8,128)} %all_to_all.15.refs_0_), custom_call_target="tpu_custom_call" | custom-call | flops 1024 | bytes 1024 | tf_op jit(solution)/shard_map/add/pallas_call | solution.py:239
  82.5 5.5 %collective-permute-done.8 = bf16[2,8,64,1280]{3,2,1,0:T(8,128)(2,1)S(1)} collective-permute-done((bf16[2,8,64,1280]{3,2,1,0:T(8,128)(2,1)}, bf16[2,8,64,1280]{3,2,1,0:T(8,128)(2,1)S(1)}, u32[]{:S(2)}, u32[]{:S(2)}) %collective-permute-start.8) | collective-permute-done | bytes 2621472 | tf_op jit(solution)/shard_map/ppermute | solution.py:378
  87.9 3.2 %collective-permute-done.7.right_a.near_a = bf16[1280,1024]{1,0:T(8,128)(2,1)S(1)} collective-permute-done((bf16[1280,1024]{1,0:T(8,128)(2,1)}, bf16[1280,1024]{1,0:T(8,128)(2,1)S(1)}, u32[]{:S(2)}, u32[]{:S(2)}) %collective-permute-start.7) | collective-permute-done | bytes 2621472 | tf_op jit(solution)/shard_map/ppermute | solution.py:379
  91.1 0.1 slice_bitcast_fusion
  91.2 0.6 collective-permute-start.10
  91.8 6.1 %collective-permute-done.10 = bf16[8,64,1280]{2,1,0:T(8,128)(2,1)S(1)} collective-permute-done((bf16[8,64,1280]{2,1,0:T(8,128)(2,1)S(1)}, bf16[8,64,1280]{2,1,0:T(8,128)(2,1)S(1)}, u32[]{:S(2)}, u32[]{:S(2)}) %collective-permute-start.10) | collective-permute-done | bytes 1310752 | tf_op jit(solution)/shard_map/ppermute | solution.py:377
  97.9 1.1 copy-done.5
  99.0 1.6 copy-done.3
  100.6 8.0 %along.1 = (f32[2,64,1024]{2,1,0:T(8,128)}, f32[2,64,1024]{2,1,0:T(8,128)}, f32[2,64,1024]{2,1,0:T(8,128)}, f32[2,64,1024]{2,1,0:T(8,128)}) custom-call(s32[4]{0:T(128)} %pad_add_fusion.1.meta, bf16[1024,1280]{1,0:T(8,128)(2,1)} %bitcast.22, bf16[512,1280]{1,0:T(8,128)(2,1)} %bitcast.20, bf16[1280,1024]{1,0:T(8,128)(2,1)} %copy-done.2, ...), custom_call_target="tpu_custom_call" | custom-call | flops 1024 | bytes 1024 | tf_op jit(solution)/shard_map/along/pallas_call | solution.py:174
  108.6 1.8 collective-permute-start.12
  110.4 2.4 %collective-permute-start.13 = (f32[2,64,1024]{2,1,0:T(8,128)}, f32[2,64,1024]{2,1,0:T(8,128)S(1)}, u32[]{:S(2)}, u32[]{:S(2)}) collective-permute-start(f32[2,64,1024]{2,1,0:T(8,128)} %get-tuple-element.50), channel_id=1, source_target_pairs={{0,6},{2,0},{4,2},{6,4},{1,7},{3,1},{5,3},{7,5},{8,14},{10,8},{12,... | collective-permute-start | bytes 1572872 | tf_op jit(solution)/shard_map/ppermute | solution.py:263
  112.7 9.5 %across.1 = (f32[2,64,1024]{2,1,0:T(8,128)}, f32[2,64,1024]{2,1,0:T(8,128)}, f32[2,64,1024]{2,1,0:T(8,128)}, f32[2,64,1024]{2,1,0:T(8,128)}) custom-call(s32[4]{0:T(128)} %pad_add_fusion.1.meta, bf16[1024,1280]{1,0:T(8,128)(2,1)} %bitcast.24, bf16[512,1280]{1,0:T(8,128)(2,1)} %bitcast.25, bf16[1280,1024]{1,0:T(8,128)(2,1)} %copy-done.2, ...), custom_call_target="tpu_custom_call" | custom-call | flops 1024 | bytes 1024 | tf_op jit(solution)/shard_map/across/pallas_call | solution.py:205
  122.2 0.1 collective-permute-start.16
  122.3 2.1 %collective-permute-start.17 = (f32[2,64,1024]{2,1,0:T(8,128)}, f32[2,64,1024]{2,1,0:T(8,128)S(1)}, u32[]{:S(2)}, u32[]{:S(2)}) collective-permute-start(f32[2,64,1024]{2,1,0:T(8,128)} %get-tuple-element.62), channel_id=1, source_target_pairs={{0,4},{2,6},{4,0},{6,2},{1,5},{3,7},{5,1},{7,3},{8,12},{10,14},{12... | collective-permute-start | bytes 1572872 | tf_op jit(solution)/shard_map/ppermute | solution.py:263
  124.4 11.6 %collective-permute-done.11.refs_1_ = f32[2,64,1024]{2,1,0:T(8,128)S(1)} collective-permute-done((f32[2,64,1024]{2,1,0:T(8,128)}, f32[2,64,1024]{2,1,0:T(8,128)S(1)}, u32[]{:S(2)}, u32[]{:S(2)}) %collective-permute-start.11) | collective-permute-done | bytes 524320 | tf_op jit(solution)/shard_map/ppermute | solution.py:263
  136.0 0.9 collective-permute-done.13.refs_3_
  137.0 0.8 copy-done.12
  137.7 2.9 %add.105 = (f32[64,1024]{1,0:T(8,128)}, f32[64,1024]{1,0:T(8,128)}) custom-call(s32[4]{0:T(128)} %pad_add_fusion.1.meta, f32[2,64,1024]{2,1,0:T(8,128)} %get-tuple-element.54.refs_0_, f32[2,64,1024]{2,1,0:T(8,128)} %copy-done.10, f32[2,64,1024]{2,1,0:T(8,128)} %copy-done.11, f32[2,64,1024]{2,1,0:T(8,128)} %copy-done.12), custom_call_target="tpu_custom_call" | custom-call | flops 1024 | bytes 1024 | tf_op jit(solution)/shard_map/add/pallas_call | solution.py:239
  140.7 0.4 collective-permute-start.14
  141.1 1.7 collective-permute-start.19
  142.8 7.4 %collective-permute-done.14.refs_1_ = f32[64,1024]{1,0:T(8,128)S(1)} collective-permute-done((f32[64,1024]{1,0:T(8,128)}, f32[64,1024]{1,0:T(8,128)S(1)}, u32[]{:S(2)}, u32[]{:S(2)}) %collective-permute-start.14) | collective-permute-done | bytes 262176 | tf_op jit(solution)/shard_map/ppermute | solution.py:252
  150.2 0.7 copy-done.13
  150.9 2.5 %gather.8 = (f32[64,1024]{1,0:T(8,128)}, f32[16,32,128]{2,1,0:T(8,128)}) custom-call(s32[4]{0:T(128)} %pad_add_fusion.1.meta, f32[64,1024]{1,0:T(8,128)} %get-tuple-element.58.refs_0_, f32[64,1024]{1,0:T(8,128)} %copy-done.13), custom_call_target="tpu_custom_call" | custom-call | flops 1024 | bytes 1024 | tf_op jit(solution)/shard_map/gather/pallas_call | solution.py:287
  153.5 4.1 %all-to-all-start.1 = ((f32[16,32,128]{2,1,0:T(8,128)}), f32[16,32,128]{2,1,0:T(8,128)S(1)}, u32[]{:S(2)}, u32[]{:S(2)}) async-start(f32[16,32,128]{2,1,0:T(8,128)} %get-tuple-element.60), calls=%async_computation.1 | async-start | bytes 524288 | tf_op jit(solution)/shard_map/all_to_all | solution.py:303
  157.6 0.1 collective-permute-done.16.refs_1_
  157.7 0.7 collective-permute-done.18.refs_3_
  158.3 7.1 %all-to-all-done.1 = f32[16,32,128]{2,1,0:T(8,128)S(1)} async-done(((f32[16,32,128]{2,1,0:T(8,128)}), f32[16,32,128]{2,1,0:T(8,128)S(1)}, u32[]{:S(2)}, u32[]{:S(2)}) %all-to-all-start.1) | async-done | bytes 262176 | tf_op jit(solution)/shard_map/all_to_all | solution.py:303
  165.4 3.0 %add.106 = (f32[64,1024]{1,0:T(8,128)}, f32[64,1024]{1,0:T(8,128)}) custom-call(s32[4]{0:T(128)} %pad_add_fusion.1.meta, f32[2,64,1024]{2,1,0:T(8,128)} %get-tuple-element.65.refs_0_, f32[2,64,1024]{2,1,0:T(8,128)} %copy-done.7, f32[2,64,1024]{2,1,0:T(8,128)} %copy-done.8, f32[2,64,1024]{2,1,0:T(8,128)} %copy-done.9), custom_call_target="tpu_custom_call" | custom-call | flops 1024 | bytes 1024 | tf_op jit(solution)/shard_map/add/pallas_call | solution.py:239
  168.4 0.6 collective-permute-start.20
  169.0 5.0 %collective-permute-start.15 = (f32[512,128]{1,0:T(8,128)S(1)}, f32[512,128]{1,0:T(8,128)S(1)}, u32[]{:S(2)}, u32[]{:S(2)}) collective-permute-start(f32[512,128]{1,0:T(8,128)S(1)} %bitcast.28), channel_id=1, source_target_pairs={{0,32},{32,64},{64,96},{96,128},{128,160},{160,192},{192,224},{48,... | collective-permute-start | bytes 786440 | tf_op jit(solution)/shard_map/ppermute | solution.py:390
  174.0 2.5 %collective-permute-done.20.refs_1_ = f32[64,1024]{1,0:T(8,128)S(1)} collective-permute-done((f32[64,1024]{1,0:T(8,128)}, f32[64,1024]{1,0:T(8,128)S(1)}, u32[]{:S(2)}, u32[]{:S(2)}) %collective-permute-start.20) | collective-permute-done | bytes 262176 | tf_op jit(solution)/shard_map/ppermute | solution.py:252
  176.5 0.7 copy-done.14
  177.2 2.5 %gather.9 = (f32[64,1024]{1,0:T(8,128)}, f32[16,32,128]{2,1,0:T(8,128)}) custom-call(s32[4]{0:T(128)} %pad_add_fusion.1.meta, f32[64,1024]{1,0:T(8,128)} %get-tuple-element.69.refs_0_, f32[64,1024]{1,0:T(8,128)} %copy-done.14), custom_call_target="tpu_custom_call" | custom-call | flops 1024 | bytes 1024 | tf_op jit(solution)/shard_map/gather/pallas_call | solution.py:287
  179.8 1.1 collective-permute-start.21
  180.9 3.5 %all-to-all-start.2 = ((f32[16,32,128]{2,1,0:T(8,128)}), f32[16,32,128]{2,1,0:T(8,128)S(1)}, u32[]{:S(2)}, u32[]{:S(2)}) async-start(f32[16,32,128]{2,1,0:T(8,128)} %get-tuple-element.71), calls=%async_computation.2 | async-start | bytes 524288 | tf_op jit(solution)/shard_map/all_to_all | solution.py:303
  184.5 0.6 dynamic_slice.3
  185.1 0.6 gather_fusion
  185.7 6.6 %all-to-all-done.2 = f32[16,32,128]{2,1,0:T(8,128)S(1)} async-done(((f32[16,32,128]{2,1,0:T(8,128)}), f32[16,32,128]{2,1,0:T(8,128)S(1)}, u32[]{:S(2)}, u32[]{:S(2)}) %all-to-all-start.2) | async-done | bytes 262176 | tf_op jit(solution)/shard_map/all_to_all | solution.py:303
  192.3 4.6 %collective-permute-start.22 = (f32[512,128]{1,0:T(8,128)S(1)}, f32[512,128]{1,0:T(8,128)S(1)}, u32[]{:S(2)}, u32[]{:S(2)}) collective-permute-start(f32[512,128]{1,0:T(8,128)S(1)} %bitcast.26), channel_id=1, source_target_pairs={{0,32},{32,64},{64,96},{96,128},{128,160},{160,192},{192,224},{1,3... | collective-permute-start | bytes 786440 | tf_op jit(solution)/shard_map/ppermute | solution.py:394
  196.9 0.7 and_convert_fusion
  197.5 0.6 pad_add_fusion.flags
  198.1 4.2 %collective-permute-done.22.near = f32[512,128]{1,0:T(8,128)S(1)} collective-permute-done((f32[512,128]{1,0:T(8,128)S(1)}, f32[512,128]{1,0:T(8,128)S(1)}, u32[]{:S(2)}, u32[]{:S(2)}) %collective-permute-start.22) | collective-permute-done | bytes 262176 | tf_op jit(solution)/shard_map/ppermute | solution.py:394
  202.3 0.7 copy-done.18
  203.0 3.9 %assemble.1 = f32[64,5120]{1,0:T(8,128)} custom-call(s32[6]{0:T(128)} %pad_add_fusion.flags, f32[512,128]{1,0:T(8,128)} %copy-done.16, f32[512,128]{1,0:T(8,128)} %copy-done.18, f32[512,128]{1,0:T(8,128)} %bitcast.27, f32[64,1024]{1,0:T(8,128)} %get-tuple-element.74.rows2, f32[64,1024]{1,0:T(8,128)} %copy-done.17, f32[64,1024]{1,0:T(8,128)} %get-tuple-element.42.rows0_a, ...), custom_call_target="tpu_custom_call" | custom-call | flops 1024 | bytes 1024 | tf_op jit(solution)/shard_map/assemble/pallas_call | solution.py:331
  (52 shorter events, 0.2 us)
Async XLA Ops:
  4.7 3.8 %collective-permute-start.1 = (f32[3,1024]{1,0:T(4,128)S(1)}, f32[3,1024]{1,0:T(4,128)S(1)}, u32[]{:S(2)}, u32[]{:S(2)}) collective-permute-start(f32[3,1024]{1,0:T(4,128)S(1)} %pad_maximum_fusion), channel_id=1, source_target_pairs={{0,8},{1,9},{8,0},{9,1},{2,10},{3,11},{10,2},{11,3},{4,12},{5,13},... | collective-permute-start | bytes 36872 | tf_op jit(solution)/shard_map/ppermute | solution.py:33
  6.3 3.2 %collective-permute-start.2 = (f32[3,1024]{1,0:T(4,128)S(1)}, f32[3,1024]{1,0:T(4,128)S(1)}, u32[]{:S(2)}, u32[]{:S(2)}) collective-permute-start(f32[3,1024]{1,0:T(4,128)S(1)} %pad_maximum_fusion), channel_id=1, source_target_pairs={{0,9},{1,8},{8,1},{9,0},{2,11},{3,10},{10,3},{11,2},{4,13},{5,12},... | collective-permute-start | bytes 36872 | tf_op jit(solution)/shard_map/ppermute | solution.py:33
  6.3 3.2 %collective-permute-start = (f32[3,1024]{1,0:T(4,128)S(1)}, f32[3,1024]{1,0:T(4,128)S(1)}, u32[]{:S(2)}, u32[]{:S(2)}) collective-permute-start(f32[3,1024]{1,0:T(4,128)S(1)} %pad_maximum_fusion), channel_id=1, source_target_pairs={{0,1},{1,0},{8,9},{9,8},{2,3},{3,2},{10,11},{11,10},{4,5},{5,4},{1... | collective-permute-start | bytes 36872 | tf_op jit(solution)/shard_map/ppermute | solution.py:33
  9.5 5.1 %collective-permute-start.5 = (f32[3,1024]{1,0:T(4,128)S(1)}, f32[3,1024]{1,0:T(4,128)S(1)}, u32[]{:S(2)}, u32[]{:S(2)}) collective-permute-start(f32[3,1024]{1,0:T(4,128)S(1)} %add_add_fusion.1), channel_id=1, source_target_pairs={{0,6},{2,0},{4,2},{6,4},{1,7},{3,1},{5,3},{7,5},{8,14},{10,8},{12,... | collective-permute-start | bytes 36872 | tf_op jit(solution)/shard_map/ppermute | solution.py:37
  12.4 5.2 %collective-permute-start.4 = (f32[3,1024]{1,0:T(4,128)S(1)}, f32[3,1024]{1,0:T(4,128)S(1)}, u32[]{:S(2)}, u32[]{:S(2)}) collective-permute-start(f32[3,1024]{1,0:T(4,128)S(1)} %add_add_fusion.1), channel_id=1, source_target_pairs={{0,4},{2,6},{4,0},{6,2},{1,5},{3,7},{5,1},{7,3},{8,12},{10,14},{12... | collective-permute-start | bytes 36872 | tf_op jit(solution)/shard_map/ppermute | solution.py:37
  13.2 4.9 %collective-permute-start.3 = (f32[3,1024]{1,0:T(4,128)S(1)}, f32[3,1024]{1,0:T(4,128)S(1)}, u32[]{:S(2)}, u32[]{:S(2)}) collective-permute-start(f32[3,1024]{1,0:T(4,128)S(1)} %add_add_fusion.1), channel_id=1, source_target_pairs={{0,2},{2,4},{4,6},{6,0},{1,3},{3,5},{5,7},{7,1},{8,10},{10,12},{12... | collective-permute-start | bytes 36872 | tf_op jit(solution)/shard_map/ppermute | solution.py:37
  26.9 5.1 %collective-permute-start.6 = (bf16[1280,1024]{1,0:T(8,128)(2,1)}, bf16[1280,1024]{1,0:T(8,128)(2,1)S(1)}, u32[]{:S(2)}, u32[]{:S(2)}) collective-permute-start(bf16[1280,1024]{1,0:T(8,128)(2,1)} %get-tuple-element.41.right_a.zed_a), channel_id=1, source_target_pairs={{0,1},{1,0},{2,3},{3,2},{4,5},{5,4},{6,7},{7,6},{8,9},{9,8},{10,11... | collective-permute-start | bytes 7864328 | tf_op jit(solution)/shard_map/ppermute | solution.py:377
  26.9 61.0 %collective-permute-start.8 = (bf16[2,8,64,1280]{3,2,1,0:T(8,128)(2,1)}, bf16[2,8,64,1280]{3,2,1,0:T(8,128)(2,1)S(1)}, u32[]{:S(2)}, u32[]{:S(2)}) collective-permute-start(bf16[2,8,64,1280]{3,2,1,0:T(8,128)(2,1)} %get-tuple-element.40), channel_id=1, source_target_pairs={{0,16},{16,0},{32,48},{48,32},{64,80},{80,64},{96,112},{112,96},{1... | collective-permute-start | bytes 7864328 | tf_op jit(solution)/shard_map/ppermute | solution.py:378
  29.8 61.2 %collective-permute-start.7 = (bf16[1280,1024]{1,0:T(8,128)(2,1)}, bf16[1280,1024]{1,0:T(8,128)(2,1)S(1)}, u32[]{:S(2)}, u32[]{:S(2)}) collective-permute-start(bf16[1280,1024]{1,0:T(8,128)(2,1)} %get-tuple-element.41.right_a.zed_a), channel_id=1, source_target_pairs={{32,0},{64,32},{96,64},{128,96},{160,128},{192,160},{224,192},{16,... | collective-permute-start | bytes 7864328 | tf_op jit(solution)/shard_map/ppermute | solution.py:379
  32.0 1.5 copy-start.1
  87.9 24.8 %copy-start.4 = (bf16[2,8,64,1280]{3,2,1,0:T(8,128)(2,1)}, bf16[2,8,64,1280]{3,2,1,0:T(8,128)(2,1)S(1)}, u32[]{:S(2)}) copy-start(bf16[2,8,64,1280]{3,2,1,0:T(8,128)(2,1)S(1)} %collective-permute-done.8) | copy-start | bytes 7864324
  91.1 7.9 %copy-start.2 = (bf16[1280,1024]{1,0:T(8,128)(2,1)}, bf16[1280,1024]{1,0:T(8,128)(2,1)S(1)}, u32[]{:S(2)}) copy-start(bf16[1280,1024]{1,0:T(8,128)(2,1)S(1)} %collective-permute-done.7.right_a.near_a) | copy-start | bytes 7864324
  91.1 7.9 %collective-permute-start.9 = (bf16[1280,1024]{1,0:T(8,128)(2,1)S(1)}, bf16[1280,1024]{1,0:T(8,128)(2,1)S(1)}, u32[]{:S(2)}, u32[]{:S(2)}) collective-permute-start(bf16[1280,1024]{1,0:T(8,128)(2,1)S(1)} %collective-permute-done.7.right_a.near_a), channel_id=1, source_target_pairs={{0,1},{1,0},{2,3},{3,2},{4,5},{5,4},{6,7},{7,6},{8,9},{9,8},{10,11... | collective-permute-start | bytes 7864328 | tf_op jit(solution)/shard_map/ppermute | solution.py:377
  91.2 6.7 %collective-permute-start.10 = (bf16[8,64,1280]{2,1,0:T(8,128)(2,1)S(1)}, bf16[8,64,1280]{2,1,0:T(8,128)(2,1)S(1)}, u32[]{:S(2)}, u32[]{:S(2)}) collective-permute-start(bf16[8,64,1280]{2,1,0:T(8,128)(2,1)S(1)} %slice_bitcast_fusion), channel_id=1, source_target_pairs={{0,1},{1,0},{2,3},{3,2},{4,5},{5,4},{6,7},{7,6},{8,9},{9,8},{10,11... | collective-permute-start | bytes 3932168 | tf_op jit(solution)/shard_map/ppermute | solution.py:377
  97.9 1.1 copy-start.5
  99.0 1.6 copy-start.3
  108.5 27.4 %collective-permute-start.11 = (f32[2,64,1024]{2,1,0:T(8,128)}, f32[2,64,1024]{2,1,0:T(8,128)S(1)}, u32[]{:S(2)}, u32[]{:S(2)}) collective-permute-start(f32[2,64,1024]{2,1,0:T(8,128)} %get-tuple-element.48), channel_id=1, source_target_pairs={{0,2},{2,4},{4,6},{6,0},{1,3},{3,5},{5,7},{7,1},{8,10},{10,12},{12... | collective-permute-start | bytes 1572872 | tf_op jit(solution)/shard_map/ppermute | solution.py:263
  108.6 27.4 %collective-permute-start.12 = (f32[2,64,1024]{2,1,0:T(8,128)}, f32[2,64,1024]{2,1,0:T(8,128)S(1)}, u32[]{:S(2)}, u32[]{:S(2)}) collective-permute-start(f32[2,64,1024]{2,1,0:T(8,128)} %get-tuple-element.49), channel_id=1, source_target_pairs={{0,4},{2,6},{4,0},{6,2},{1,5},{3,7},{5,1},{7,3},{8,12},{10,14},{12... | collective-permute-start | bytes 1572872 | tf_op jit(solution)/shard_map/ppermute | solution.py:263
  110.4 26.5 %collective-permute-start.13 = (f32[2,64,1024]{2,1,0:T(8,128)}, f32[2,64,1024]{2,1,0:T(8,128)S(1)}, u32[]{:S(2)}, u32[]{:S(2)}) collective-permute-start(f32[2,64,1024]{2,1,0:T(8,128)} %get-tuple-element.50), channel_id=1, source_target_pairs={{0,6},{2,0},{4,2},{6,4},{1,7},{3,1},{5,3},{7,5},{8,14},{10,8},{12,... | collective-permute-start | bytes 1572872 | tf_op jit(solution)/shard_map/ppermute | solution.py:263
  112.7 28.3 %copy-start.19 = (f32[64,1024]{1,0:T(8,128)S(1)}, f32[64,1024]{1,0:T(8,128)}, u32[]{:S(2)}) copy-start(f32[64,1024]{1,0:T(8,128)} %get-tuple-element.64) | copy-start | bytes 786436
  122.2 35.4 %collective-permute-start.16 = (f32[2,64,1024]{2,1,0:T(8,128)}, f32[2,64,1024]{2,1,0:T(8,128)S(1)}, u32[]{:S(2)}, u32[]{:S(2)}) collective-permute-start(f32[2,64,1024]{2,1,0:T(8,128)} %get-tuple-element.61), channel_id=1, source_target_pairs={{0,2},{2,4},{4,6},{6,0},{1,3},{3,5},{5,7},{7,1},{8,10},{10,12},{12... | collective-permute-start | bytes 1572872 | tf_op jit(solution)/shard_map/ppermute | solution.py:263
  122.3 35.3 %collective-permute-start.17 = (f32[2,64,1024]{2,1,0:T(8,128)}, f32[2,64,1024]{2,1,0:T(8,128)S(1)}, u32[]{:S(2)}, u32[]{:S(2)}) collective-permute-start(f32[2,64,1024]{2,1,0:T(8,128)} %get-tuple-element.62), channel_id=1, source_target_pairs={{0,4},{2,6},{4,0},{6,2},{1,5},{3,7},{5,1},{7,3},{8,12},{10,14},{12... | collective-permute-start | bytes 1572872 | tf_op jit(solution)/shard_map/ppermute | solution.py:263
  136.0 0.9 copy-start.10
  136.0 22.3 %collective-permute-start.18 = (f32[2,64,1024]{2,1,0:T(8,128)}, f32[2,64,1024]{2,1,0:T(8,128)S(1)}, u32[]{:S(2)}, u32[]{:S(2)}) collective-permute-start(f32[2,64,1024]{2,1,0:T(8,128)} %get-tuple-element.63), channel_id=1, source_target_pairs={{0,6},{2,0},{4,2},{6,4},{1,7},{3,1},{5,3},{7,5},{8,14},{10,8},{12,... | collective-permute-start | bytes 1572872 | tf_op jit(solution)/shard_map/ppermute | solution.py:263
  136.0 1.0 copy-start.11
  136.9 0.8 copy-start.12
  140.7 43.8 %copy-start = (s32[16]{0:T(128)S(1)}, s32[16]{0:T(128)}, u32[]{:S(2)}) copy-start(s32[16]{0:T(128)} %param.5) | copy-start | bytes 196
  140.7 9.5 %collective-permute-start.14 = (f32[64,1024]{1,0:T(8,128)}, f32[64,1024]{1,0:T(8,128)S(1)}, u32[]{:S(2)}, u32[]{:S(2)}) collective-permute-start(f32[64,1024]{1,0:T(8,128)} %get-tuple-element.59), channel_id=1, source_target_pairs={{0,8},{8,0},{1,9},{9,1},{2,10},{10,2},{3,11},{11,3},{4,12},{12,4},... | collective-permute-start | bytes 786440 | tf_op jit(solution)/shard_map/ppermute | solution.py:252
  141.1 16.5 %collective-permute-start.19 = (f32[64,1024]{1,0:T(8,128)S(1)}, f32[64,1024]{1,0:T(8,128)S(1)}, u32[]{:S(2)}, u32[]{:S(2)}) collective-permute-start(f32[64,1024]{1,0:T(8,128)S(1)} %copy-done.19), channel_id=1, source_target_pairs={{0,8},{8,0},{1,9},{9,1},{2,10},{10,2},{3,11},{11,3},{4,12},{12,4},... | collective-permute-start | bytes 786440 | tf_op jit(solution)/shard_map/ppermute | solution.py:252
  150.2 0.7 copy-start.13
  153.5 12.0 %all-to-all-start.1 = ((f32[16,32,128]{2,1,0:T(8,128)}), f32[16,32,128]{2,1,0:T(8,128)S(1)}, u32[]{:S(2)}, u32[]{:S(2)}) async-start(f32[16,32,128]{2,1,0:T(8,128)} %get-tuple-element.60), calls=%async_computation.1 | async-start | bytes 524288 | tf_op jit(solution)/shard_map/all_to_all | solution.py:303
  157.6 44.7 %copy-start.15 = (f32[64,1024]{1,0:T(8,128)}, f32[64,1024]{1,0:T(8,128)S(1)}, u32[]{:S(2)}) copy-start(f32[64,1024]{1,0:T(8,128)S(1)} %collective-permute-done.19.rows0_b) | copy-start | bytes 786436
  157.6 7.8 %copy-start.7 = (f32[2,64,1024]{2,1,0:T(8,128)}, f32[2,64,1024]{2,1,0:T(8,128)S(1)}, u32[]{:S(2)}) copy-start(f32[2,64,1024]{2,1,0:T(8,128)S(1)} %collective-permute-done.16.refs_1_) | copy-start | bytes 1572868
  157.6 7.8 %copy-start.8 = (f32[2,64,1024]{2,1,0:T(8,128)}, f32[2,64,1024]{2,1,0:T(8,128)S(1)}, u32[]{:S(2)}) copy-start(f32[2,64,1024]{2,1,0:T(8,128)S(1)} %collective-permute-done.17.refs_2_) | copy-start | bytes 1572868
  158.3 7.1 %copy-start.9 = (f32[2,64,1024]{2,1,0:T(8,128)}, f32[2,64,1024]{2,1,0:T(8,128)S(1)}, u32[]{:S(2)}) copy-start(f32[2,64,1024]{2,1,0:T(8,128)S(1)} %collective-permute-done.18.refs_3_) | copy-start | bytes 1572868
  168.4 8.1 %collective-permute-start.20 = (f32[64,1024]{1,0:T(8,128)}, f32[64,1024]{1,0:T(8,128)S(1)}, u32[]{:S(2)}, u32[]{:S(2)}) collective-permute-start(f32[64,1024]{1,0:T(8,128)} %get-tuple-element.70), channel_id=1, source_target_pairs={{0,8},{8,0},{1,9},{9,1},{2,10},{10,2},{3,11},{11,3},{4,12},{12,4},... | collective-permute-start | bytes 786440 | tf_op jit(solution)/shard_map/ppermute | solution.py:252
  169.0 16.7 %collective-permute-start.15 = (f32[512,128]{1,0:T(8,128)S(1)}, f32[512,128]{1,0:T(8,128)S(1)}, u32[]{:S(2)}, u32[]{:S(2)}) collective-permute-start(f32[512,128]{1,0:T(8,128)S(1)} %bitcast.28), channel_id=1, source_target_pairs={{0,32},{32,64},{64,96},{96,128},{128,160},{160,192},{192,224},{48,... | collective-permute-start | bytes 786440 | tf_op jit(solution)/shard_map/ppermute | solution.py:390
  176.5 0.7 copy-start.14
  179.8 12.5 %collective-permute-start.21 = (f32[64,1024]{1,0:T(8,128)}, f32[64,1024]{1,0:T(8,128)S(1)}, u32[]{:S(2)}, u32[]{:S(2)}) collective-permute-start(f32[64,1024]{1,0:T(8,128)} %get-tuple-element.72), channel_id=1, source_target_pairs={{0,16},{16,0},{32,48},{48,32},{64,80},{80,64},{96,112},{112,96},{1... | collective-permute-start | bytes 786440 | tf_op jit(solution)/shard_map/ppermute | solution.py:393
  180.9 11.4 %all-to-all-start.2 = ((f32[16,32,128]{2,1,0:T(8,128)}), f32[16,32,128]{2,1,0:T(8,128)S(1)}, u32[]{:S(2)}, u32[]{:S(2)}) async-start(f32[16,32,128]{2,1,0:T(8,128)} %get-tuple-element.71), calls=%async_computation.2 | async-start | bytes 524288 | tf_op jit(solution)/shard_map/all_to_all | solution.py:303
  185.7 16.6 %copy-start.16 = (f32[512,128]{1,0:T(8,128)}, f32[512,128]{1,0:T(8,128)S(1)}, u32[]{:S(2)}) copy-start(f32[512,128]{1,0:T(8,128)S(1)} %collective-permute-done.15.far) | copy-start | bytes 786436
  192.3 10.0 %copy-start.6 = (f32[16,32,128]{2,1,0:T(8,128)}, f32[16,32,128]{2,1,0:T(8,128)S(1)}, u32[]{:S(2)}) copy-start(f32[16,32,128]{2,1,0:T(8,128)S(1)} %all-to-all-done.2) | copy-start | bytes 786436
  192.3 10.0 %copy-start.17 = (f32[64,1024]{1,0:T(8,128)}, f32[64,1024]{1,0:T(8,128)S(1)}, u32[]{:S(2)}) copy-start(f32[64,1024]{1,0:T(8,128)S(1)} %collective-permute-done.21.beside) | copy-start | bytes 786436
  192.3 10.0 %collective-permute-start.22 = (f32[512,128]{1,0:T(8,128)S(1)}, f32[512,128]{1,0:T(8,128)S(1)}, u32[]{:S(2)}, u32[]{:S(2)}) collective-permute-start(f32[512,128]{1,0:T(8,128)S(1)} %bitcast.26), channel_id=1, source_target_pairs={{0,32},{32,64},{64,96},{96,128},{128,160},{160,192},{192,224},{1,3... | collective-permute-start | bytes 786440 | tf_op jit(solution)/shard_map/ppermute | solution.py:394
  202.3 0.7 copy-start.18

commit v10 on v9

--- a/solution.py
+++ b/solution.py
@@ -388,8 +388,8 @@
     rows2 = fold_pieces(meta, rows2, pieces[0])
     rows2, turned2 = gather(meta, *rows2)
     far = lax.ppermute(turned2, SNP, EVEN_UP + ODD_DOWN)
-    rows1 = fold_pieces(meta, pieces, turned2, rows0[1])
-    rows1, turned1 = gather(meta, *rows1)
+    rows1 = fold_pieces(meta, pieces, rows2, rows0[1])
+    rows1, turned1 = gather(meta, *after(rows1, turned2))
     beside = lax.ppermute(rows1, SNP, TO_OTHER)
     near = lax.ppermute(after(turned1, far, beside), SNP, EVEN_UP)
     flags = jnp.concatenate([kept_flags(band, mine), odd]).astype(jnp.int32)

time: 210 us -> 211 us (level)
  blocking collectives: 31.4 us -> 44.4 us
  starting transfers between devices: 39.6 us -> 33.2 us
  waiting for transfers between devices: 62 us -> 57.1 us
    all_to_all x0 -> x1, blocking collectives: none -> 13 us  [gather(): return (rows, lax.all_to_all(packed, SAMP, 0, 0).reshape(HALF, 2 * ROWS))]
    all_to_all x2 -> x1, waiting for transfers between devices: 13.7 us -> 6.56 us  [gather(): return (rows, lax.all_to_all(packed, SAMP, 0, 0).reshape(HALF, 2 * ROWS))]
    ppermute x6, waiting for transfers between devices: 13.2 us -> 17.3 us  [fold_pieces(): lax.ppermute(pieces[k], 'x', [(i, (i + k) % 4) for i in range(4)])]
    all_to_all x2 -> x1, starting transfers between devices: 7.6 us -> 3.53 us  [gather(): return (rows, lax.all_to_all(packed, SAMP, 0, 0).reshape(HALF, 2 * ROWS))]
    ppermute x3, waiting for transfers between devices: 9.97 us -> 7.43 us  [add(): return (keep, lax.ppermute(send, 'yl', SWAP))]
  transfers between devices with their start and end apart: 25 -> 24, of which waited for: 17 -> 15; matrix products, arithmetic and copies ran while one was open for 2% -> 2% of each run, Pallas kernels for 17% -> 17%
where the time goes in v10:
time: 211 us; the launch traced here: 210 us
  Pallas kernels  58 us (27%)
  waiting for transfers between devices  57.1 us (27%)
  blocking collectives  44.4 us (21%)
  starting transfers between devices  33.2 us (16%)
  local copies, waits for them, and re-layouts  9.34 us (4%)
  other arithmetic  7.28 us (3%)
    all_to_all x1, blocking collectives, fold(): parts = lax.all_to_all(parts.reshape(4, 2, rows, columns), 'x', 0, 0)  31.4 us
    ppermute x6, waiting for transfers between devices, fold_pieces(): lax.ppermute(pieces[k], 'x', [(i, (i + k) % 4) for i in range(4)])  17.3 us
    all_to_all x1, blocking collectives, gather(): return (rows, lax.all_to_all(packed, SAMP, 0, 0).reshape(HALF, 2 * ROWS))  13 us
    pallas_call x1, Pallas kernels, across_product(): pl.pallas_call(across_kernel, name='across', out_shape=(f32(2, ROWS, B),)...  9.5 us
    pallas_call x3, Pallas kernels, add(): pl.pallas_call(add_kernel, name='add', out_shape=(f32(rows, columns),) *...  8.86 us
    pallas_call x1, Pallas kernels, standardize(): pl.pallas_call(standard_kernel, name='standardize', out_shape=(bf16(DEPTH...  8.11 us
    unnamed x40, local copies, waits for them, and re-layouts  8.03 us
    pallas_call x1, Pallas kernels, along_product(): pl.pallas_call(along_kernel, name='along', out_shape=(f32(2, ROWS, B),) *...  7.98 us
  transfers between devices with their start and end apart: 24, of which 15 were waited for; matrix products, arithmetic and copies ran while one was open for 2% of the time, Pallas kernels for 17%

profile of v10, /device:TPU:64, one launch (start us, length us, event | category | flops | bytes accessed | tf_op | source)
XLA Modules:
  0.0 209.5 jit_solution(13461949267995532572)
XLA Ops:
  0.0 4.7 %fusion.1 = (f32[1024]{0:T(1024)S(1)}, f32[1024]{0:T(1024)S(1)}, f32[1024]{0:T(1024)S(1)}) fusion(bf16[1280,1024]{1,0:T(8,128)(2,1)} %dosage.1, s32[1280,1024]{1,0:T(8,128)} %observed.1), kind=kLoop, calls=%fused_computation.5 | loop fusion | flops 9171968 | bytes 7876608 | tf_op jit(solution)/shard_map/reduce_sum | solution.py:367
  4.7 1.7 collective-permute-start.1
  6.3 0.6 collective-permute-start
  6.9 1.6 collective-permute-done.1
  8.5 1.0 collective-permute-done.2
  9.5 2.8 %collective-permute-start.5 = (f32[3,1024]{1,0:T(4,128)S(1)}, f32[3,1024]{1,0:T(4,128)S(1)}, u32[]{:S(2)}, u32[]{:S(2)}) collective-permute-start(f32[3,1024]{1,0:T(4,128)S(1)} %add_add_fusion.1), channel_id=1, source_target_pairs={{0,6},{2,0},{4,2},{6,4},{1,7},{3,1},{5,3},{7,5},{8,14},{10,8},{12,... | collective-permute-start | bytes 36872 | tf_op jit(solution)/shard_map/ppermute | solution.py:37
  12.4 0.8 collective-permute-start.4
  13.2 0.9 collective-permute-start.3
  14.1 0.7 pad_add_fusion.1.meta
  14.7 2.9 %collective-permute-done.4 = f32[3,1024]{1,0:T(4,128)S(1)} collective-permute-done((f32[3,1024]{1,0:T(4,128)S(1)}, f32[3,1024]{1,0:T(4,128)S(1)}, u32[]{:S(2)}, u32[]{:S(2)}) %collective-permute-start.4) | collective-permute-done | bytes 12320 | tf_op jit(solution)/shard_map/ppermute | solution.py:37
  17.6 0.5 collective-permute-done.3
  18.2 0.6 pad_maximum_fusion.1.stats
  18.8 8.1 %standardize.1 = (bf16[1280,1024]{1,0:T(8,128)(2,1)}, bf16[2,8,64,1280]{3,2,1,0:T(8,128)(2,1)}) custom-call(s32[4]{0:T(128)} %pad_add_fusion.1.meta, bf16[1280,1024]{1,0:T(8,128)(2,1)} %dosage.1, s32[1280,1024]{1,0:T(8,128)} %observed.1, f32[2,1024]{1,0:T(2,128)} %pad_maximum_fusion.1.stats), custom_call_target="tpu_custom_call" | custom-call | flops 1024 | bytes 1024 | tf_op jit(solution)/shard_map/standardize/pallas_call | solution.py:86
  26.9 2.9 %collective-permute-start.8 = (bf16[2,8,64,1280]{3,2,1,0:T(8,128)(2,1)}, bf16[2,8,64,1280]{3,2,1,0:T(8,128)(2,1)S(1)}, u32[]{:S(2)}, u32[]{:S(2)}) collective-permute-start(bf16[2,8,64,1280]{3,2,1,0:T(8,128)(2,1)} %get-tuple-element.42), channel_id=1, source_target_pairs={{0,16},{16,0},{32,48},{48,32},{64,80},{80,64},{96,112},{112,96},{1... | collective-permute-start | bytes 7864328 | tf_op jit(solution)/shard_map/ppermute | solution.py:378
  29.8 2.0 collective-permute-start.7
  31.8 0.2 collective-permute-done.6.zed.right_b.zed_b
  32.0 1.5 copy-done.1
  33.5 6.7 %turn.1 = bf16[8,64,1280]{2,1,0:T(8,128)(2,1)} custom-call(s32[4]{0:T(128)} %pad_add_fusion.1.meta, bf16[1280,1024]{1,0:T(8,128)(2,1)} %copy-done.1), custom_call_target="tpu_custom_call" | custom-call | flops 1024 | bytes 1024 | tf_op jit(solution)/shard_map/turn/pallas_call | solution.py:120
  40.3 7.8 %own.1 = f32[8,64,1024]{2,1,0:T(8,128)} custom-call(s32[4]{0:T(128)} %pad_add_fusion.1.meta, bf16[1024,1280]{1,0:T(8,128)(2,1)} %bitcast.21, bf16[512,1280]{1,0:T(8,128)(2,1)} %bitcast.19, bf16[1280,1024]{1,0:T(8,128)(2,1)} %get-tuple-element.43.right_a.zed_a, bf16[1280,1024]{1,0:T(8,128)(2,1)} %copy-done.1), custom_call_target="tpu_custom_call" | custom-call | flops 1024 | bytes 1024 | tf_op jit(solution)/shard_map/own/pallas_call | solution.py:142
  48.1 31.4 %all_to_all.15.refs_0_ = f32[4,2,64,1024]{3,2,1,0:T(8,128)} all-to-all(f32[4,2,64,1024]{3,2,1,0:T(8,128)} %bitcast.23), channel_id=1, replica_groups=mesh['z'=8,'yh'=2,'yl'=2,'x'=4,'core'=2] {'x'}, dimensions={0} | all-to-all | bytes 4194304 | tf_op jit(solution)/shard_map/all_to_all | solution.py:257
  79.5 3.0 %add.104 = (f32[64,1024]{1,0:T(8,128)}, f32[64,1024]{1,0:T(8,128)}) custom-call(s32[4]{0:T(128)} %pad_add_fusion.1.meta, f32[4,2,64,1024]{3,2,1,0:T(8,128)} %all_to_all.15.refs_0_), custom_call_target="tpu_custom_call" | custom-call | flops 1024 | bytes 1024 | tf_op jit(solution)/shard_map/add/pallas_call | solution.py:239
  82.4 5.5 %collective-permute-done.8 = bf16[2,8,64,1280]{3,2,1,0:T(8,128)(2,1)S(1)} collective-permute-done((bf16[2,8,64,1280]{3,2,1,0:T(8,128)(2,1)}, bf16[2,8,64,1280]{3,2,1,0:T(8,128)(2,1)S(1)}, u32[]{:S(2)}, u32[]{:S(2)}) %collective-permute-start.8) | collective-permute-done | bytes 2621472 | tf_op jit(solution)/shard_map/ppermute | solution.py:378
  87.9 3.2 %collective-permute-done.7.right_a.near_a = bf16[1280,1024]{1,0:T(8,128)(2,1)S(1)} collective-permute-done((bf16[1280,1024]{1,0:T(8,128)(2,1)}, bf16[1280,1024]{1,0:T(8,128)(2,1)S(1)}, u32[]{:S(2)}, u32[]{:S(2)}) %collective-permute-start.7) | collective-permute-done | bytes 2621472 | tf_op jit(solution)/shard_map/ppermute | solution.py:379
  91.1 0.1 slice_bitcast_fusion
  91.2 0.6 collective-permute-start.10
  91.8 6.1 %collective-permute-done.10 = bf16[8,64,1280]{2,1,0:T(8,128)(2,1)S(1)} collective-permute-done((bf16[8,64,1280]{2,1,0:T(8,128)(2,1)S(1)}, bf16[8,64,1280]{2,1,0:T(8,128)(2,1)S(1)}, u32[]{:S(2)}, u32[]{:S(2)}) %collective-permute-start.10) | collective-permute-done | bytes 1310752 | tf_op jit(solution)/shard_map/ppermute | solution.py:377
  97.9 1.1 copy-done.5
  98.9 1.6 copy-done.3
  100.6 8.0 %along.1 = (f32[2,64,1024]{2,1,0:T(8,128)}, f32[2,64,1024]{2,1,0:T(8,128)}, f32[2,64,1024]{2,1,0:T(8,128)}, f32[2,64,1024]{2,1,0:T(8,128)}) custom-call(s32[4]{0:T(128)} %pad_add_fusion.1.meta, bf16[1024,1280]{1,0:T(8,128)(2,1)} %bitcast.22, bf16[512,1280]{1,0:T(8,128)(2,1)} %bitcast.20, bf16[1280,1024]{1,0:T(8,128)(2,1)} %copy-done.2, ...), custom_call_target="tpu_custom_call" | custom-call | flops 1024 | bytes 1024 | tf_op jit(solution)/shard_map/along/pallas_call | solution.py:174
  108.6 1.8 collective-permute-start.12
  110.4 2.4 %collective-permute-start.13 = (f32[2,64,1024]{2,1,0:T(8,128)}, f32[2,64,1024]{2,1,0:T(8,128)S(1)}, u32[]{:S(2)}, u32[]{:S(2)}) collective-permute-start(f32[2,64,1024]{2,1,0:T(8,128)} %get-tuple-element.52), channel_id=1, source_target_pairs={{0,6},{2,0},{4,2},{6,4},{1,7},{3,1},{5,3},{7,5},{8,14},{10,8},{12,... | collective-permute-start | bytes 1572872 | tf_op jit(solution)/shard_map/ppermute | solution.py:263
  112.8 9.5 %across.1 = (f32[2,64,1024]{2,1,0:T(8,128)}, f32[2,64,1024]{2,1,0:T(8,128)}, f32[2,64,1024]{2,1,0:T(8,128)}, f32[2,64,1024]{2,1,0:T(8,128)}) custom-call(s32[4]{0:T(128)} %pad_add_fusion.1.meta, bf16[1024,1280]{1,0:T(8,128)(2,1)} %bitcast.24, bf16[512,1280]{1,0:T(8,128)(2,1)} %bitcast.25, bf16[1280,1024]{1,0:T(8,128)(2,1)} %copy-done.2, ...), custom_call_target="tpu_custom_call" | custom-call | flops 1024 | bytes 1024 | tf_op jit(solution)/shard_map/across/pallas_call | solution.py:205
  122.3 0.1 collective-permute-start.16
  122.3 2.1 %collective-permute-start.17 = (f32[2,64,1024]{2,1,0:T(8,128)}, f32[2,64,1024]{2,1,0:T(8,128)S(1)}, u32[]{:S(2)}, u32[]{:S(2)}) collective-permute-start(f32[2,64,1024]{2,1,0:T(8,128)} %get-tuple-element.64), channel_id=1, source_target_pairs={{0,4},{2,6},{4,0},{6,2},{1,5},{3,7},{5,1},{7,3},{8,12},{10,14},{12... | collective-permute-start | bytes 1572872 | tf_op jit(solution)/shard_map/ppermute | solution.py:263
  124.4 11.6 %collective-permute-done.11.refs_1_ = f32[2,64,1024]{2,1,0:T(8,128)S(1)} collective-permute-done((f32[2,64,1024]{2,1,0:T(8,128)}, f32[2,64,1024]{2,1,0:T(8,128)S(1)}, u32[]{:S(2)}, u32[]{:S(2)}) %collective-permute-start.11) | collective-permute-done | bytes 524320 | tf_op jit(solution)/shard_map/ppermute | solution.py:263
  136.0 0.9 collective-permute-done.13.refs_3_
  137.0 0.8 copy-done.12
  137.8 2.9 %add.105 = (f32[64,1024]{1,0:T(8,128)}, f32[64,1024]{1,0:T(8,128)}) custom-call(s32[4]{0:T(128)} %pad_add_fusion.1.meta, f32[2,64,1024]{2,1,0:T(8,128)} %get-tuple-element.56.refs_0_, f32[2,64,1024]{2,1,0:T(8,128)} %copy-done.10, f32[2,64,1024]{2,1,0:T(8,128)} %copy-done.11, f32[2,64,1024]{2,1,0:T(8,128)} %copy-done.12), custom_call_target="tpu_custom_call" | custom-call | flops 1024 | bytes 1024 | tf_op jit(solution)/shard_map/add/pallas_call | solution.py:239
  140.7 0.4 collective-permute-start.14
  141.1 1.7 collective-permute-start.19
  142.8 7.4 %collective-permute-done.14.refs_1_ = f32[64,1024]{1,0:T(8,128)S(1)} collective-permute-done((f32[64,1024]{1,0:T(8,128)}, f32[64,1024]{1,0:T(8,128)S(1)}, u32[]{:S(2)}, u32[]{:S(2)}) %collective-permute-start.14) | collective-permute-done | bytes 262176 | tf_op jit(solution)/shard_map/ppermute | solution.py:252
  150.2 0.7 copy-done.14
  150.9 2.5 %gather.8 = (f32[64,1024]{1,0:T(8,128)}, f32[16,32,128]{2,1,0:T(8,128)}) custom-call(s32[4]{0:T(128)} %pad_add_fusion.1.meta, f32[64,1024]{1,0:T(8,128)} %get-tuple-element.60.refs_0_, f32[64,1024]{1,0:T(8,128)} %copy-done.14), custom_call_target="tpu_custom_call" | custom-call | flops 1024 | bytes 1024 | tf_op jit(solution)/shard_map/gather/pallas_call | solution.py:287
  153.5 4.2 %collective-permute-done.16.refs_1_ = f32[2,64,1024]{2,1,0:T(8,128)S(1)} collective-permute-done((f32[2,64,1024]{2,1,0:T(8,128)}, f32[2,64,1024]{2,1,0:T(8,128)S(1)}, u32[]{:S(2)}, u32[]{:S(2)}) %collective-permute-start.16) | collective-permute-done | bytes 524320 | tf_op jit(solution)/shard_map/ppermute | solution.py:263
  157.7 0.7 collective-permute-done.18.refs_3_
  158.3 0.1 copy-done.7
  158.4 0.2 copy-done.8
  158.6 0.5 copy-done.9
  159.1 2.9 %add.106 = (f32[64,1024]{1,0:T(8,128)}, f32[64,1024]{1,0:T(8,128)}) custom-call(s32[4]{0:T(128)} %pad_add_fusion.1.meta, f32[2,64,1024]{2,1,0:T(8,128)} %get-tuple-element.68.refs_0_, f32[2,64,1024]{2,1,0:T(8,128)} %copy-done.7, f32[2,64,1024]{2,1,0:T(8,128)} %copy-done.8, f32[2,64,1024]{2,1,0:T(8,128)} %copy-done.9), custom_call_target="tpu_custom_call" | custom-call | flops 1024 | bytes 1024 | tf_op jit(solution)/shard_map/add/pallas_call | solution.py:239
  162.1 0.3 collective-permute-start.20
  162.4 13.0 %all_to_all.16 = f32[16,32,128]{2,1,0:T(8,128)S(1)} all-to-all(f32[16,32,128]{2,1,0:T(8,128)} %get-tuple-element.62), channel_id=1, replica_groups=mesh['z'=8,'yh'=2,'yl'=2,'x'=4,'core'=2] {'yl','x','core'}, dimensions={0} | all-to-all | bytes 524288 | tf_op jit(solution)/shard_map/all_to_all | solution.py:303
  175.4 5.0 %collective-permute-start.15 = (f32[512,128]{1,0:T(8,128)S(1)}, f32[512,128]{1,0:T(8,128)S(1)}, u32[]{:S(2)}, u32[]{:S(2)}) collective-permute-start(f32[512,128]{1,0:T(8,128)S(1)} %bitcast.28), channel_id=1, source_target_pairs={{0,32},{32,64},{64,96},{96,128},{128,160},{160,192},{192,224},{48,... | collective-permute-start | bytes 786440 | tf_op jit(solution)/shard_map/ppermute | solution.py:390
  180.5 0.7 copy-done.13
  181.1 2.5 %gather.9 = (f32[64,1024]{1,0:T(8,128)}, f32[16,32,128]{2,1,0:T(8,128)}) custom-call(s32[4]{0:T(128)} %pad_add_fusion.1.meta, f32[64,1024]{1,0:T(8,128)} %get-tuple-element.74.refs_0_, f32[64,1024]{1,0:T(8,128)} %copy-done.13), custom_call_target="tpu_custom_call" | custom-call | flops 1024 | bytes 1024 | tf_op jit(solution)/shard_map/gather/pallas_call | solution.py:287
  183.7 3.5 %all-to-all-start.2 = ((f32[16,32,128]{2,1,0:T(8,128)}), f32[16,32,128]{2,1,0:T(8,128)S(1)}, u32[]{:S(2)}, u32[]{:S(2)}) async-start(f32[16,32,128]{2,1,0:T(8,128)} %get-tuple-element.76), calls=%async_computation.2 | async-start | bytes 524288 | tf_op jit(solution)/shard_map/all_to_all | solution.py:303
  187.2 0.6 dynamic_slice.3
  187.8 0.6 gather_fusion
  188.5 6.6 %all-to-all-done.2 = f32[16,32,128]{2,1,0:T(8,128)S(1)} async-done(((f32[16,32,128]{2,1,0:T(8,128)}), f32[16,32,128]{2,1,0:T(8,128)S(1)}, u32[]{:S(2)}, u32[]{:S(2)}) %all-to-all-start.2) | async-done | bytes 262176 | tf_op jit(solution)/shard_map/all_to_all | solution.py:303
  195.1 3.6 %collective-permute-start.22 = (f32[512,128]{1,0:T(8,128)S(1)}, f32[512,128]{1,0:T(8,128)S(1)}, u32[]{:S(2)}, u32[]{:S(2)}) collective-permute-start(f32[512,128]{1,0:T(8,128)S(1)} %bitcast.26), channel_id=1, source_target_pairs={{0,32},{32,64},{64,96},{96,128},{128,160},{160,192},{192,224},{1,3... | collective-permute-start | bytes 786440 | tf_op jit(solution)/shard_map/ppermute | solution.py:394
  198.7 0.7 and_convert_fusion
  199.4 0.6 pad_add_fusion.flags
  200.0 4.9 %collective-permute-done.22.near = f32[512,128]{1,0:T(8,128)S(1)} collective-permute-done((f32[512,128]{1,0:T(8,128)S(1)}, f32[512,128]{1,0:T(8,128)S(1)}, u32[]{:S(2)}, u32[]{:S(2)}) %collective-permute-start.22) | collective-permute-done | bytes 262176 | tf_op jit(solution)/shard_map/ppermute | solution.py:394
  204.9 0.7 copy-done.18
  205.6 3.9 %assemble.1 = f32[64,5120]{1,0:T(8,128)} custom-call(s32[6]{0:T(128)} %pad_add_fusion.flags, f32[512,128]{1,0:T(8,128)} %copy-done.16, f32[512,128]{1,0:T(8,128)} %copy-done.18, f32[512,128]{1,0:T(8,128)} %bitcast.27, f32[64,1024]{1,0:T(8,128)} %get-tuple-element.66.rows2, f32[64,1024]{1,0:T(8,128)} %copy-done.17, f32[64,1024]{1,0:T(8,128)} %get-tuple-element.44.rows0_a, ...), custom_call_target="tpu_custom_call" | custom-call | flops 1024 | bytes 1024 | tf_op jit(solution)/shard_map/assemble/pallas_call | solution.py:331
  (51 shorter events, 0.2 us)
Async XLA Ops:
  4.7 3.8 %collective-permute-start.1 = (f32[3,1024]{1,0:T(4,128)S(1)}, f32[3,1024]{1,0:T(4,128)S(1)}, u32[]{:S(2)}, u32[]{:S(2)}) collective-permute-start(f32[3,1024]{1,0:T(4,128)S(1)} %pad_maximum_fusion), channel_id=1, source_target_pairs={{0,8},{1,9},{8,0},{9,1},{2,10},{3,11},{10,2},{11,3},{4,12},{5,13},... | collective-permute-start | bytes 36872 | tf_op jit(solution)/shard_map/ppermute | solution.py:33
  6.3 3.2 %collective-permute-start.2 = (f32[3,1024]{1,0:T(4,128)S(1)}, f32[3,1024]{1,0:T(4,128)S(1)}, u32[]{:S(2)}, u32[]{:S(2)}) collective-permute-start(f32[3,1024]{1,0:T(4,128)S(1)} %pad_maximum_fusion), channel_id=1, source_target_pairs={{0,9},{1,8},{8,1},{9,0},{2,11},{3,10},{10,3},{11,2},{4,13},{5,12},... | collective-permute-start | bytes 36872 | tf_op jit(solution)/shard_map/ppermute | solution.py:33
  6.3 3.2 %collective-permute-start = (f32[3,1024]{1,0:T(4,128)S(1)}, f32[3,1024]{1,0:T(4,128)S(1)}, u32[]{:S(2)}, u32[]{:S(2)}) collective-permute-start(f32[3,1024]{1,0:T(4,128)S(1)} %pad_maximum_fusion), channel_id=1, source_target_pairs={{0,1},{1,0},{8,9},{9,8},{2,3},{3,2},{10,11},{11,10},{4,5},{5,4},{1... | collective-permute-start | bytes 36872 | tf_op jit(solution)/shard_map/ppermute | solution.py:33
  9.5 5.2 %collective-permute-start.5 = (f32[3,1024]{1,0:T(4,128)S(1)}, f32[3,1024]{1,0:T(4,128)S(1)}, u32[]{:S(2)}, u32[]{:S(2)}) collective-permute-start(f32[3,1024]{1,0:T(4,128)S(1)} %add_add_fusion.1), channel_id=1, source_target_pairs={{0,6},{2,0},{4,2},{6,4},{1,7},{3,1},{5,3},{7,5},{8,14},{10,8},{12,... | collective-permute-start | bytes 36872 | tf_op jit(solution)/shard_map/ppermute | solution.py:37
  12.4 5.2 %collective-permute-start.4 = (f32[3,1024]{1,0:T(4,128)S(1)}, f32[3,1024]{1,0:T(4,128)S(1)}, u32[]{:S(2)}, u32[]{:S(2)}) collective-permute-start(f32[3,1024]{1,0:T(4,128)S(1)} %add_add_fusion.1), channel_id=1, source_target_pairs={{0,4},{2,6},{4,0},{6,2},{1,5},{3,7},{5,1},{7,3},{8,12},{10,14},{12... | collective-permute-start | bytes 36872 | tf_op jit(solution)/shard_map/ppermute | solution.py:37
  13.2 4.9 %collective-permute-start.3 = (f32[3,1024]{1,0:T(4,128)S(1)}, f32[3,1024]{1,0:T(4,128)S(1)}, u32[]{:S(2)}, u32[]{:S(2)}) collective-permute-start(f32[3,1024]{1,0:T(4,128)S(1)} %add_add_fusion.1), channel_id=1, source_target_pairs={{0,2},{2,4},{4,6},{6,0},{1,3},{3,5},{5,7},{7,1},{8,10},{10,12},{12... | collective-permute-start | bytes 36872 | tf_op jit(solution)/shard_map/ppermute | solution.py:37
  26.9 5.1 %collective-permute-start.6 = (bf16[1280,1024]{1,0:T(8,128)(2,1)}, bf16[1280,1024]{1,0:T(8,128)(2,1)S(1)}, u32[]{:S(2)}, u32[]{:S(2)}) collective-permute-start(bf16[1280,1024]{1,0:T(8,128)(2,1)} %get-tuple-element.43.right_a.zed_a), channel_id=1, source_target_pairs={{0,1},{1,0},{2,3},{3,2},{4,5},{5,4},{6,7},{7,6},{8,9},{9,8},{10,11... | collective-permute-start | bytes 7864328 | tf_op jit(solution)/shard_map/ppermute | solution.py:377
  26.9 61.0 %collective-permute-start.8 = (bf16[2,8,64,1280]{3,2,1,0:T(8,128)(2,1)}, bf16[2,8,64,1280]{3,2,1,0:T(8,128)(2,1)S(1)}, u32[]{:S(2)}, u32[]{:S(2)}) collective-permute-start(bf16[2,8,64,1280]{3,2,1,0:T(8,128)(2,1)} %get-tuple-element.42), channel_id=1, source_target_pairs={{0,16},{16,0},{32,48},{48,32},{64,80},{80,64},{96,112},{112,96},{1... | collective-permute-start | bytes 7864328 | tf_op jit(solution)/shard_map/ppermute | solution.py:378
  29.8 61.2 %collective-permute-start.7 = (bf16[1280,1024]{1,0:T(8,128)(2,1)}, bf16[1280,1024]{1,0:T(8,128)(2,1)S(1)}, u32[]{:S(2)}, u32[]{:S(2)}) collective-permute-start(bf16[1280,1024]{1,0:T(8,128)(2,1)} %get-tuple-element.43.right_a.zed_a), channel_id=1, source_target_pairs={{32,0},{64,32},{96,64},{128,96},{160,128},{192,160},{224,192},{16,... | collective-permute-start | bytes 7864328 | tf_op jit(solution)/shard_map/ppermute | solution.py:379
  32.0 1.5 copy-start.1
  87.9 24.9 %copy-start.4 = (bf16[2,8,64,1280]{3,2,1,0:T(8,128)(2,1)}, bf16[2,8,64,1280]{3,2,1,0:T(8,128)(2,1)S(1)}, u32[]{:S(2)}) copy-start(bf16[2,8,64,1280]{3,2,1,0:T(8,128)(2,1)S(1)} %collective-permute-done.8) | copy-start | bytes 7864324
  91.1 7.9 %copy-start.2 = (bf16[1280,1024]{1,0:T(8,128)(2,1)}, bf16[1280,1024]{1,0:T(8,128)(2,1)S(1)}, u32[]{:S(2)}) copy-start(bf16[1280,1024]{1,0:T(8,128)(2,1)S(1)} %collective-permute-done.7.right_a.near_a) | copy-start | bytes 7864324
  91.1 7.9 %collective-permute-start.9 = (bf16[1280,1024]{1,0:T(8,128)(2,1)S(1)}, bf16[1280,1024]{1,0:T(8,128)(2,1)S(1)}, u32[]{:S(2)}, u32[]{:S(2)}) collective-permute-start(bf16[1280,1024]{1,0:T(8,128)(2,1)S(1)} %collective-permute-done.7.right_a.near_a), channel_id=1, source_target_pairs={{0,1},{1,0},{2,3},{3,2},{4,5},{5,4},{6,7},{7,6},{8,9},{9,8},{10,11... | collective-permute-start | bytes 7864328 | tf_op jit(solution)/shard_map/ppermute | solution.py:377
  91.2 6.7 %collective-permute-start.10 = (bf16[8,64,1280]{2,1,0:T(8,128)(2,1)S(1)}, bf16[8,64,1280]{2,1,0:T(8,128)(2,1)S(1)}, u32[]{:S(2)}, u32[]{:S(2)}) collective-permute-start(bf16[8,64,1280]{2,1,0:T(8,128)(2,1)S(1)} %slice_bitcast_fusion), channel_id=1, source_target_pairs={{0,1},{1,0},{2,3},{3,2},{4,5},{5,4},{6,7},{7,6},{8,9},{9,8},{10,11... | collective-permute-start | bytes 3932168 | tf_op jit(solution)/shard_map/ppermute | solution.py:377
  97.9 1.1 copy-start.5
  98.9 1.6 copy-start.3
  108.6 27.4 %collective-permute-start.11 = (f32[2,64,1024]{2,1,0:T(8,128)}, f32[2,64,1024]{2,1,0:T(8,128)S(1)}, u32[]{:S(2)}, u32[]{:S(2)}) collective-permute-start(f32[2,64,1024]{2,1,0:T(8,128)} %get-tuple-element.50), channel_id=1, source_target_pairs={{0,2},{2,4},{4,6},{6,0},{1,3},{3,5},{5,7},{7,1},{8,10},{10,12},{12... | collective-permute-start | bytes 1572872 | tf_op jit(solution)/shard_map/ppermute | solution.py:263
  108.6 27.4 %collective-permute-start.12 = (f32[2,64,1024]{2,1,0:T(8,128)}, f32[2,64,1024]{2,1,0:T(8,128)S(1)}, u32[]{:S(2)}, u32[]{:S(2)}) collective-permute-start(f32[2,64,1024]{2,1,0:T(8,128)} %get-tuple-element.51), channel_id=1, source_target_pairs={{0,4},{2,6},{4,0},{6,2},{1,5},{3,7},{5,1},{7,3},{8,12},{10,14},{12... | collective-permute-start | bytes 1572872 | tf_op jit(solution)/shard_map/ppermute | solution.py:263
  110.4 26.5 %collective-permute-start.13 = (f32[2,64,1024]{2,1,0:T(8,128)}, f32[2,64,1024]{2,1,0:T(8,128)S(1)}, u32[]{:S(2)}, u32[]{:S(2)}) collective-permute-start(f32[2,64,1024]{2,1,0:T(8,128)} %get-tuple-element.52), channel_id=1, source_target_pairs={{0,6},{2,0},{4,2},{6,4},{1,7},{3,1},{5,3},{7,5},{8,14},{10,8},{12,... | collective-permute-start | bytes 1572872 | tf_op jit(solution)/shard_map/ppermute | solution.py:263
  112.7 28.3 %copy-start.19 = (f32[64,1024]{1,0:T(8,128)S(1)}, f32[64,1024]{1,0:T(8,128)}, u32[]{:S(2)}) copy-start(f32[64,1024]{1,0:T(8,128)} %get-tuple-element.67) | copy-start | bytes 786436
  122.3 35.4 %collective-permute-start.16 = (f32[2,64,1024]{2,1,0:T(8,128)}, f32[2,64,1024]{2,1,0:T(8,128)S(1)}, u32[]{:S(2)}, u32[]{:S(2)}) collective-permute-start(f32[2,64,1024]{2,1,0:T(8,128)} %get-tuple-element.63), channel_id=1, source_target_pairs={{0,2},{2,4},{4,6},{6,0},{1,3},{3,5},{5,7},{7,1},{8,10},{10,12},{12... | collective-permute-start | bytes 1572872 | tf_op jit(solution)/shard_map/ppermute | solution.py:263
  122.3 35.3 %collective-permute-start.17 = (f32[2,64,1024]{2,1,0:T(8,128)}, f32[2,64,1024]{2,1,0:T(8,128)S(1)}, u32[]{:S(2)}, u32[]{:S(2)}) collective-permute-start(f32[2,64,1024]{2,1,0:T(8,128)} %get-tuple-element.64), channel_id=1, source_target_pairs={{0,4},{2,6},{4,0},{6,2},{1,5},{3,7},{5,1},{7,3},{8,12},{10,14},{12... | collective-permute-start | bytes 1572872 | tf_op jit(solution)/shard_map/ppermute | solution.py:263
  136.0 0.9 copy-start.10
  136.0 22.3 %collective-permute-start.18 = (f32[2,64,1024]{2,1,0:T(8,128)}, f32[2,64,1024]{2,1,0:T(8,128)S(1)}, u32[]{:S(2)}, u32[]{:S(2)}) collective-permute-start(f32[2,64,1024]{2,1,0:T(8,128)} %get-tuple-element.65), channel_id=1, source_target_pairs={{0,6},{2,0},{4,2},{6,4},{1,7},{3,1},{5,3},{7,5},{8,14},{10,8},{12,... | collective-permute-start | bytes 1572872 | tf_op jit(solution)/shard_map/ppermute | solution.py:263
  136.0 1.0 copy-start.11
  136.9 0.8 copy-start.12
  140.7 46.5 %copy-start = (s32[16]{0:T(128)S(1)}, s32[16]{0:T(128)}, u32[]{:S(2)}) copy-start(s32[16]{0:T(128)} %param.5) | copy-start | bytes 196
  140.7 9.5 %collective-permute-start.14 = (f32[64,1024]{1,0:T(8,128)}, f32[64,1024]{1,0:T(8,128)S(1)}, u32[]{:S(2)}, u32[]{:S(2)}) collective-permute-start(f32[64,1024]{1,0:T(8,128)} %get-tuple-element.61), channel_id=1, source_target_pairs={{0,8},{8,0},{1,9},{9,1},{2,10},{10,2},{3,11},{11,3},{4,12},{12,4},... | collective-permute-start | bytes 786440 | tf_op jit(solution)/shard_map/ppermute | solution.py:252
  141.1 12.4 %collective-permute-start.19 = (f32[64,1024]{1,0:T(8,128)S(1)}, f32[64,1024]{1,0:T(8,128)S(1)}, u32[]{:S(2)}, u32[]{:S(2)}) collective-permute-start(f32[64,1024]{1,0:T(8,128)S(1)} %copy-done.19), channel_id=1, source_target_pairs={{0,8},{8,0},{1,9},{9,1},{2,10},{10,2},{3,11},{11,3},{4,12},{12,4},... | collective-permute-start | bytes 786440 | tf_op jit(solution)/shard_map/ppermute | solution.py:252
  150.2 0.7 copy-start.14
  153.5 51.4 %copy-start.15 = (f32[64,1024]{1,0:T(8,128)}, f32[64,1024]{1,0:T(8,128)S(1)}, u32[]{:S(2)}) copy-start(f32[64,1024]{1,0:T(8,128)S(1)} %collective-permute-done.19.rows0_b) | copy-start | bytes 786436
  157.6 0.8 copy-start.7
  157.7 1.0 copy-start.8
  158.3 0.8 copy-start.9
  162.1 18.3 %collective-permute-start.20 = (f32[64,1024]{1,0:T(8,128)}, f32[64,1024]{1,0:T(8,128)S(1)}, u32[]{:S(2)}, u32[]{:S(2)}) collective-permute-start(f32[64,1024]{1,0:T(8,128)} %get-tuple-element.73), channel_id=1, source_target_pairs={{0,8},{8,0},{1,9},{9,1},{2,10},{10,2},{3,11},{11,3},{4,12},{12,4},... | collective-permute-start | bytes 786440 | tf_op jit(solution)/shard_map/ppermute | solution.py:252
  175.4 13.1 %collective-permute-start.15 = (f32[512,128]{1,0:T(8,128)S(1)}, f32[512,128]{1,0:T(8,128)S(1)}, u32[]{:S(2)}, u32[]{:S(2)}) collective-permute-start(f32[512,128]{1,0:T(8,128)S(1)} %bitcast.28), channel_id=1, source_target_pairs={{0,32},{32,64},{64,96},{96,128},{128,160},{160,192},{192,224},{48,... | collective-permute-start | bytes 786440 | tf_op jit(solution)/shard_map/ppermute | solution.py:390
  180.4 0.7 copy-start.13
  183.7 11.4 %collective-permute-start.21 = (f32[64,1024]{1,0:T(8,128)}, f32[64,1024]{1,0:T(8,128)S(1)}, u32[]{:S(2)}, u32[]{:S(2)}) collective-permute-start(f32[64,1024]{1,0:T(8,128)} %get-tuple-element.77), channel_id=1, source_target_pairs={{0,16},{16,0},{32,48},{48,32},{64,80},{80,64},{96,112},{112,96},{1... | collective-permute-start | bytes 786440 | tf_op jit(solution)/shard_map/ppermute | solution.py:393
  183.7 11.4 %all-to-all-start.2 = ((f32[16,32,128]{2,1,0:T(8,128)}), f32[16,32,128]{2,1,0:T(8,128)S(1)}, u32[]{:S(2)}, u32[]{:S(2)}) async-start(f32[16,32,128]{2,1,0:T(8,128)} %get-tuple-element.76), calls=%async_computation.2 | async-start | bytes 524288 | tf_op jit(solution)/shard_map/all_to_all | solution.py:303
  188.5 16.4 %copy-start.16 = (f32[512,128]{1,0:T(8,128)}, f32[512,128]{1,0:T(8,128)S(1)}, u32[]{:S(2)}) copy-start(f32[512,128]{1,0:T(8,128)S(1)} %collective-permute-done.15.far) | copy-start | bytes 786436
  195.1 9.8 %copy-start.6 = (f32[16,32,128]{2,1,0:T(8,128)}, f32[16,32,128]{2,1,0:T(8,128)S(1)}, u32[]{:S(2)}) copy-start(f32[16,32,128]{2,1,0:T(8,128)S(1)} %all-to-all-done.2) | copy-start | bytes 786436
  195.1 9.8 %copy-start.17 = (f32[64,1024]{1,0:T(8,128)}, f32[64,1024]{1,0:T(8,128)S(1)}, u32[]{:S(2)}) copy-start(f32[64,1024]{1,0:T(8,128)S(1)} %collective-permute-done.21.beside) | copy-start | bytes 786436
  195.1 9.8 %collective-permute-start.22 = (f32[512,128]{1,0:T(8,128)S(1)}, f32[512,128]{1,0:T(8,128)S(1)}, u32[]{:S(2)}, u32[]{:S(2)}) collective-permute-start(f32[512,128]{1,0:T(8,128)S(1)} %bitcast.26), channel_id=1, source_target_pairs={{0,32},{32,64},{64,96},{96,128},{128,160},{160,192},{192,224},{1,3... | collective-permute-start | bytes 786440 | tf_op jit(solution)/shard_map/ppermute | solution.py:394
  204.9 0.7 copy-start.18

commit v11 on v10

--- a/solution.py
+++ b/solution.py
@@ -15,11 +15,9 @@
 NSNP = 16
 B = 1024
 DEPTH = 1280
-HALF = B // 2
 STEP = 256
 PIECES = 8
 ROWS = 64
-TURN = 32
 SWAP = [(0, 1), (1, 0)]
 TO_OTHER = [(i, i ^ 1) for i in range(NSNP)]
 EVEN_DOWN = [(i + 2, i) for i in range(0, NSNP - 2, 2)]
@@ -265,69 +263,49 @@
     return add(meta, *after((pieces[0], *moved), *others))
 
 
-def gather_kernel(meta, *refs):
-    parts, (rows, packed) = refs[:-2], refs[-2:]
-    if len(parts) == 1:
-        parts = [parts[0].at[r] for r in range(PIECES)]
-    total = parts[0][...]
-    for part in parts[1:]:
-        total = total + part[...]
-    rows[...] = total
-    for s in range(2 * STEP // ROWS):
-        packed[s, :, :ROWS] = total[:TURN, ROWS * s : ROWS * (s + 1)]
-        packed[s, :, ROWS:] = total[TURN:, ROWS * s : ROWS * (s + 1)]
+def gather_kernel(meta, along_a, along_b, across_a, across_b, rows2, rows1, both):
+    rows2[...] = along_a[...] + along_b[...]
+    rows1[...] = across_a[...] + across_b[...]
+    for s in range(2 * PIECES):
+        both[s, :, :ROWS] = rows2[:, ROWS * s : ROWS * (s + 1)]
+        both[s, :, ROWS:] = rows1[:, ROWS * s : ROWS * (s + 1)]
 
 
 def gather(meta, *parts):
-    step = 2 * STEP
-    packed = (2 * PIECES, TURN, 2 * ROWS)
-    spec = lambda t: pl.BlockSpec(
-        t.shape[:-1] + (step,), lambda j, m: (0,) * (t.ndim - 1) + (j,)
-    )
-    rows, packed = pl.pallas_call(
+    both = (2 * PIECES, ROWS, 2 * ROWS)
+    return pl.pallas_call(
         gather_kernel,
         name="gather",
-        out_shape=(f32(ROWS, B), f32(*packed)),
-        grid_spec=pltpu.PrefetchScalarGridSpec(
-            num_scalar_prefetch=1,
-            grid=(B // step,),
-            in_specs=[spec(t) for t in parts],
-            out_specs=(
-                pl.BlockSpec((ROWS, step), lambda j, m: (0, j)),
-                pl.BlockSpec((step // ROWS, TURN, 2 * ROWS), lambda j, m: (j, 0, 0)),
-            ),
-        ),
-        compiler_params=params(),
-        cost_estimate=cost(ROWS * B, 16 * ROWS * B),
+        out_shape=(f32(ROWS, B), f32(ROWS, B), f32(*both)),
+        grid_spec=pltpu.PrefetchScalarGridSpec(
+            num_scalar_prefetch=1,
+            grid=(1,),
+            in_specs=[whole((ROWS, B))] * 4,
+            out_specs=(whole((ROWS, B)), whole((ROWS, B)), whole(both)),
+        ),
+        compiler_params=params(),
+        cost_estimate=cost(2 * ROWS * B, 32 * ROWS * B),
     )(meta, *parts)
-    return rows, lax.all_to_all(packed, SAMP, 0, 0).reshape(HALF, 2 * ROWS)
-
-
-def unpack(out, packed):
-    turned = packed[...].T
-    for s in range(2 * PIECES):
-        out[:, ROWS * s : ROWS * s + TURN] = turned[:ROWS, TURN * s : TURN * (s + 1)]
-        out[:, ROWS * s + TURN : ROWS * (s + 1)] = turned[ROWS:, TURN * s : TURN * (s + 1)]
-
-
-def assemble_kernel(flags, far, near, here, rows2, beside, rows0_a, rows0_b, out, far_t, near_t):
+
+
+def assemble_kernel(flags, far, here, rows2, beside, rows0_a, rows0_b, out):
     even = flags[5] == 0
-    unpack(far_t, far)
-    pl.when(even)(lambda: unpack(near_t, near))
-    pl.when(~even)(lambda: unpack(near_t, here))
-    turned, mine = far_t[...], rows2[...]
+    far_turned = far[...].T
+    near = jnp.where(even, far_turned[ROWS:], here[...].T[ROWS:])
+    far2 = far_turned[:ROWS]
+    mine2 = rows2[...]
     blocks = (
-        jnp.where(even, turned, mine),
-        near_t[...],
+        jnp.where(even, far2, mine2),
+        near,
         rows0_a[...] + rows0_b[...],
         beside[...],
-        jnp.where(even, mine, turned),
+        jnp.where(even, mine2, far2),
     )
     for d, block in enumerate(blocks):
         out[:, B * d : B * (d + 1)] = jnp.where(flags[d] > 0, block, 0.0)
 
 
-def assemble(flags, far, near, here, rows2, beside, rows0):
+def assemble(flags, far, here, rows2, beside, rows0):
     return pl.pallas_call(
         assemble_kernel,
         name="assemble",
@@ -335,13 +313,12 @@
         grid_spec=pltpu.PrefetchScalarGridSpec(
             num_scalar_prefetch=1,
             grid=(1,),
-            in_specs=[whole((HALF, 2 * ROWS))] * 3 + [whole((ROWS, B))] * 4,
+            in_specs=[whole((B, 2 * ROWS))] * 2 + [whole((ROWS, B))] * 4,
             out_specs=whole((ROWS, 5 * B)),
-            scratch_shapes=[pltpu.VMEM((ROWS, B), jnp.float32)] * 2,
         ),
         compiler_params=params(),
         cost_estimate=cost(ROWS * 5 * B, 40 * ROWS * B),
-    )(flags, far, near, here, rows2, beside, *rows0)
+    )(flags, far, here, rows2, beside, *rows0)
 
 
 def kept_flags(band, mine):
@@ -386,14 +363,13 @@
     rows2 = along_product(meta, own, after(near, other[1]))
     pieces = across_product(meta, after(other, rows2[0]), near, (zed, zed_b))
     rows2 = fold_pieces(meta, rows2, pieces[0])
-    rows2, turned2 = gather(meta, *rows2)
-    far = lax.ppermute(turned2, SNP, EVEN_UP + ODD_DOWN)
-    rows1 = fold_pieces(meta, pieces, rows2, rows0[1])
-    rows1, turned1 = gather(meta, *after(rows1, turned2))
+    rows1 = fold_pieces(meta, pieces, rows2[1], rows0[1])
+    rows2, rows1, both = gather(meta, *rows2, *rows1)
     beside = lax.ppermute(rows1, SNP, TO_OTHER)
-    near = lax.ppermute(after(turned1, far, beside), SNP, EVEN_UP)
+    here = lax.all_to_all(both, SAMP, 0, 0).reshape(B, 2 * ROWS)
+    far = lax.ppermute(after(here, beside), SNP, EVEN_UP + ODD_DOWN)
     flags = jnp.concatenate([kept_flags(band, mine), odd]).astype(jnp.int32)
-    return assemble(flags, far, near, turned1, rows2, beside, rows0)
+    return assemble(flags, far, here, rows2, beside, rows0)
 
 
 def solution(mesh):

time: 211 us -> 215 us (1.019)
  waiting for transfers between devices: 57.1 us -> 78.3 us
  blocking collectives: 44.4 us -> 31.4 us
  Pallas kernels: 58 us -> 55.5 us
    all_to_all x1 -> x0, blocking collectives: 13 us -> none  [gather(): return (rows, lax.all_to_all(packed, SAMP, 0, 0).reshape(HALF, 2 * ROWS))]
    ppermute x1, waiting for transfers between devices: 0.01 us -> 12.4 us  [on_device(): beside = lax.ppermute(rows1, SNP, TO_OTHER)]
    ppermute x6, waiting for transfers between devices: 17.3 us -> 27.3 us  [fold_pieces(): lax.ppermute(pieces[k], 'x', [(i, (i + k) % 4) for i in range(4)])]
    all_to_all x1, waiting for transfers between devices: 6.56 us -> 0.01 us  [on_device(): here = lax.all_to_all(both, SAMP, 0, 0).reshape(B, 2 * ROWS)]
    ppermute x2 -> x1, waiting for transfers between devices: 4.88 us -> 9.46 us  [on_device(): far = lax.ppermute(after(here, beside), SNP, EVEN_UP + ODD_DOWN)]
    ppermute x2 -> x1, starting transfers between devices: 8.66 us -> 4.87 us  [on_device(): far = lax.ppermute(after(here, beside), SNP, EVEN_UP + ODD_DOWN)]
    pallas_call x2 -> x1, Pallas kernels: 5.06 us -> 2.89 us  [gather(): pl.pallas_call(gather_kernel, name='gather', out_shape=(f32(ROWS, B), f32...]
    unnamed x40 -> x38, local copies, waits for them, and re-layouts: 8.03 us -> 7.35 us
  transfers between devices with their start and end apart: 24 -> 23, of which waited for: 15 -> 16; matrix products, arithmetic and copies ran while one was open for 2% -> 1% of each run, Pallas kernels for 17% -> 14%
where the time goes in v11:
time: 215 us; the launch traced here: 213 us
  waiting for transfers between devices  78.3 us (36%)
  Pallas kernels  55.5 us (26%)
  starting transfers between devices  31.5 us (15%)
  blocking collectives  31.4 us (15%)
  local copies, waits for them, and re-layouts  8.67 us (4%)
  other arithmetic  7.16 us (3%)
    all_to_all x1, blocking collectives, fold(): parts = lax.all_to_all(parts.reshape(4, 2, rows, columns), 'x', 0, 0)  31.4 us
    ppermute x6, waiting for transfers between devices, fold_pieces(): lax.ppermute(pieces[k], 'x', [(i, (i + k) % 4) for i in range(4)])  27.3 us
    ppermute x1, waiting for transfers between devices, on_device(): beside = lax.ppermute(rows1, SNP, TO_OTHER)  12.4 us
    pallas_call x1, Pallas kernels, across_product(): pl.pallas_call(across_kernel, name='across', out_shape=(f32(2, ROWS, B),)...  9.53 us
    ppermute x1, waiting for transfers between devices, on_device(): far = lax.ppermute(after(here, beside), SNP, EVEN_UP + ODD_DOWN)  9.46 us
    pallas_call x3, Pallas kernels, add(): pl.pallas_call(add_kernel, name='add', out_shape=(f32(rows, columns),) *...  8.9 us
    ppermute x3, waiting for transfers between devices, add(): return (keep, lax.ppermute(send, 'yl', SWAP))  8.25 us
    pallas_call x1, Pallas kernels, standardize(): pl.pallas_call(standard_kernel, name='standardize', out_shape=(bf16(DEPTH...  8.14 us
  transfers between devices with their start and end apart: 23, of which 16 were waited for; matrix products, arithmetic and copies ran while one was open for 1% of the time, Pallas kernels for 14%

profile of v11, /device:TPU:64, one launch (start us, length us, event | category | flops | bytes accessed | tf_op | source)
XLA Modules:
  0.0 212.7 jit_solution(15242581265704076760)
XLA Ops:
  0.0 4.7 %fusion.1 = (f32[1024]{0:T(1024)S(1)}, f32[1024]{0:T(1024)S(1)}, f32[1024]{0:T(1024)S(1)}) fusion(bf16[1280,1024]{1,0:T(8,128)(2,1)} %dosage.1, s32[1280,1024]{1,0:T(8,128)} %observed.1), kind=kLoop, calls=%fused_computation.5 | loop fusion | flops 9171968 | bytes 7876608 | tf_op jit(solution)/shard_map/reduce_sum | solution.py:344
  4.7 1.7 collective-permute-start.1
  6.3 0.6 collective-permute-start
  6.9 1.6 collective-permute-done.1
  8.5 1.0 collective-permute-done.2
  9.5 0.0 collective-permute-done
  9.5 2.8 %collective-permute-start.5 = (f32[3,1024]{1,0:T(4,128)S(1)}, f32[3,1024]{1,0:T(4,128)S(1)}, u32[]{:S(2)}, u32[]{:S(2)}) collective-permute-start(f32[3,1024]{1,0:T(4,128)S(1)} %add_add_fusion.1), channel_id=1, source_target_pairs={{0,6},{2,0},{4,2},{6,4},{1,7},{3,1},{5,3},{7,5},{8,14},{10,8},{12,... | collective-permute-start | bytes 36872 | tf_op jit(solution)/shard_map/ppermute | solution.py:35
  12.4 0.8 collective-permute-start.4
  13.2 0.9 collective-permute-start.3
  14.1 0.6 pad_add_fusion.1.meta
  14.7 2.9 %collective-permute-done.4 = f32[3,1024]{1,0:T(4,128)S(1)} collective-permute-done((f32[3,1024]{1,0:T(4,128)S(1)}, f32[3,1024]{1,0:T(4,128)S(1)}, u32[]{:S(2)}, u32[]{:S(2)}) %collective-permute-start.4) | collective-permute-done | bytes 12320 | tf_op jit(solution)/shard_map/ppermute | solution.py:35
  17.6 0.5 collective-permute-done.3
  18.2 0.6 pad_maximum_fusion.1.stats
  18.8 8.1 %standardize.1 = (bf16[1280,1024]{1,0:T(8,128)(2,1)}, bf16[2,8,64,1280]{3,2,1,0:T(8,128)(2,1)}) custom-call(s32[4]{0:T(128)} %pad_add_fusion.1.meta, bf16[1280,1024]{1,0:T(8,128)(2,1)} %dosage.1, s32[1280,1024]{1,0:T(8,128)} %observed.1, f32[2,1024]{1,0:T(2,128)} %pad_maximum_fusion.1.stats), custom_call_target="tpu_custom_call" | custom-call | flops 1024 | bytes 1024 | tf_op jit(solution)/shard_map/standardize/pallas_call | solution.py:84
  26.9 2.9 %collective-permute-start.8 = (bf16[2,8,64,1280]{3,2,1,0:T(8,128)(2,1)}, bf16[2,8,64,1280]{3,2,1,0:T(8,128)(2,1)S(1)}, u32[]{:S(2)}, u32[]{:S(2)}) collective-permute-start(bf16[2,8,64,1280]{3,2,1,0:T(8,128)(2,1)} %get-tuple-element.39), channel_id=1, source_target_pairs={{0,16},{16,0},{32,48},{48,32},{64,80},{80,64},{96,112},{112,96},{1... | collective-permute-start | bytes 7864328 | tf_op jit(solution)/shard_map/ppermute | solution.py:355
  29.8 2.0 collective-permute-start.7
  31.9 0.2 collective-permute-done.6.zed.right_b.zed_b
  32.0 1.5 copy-done.1
  33.6 6.7 %turn.1 = bf16[8,64,1280]{2,1,0:T(8,128)(2,1)} custom-call(s32[4]{0:T(128)} %pad_add_fusion.1.meta, bf16[1280,1024]{1,0:T(8,128)(2,1)} %copy-done.1), custom_call_target="tpu_custom_call" | custom-call | flops 1024 | bytes 1024 | tf_op jit(solution)/shard_map/turn/pallas_call | solution.py:118
  40.3 7.8 %own.1 = f32[8,64,1024]{2,1,0:T(8,128)} custom-call(s32[4]{0:T(128)} %pad_add_fusion.1.meta, bf16[1024,1280]{1,0:T(8,128)(2,1)} %bitcast.20, bf16[512,1280]{1,0:T(8,128)(2,1)} %bitcast.18, bf16[1280,1024]{1,0:T(8,128)(2,1)} %get-tuple-element.40.right_a.zed_a, bf16[1280,1024]{1,0:T(8,128)(2,1)} %copy-done.1), custom_call_target="tpu_custom_call" | custom-call | flops 1024 | bytes 1024 | tf_op jit(solution)/shard_map/own/pallas_call | solution.py:140
  48.1 31.4 %all_to_all.10.refs_0_ = f32[4,2,64,1024]{3,2,1,0:T(8,128)} all-to-all(f32[4,2,64,1024]{3,2,1,0:T(8,128)} %bitcast.22), channel_id=1, replica_groups=mesh['z'=8,'yh'=2,'yl'=2,'x'=4,'core'=2] {'x'}, dimensions={0} | all-to-all | bytes 4194304 | tf_op jit(solution)/shard_map/all_to_all | solution.py:255
  79.5 3.0 %add.104 = (f32[64,1024]{1,0:T(8,128)}, f32[64,1024]{1,0:T(8,128)}) custom-call(s32[4]{0:T(128)} %pad_add_fusion.1.meta, f32[4,2,64,1024]{3,2,1,0:T(8,128)} %all_to_all.10.refs_0_), custom_call_target="tpu_custom_call" | custom-call | flops 1024 | bytes 1024 | tf_op jit(solution)/shard_map/add/pallas_call | solution.py:237
  82.5 5.4 %collective-permute-done.8 = bf16[2,8,64,1280]{3,2,1,0:T(8,128)(2,1)S(1)} collective-permute-done((bf16[2,8,64,1280]{3,2,1,0:T(8,128)(2,1)}, bf16[2,8,64,1280]{3,2,1,0:T(8,128)(2,1)S(1)}, u32[]{:S(2)}, u32[]{:S(2)}) %collective-permute-start.8) | collective-permute-done | bytes 2621472 | tf_op jit(solution)/shard_map/ppermute | solution.py:355
  87.9 3.2 %collective-permute-done.7.right_a.near_a = bf16[1280,1024]{1,0:T(8,128)(2,1)S(1)} collective-permute-done((bf16[1280,1024]{1,0:T(8,128)(2,1)}, bf16[1280,1024]{1,0:T(8,128)(2,1)S(1)}, u32[]{:S(2)}, u32[]{:S(2)}) %collective-permute-start.7) | collective-permute-done | bytes 2621472 | tf_op jit(solution)/shard_map/ppermute | solution.py:356
  91.1 0.1 slice_bitcast_fusion
  91.2 0.6 collective-permute-start.10
  91.8 6.1 %collective-permute-done.10 = bf16[8,64,1280]{2,1,0:T(8,128)(2,1)S(1)} collective-permute-done((bf16[8,64,1280]{2,1,0:T(8,128)(2,1)S(1)}, bf16[8,64,1280]{2,1,0:T(8,128)(2,1)S(1)}, u32[]{:S(2)}, u32[]{:S(2)}) %collective-permute-start.10) | collective-permute-done | bytes 1310752 | tf_op jit(solution)/shard_map/ppermute | solution.py:354
  97.9 1.1 copy-done.6
  98.9 1.6 copy-done.3
  100.5 7.9 %along.1 = (f32[2,64,1024]{2,1,0:T(8,128)}, f32[2,64,1024]{2,1,0:T(8,128)}, f32[2,64,1024]{2,1,0:T(8,128)}, f32[2,64,1024]{2,1,0:T(8,128)}) custom-call(s32[4]{0:T(128)} %pad_add_fusion.1.meta, bf16[1024,1280]{1,0:T(8,128)(2,1)} %bitcast.21, bf16[512,1280]{1,0:T(8,128)(2,1)} %bitcast.19, bf16[1280,1024]{1,0:T(8,128)(2,1)} %copy-done.2, ...), custom_call_target="tpu_custom_call" | custom-call | flops 1024 | bytes 1024 | tf_op jit(solution)/shard_map/along/pallas_call | solution.py:172
  108.5 1.8 collective-permute-start.12
  110.3 2.4 %collective-permute-start.13 = (f32[2,64,1024]{2,1,0:T(8,128)}, f32[2,64,1024]{2,1,0:T(8,128)S(1)}, u32[]{:S(2)}, u32[]{:S(2)}) collective-permute-start(f32[2,64,1024]{2,1,0:T(8,128)} %get-tuple-element.49), channel_id=1, source_target_pairs={{0,6},{2,0},{4,2},{6,4},{1,7},{3,1},{5,3},{7,5},{8,14},{10,8},{12,... | collective-permute-start | bytes 1572872 | tf_op jit(solution)/shard_map/ppermute | solution.py:261
  112.7 9.5 %across.1 = (f32[2,64,1024]{2,1,0:T(8,128)}, f32[2,64,1024]{2,1,0:T(8,128)}, f32[2,64,1024]{2,1,0:T(8,128)}, f32[2,64,1024]{2,1,0:T(8,128)}) custom-call(s32[4]{0:T(128)} %pad_add_fusion.1.meta, bf16[1024,1280]{1,0:T(8,128)(2,1)} %bitcast.23, bf16[512,1280]{1,0:T(8,128)(2,1)} %bitcast.26, bf16[1280,1024]{1,0:T(8,128)(2,1)} %copy-done.2, ...), custom_call_target="tpu_custom_call" | custom-call | flops 1024 | bytes 1024 | tf_op jit(solution)/shard_map/across/pallas_call | solution.py:203
  122.2 0.0 collective-permute-start.15
  122.3 2.1 collective-permute-start.16
  124.4 11.6 %collective-permute-done.11.refs_1_ = f32[2,64,1024]{2,1,0:T(8,128)S(1)} collective-permute-done((f32[2,64,1024]{2,1,0:T(8,128)}, f32[2,64,1024]{2,1,0:T(8,128)S(1)}, u32[]{:S(2)}, u32[]{:S(2)}) %collective-permute-start.11) | collective-permute-done | bytes 524320 | tf_op jit(solution)/shard_map/ppermute | solution.py:261
  135.9 0.4 collective-permute-start.18
  136.4 0.5 collective-permute-done.13.refs_3_
  136.9 0.0 copy-done.10
  136.9 0.8 copy-done.12
  137.7 2.9 %add.105 = (f32[64,1024]{1,0:T(8,128)}, f32[64,1024]{1,0:T(8,128)}) custom-call(s32[4]{0:T(128)} %pad_add_fusion.1.meta, f32[2,64,1024]{2,1,0:T(8,128)} %get-tuple-element.53.refs_0_, f32[2,64,1024]{2,1,0:T(8,128)} %copy-done.9, f32[2,64,1024]{2,1,0:T(8,128)} %copy-done.10, f32[2,64,1024]{2,1,0:T(8,128)} %copy-done.12), custom_call_target="tpu_custom_call" | custom-call | flops 1024 | bytes 1024 | tf_op jit(solution)/shard_map/add/pallas_call | solution.py:237
  140.6 1.3 collective-permute-start.14
  141.9 1.1 collective-permute-done.18.rows0_b
  143.0 14.6 %collective-permute-done.15.refs_1_ = f32[2,64,1024]{2,1,0:T(8,128)S(1)} collective-permute-done((f32[2,64,1024]{2,1,0:T(8,128)}, f32[2,64,1024]{2,1,0:T(8,128)S(1)}, u32[]{:S(2)}, u32[]{:S(2)}) %collective-permute-start.15) | collective-permute-done | bytes 524320 | tf_op jit(solution)/shard_map/ppermute | solution.py:261
  157.6 0.7 collective-permute-done.17.refs_3_
  158.3 0.1 copy-done.7
  158.4 0.2 copy-done.8
  158.5 0.5 copy-done.11
  159.1 3.0 %add.106 = (f32[64,1024]{1,0:T(8,128)}, f32[64,1024]{1,0:T(8,128)}) custom-call(s32[4]{0:T(128)} %pad_add_fusion.1.meta, f32[2,64,1024]{2,1,0:T(8,128)} %get-tuple-element.63.refs_0_, f32[2,64,1024]{2,1,0:T(8,128)} %copy-done.7, f32[2,64,1024]{2,1,0:T(8,128)} %copy-done.8, f32[2,64,1024]{2,1,0:T(8,128)} %copy-done.11), custom_call_target="tpu_custom_call" | custom-call | flops 1024 | bytes 1024 | tf_op jit(solution)/shard_map/add/pallas_call | solution.py:237
  162.0 0.3 collective-permute-start.19
  162.3 7.1 %collective-permute-done.19.across_b = f32[64,1024]{1,0:T(8,128)S(1)} collective-permute-done((f32[64,1024]{1,0:T(8,128)}, f32[64,1024]{1,0:T(8,128)S(1)}, u32[]{:S(2)}, u32[]{:S(2)}) %collective-permute-start.19) | collective-permute-done | bytes 262176 | tf_op jit(solution)/shard_map/ppermute | solution.py:250
  169.4 0.7 copy-done.17
  170.1 2.9 %gather.7 = (f32[64,1024]{1,0:T(8,128)}, f32[64,1024]{1,0:T(8,128)}, f32[16,64,128]{2,1,0:T(8,128)}) custom-call(s32[4]{0:T(128)} %pad_add_fusion.1.meta, f32[64,1024]{1,0:T(8,128)} %get-tuple-element.57.along_a, f32[64,1024]{1,0:T(8,128)} %copy-done.16, f32[64,1024]{1,0:T(8,128)} %get-tuple-element.67.across_a, f32[64,1024]{1,0:T(8,128)} %copy-done.17), custom_call_target="tpu_custom_call" | custom-call | flops 1024 | bytes 1024 | tf_op jit(solution)/shard_map/gather/pallas_call | solution.py:276
  173.0 4.9 %all-to-all-start.1 = ((f32[16,64,128]{2,1,0:T(8,128)}), f32[16,64,128]{2,1,0:T(8,128)S(1)}, u32[]{:S(2)}, u32[]{:S(2)}) async-start(f32[16,64,128]{2,1,0:T(8,128)} %get-tuple-element.69), calls=%async_computation.1 | async-start | bytes 1048576 | tf_op jit(solution)/shard_map/all_to_all | solution.py:369
  177.9 1.2 collective-permute-start.20
  179.1 0.6 dynamic_slice.3
  179.7 12.4 %collective-permute-done.20.beside = f32[64,1024]{1,0:T(8,128)S(1)} collective-permute-done((f32[64,1024]{1,0:T(8,128)}, f32[64,1024]{1,0:T(8,128)S(1)}, u32[]{:S(2)}, u32[]{:S(2)}) %collective-permute-start.20) | collective-permute-done | bytes 262176 | tf_op jit(solution)/shard_map/ppermute | solution.py:368
  192.1 4.9 %collective-permute-start.21 = (f32[1024,128]{1,0:T(8,128)S(1)}, f32[1024,128]{1,0:T(8,128)S(1)}, u32[]{:S(2)}, u32[]{:S(2)}) collective-permute-start(f32[1024,128]{1,0:T(8,128)S(1)} %bitcast.24), channel_id=1, source_target_pairs={{0,32},{32,64},{64,96},{96,128},{128,160},{160,192},{192,224},{48,... | collective-permute-start | bytes 1572872 | tf_op jit(solution)/shard_map/ppermute | solution.py:370
  197.0 0.6 gather_fusion
  197.7 0.6 and_convert_fusion
  198.3 0.6 pad_add_fusion.flags
  198.9 9.5 %collective-permute-done.21.far = f32[1024,128]{1,0:T(8,128)S(1)} collective-permute-done((f32[1024,128]{1,0:T(8,128)S(1)}, f32[1024,128]{1,0:T(8,128)S(1)}, u32[]{:S(2)}, u32[]{:S(2)}) %collective-permute-start.21) | collective-permute-done | bytes 524320 | tf_op jit(solution)/shard_map/ppermute | solution.py:370
  208.4 0.8 copy-done.13
  209.2 3.6 %assemble.1 = f32[64,5120]{1,0:T(8,128)} custom-call(s32[6]{0:T(128)} %pad_add_fusion.flags, f32[1024,128]{1,0:T(8,128)} %copy-done.13, f32[1024,128]{1,0:T(8,128)} %bitcast.25, f32[64,1024]{1,0:T(8,128)} %get-tuple-element.72.rows2, f32[64,1024]{1,0:T(8,128)} %copy-done.15, f32[64,1024]{1,0:T(8,128)} %get-tuple-element.41.rows0_a, f32[64,1024]{1,0:T(8,128)} %copy-done.14), custom_call_target="tpu_custom_call" | custom-call | flops 1024 | bytes 1024 | tf_op jit(solution)/shard_map/assemble/pallas_call | solution.py:309
  (45 shorter events, 0.2 us)
Async XLA Ops:
  4.7 3.8 %collective-permute-start.1 = (f32[3,1024]{1,0:T(4,128)S(1)}, f32[3,1024]{1,0:T(4,128)S(1)}, u32[]{:S(2)}, u32[]{:S(2)}) collective-permute-start(f32[3,1024]{1,0:T(4,128)S(1)} %pad_maximum_fusion), channel_id=1, source_target_pairs={{0,8},{1,9},{8,0},{9,1},{2,10},{3,11},{10,2},{11,3},{4,12},{5,13},... | collective-permute-start | bytes 36872 | tf_op jit(solution)/shard_map/ppermute | solution.py:31
  6.3 3.2 %collective-permute-start.2 = (f32[3,1024]{1,0:T(4,128)S(1)}, f32[3,1024]{1,0:T(4,128)S(1)}, u32[]{:S(2)}, u32[]{:S(2)}) collective-permute-start(f32[3,1024]{1,0:T(4,128)S(1)} %pad_maximum_fusion), channel_id=1, source_target_pairs={{0,9},{1,8},{8,1},{9,0},{2,11},{3,10},{10,3},{11,2},{4,13},{5,12},... | collective-permute-start | bytes 36872 | tf_op jit(solution)/shard_map/ppermute | solution.py:31
  6.3 3.2 %collective-permute-start = (f32[3,1024]{1,0:T(4,128)S(1)}, f32[3,1024]{1,0:T(4,128)S(1)}, u32[]{:S(2)}, u32[]{:S(2)}) collective-permute-start(f32[3,1024]{1,0:T(4,128)S(1)} %pad_maximum_fusion), channel_id=1, source_target_pairs={{0,1},{1,0},{8,9},{9,8},{2,3},{3,2},{10,11},{11,10},{4,5},{5,4},{1... | collective-permute-start | bytes 36872 | tf_op jit(solution)/shard_map/ppermute | solution.py:31
  9.5 5.1 %collective-permute-start.5 = (f32[3,1024]{1,0:T(4,128)S(1)}, f32[3,1024]{1,0:T(4,128)S(1)}, u32[]{:S(2)}, u32[]{:S(2)}) collective-permute-start(f32[3,1024]{1,0:T(4,128)S(1)} %add_add_fusion.1), channel_id=1, source_target_pairs={{0,6},{2,0},{4,2},{6,4},{1,7},{3,1},{5,3},{7,5},{8,14},{10,8},{12,... | collective-permute-start | bytes 36872 | tf_op jit(solution)/shard_map/ppermute | solution.py:35
  12.4 5.2 %collective-permute-start.4 = (f32[3,1024]{1,0:T(4,128)S(1)}, f32[3,1024]{1,0:T(4,128)S(1)}, u32[]{:S(2)}, u32[]{:S(2)}) collective-permute-start(f32[3,1024]{1,0:T(4,128)S(1)} %add_add_fusion.1), channel_id=1, source_target_pairs={{0,4},{2,6},{4,0},{6,2},{1,5},{3,7},{5,1},{7,3},{8,12},{10,14},{12... | collective-permute-start | bytes 36872 | tf_op jit(solution)/shard_map/ppermute | solution.py:35
  13.2 4.9 %collective-permute-start.3 = (f32[3,1024]{1,0:T(4,128)S(1)}, f32[3,1024]{1,0:T(4,128)S(1)}, u32[]{:S(2)}, u32[]{:S(2)}) collective-permute-start(f32[3,1024]{1,0:T(4,128)S(1)} %add_add_fusion.1), channel_id=1, source_target_pairs={{0,2},{2,4},{4,6},{6,0},{1,3},{3,5},{5,7},{7,1},{8,10},{10,12},{12... | collective-permute-start | bytes 36872 | tf_op jit(solution)/shard_map/ppermute | solution.py:35
  26.9 5.1 %collective-permute-start.6 = (bf16[1280,1024]{1,0:T(8,128)(2,1)}, bf16[1280,1024]{1,0:T(8,128)(2,1)S(1)}, u32[]{:S(2)}, u32[]{:S(2)}) collective-permute-start(bf16[1280,1024]{1,0:T(8,128)(2,1)} %get-tuple-element.40.right_a.zed_a), channel_id=1, source_target_pairs={{0,1},{1,0},{2,3},{3,2},{4,5},{5,4},{6,7},{7,6},{8,9},{9,8},{10,11... | collective-permute-start | bytes 7864328 | tf_op jit(solution)/shard_map/ppermute | solution.py:354
  26.9 61.0 %collective-permute-start.8 = (bf16[2,8,64,1280]{3,2,1,0:T(8,128)(2,1)}, bf16[2,8,64,1280]{3,2,1,0:T(8,128)(2,1)S(1)}, u32[]{:S(2)}, u32[]{:S(2)}) collective-permute-start(bf16[2,8,64,1280]{3,2,1,0:T(8,128)(2,1)} %get-tuple-element.39), channel_id=1, source_target_pairs={{0,16},{16,0},{32,48},{48,32},{64,80},{80,64},{96,112},{112,96},{1... | collective-permute-start | bytes 7864328 | tf_op jit(solution)/shard_map/ppermute | solution.py:355
  29.8 61.2 %collective-permute-start.7 = (bf16[1280,1024]{1,0:T(8,128)(2,1)}, bf16[1280,1024]{1,0:T(8,128)(2,1)S(1)}, u32[]{:S(2)}, u32[]{:S(2)}) collective-permute-start(bf16[1280,1024]{1,0:T(8,128)(2,1)} %get-tuple-element.40.right_a.zed_a), channel_id=1, source_target_pairs={{32,0},{64,32},{96,64},{128,96},{160,128},{192,160},{224,192},{16,... | collective-permute-start | bytes 7864328 | tf_op jit(solution)/shard_map/ppermute | solution.py:356
  32.0 1.5 copy-start.1
  87.9 24.8 %copy-start.4 = (bf16[2,8,64,1280]{3,2,1,0:T(8,128)(2,1)}, bf16[2,8,64,1280]{3,2,1,0:T(8,128)(2,1)S(1)}, u32[]{:S(2)}) copy-start(bf16[2,8,64,1280]{3,2,1,0:T(8,128)(2,1)S(1)} %collective-permute-done.8) | copy-start | bytes 7864324
  91.1 7.9 %copy-start.2 = (bf16[1280,1024]{1,0:T(8,128)(2,1)}, bf16[1280,1024]{1,0:T(8,128)(2,1)S(1)}, u32[]{:S(2)}) copy-start(bf16[1280,1024]{1,0:T(8,128)(2,1)S(1)} %collective-permute-done.7.right_a.near_a) | copy-start | bytes 7864324
  91.1 7.8 %collective-permute-start.9 = (bf16[1280,1024]{1,0:T(8,128)(2,1)S(1)}, bf16[1280,1024]{1,0:T(8,128)(2,1)S(1)}, u32[]{:S(2)}, u32[]{:S(2)}) collective-permute-start(bf16[1280,1024]{1,0:T(8,128)(2,1)S(1)} %collective-permute-done.7.right_a.near_a), channel_id=1, source_target_pairs={{0,1},{1,0},{2,3},{3,2},{4,5},{5,4},{6,7},{7,6},{8,9},{9,8},{10,11... | collective-permute-start | bytes 7864328 | tf_op jit(solution)/shard_map/ppermute | solution.py:354
  91.2 6.7 %collective-permute-start.10 = (bf16[8,64,1280]{2,1,0:T(8,128)(2,1)S(1)}, bf16[8,64,1280]{2,1,0:T(8,128)(2,1)S(1)}, u32[]{:S(2)}, u32[]{:S(2)}) collective-permute-start(bf16[8,64,1280]{2,1,0:T(8,128)(2,1)S(1)} %slice_bitcast_fusion), channel_id=1, source_target_pairs={{0,1},{1,0},{2,3},{3,2},{4,5},{5,4},{6,7},{7,6},{8,9},{9,8},{10,11... | collective-permute-start | bytes 3932168 | tf_op jit(solution)/shard_map/ppermute | solution.py:354
  97.9 1.1 copy-start.6
  98.9 1.6 copy-start.3
  108.5 27.4 %collective-permute-start.11 = (f32[2,64,1024]{2,1,0:T(8,128)}, f32[2,64,1024]{2,1,0:T(8,128)S(1)}, u32[]{:S(2)}, u32[]{:S(2)}) collective-permute-start(f32[2,64,1024]{2,1,0:T(8,128)} %get-tuple-element.47), channel_id=1, source_target_pairs={{0,2},{2,4},{4,6},{6,0},{1,3},{3,5},{5,7},{7,1},{8,10},{10,12},{12... | collective-permute-start | bytes 1572872 | tf_op jit(solution)/shard_map/ppermute | solution.py:261
  108.5 27.4 %collective-permute-start.12 = (f32[2,64,1024]{2,1,0:T(8,128)}, f32[2,64,1024]{2,1,0:T(8,128)S(1)}, u32[]{:S(2)}, u32[]{:S(2)}) collective-permute-start(f32[2,64,1024]{2,1,0:T(8,128)} %get-tuple-element.48), channel_id=1, source_target_pairs={{0,4},{2,6},{4,0},{6,2},{1,5},{3,7},{5,1},{7,3},{8,12},{10,14},{12... | collective-permute-start | bytes 1572872 | tf_op jit(solution)/shard_map/ppermute | solution.py:261
  110.3 26.5 %collective-permute-start.13 = (f32[2,64,1024]{2,1,0:T(8,128)}, f32[2,64,1024]{2,1,0:T(8,128)S(1)}, u32[]{:S(2)}, u32[]{:S(2)}) collective-permute-start(f32[2,64,1024]{2,1,0:T(8,128)} %get-tuple-element.49), channel_id=1, source_target_pairs={{0,6},{2,0},{4,2},{6,4},{1,7},{3,1},{5,3},{7,5},{8,14},{10,8},{12,... | collective-permute-start | bytes 1572872 | tf_op jit(solution)/shard_map/ppermute | solution.py:261
  112.7 23.3 %copy-start.18 = (f32[64,1024]{1,0:T(8,128)S(1)}, f32[64,1024]{1,0:T(8,128)}, u32[]{:S(2)}) copy-start(f32[64,1024]{1,0:T(8,128)} %get-tuple-element.62) | copy-start | bytes 786436
  122.2 35.4 %collective-permute-start.15 = (f32[2,64,1024]{2,1,0:T(8,128)}, f32[2,64,1024]{2,1,0:T(8,128)S(1)}, u32[]{:S(2)}, u32[]{:S(2)}) collective-permute-start(f32[2,64,1024]{2,1,0:T(8,128)} %get-tuple-element.59), channel_id=1, source_target_pairs={{0,2},{2,4},{4,6},{6,0},{1,3},{3,5},{5,7},{7,1},{8,10},{10,12},{12... | collective-permute-start | bytes 1572872 | tf_op jit(solution)/shard_map/ppermute | solution.py:261
  122.3 35.3 %collective-permute-start.16 = (f32[2,64,1024]{2,1,0:T(8,128)}, f32[2,64,1024]{2,1,0:T(8,128)S(1)}, u32[]{:S(2)}, u32[]{:S(2)}) collective-permute-start(f32[2,64,1024]{2,1,0:T(8,128)} %get-tuple-element.60), channel_id=1, source_target_pairs={{0,4},{2,6},{4,0},{6,2},{1,5},{3,7},{5,1},{7,3},{8,12},{10,14},{12... | collective-permute-start | bytes 1572872 | tf_op jit(solution)/shard_map/ppermute | solution.py:261
  135.9 0.9 copy-start.9
  135.9 22.3 %collective-permute-start.17 = (f32[2,64,1024]{2,1,0:T(8,128)}, f32[2,64,1024]{2,1,0:T(8,128)S(1)}, u32[]{:S(2)}, u32[]{:S(2)}) collective-permute-start(f32[2,64,1024]{2,1,0:T(8,128)} %get-tuple-element.61), channel_id=1, source_target_pairs={{0,6},{2,0},{4,2},{6,4},{1,7},{3,1},{5,3},{7,5},{8,14},{10,8},{12,... | collective-permute-start | bytes 1572872 | tf_op jit(solution)/shard_map/ppermute | solution.py:261
  135.9 0.9 copy-start.10
  135.9 7.1 %collective-permute-start.18 = (f32[64,1024]{1,0:T(8,128)S(1)}, f32[64,1024]{1,0:T(8,128)S(1)}, u32[]{:S(2)}, u32[]{:S(2)}) collective-permute-start(f32[64,1024]{1,0:T(8,128)S(1)} %copy-done.18), channel_id=1, source_target_pairs={{0,8},{8,0},{1,9},{9,1},{2,10},{10,2},{3,11},{11,3},{4,12},{12,4},... | collective-permute-start | bytes 786440 | tf_op jit(solution)/shard_map/ppermute | solution.py:250
  136.9 0.8 copy-start.12
  140.6 38.5 %copy-start = (s32[16]{0:T(128)S(1)}, s32[16]{0:T(128)}, u32[]{:S(2)}) copy-start(s32[16]{0:T(128)} %param.5) | copy-start | bytes 196
  140.6 17.6 %collective-permute-start.14 = (f32[64,1024]{1,0:T(8,128)}, f32[64,1024]{1,0:T(8,128)S(1)}, u32[]{:S(2)}, u32[]{:S(2)}) collective-permute-start(f32[64,1024]{1,0:T(8,128)} %get-tuple-element.58), channel_id=1, source_target_pairs={{0,8},{8,0},{1,9},{9,1},{2,10},{10,2},{3,11},{11,3},{4,12},{12,4},... | collective-permute-start | bytes 786440 | tf_op jit(solution)/shard_map/ppermute | solution.py:250
  143.0 65.3 %copy-start.14 = (f32[64,1024]{1,0:T(8,128)}, f32[64,1024]{1,0:T(8,128)S(1)}, u32[]{:S(2)}) copy-start(f32[64,1024]{1,0:T(8,128)S(1)} %collective-permute-done.18.rows0_b) | copy-start | bytes 786436
  157.6 0.8 copy-start.7
  157.6 0.9 copy-start.8
  158.3 0.8 copy-start.11
  159.1 10.4 %copy-start.16 = (f32[64,1024]{1,0:T(8,128)}, f32[64,1024]{1,0:T(8,128)S(1)}, u32[]{:S(2)}) copy-start(f32[64,1024]{1,0:T(8,128)S(1)} %collective-permute-done.14.along_b) | copy-start | bytes 786436
  162.0 7.4 %collective-permute-start.19 = (f32[64,1024]{1,0:T(8,128)}, f32[64,1024]{1,0:T(8,128)S(1)}, u32[]{:S(2)}, u32[]{:S(2)}) collective-permute-start(f32[64,1024]{1,0:T(8,128)} %get-tuple-element.68), channel_id=1, source_target_pairs={{0,8},{8,0},{1,9},{9,1},{2,10},{10,2},{3,11},{11,3},{4,12},{12,4},... | collective-permute-start | bytes 786440 | tf_op jit(solution)/shard_map/ppermute | solution.py:250
  169.4 0.7 copy-start.17
  173.0 19.1 %all-to-all-start.1 = ((f32[16,64,128]{2,1,0:T(8,128)}), f32[16,64,128]{2,1,0:T(8,128)S(1)}, u32[]{:S(2)}, u32[]{:S(2)}) async-start(f32[16,64,128]{2,1,0:T(8,128)} %get-tuple-element.69), calls=%async_computation.1 | async-start | bytes 1048576 | tf_op jit(solution)/shard_map/all_to_all | solution.py:369
  177.9 14.2 %collective-permute-start.20 = (f32[64,1024]{1,0:T(8,128)}, f32[64,1024]{1,0:T(8,128)S(1)}, u32[]{:S(2)}, u32[]{:S(2)}) collective-permute-start(f32[64,1024]{1,0:T(8,128)} %get-tuple-element.70), channel_id=1, source_target_pairs={{0,16},{16,0},{32,48},{48,32},{64,80},{80,64},{96,112},{112,96},{1... | collective-permute-start | bytes 786440 | tf_op jit(solution)/shard_map/ppermute | solution.py:368
  192.1 16.2 %copy-start.15 = (f32[64,1024]{1,0:T(8,128)}, f32[64,1024]{1,0:T(8,128)S(1)}, u32[]{:S(2)}) copy-start(f32[64,1024]{1,0:T(8,128)S(1)} %collective-permute-done.20.beside) | copy-start | bytes 786436
  192.1 16.2 %copy-start.5 = (f32[16,64,128]{2,1,0:T(8,128)}, f32[16,64,128]{2,1,0:T(8,128)S(1)}, u32[]{:S(2)}) copy-start(f32[16,64,128]{2,1,0:T(8,128)S(1)} %all-to-all-done.1) | copy-start | bytes 1572868
  192.1 16.2 %collective-permute-start.21 = (f32[1024,128]{1,0:T(8,128)S(1)}, f32[1024,128]{1,0:T(8,128)S(1)}, u32[]{:S(2)}, u32[]{:S(2)}) collective-permute-start(f32[1024,128]{1,0:T(8,128)S(1)} %bitcast.24), channel_id=1, source_target_pairs={{0,32},{32,64},{64,96},{96,128},{128,160},{160,192},{192,224},{48,... | collective-permute-start | bytes 1572872 | tf_op jit(solution)/shard_map/ppermute | solution.py:370
  208.3 0.8 copy-start.13

commit v12 on v9

--- a/solution.py
+++ b/solution.py
@@ -16,7 +16,7 @@
 B = 1024
 DEPTH = 1280
 HALF = B // 2
-STEP = 256
+STEP = 512
 PIECES = 8
 ROWS = 64
 TURN = 32

time: 210 us -> 210 us (level)
  transfers between devices with their start and end apart: 25 -> 25, of which waited for: 17 -> 16; matrix products, arithmetic and copies ran while one was open for 2% -> 2% of each run, Pallas kernels for 17% -> 17%
where the time goes in v12:
time: 210 us; the launch traced here: 206 us
  waiting for transfers between devices  62.8 us (30%)
  Pallas kernels  57 us (27%)
  starting transfers between devices  39.5 us (19%)
  blocking collectives  31.4 us (15%)
  local copies, waits for them, and re-layouts  8.48 us (4%)
  other arithmetic  7.19 us (3%)
    all_to_all x1, blocking collectives, fold(): parts = lax.all_to_all(parts.reshape(4, 2, rows, columns), 'x', 0, 0)  31.4 us
    all_to_all x2, waiting for transfers between devices, gather(): return (rows, lax.all_to_all(packed, SAMP, 0, 0).reshape(HALF, 2 * ROWS))  13.7 us
    ppermute x6, waiting for transfers between devices, fold_pieces(): lax.ppermute(pieces[k], 'x', [(i, (i + k) % 4) for i in range(4)])  13.6 us
    ppermute x3, waiting for transfers between devices, add(): return (keep, lax.ppermute(send, 'yl', SWAP))  9.96 us
    pallas_call x3, Pallas kernels, add(): pl.pallas_call(add_kernel, name='add', out_shape=(f32(rows, columns),) *...  9.28 us
    pallas_call x1, Pallas kernels, across_product(): pl.pallas_call(across_kernel, name='across', out_shape=(f32(2, ROWS, B),)...  9.12 us
    pallas_call x1, Pallas kernels, standardize(): pl.pallas_call(standard_kernel, name='standardize', out_shape=(bf16(DEPTH...  8.13 us
    all_to_all x2, starting transfers between devices, gather(): return (rows, lax.all_to_all(packed, SAMP, 0, 0).reshape(HALF, 2 * ROWS))  7.6 us
  transfers between devices with their start and end apart: 25, of which 16 were waited for; matrix products, arithmetic and copies ran while one was open for 2% of the time, Pallas kernels for 17%

profile of v12, /device:TPU:64, one launch (start us, length us, event | category | flops | bytes accessed | tf_op | source)
XLA Modules:
  0.0 206.5 jit_solution(6289542580501675086)
XLA Ops:
  0.0 4.7 %fusion.1 = (f32[1024]{0:T(1024)S(1)}, f32[1024]{0:T(1024)S(1)}, f32[1024]{0:T(1024)S(1)}) fusion(bf16[1280,1024]{1,0:T(8,128)(2,1)} %dosage.1, s32[1280,1024]{1,0:T(8,128)} %observed.1), kind=kLoop, calls=%fused_computation.5 | loop fusion | flops 9171968 | bytes 7876608 | tf_op jit(solution)/shard_map/reduce_sum | solution.py:367
  4.7 1.7 collective-permute-start.1
  6.3 0.6 collective-permute-start
  6.9 1.6 collective-permute-done.1
  8.5 1.0 collective-permute-done.2
  9.5 2.8 %collective-permute-start.5 = (f32[3,1024]{1,0:T(4,128)S(1)}, f32[3,1024]{1,0:T(4,128)S(1)}, u32[]{:S(2)}, u32[]{:S(2)}) collective-permute-start(f32[3,1024]{1,0:T(4,128)S(1)} %add_add_fusion.1), channel_id=1, source_target_pairs={{0,6},{2,0},{4,2},{6,4},{1,7},{3,1},{5,3},{7,5},{8,14},{10,8},{12,... | collective-permute-start | bytes 36872 | tf_op jit(solution)/shard_map/ppermute | solution.py:37
  12.4 0.8 collective-permute-start.4
  13.2 0.9 collective-permute-start.3
  14.1 0.6 pad_add_fusion.1.meta
  14.7 3.0 %collective-permute-done.4 = f32[3,1024]{1,0:T(4,128)S(1)} collective-permute-done((f32[3,1024]{1,0:T(4,128)S(1)}, f32[3,1024]{1,0:T(4,128)S(1)}, u32[]{:S(2)}, u32[]{:S(2)}) %collective-permute-start.4) | collective-permute-done | bytes 12320 | tf_op jit(solution)/shard_map/ppermute | solution.py:37
  17.6 0.5 collective-permute-done.3
  18.2 0.6 pad_maximum_fusion.1.stats
  18.8 8.1 %standardize.1 = (bf16[1280,1024]{1,0:T(8,128)(2,1)}, bf16[2,8,64,1280]{3,2,1,0:T(8,128)(2,1)}) custom-call(s32[4]{0:T(128)} %pad_add_fusion.1.meta, bf16[1280,1024]{1,0:T(8,128)(2,1)} %dosage.1, s32[1280,1024]{1,0:T(8,128)} %observed.1, f32[2,1024]{1,0:T(2,128)} %pad_maximum_fusion.1.stats), custom_call_target="tpu_custom_call" | custom-call | flops 1024 | bytes 1024 | tf_op jit(solution)/shard_map/standardize/pallas_call | solution.py:86
  26.9 2.9 %collective-permute-start.8 = (bf16[2,8,64,1280]{3,2,1,0:T(8,128)(2,1)}, bf16[2,8,64,1280]{3,2,1,0:T(8,128)(2,1)S(1)}, u32[]{:S(2)}, u32[]{:S(2)}) collective-permute-start(bf16[2,8,64,1280]{3,2,1,0:T(8,128)(2,1)} %get-tuple-element.40), channel_id=1, source_target_pairs={{0,16},{16,0},{32,48},{48,32},{64,80},{80,64},{96,112},{112,96},{1... | collective-permute-start | bytes 7864328 | tf_op jit(solution)/shard_map/ppermute | solution.py:378
  29.8 2.0 collective-permute-start.7
  31.9 0.2 collective-permute-done.6.zed.right_b.zed_b
  32.0 1.5 copy-done.1
  33.6 6.7 %turn.1 = bf16[8,64,1280]{2,1,0:T(8,128)(2,1)} custom-call(s32[4]{0:T(128)} %pad_add_fusion.1.meta, bf16[1280,1024]{1,0:T(8,128)(2,1)} %copy-done.1), custom_call_target="tpu_custom_call" | custom-call | flops 1024 | bytes 1024 | tf_op jit(solution)/shard_map/turn/pallas_call | solution.py:120
  40.3 7.3 %own.1 = f32[8,64,1024]{2,1,0:T(8,128)} custom-call(s32[4]{0:T(128)} %pad_add_fusion.1.meta, bf16[1024,1280]{1,0:T(8,128)(2,1)} %bitcast.21, bf16[512,1280]{1,0:T(8,128)(2,1)} %bitcast.19, bf16[1280,1024]{1,0:T(8,128)(2,1)} %get-tuple-element.41.right_a.zed_a, bf16[1280,1024]{1,0:T(8,128)(2,1)} %copy-done.1), custom_call_target="tpu_custom_call" | custom-call | flops 1024 | bytes 1024 | tf_op jit(solution)/shard_map/own/pallas_call | solution.py:142
  47.6 31.4 %all_to_all.15.refs_0_ = f32[4,2,64,1024]{3,2,1,0:T(8,128)} all-to-all(f32[4,2,64,1024]{3,2,1,0:T(8,128)} %bitcast.23), channel_id=1, replica_groups=mesh['z'=8,'yh'=2,'yl'=2,'x'=4,'core'=2] {'x'}, dimensions={0} | all-to-all | bytes 4194304 | tf_op jit(solution)/shard_map/all_to_all | solution.py:257
  78.9 3.1 %add.104 = (f32[64,1024]{1,0:T(8,128)}, f32[64,1024]{1,0:T(8,128)}) custom-call(s32[4]{0:T(128)} %pad_add_fusion.1.meta, f32[4,2,64,1024]{3,2,1,0:T(8,128)} %all_to_all.15.refs_0_), custom_call_target="tpu_custom_call" | custom-call | flops 1024 | bytes 1024 | tf_op jit(solution)/shard_map/add/pallas_call | solution.py:239
  82.1 5.8 %collective-permute-done.8 = bf16[2,8,64,1280]{3,2,1,0:T(8,128)(2,1)S(1)} collective-permute-done((bf16[2,8,64,1280]{3,2,1,0:T(8,128)(2,1)}, bf16[2,8,64,1280]{3,2,1,0:T(8,128)(2,1)S(1)}, u32[]{:S(2)}, u32[]{:S(2)}) %collective-permute-start.8) | collective-permute-done | bytes 2621472 | tf_op jit(solution)/shard_map/ppermute | solution.py:378
  87.9 3.2 %collective-permute-done.7.right_a.near_a = bf16[1280,1024]{1,0:T(8,128)(2,1)S(1)} collective-permute-done((bf16[1280,1024]{1,0:T(8,128)(2,1)}, bf16[1280,1024]{1,0:T(8,128)(2,1)S(1)}, u32[]{:S(2)}, u32[]{:S(2)}) %collective-permute-start.7) | collective-permute-done | bytes 2621472 | tf_op jit(solution)/shard_map/ppermute | solution.py:379
  91.1 0.1 slice_bitcast_fusion
  91.2 0.6 collective-permute-start.10
  91.8 6.1 %collective-permute-done.10 = bf16[8,64,1280]{2,1,0:T(8,128)(2,1)S(1)} collective-permute-done((bf16[8,64,1280]{2,1,0:T(8,128)(2,1)S(1)}, bf16[8,64,1280]{2,1,0:T(8,128)(2,1)S(1)}, u32[]{:S(2)}, u32[]{:S(2)}) %collective-permute-start.10) | collective-permute-done | bytes 1310752 | tf_op jit(solution)/shard_map/ppermute | solution.py:377
  97.9 1.1 copy-done.5
  99.0 1.6 copy-done.3
  100.6 7.4 %along.1 = (f32[2,64,1024]{2,1,0:T(8,128)}, f32[2,64,1024]{2,1,0:T(8,128)}, f32[2,64,1024]{2,1,0:T(8,128)}, f32[2,64,1024]{2,1,0:T(8,128)}) custom-call(s32[4]{0:T(128)} %pad_add_fusion.1.meta, bf16[1024,1280]{1,0:T(8,128)(2,1)} %bitcast.22, bf16[512,1280]{1,0:T(8,128)(2,1)} %bitcast.20, bf16[1280,1024]{1,0:T(8,128)(2,1)} %copy-done.2, ...), custom_call_target="tpu_custom_call" | custom-call | flops 1024 | bytes 1024 | tf_op jit(solution)/shard_map/along/pallas_call | solution.py:174
  108.0 1.8 collective-permute-start.12
  109.8 2.4 %collective-permute-start.13 = (f32[2,64,1024]{2,1,0:T(8,128)}, f32[2,64,1024]{2,1,0:T(8,128)S(1)}, u32[]{:S(2)}, u32[]{:S(2)}) collective-permute-start(f32[2,64,1024]{2,1,0:T(8,128)} %get-tuple-element.50), channel_id=1, source_target_pairs={{0,6},{2,0},{4,2},{6,4},{1,7},{3,1},{5,3},{7,5},{8,14},{10,8},{12,... | collective-permute-start | bytes 1572872 | tf_op jit(solution)/shard_map/ppermute | solution.py:263
  112.2 9.1 %across.1 = (f32[2,64,1024]{2,1,0:T(8,128)}, f32[2,64,1024]{2,1,0:T(8,128)}, f32[2,64,1024]{2,1,0:T(8,128)}, f32[2,64,1024]{2,1,0:T(8,128)}) custom-call(s32[4]{0:T(128)} %pad_add_fusion.1.meta, bf16[1024,1280]{1,0:T(8,128)(2,1)} %bitcast.24, bf16[512,1280]{1,0:T(8,128)(2,1)} %bitcast.25, bf16[1280,1024]{1,0:T(8,128)(2,1)} %copy-done.2, ...), custom_call_target="tpu_custom_call" | custom-call | flops 1024 | bytes 1024 | tf_op jit(solution)/shard_map/across/pallas_call | solution.py:205
  121.3 2.1 %collective-permute-start.17 = (f32[2,64,1024]{2,1,0:T(8,128)}, f32[2,64,1024]{2,1,0:T(8,128)S(1)}, u32[]{:S(2)}, u32[]{:S(2)}) collective-permute-start(f32[2,64,1024]{2,1,0:T(8,128)} %get-tuple-element.62), channel_id=1, source_target_pairs={{0,4},{2,6},{4,0},{6,2},{1,5},{3,7},{5,1},{7,3},{8,12},{10,14},{12... | collective-permute-start | bytes 1572872 | tf_op jit(solution)/shard_map/ppermute | solution.py:263
  123.4 12.0 %collective-permute-done.11.refs_1_ = f32[2,64,1024]{2,1,0:T(8,128)S(1)} collective-permute-done((f32[2,64,1024]{2,1,0:T(8,128)}, f32[2,64,1024]{2,1,0:T(8,128)S(1)}, u32[]{:S(2)}, u32[]{:S(2)}) %collective-permute-start.11) | collective-permute-done | bytes 524320 | tf_op jit(solution)/shard_map/ppermute | solution.py:263
  135.4 0.9 collective-permute-done.13.refs_3_
  136.4 0.0 copy-done.11
  136.4 0.8 copy-done.12
  137.2 3.1 %add.105 = (f32[64,1024]{1,0:T(8,128)}, f32[64,1024]{1,0:T(8,128)}) custom-call(s32[4]{0:T(128)} %pad_add_fusion.1.meta, f32[2,64,1024]{2,1,0:T(8,128)} %get-tuple-element.54.refs_0_, f32[2,64,1024]{2,1,0:T(8,128)} %copy-done.10, f32[2,64,1024]{2,1,0:T(8,128)} %copy-done.11, f32[2,64,1024]{2,1,0:T(8,128)} %copy-done.12), custom_call_target="tpu_custom_call" | custom-call | flops 1024 | bytes 1024 | tf_op jit(solution)/shard_map/add/pallas_call | solution.py:239
  140.2 0.3 collective-permute-start.14
  140.6 1.7 collective-permute-start.19
  142.3 7.4 %collective-permute-done.14.refs_1_ = f32[64,1024]{1,0:T(8,128)S(1)} collective-permute-done((f32[64,1024]{1,0:T(8,128)}, f32[64,1024]{1,0:T(8,128)S(1)}, u32[]{:S(2)}, u32[]{:S(2)}) %collective-permute-start.14) | collective-permute-done | bytes 262176 | tf_op jit(solution)/shard_map/ppermute | solution.py:252
  149.7 0.7 copy-done.13
  150.4 2.5 %gather.8 = (f32[64,1024]{1,0:T(8,128)}, f32[16,32,128]{2,1,0:T(8,128)}) custom-call(s32[4]{0:T(128)} %pad_add_fusion.1.meta, f32[64,1024]{1,0:T(8,128)} %get-tuple-element.58.refs_0_, f32[64,1024]{1,0:T(8,128)} %copy-done.13), custom_call_target="tpu_custom_call" | custom-call | flops 1024 | bytes 1024 | tf_op jit(solution)/shard_map/gather/pallas_call | solution.py:287
  152.9 4.1 %all-to-all-start.1 = ((f32[16,32,128]{2,1,0:T(8,128)}), f32[16,32,128]{2,1,0:T(8,128)S(1)}, u32[]{:S(2)}, u32[]{:S(2)}) async-start(f32[16,32,128]{2,1,0:T(8,128)} %get-tuple-element.60), calls=%async_computation.1 | async-start | bytes 524288 | tf_op jit(solution)/shard_map/all_to_all | solution.py:303
  157.0 0.0 collective-permute-done.16.refs_1_
  157.1 0.7 collective-permute-done.18.refs_3_
  157.7 7.2 %all-to-all-done.1 = f32[16,32,128]{2,1,0:T(8,128)S(1)} async-done(((f32[16,32,128]{2,1,0:T(8,128)}), f32[16,32,128]{2,1,0:T(8,128)S(1)}, u32[]{:S(2)}, u32[]{:S(2)}) %all-to-all-start.1) | async-done | bytes 262176 | tf_op jit(solution)/shard_map/all_to_all | solution.py:303
  164.9 3.1 %add.106 = (f32[64,1024]{1,0:T(8,128)}, f32[64,1024]{1,0:T(8,128)}) custom-call(s32[4]{0:T(128)} %pad_add_fusion.1.meta, f32[2,64,1024]{2,1,0:T(8,128)} %get-tuple-element.65.refs_0_, f32[2,64,1024]{2,1,0:T(8,128)} %copy-done.7, f32[2,64,1024]{2,1,0:T(8,128)} %copy-done.8, f32[2,64,1024]{2,1,0:T(8,128)} %copy-done.9), custom_call_target="tpu_custom_call" | custom-call | flops 1024 | bytes 1024 | tf_op jit(solution)/shard_map/add/pallas_call | solution.py:239
  168.0 0.6 collective-permute-start.20
  168.6 5.0 %collective-permute-start.15 = (f32[512,128]{1,0:T(8,128)S(1)}, f32[512,128]{1,0:T(8,128)S(1)}, u32[]{:S(2)}, u32[]{:S(2)}) collective-permute-start(f32[512,128]{1,0:T(8,128)S(1)} %bitcast.28), channel_id=1, source_target_pairs={{0,32},{32,64},{64,96},{96,128},{128,160},{160,192},{192,224},{48,... | collective-permute-start | bytes 786440 | tf_op jit(solution)/shard_map/ppermute | solution.py:390
  173.6 2.5 %collective-permute-done.20.refs_1_ = f32[64,1024]{1,0:T(8,128)S(1)} collective-permute-done((f32[64,1024]{1,0:T(8,128)}, f32[64,1024]{1,0:T(8,128)S(1)}, u32[]{:S(2)}, u32[]{:S(2)}) %collective-permute-start.20) | collective-permute-done | bytes 262176 | tf_op jit(solution)/shard_map/ppermute | solution.py:252
  176.1 0.7 copy-done.14
  176.8 2.5 %gather.9 = (f32[64,1024]{1,0:T(8,128)}, f32[16,32,128]{2,1,0:T(8,128)}) custom-call(s32[4]{0:T(128)} %pad_add_fusion.1.meta, f32[64,1024]{1,0:T(8,128)} %get-tuple-element.69.refs_0_, f32[64,1024]{1,0:T(8,128)} %copy-done.14), custom_call_target="tpu_custom_call" | custom-call | flops 1024 | bytes 1024 | tf_op jit(solution)/shard_map/gather/pallas_call | solution.py:287
  179.4 1.1 collective-permute-start.21
  180.5 3.5 %all-to-all-start.2 = ((f32[16,32,128]{2,1,0:T(8,128)}), f32[16,32,128]{2,1,0:T(8,128)S(1)}, u32[]{:S(2)}, u32[]{:S(2)}) async-start(f32[16,32,128]{2,1,0:T(8,128)} %get-tuple-element.71), calls=%async_computation.2 | async-start | bytes 524288 | tf_op jit(solution)/shard_map/all_to_all | solution.py:303
  184.1 0.6 dynamic_slice.3
  184.7 0.6 gather_fusion
  185.3 6.6 %all-to-all-done.2 = f32[16,32,128]{2,1,0:T(8,128)S(1)} async-done(((f32[16,32,128]{2,1,0:T(8,128)}), f32[16,32,128]{2,1,0:T(8,128)S(1)}, u32[]{:S(2)}, u32[]{:S(2)}) %all-to-all-start.2) | async-done | bytes 262176 | tf_op jit(solution)/shard_map/all_to_all | solution.py:303
  191.9 4.6 %collective-permute-start.22 = (f32[512,128]{1,0:T(8,128)S(1)}, f32[512,128]{1,0:T(8,128)S(1)}, u32[]{:S(2)}, u32[]{:S(2)}) collective-permute-start(f32[512,128]{1,0:T(8,128)S(1)} %bitcast.26), channel_id=1, source_target_pairs={{0,32},{32,64},{64,96},{96,128},{128,160},{160,192},{192,224},{1,3... | collective-permute-start | bytes 786440 | tf_op jit(solution)/shard_map/ppermute | solution.py:394
  196.5 0.7 and_convert_fusion
  197.1 0.6 pad_add_fusion.flags
  197.7 4.2 %collective-permute-done.22.near = f32[512,128]{1,0:T(8,128)S(1)} collective-permute-done((f32[512,128]{1,0:T(8,128)S(1)}, f32[512,128]{1,0:T(8,128)S(1)}, u32[]{:S(2)}, u32[]{:S(2)}) %collective-permute-start.22) | collective-permute-done | bytes 262176 | tf_op jit(solution)/shard_map/ppermute | solution.py:394
  201.9 0.7 copy-done.18
  202.6 3.9 %assemble.1 = f32[64,5120]{1,0:T(8,128)} custom-call(s32[6]{0:T(128)} %pad_add_fusion.flags, f32[512,128]{1,0:T(8,128)} %copy-done.16, f32[512,128]{1,0:T(8,128)} %copy-done.18, f32[512,128]{1,0:T(8,128)} %bitcast.27, f32[64,1024]{1,0:T(8,128)} %get-tuple-element.74.rows2, f32[64,1024]{1,0:T(8,128)} %copy-done.17, f32[64,1024]{1,0:T(8,128)} %get-tuple-element.42.rows0_a, ...), custom_call_target="tpu_custom_call" | custom-call | flops 1024 | bytes 1024 | tf_op jit(solution)/shard_map/assemble/pallas_call | solution.py:331
  (52 shorter events, 0.2 us)
Async XLA Ops:
  4.7 3.8 %collective-permute-start.1 = (f32[3,1024]{1,0:T(4,128)S(1)}, f32[3,1024]{1,0:T(4,128)S(1)}, u32[]{:S(2)}, u32[]{:S(2)}) collective-permute-start(f32[3,1024]{1,0:T(4,128)S(1)} %pad_maximum_fusion), channel_id=1, source_target_pairs={{0,8},{1,9},{8,0},{9,1},{2,10},{3,11},{10,2},{11,3},{4,12},{5,13},... | collective-permute-start | bytes 36872 | tf_op jit(solution)/shard_map/ppermute | solution.py:33
  6.3 3.2 %collective-permute-start.2 = (f32[3,1024]{1,0:T(4,128)S(1)}, f32[3,1024]{1,0:T(4,128)S(1)}, u32[]{:S(2)}, u32[]{:S(2)}) collective-permute-start(f32[3,1024]{1,0:T(4,128)S(1)} %pad_maximum_fusion), channel_id=1, source_target_pairs={{0,9},{1,8},{8,1},{9,0},{2,11},{3,10},{10,3},{11,2},{4,13},{5,12},... | collective-permute-start | bytes 36872 | tf_op jit(solution)/shard_map/ppermute | solution.py:33
  6.3 3.2 %collective-permute-start = (f32[3,1024]{1,0:T(4,128)S(1)}, f32[3,1024]{1,0:T(4,128)S(1)}, u32[]{:S(2)}, u32[]{:S(2)}) collective-permute-start(f32[3,1024]{1,0:T(4,128)S(1)} %pad_maximum_fusion), channel_id=1, source_target_pairs={{0,1},{1,0},{8,9},{9,8},{2,3},{3,2},{10,11},{11,10},{4,5},{5,4},{1... | collective-permute-start | bytes 36872 | tf_op jit(solution)/shard_map/ppermute | solution.py:33
  9.5 5.1 %collective-permute-start.5 = (f32[3,1024]{1,0:T(4,128)S(1)}, f32[3,1024]{1,0:T(4,128)S(1)}, u32[]{:S(2)}, u32[]{:S(2)}) collective-permute-start(f32[3,1024]{1,0:T(4,128)S(1)} %add_add_fusion.1), channel_id=1, source_target_pairs={{0,6},{2,0},{4,2},{6,4},{1,7},{3,1},{5,3},{7,5},{8,14},{10,8},{12,... | collective-permute-start | bytes 36872 | tf_op jit(solution)/shard_map/ppermute | solution.py:37
  12.4 5.2 %collective-permute-start.4 = (f32[3,1024]{1,0:T(4,128)S(1)}, f32[3,1024]{1,0:T(4,128)S(1)}, u32[]{:S(2)}, u32[]{:S(2)}) collective-permute-start(f32[3,1024]{1,0:T(4,128)S(1)} %add_add_fusion.1), channel_id=1, source_target_pairs={{0,4},{2,6},{4,0},{6,2},{1,5},{3,7},{5,1},{7,3},{8,12},{10,14},{12... | collective-permute-start | bytes 36872 | tf_op jit(solution)/shard_map/ppermute | solution.py:37
  13.2 4.9 %collective-permute-start.3 = (f32[3,1024]{1,0:T(4,128)S(1)}, f32[3,1024]{1,0:T(4,128)S(1)}, u32[]{:S(2)}, u32[]{:S(2)}) collective-permute-start(f32[3,1024]{1,0:T(4,128)S(1)} %add_add_fusion.1), channel_id=1, source_target_pairs={{0,2},{2,4},{4,6},{6,0},{1,3},{3,5},{5,7},{7,1},{8,10},{10,12},{12... | collective-permute-start | bytes 36872 | tf_op jit(solution)/shard_map/ppermute | solution.py:37
  26.9 5.1 %collective-permute-start.6 = (bf16[1280,1024]{1,0:T(8,128)(2,1)}, bf16[1280,1024]{1,0:T(8,128)(2,1)S(1)}, u32[]{:S(2)}, u32[]{:S(2)}) collective-permute-start(bf16[1280,1024]{1,0:T(8,128)(2,1)} %get-tuple-element.41.right_a.zed_a), channel_id=1, source_target_pairs={{0,1},{1,0},{2,3},{3,2},{4,5},{5,4},{6,7},{7,6},{8,9},{9,8},{10,11... | collective-permute-start | bytes 7864328 | tf_op jit(solution)/shard_map/ppermute | solution.py:377
  26.9 61.0 %collective-permute-start.8 = (bf16[2,8,64,1280]{3,2,1,0:T(8,128)(2,1)}, bf16[2,8,64,1280]{3,2,1,0:T(8,128)(2,1)S(1)}, u32[]{:S(2)}, u32[]{:S(2)}) collective-permute-start(bf16[2,8,64,1280]{3,2,1,0:T(8,128)(2,1)} %get-tuple-element.40), channel_id=1, source_target_pairs={{0,16},{16,0},{32,48},{48,32},{64,80},{80,64},{96,112},{112,96},{1... | collective-permute-start | bytes 7864328 | tf_op jit(solution)/shard_map/ppermute | solution.py:378
  29.8 61.2 %collective-permute-start.7 = (bf16[1280,1024]{1,0:T(8,128)(2,1)}, bf16[1280,1024]{1,0:T(8,128)(2,1)S(1)}, u32[]{:S(2)}, u32[]{:S(2)}) collective-permute-start(bf16[1280,1024]{1,0:T(8,128)(2,1)} %get-tuple-element.41.right_a.zed_a), channel_id=1, source_target_pairs={{32,0},{64,32},{96,64},{128,96},{160,128},{192,160},{224,192},{16,... | collective-permute-start | bytes 7864328 | tf_op jit(solution)/shard_map/ppermute | solution.py:379
  32.0 1.5 copy-start.1
  87.9 24.3 %copy-start.4 = (bf16[2,8,64,1280]{3,2,1,0:T(8,128)(2,1)}, bf16[2,8,64,1280]{3,2,1,0:T(8,128)(2,1)S(1)}, u32[]{:S(2)}) copy-start(bf16[2,8,64,1280]{3,2,1,0:T(8,128)(2,1)S(1)} %collective-permute-done.8) | copy-start | bytes 7864324
  91.1 7.9 %copy-start.2 = (bf16[1280,1024]{1,0:T(8,128)(2,1)}, bf16[1280,1024]{1,0:T(8,128)(2,1)S(1)}, u32[]{:S(2)}) copy-start(bf16[1280,1024]{1,0:T(8,128)(2,1)S(1)} %collective-permute-done.7.right_a.near_a) | copy-start | bytes 7864324
  91.1 7.9 %collective-permute-start.9 = (bf16[1280,1024]{1,0:T(8,128)(2,1)S(1)}, bf16[1280,1024]{1,0:T(8,128)(2,1)S(1)}, u32[]{:S(2)}, u32[]{:S(2)}) collective-permute-start(bf16[1280,1024]{1,0:T(8,128)(2,1)S(1)} %collective-permute-done.7.right_a.near_a), channel_id=1, source_target_pairs={{0,1},{1,0},{2,3},{3,2},{4,5},{5,4},{6,7},{7,6},{8,9},{9,8},{10,11... | collective-permute-start | bytes 7864328 | tf_op jit(solution)/shard_map/ppermute | solution.py:377
  91.2 6.7 %collective-permute-start.10 = (bf16[8,64,1280]{2,1,0:T(8,128)(2,1)S(1)}, bf16[8,64,1280]{2,1,0:T(8,128)(2,1)S(1)}, u32[]{:S(2)}, u32[]{:S(2)}) collective-permute-start(bf16[8,64,1280]{2,1,0:T(8,128)(2,1)S(1)} %slice_bitcast_fusion), channel_id=1, source_target_pairs={{0,1},{1,0},{2,3},{3,2},{4,5},{5,4},{6,7},{7,6},{8,9},{9,8},{10,11... | collective-permute-start | bytes 3932168 | tf_op jit(solution)/shard_map/ppermute | solution.py:377
  97.9 1.1 copy-start.5
  99.0 1.6 copy-start.3
  108.0 27.4 %collective-permute-start.11 = (f32[2,64,1024]{2,1,0:T(8,128)}, f32[2,64,1024]{2,1,0:T(8,128)S(1)}, u32[]{:S(2)}, u32[]{:S(2)}) collective-permute-start(f32[2,64,1024]{2,1,0:T(8,128)} %get-tuple-element.48), channel_id=1, source_target_pairs={{0,2},{2,4},{4,6},{6,0},{1,3},{3,5},{5,7},{7,1},{8,10},{10,12},{12... | collective-permute-start | bytes 1572872 | tf_op jit(solution)/shard_map/ppermute | solution.py:263
  108.0 27.4 %collective-permute-start.12 = (f32[2,64,1024]{2,1,0:T(8,128)}, f32[2,64,1024]{2,1,0:T(8,128)S(1)}, u32[]{:S(2)}, u32[]{:S(2)}) collective-permute-start(f32[2,64,1024]{2,1,0:T(8,128)} %get-tuple-element.49), channel_id=1, source_target_pairs={{0,4},{2,6},{4,0},{6,2},{1,5},{3,7},{5,1},{7,3},{8,12},{10,14},{12... | collective-permute-start | bytes 1572872 | tf_op jit(solution)/shard_map/ppermute | solution.py:263
  109.8 26.5 %collective-permute-start.13 = (f32[2,64,1024]{2,1,0:T(8,128)}, f32[2,64,1024]{2,1,0:T(8,128)S(1)}, u32[]{:S(2)}, u32[]{:S(2)}) collective-permute-start(f32[2,64,1024]{2,1,0:T(8,128)} %get-tuple-element.50), channel_id=1, source_target_pairs={{0,6},{2,0},{4,2},{6,4},{1,7},{3,1},{5,3},{7,5},{8,14},{10,8},{12,... | collective-permute-start | bytes 1572872 | tf_op jit(solution)/shard_map/ppermute | solution.py:263
  112.2 28.4 %copy-start.19 = (f32[64,1024]{1,0:T(8,128)S(1)}, f32[64,1024]{1,0:T(8,128)}, u32[]{:S(2)}) copy-start(f32[64,1024]{1,0:T(8,128)} %get-tuple-element.64) | copy-start | bytes 786436
  121.3 35.8 %collective-permute-start.16 = (f32[2,64,1024]{2,1,0:T(8,128)}, f32[2,64,1024]{2,1,0:T(8,128)S(1)}, u32[]{:S(2)}, u32[]{:S(2)}) collective-permute-start(f32[2,64,1024]{2,1,0:T(8,128)} %get-tuple-element.61), channel_id=1, source_target_pairs={{0,2},{2,4},{4,6},{6,0},{1,3},{3,5},{5,7},{7,1},{8,10},{10,12},{12... | collective-permute-start | bytes 1572872 | tf_op jit(solution)/shard_map/ppermute | solution.py:263
  121.3 35.7 %collective-permute-start.17 = (f32[2,64,1024]{2,1,0:T(8,128)}, f32[2,64,1024]{2,1,0:T(8,128)S(1)}, u32[]{:S(2)}, u32[]{:S(2)}) collective-permute-start(f32[2,64,1024]{2,1,0:T(8,128)} %get-tuple-element.62), channel_id=1, source_target_pairs={{0,4},{2,6},{4,0},{6,2},{1,5},{3,7},{5,1},{7,3},{8,12},{10,14},{12... | collective-permute-start | bytes 1572872 | tf_op jit(solution)/shard_map/ppermute | solution.py:263
  135.4 0.9 copy-start.10
  135.4 22.3 %collective-permute-start.18 = (f32[2,64,1024]{2,1,0:T(8,128)}, f32[2,64,1024]{2,1,0:T(8,128)S(1)}, u32[]{:S(2)}, u32[]{:S(2)}) collective-permute-start(f32[2,64,1024]{2,1,0:T(8,128)} %get-tuple-element.63), channel_id=1, source_target_pairs={{0,6},{2,0},{4,2},{6,4},{1,7},{3,1},{5,3},{7,5},{8,14},{10,8},{12,... | collective-permute-start | bytes 1572872 | tf_op jit(solution)/shard_map/ppermute | solution.py:263
  135.4 1.0 copy-start.11
  136.4 0.8 copy-start.12
  140.2 43.8 %copy-start = (s32[16]{0:T(128)S(1)}, s32[16]{0:T(128)}, u32[]{:S(2)}) copy-start(s32[16]{0:T(128)} %param.5) | copy-start | bytes 196
  140.2 9.5 %collective-permute-start.14 = (f32[64,1024]{1,0:T(8,128)}, f32[64,1024]{1,0:T(8,128)S(1)}, u32[]{:S(2)}, u32[]{:S(2)}) collective-permute-start(f32[64,1024]{1,0:T(8,128)} %get-tuple-element.59), channel_id=1, source_target_pairs={{0,8},{8,0},{1,9},{9,1},{2,10},{10,2},{3,11},{11,3},{4,12},{12,4},... | collective-permute-start | bytes 786440 | tf_op jit(solution)/shard_map/ppermute | solution.py:252
  140.6 16.5 %collective-permute-start.19 = (f32[64,1024]{1,0:T(8,128)S(1)}, f32[64,1024]{1,0:T(8,128)S(1)}, u32[]{:S(2)}, u32[]{:S(2)}) collective-permute-start(f32[64,1024]{1,0:T(8,128)S(1)} %copy-done.19), channel_id=1, source_target_pairs={{0,8},{8,0},{1,9},{9,1},{2,10},{10,2},{3,11},{11,3},{4,12},{12,4},... | collective-permute-start | bytes 786440 | tf_op jit(solution)/shard_map/ppermute | solution.py:252
  149.7 0.7 copy-start.13
  152.9 12.0 %all-to-all-start.1 = ((f32[16,32,128]{2,1,0:T(8,128)}), f32[16,32,128]{2,1,0:T(8,128)S(1)}, u32[]{:S(2)}, u32[]{:S(2)}) async-start(f32[16,32,128]{2,1,0:T(8,128)} %get-tuple-element.60), calls=%async_computation.1 | async-start | bytes 524288 | tf_op jit(solution)/shard_map/all_to_all | solution.py:303
  157.0 44.8 %copy-start.15 = (f32[64,1024]{1,0:T(8,128)}, f32[64,1024]{1,0:T(8,128)S(1)}, u32[]{:S(2)}) copy-start(f32[64,1024]{1,0:T(8,128)S(1)} %collective-permute-done.19.rows0_b) | copy-start | bytes 786436
  157.1 7.8 %copy-start.7 = (f32[2,64,1024]{2,1,0:T(8,128)}, f32[2,64,1024]{2,1,0:T(8,128)S(1)}, u32[]{:S(2)}) copy-start(f32[2,64,1024]{2,1,0:T(8,128)S(1)} %collective-permute-done.16.refs_1_) | copy-start | bytes 1572868
  157.1 7.8 %copy-start.8 = (f32[2,64,1024]{2,1,0:T(8,128)}, f32[2,64,1024]{2,1,0:T(8,128)S(1)}, u32[]{:S(2)}) copy-start(f32[2,64,1024]{2,1,0:T(8,128)S(1)} %collective-permute-done.17.refs_2_) | copy-start | bytes 1572868
  157.7 7.2 %copy-start.9 = (f32[2,64,1024]{2,1,0:T(8,128)}, f32[2,64,1024]{2,1,0:T(8,128)S(1)}, u32[]{:S(2)}) copy-start(f32[2,64,1024]{2,1,0:T(8,128)S(1)} %collective-permute-done.18.refs_3_) | copy-start | bytes 1572868
  168.0 8.1 %collective-permute-start.20 = (f32[64,1024]{1,0:T(8,128)}, f32[64,1024]{1,0:T(8,128)S(1)}, u32[]{:S(2)}, u32[]{:S(2)}) collective-permute-start(f32[64,1024]{1,0:T(8,128)} %get-tuple-element.70), channel_id=1, source_target_pairs={{0,8},{8,0},{1,9},{9,1},{2,10},{10,2},{3,11},{11,3},{4,12},{12,4},... | collective-permute-start | bytes 786440 | tf_op jit(solution)/shard_map/ppermute | solution.py:252
  168.6 16.7 %collective-permute-start.15 = (f32[512,128]{1,0:T(8,128)S(1)}, f32[512,128]{1,0:T(8,128)S(1)}, u32[]{:S(2)}, u32[]{:S(2)}) collective-permute-start(f32[512,128]{1,0:T(8,128)S(1)} %bitcast.28), channel_id=1, source_target_pairs={{0,32},{32,64},{64,96},{96,128},{128,160},{160,192},{192,224},{48,... | collective-permute-start | bytes 786440 | tf_op jit(solution)/shard_map/ppermute | solution.py:390
  176.1 0.7 copy-start.14
  179.4 12.5 %collective-permute-start.21 = (f32[64,1024]{1,0:T(8,128)}, f32[64,1024]{1,0:T(8,128)S(1)}, u32[]{:S(2)}, u32[]{:S(2)}) collective-permute-start(f32[64,1024]{1,0:T(8,128)} %get-tuple-element.72), channel_id=1, source_target_pairs={{0,16},{16,0},{32,48},{48,32},{64,80},{80,64},{96,112},{112,96},{1... | collective-permute-start | bytes 786440 | tf_op jit(solution)/shard_map/ppermute | solution.py:393
  180.5 11.4 %all-to-all-start.2 = ((f32[16,32,128]{2,1,0:T(8,128)}), f32[16,32,128]{2,1,0:T(8,128)S(1)}, u32[]{:S(2)}, u32[]{:S(2)}) async-start(f32[16,32,128]{2,1,0:T(8,128)} %get-tuple-element.71), calls=%async_computation.2 | async-start | bytes 524288 | tf_op jit(solution)/shard_map/all_to_all | solution.py:303
  185.3 16.6 %copy-start.16 = (f32[512,128]{1,0:T(8,128)}, f32[512,128]{1,0:T(8,128)S(1)}, u32[]{:S(2)}) copy-start(f32[512,128]{1,0:T(8,128)S(1)} %collective-permute-done.15.far) | copy-start | bytes 786436
  191.9 10.0 %copy-start.6 = (f32[16,32,128]{2,1,0:T(8,128)}, f32[16,32,128]{2,1,0:T(8,128)S(1)}, u32[]{:S(2)}) copy-start(f32[16,32,128]{2,1,0:T(8,128)S(1)} %all-to-all-done.2) | copy-start | bytes 786436
  191.9 10.0 %copy-start.17 = (f32[64,1024]{1,0:T(8,128)}, f32[64,1024]{1,0:T(8,128)S(1)}, u32[]{:S(2)}) copy-start(f32[64,1024]{1,0:T(8,128)S(1)} %collective-permute-done.21.beside) | copy-start | bytes 786436
  191.9 10.0 %collective-permute-start.22 = (f32[512,128]{1,0:T(8,128)S(1)}, f32[512,128]{1,0:T(8,128)S(1)}, u32[]{:S(2)}, u32[]{:S(2)}) collective-permute-start(f32[512,128]{1,0:T(8,128)S(1)} %bitcast.26), channel_id=1, source_target_pairs={{0,32},{32,64},{64,96},{96,128},{128,160},{160,192},{192,224},{1,3... | collective-permute-start | bytes 786440 | tf_op jit(solution)/shard_map/ppermute | solution.py:394
  201.9 0.7 copy-start.18
